TPU v7x, 512 devices: a whole 4x8x8 slice. The times are simulated.
512 devices in a mesh: group: 16 (over z, core), member: 32 (over y, x).
Axes of the slice: x: 4, y: 8, z: 8, core: 2. Of those that a mesh axis runs over, the one named last changes fastest.
Arguments:
- tokens: bfloat16 [8192, 7168], P('group', 'member'), may hold values from -6 to 6
- grad_output: bfloat16 [8192, 7168], P('group', 'member'), may hold values from -6 to 6
- gate_prob: bfloat16 [8192, 16], P('group'), may hold values from 0.099609375 to 1
- w_gate: bfloat16 [16, 7168, 1024], P('group', 'member'), may hold values from -0.0625 to 0.0625
- w_up: bfloat16 [16, 7168, 1024], P('group', 'member'), may hold values from -0.0625 to 0.0625
- w_down: bfloat16 [16, 1024, 7168], P('group', None, 'member'), may hold values from -0.1875 to 0.1875
- expert_slot: int32 [16], replicated, may hold values from 0 to 15, each once
- block_counts: int32 [16, 16], replicated, may hold values from 0 to 10, as said below
- block_lists: int32 [16, 16, 10], P('group'), may hold values from 0 to 15, as said below
Outputs:
- layer_output: bfloat16 [8192, 7168], P('group', 'member')
- grad_input: bfloat16 [8192, 7168], P('group', 'member')
- grad_w_gate: bfloat16 [16, 7168, 1024], P('group', 'member')
- grad_w_up: bfloat16 [16, 7168, 1024], P('group', 'member')
- grad_w_down: bfloat16 [16, 1024, 7168], P('group', None, 'member')
Inputs may be any that keep to these rules, and one draw needn't show every extreme that they name: `block_counts`: each group sends blocks to 1 to 2 experts and some group to exactly 2; each expert receives blocks from 1 to 2 groups and some expert from exactly 2; some count equals 10. `block_lists`: the first block_counts[g, e] entries of a list are distinct blocks of group g; later entries are block numbers that play no part. `expert_slot`: a permutation of the slots; slot s lies on group s.
All inputs are finite; a program needn't handle non-finite values.
Results may differ from a plain program's by a relative error of at most 0.034.
Values may be sent and summed in bfloat16 or wider, within the bound.
No kernel may reach another device: no remote copies, remote signals or barrier semaphores. Data moves between devices by JAX's collectives and lax.ppermute only.
A program may use at most 64 MiB of HBM per device.

v0:
```python
import jax
import jax.numpy as jnp
from jax import lax
from jax.sharding import PartitionSpec as P

MAXE = 2
BLK = 32


def expert_pass(input_rows, rows_dy, rows_p, gate_w, up_w, down_w):
    form_in, form_out, form_back, form_dx = (
        "xjb,bxl->xjl",
        "wzq,wqi->wzi",
        "eph,ezh->epz",
        "bya,qba->byq",
    )
    part_gate = jnp.einsum(form_in, input_rows, gate_w, preferred_element_type=jnp.float32)
    part_up = jnp.einsum(form_in, input_rows, up_w, preferred_element_type=jnp.float32)
    gate, up = (
        lax.psum(part_gate.astype(jnp.bfloat16), "member").astype(jnp.float32),
        lax.psum(part_up.astype(jnp.bfloat16), "member").astype(jnp.float32),
    )
    sigma = jax.nn.sigmoid(gate)
    hidden_state = (gate * sigma * up).astype(jnp.bfloat16)
    outcome = (
        rows_p[:, :, None]
        * jnp.einsum(form_out, hidden_state, down_w, preferred_element_type=jnp.float32)
    ).astype(jnp.bfloat16)
    gradient_rows = (rows_p[:, :, None] * rows_dy.astype(jnp.float32)).astype(jnp.bfloat16)
    part_hidden = jnp.einsum(form_back, gradient_rows, down_w, preferred_element_type=jnp.float32)
    grad_hidden = lax.psum(part_hidden.astype(jnp.bfloat16), "member").astype(jnp.float32)
    gate_gradient = (grad_hidden * up * sigma * (1.0 + gate * (1.0 - sigma))).astype(jnp.bfloat16)
    up_gradient = (grad_hidden * gate * sigma).astype(jnp.bfloat16)
    rows_dx = (
        jnp.einsum(form_dx, gate_gradient, gate_w, preferred_element_type=jnp.float32)
        + jnp.einsum(form_dx, up_gradient, up_w, preferred_element_type=jnp.float32)
    ).astype(jnp.bfloat16)
    weight_gate = jnp.einsum(
        "tgw,tgs->wts", input_rows, gate_gradient, preferred_element_type=jnp.float32
    ).astype(jnp.bfloat16)
    weight_up = jnp.einsum(
        "tgw,tgs->wts", input_rows, up_gradient, preferred_element_type=jnp.float32
    ).astype(jnp.bfloat16)
    weight_down = jnp.einsum(
        "sui,sug->sig", hidden_state, gradient_rows, preferred_element_type=jnp.float32
    ).astype(jnp.bfloat16)
    return (outcome, rows_dx, weight_gate, weight_up, weight_down)


def gather_rows(blocked, listed, keep_rows):
    picked = jnp.take(blocked, listed, axis=0)
    return picked * keep_rows[:, :, None, None].astype(blocked.dtype)


def place_rows(pieces, listed, keep_rows, block_total):
    placing = (
        (listed[:, :, None] == jnp.arange(block_total, dtype=jnp.int32)[None, None, :])
        & (keep_rows[:, :, None] > 0)
    ).astype(jnp.bfloat16)
    return jnp.einsum("kbn,kbtd->ntd", placing, pieces, preferred_element_type=jnp.float32)


def body(
    tokens, grad_output, gate_prob, w_gate, w_up, w_down, expert_slot, block_counts, block_lists
):
    width_share = tokens.shape[1]
    hidden_total = w_gate.shape[2]
    group_total = lax.axis_size("group")
    piece_size = hidden_total // group_total
    block_total = tokens.shape[0] // BLK
    entry_total = block_lists.shape[2]
    row_total = entry_total * BLK
    experts_total = block_counts.shape[1]
    group_index = lax.axis_index("group")
    entry_ids = jnp.arange(entry_total, dtype=jnp.int32)
    group_ids = jnp.arange(group_total, dtype=jnp.int32)
    ranks_wanted = jnp.arange(MAXE, dtype=jnp.int32)
    tok_blocks = tokens.reshape(block_total, BLK, width_share)
    grad_blocks = grad_output.reshape(block_total, BLK, width_share)
    prob_blocks = gate_prob.reshape(block_total, BLK, experts_total)
    my_counts = lax.dynamic_index_in_dim(block_counts, group_index, 0, keepdims=False)
    my_lists = block_lists[0]
    in_use = (block_counts > 0).astype(jnp.int32)
    use_rank = jnp.cumsum(in_use, axis=1) - 1
    selected = in_use[:, None, :] * (use_rank[:, None, :] == ranks_wanted[None, :, None]).astype(
        jnp.int32
    )
    need_slot = jnp.sum(selected * expert_slot[None, None, :], axis=2)
    need_valid = jnp.sum(selected, axis=2)
    own_select = lax.dynamic_index_in_dim(selected, group_index, 0, keepdims=False)
    my_amount = jnp.sum(own_select * my_counts[None, :], axis=1)
    listed = jnp.sum(own_select[:, :, None] * my_lists[None, :, :], axis=1)
    keep_rows = (entry_ids[None, :] < my_amount[:, None]).astype(jnp.int32)
    input_rows = gather_rows(tok_blocks, listed, keep_rows).reshape(MAXE, row_total, width_share)
    rows_dy = gather_rows(grad_blocks, listed, keep_rows).reshape(MAXE, row_total, width_share)
    prob_rows = gather_rows(prob_blocks, listed, keep_rows)
    rows_p = jnp.sum(
        prob_rows.astype(jnp.float32) * own_select[:, None, None, :].astype(jnp.float32), axis=3
    ).reshape(MAXE, row_total)
    gate_spread, up_spread, down_spread = (
        lax.all_to_all(
            w_gate[0].reshape(width_share, group_total, piece_size),
            "group",
            split_axis=1,
            concat_axis=1,
            tiled=True,
        ),
        lax.all_to_all(
            w_up[0].reshape(width_share, group_total, piece_size),
            "group",
            split_axis=1,
            concat_axis=1,
            tiled=True,
        ),
        lax.all_to_all(
            w_down.reshape(1, group_total, piece_size * width_share),
            "group",
            split_axis=1,
            concat_axis=1,
            tiled=True,
        ),
    )
    slot_order = need_slot.T
    gate_sent = jnp.take(gate_spread, slot_order, axis=1)
    up_sent = jnp.take(up_spread, slot_order, axis=1)
    down_sent = jnp.take(down_spread, slot_order, axis=1)
    gate_got, up_got, down_got = (
        lax.all_to_all(gate_sent, "group", split_axis=2, concat_axis=2, tiled=True),
        lax.all_to_all(up_sent, "group", split_axis=2, concat_axis=2, tiled=True),
        lax.all_to_all(down_sent, "group", split_axis=2, concat_axis=2, tiled=True),
    )
    outcome, rows_dx, weight_gate, weight_up, weight_down = expert_pass(
        input_rows,
        rows_dy,
        rows_p,
        gate_got.reshape(width_share, MAXE, hidden_total),
        up_got.reshape(width_share, MAXE, hidden_total),
        down_got.reshape(MAXE, hidden_total, width_share),
    )
    back_gate, back_up, back_down = (
        lax.all_to_all(
            weight_gate.reshape(width_share, MAXE, group_total, piece_size),
            "group",
            split_axis=2,
            concat_axis=2,
            tiled=True,
        ),
        lax.all_to_all(
            weight_up.reshape(width_share, MAXE, group_total, piece_size),
            "group",
            split_axis=2,
            concat_axis=2,
            tiled=True,
        ),
        lax.all_to_all(
            weight_down.reshape(1, MAXE, group_total, piece_size * width_share),
            "group",
            split_axis=2,
            concat_axis=2,
            tiled=True,
        ),
    )
    slot_match = (
        (slot_order[:, :, None] == group_ids[None, None, :]) & (need_valid.T[:, :, None] > 0)
    ).astype(jnp.bfloat16)
    summed_gate = jnp.einsum(
        "dmgk,mgs->dsk", back_gate, slot_match, preferred_element_type=jnp.float32
    ).astype(jnp.bfloat16)
    summed_up = jnp.einsum(
        "dmgk,mgs->dsk", back_up, slot_match, preferred_element_type=jnp.float32
    ).astype(jnp.bfloat16)
    summed_down = jnp.einsum(
        "amgq,mgs->asq", back_down, slot_match, preferred_element_type=jnp.float32
    ).astype(jnp.bfloat16)
    home_gate, home_up, home_down = (
        lax.all_to_all(summed_gate, "group", split_axis=1, concat_axis=1, tiled=True),
        lax.all_to_all(summed_up, "group", split_axis=1, concat_axis=1, tiled=True),
        lax.all_to_all(summed_down, "group", split_axis=1, concat_axis=1, tiled=True),
    )
    grad_w_gate = home_gate.reshape(1, width_share, hidden_total)
    grad_w_up = home_up.reshape(1, width_share, hidden_total)
    grad_w_down = home_down.reshape(1, hidden_total, width_share)
    out_blocks = place_rows(
        outcome.reshape(MAXE, entry_total, BLK, width_share), listed, keep_rows, block_total
    )
    dx_blocks = place_rows(
        rows_dx.reshape(MAXE, entry_total, BLK, width_share), listed, keep_rows, block_total
    )
    layer_output = out_blocks.reshape(block_total * BLK, width_share).astype(jnp.bfloat16)
    grad_input = dx_blocks.reshape(block_total * BLK, width_share).astype(jnp.bfloat16)
    return (layer_output, grad_input, grad_w_gate, grad_w_up, grad_w_down)


def solution(mesh):
    in_specs = (
        P("group", "member"),
        P("group", "member"),
        P("group", None),
        P("group", "member", None),
        P("group", "member", None),
        P("group", None, "member"),
        P(),
        P(),
        P("group", None, None),
    )
    out_specs = (
        P("group", "member"),
        P("group", "member"),
        P("group", "member", None),
        P("group", "member", None),
        P("group", None, "member"),
    )
    return jax.shard_map(body, mesh=mesh, in_specs=in_specs, out_specs=out_specs, check_vma=False)
```

profile of v0, /device:TPU:1, one launch (start us, length us, event | category | flops | bytes accessed | tf_op | source)
XLA Modules:
  0.0 531.6 jit_solution(10994055985351064944)
XLA Ops:
  10.1 3.4 reduce.2
  14.7 12.0 %all-to-all-start.4 = ((bf16[16,2,7168]{2,1,0:T(2,128)(2,1)}), bf16[16,2,7168]{2,1,0:T(2,128)(2,1)S(1)}, u32[]{:S(2)}, u32[]{:S(2)}) async-start(bf16[16,2,7168]{2,1,0:T(2,128)(2,1)} %reshape.287), calls=%async_computation.4 | async-start | bytes 917504 | tf_op jit(solution)/shard_map/all_to_all | solution.py:115
  27.8 14.8 %all-to-all-done.4 = bf16[16,2,7168]{2,1,0:T(2,128)(2,1)S(1)} async-done(((bf16[16,2,7168]{2,1,0:T(2,128)(2,1)}), bf16[16,2,7168]{2,1,0:T(2,128)(2,1)S(1)}, u32[]{:S(2)}, u32[]{:S(2)}) %all-to-all-start.4) | async-done | bytes 458784 | tf_op jit(solution)/shard_map/all_to_all | solution.py:115
  42.6 3.5 all-to-all-start
  49.7 13.0 %all-to-all-done = bf16[224,16,64]{0,2,1:T(8,128)(2,1)S(1)} async-done(((bf16[224,16,64]{0,2,1:T(8,128)(2,1)}), bf16[224,16,64]{0,2,1:T(8,128)(2,1)S(1)}, u32[]{:S(2)}, u32[]{:S(2)}) %all-to-all-start) | async-done | bytes 458784 | tf_op jit(solution)/shard_map/all_to_all | solution.py:101
  62.7 3.5 all-to-all-start.2
  66.2 2.5 broadcast_select_fusion
  68.7 14.2 %all-to-all-done.2 = bf16[224,16,64]{0,2,1:T(8,128)(2,1)S(1)} async-done(((bf16[224,16,64]{0,2,1:T(8,128)(2,1)}), bf16[224,16,64]{0,2,1:T(8,128)(2,1)S(1)}, u32[]{:S(2)}, u32[]{:S(2)}) %all-to-all-start.2) | async-done | bytes 458784 | tf_op jit(solution)/shard_map/all_to_all | solution.py:108
  82.9 4.2 all-to-all-start.5
  89.8 21.5 %all-to-all-done.5 = bf16[1,2,16,14336]{3,1,0,2:T(2,128)(2,1)} async-done(((bf16[1,2,16,14336]{3,1,0,2:T(2,128)(2,1)}), bf16[1,2,16,14336]{3,1,0,2:T(2,128)(2,1)}, u32[]{:S(2)}, u32[]{:S(2)}) %all-to-all-start.5) | async-done | bytes 917536 | tf_op jit(solution)/shard_map/all_to_all | solution.py:130
  111.3 3.6 all-to-all-start.3
  116.5 26.2 %all-to-all-done.3 = bf16[224,2,16,64]{0,3,1,2:T(8,128)(2,1)S(1)} async-done(((bf16[224,2,16,64]{0,3,1,2:T(8,128)(2,1)}), bf16[224,2,16,64]{0,3,1,2:T(8,128)(2,1)S(1)}, u32[]{:S(2)}, u32[]{:S(2)}) %all-to-all-start.3) | async-done | bytes 917536 | tf_op jit(solution)/shard_map/all_to_all | solution.py:129
  142.7 3.6 all-to-all-start.1
  149.9 2.4 copy.259
  152.3 3.4 reshape.188
  158.4 15.8 %all-to-all-done.1 = bf16[224,2,16,64]{0,3,1,2:T(8,128)(2,1)S(1)} async-done(((bf16[224,2,16,64]{0,3,1,2:T(8,128)(2,1)}), bf16[224,2,16,64]{0,3,1,2:T(8,128)(2,1)S(1)}, u32[]{:S(2)}, u32[]{:S(2)}) %all-to-all-start.1) | async-done | bytes 917536 | tf_op jit(solution)/shard_map/all_to_all | solution.py:128
  174.3 1.7 convolution_convert_fusion.2
  177.8 167.9 %all-reduce.3.cloned.1.call-done = (bf16[2,320,1024]{2,1,0:T(8,128)(2,1)}, bf16[2,320,1024]{2,1,0:T(8,128)(2,1)}, bf16[2,320,1024]{2,1,0:T(8,128)(2,1)}) async-done(((bf16[2,320,1024]{2,1,0:T(8,128)(2,1)}, bf16[2,320,1024]{2,1,0:T(8,128)(2,1)}, bf16[2,320,1024]{2,1,0:T(8,128)(2,1)}), (bf16[2,320,1024]{2,1,0:T(8,128)(2,1)}, bf16[2,320,1024]{2,1,0:T(8,128)(2,1)}, ...) | async-done | bytes 3932176 | tf_op jit(solution)/shard_map/psum | solution.py:21
  345.7 5.0 fusion.11
  352.3 2.2 copy.273
  354.5 3.3 copy.274
  357.8 10.6 %all-to-all-start.6 = ((bf16[224,2,16,64]{0,1,3,2:T(2,128)(2,1)}), bf16[224,2,16,64]{0,1,3,2:T(2,128)(2,1)}, u32[]{:S(2)}, u32[]{:S(2)}) async-start(bf16[224,2,16,64]{0,1,3,2:T(2,128)(2,1)} %copy.274), calls=%async_computation.6 | async-start | bytes 2097152 | tf_op jit(solution)/shard_map/all_to_all | solution.py:141
  370.1 2.3 copy.277
  372.3 3.3 copy.278
  375.6 20.9 %all-to-all-done.6 = bf16[224,2,16,64]{0,1,3,2:T(2,128)(2,1)} async-done(((bf16[224,2,16,64]{0,1,3,2:T(2,128)(2,1)}), bf16[224,2,16,64]{0,1,3,2:T(2,128)(2,1)}, u32[]{:S(2)}, u32[]{:S(2)}) %all-to-all-start.6) | async-done | bytes 917536 | tf_op jit(solution)/shard_map/all_to_all | solution.py:141
  396.5 4.4 all-to-all-start.8
  400.9 2.9 convolution_convert_fusion.3
  403.9 2.3 copy.281
  406.1 3.4 reshape.196
  409.5 3.1 copy.282
  412.6 15.6 %all-to-all-done.8 = bf16[224,2,16,64]{0,1,3,2:T(2,128)(2,1)} async-done(((bf16[224,2,16,64]{0,1,3,2:T(2,128)(2,1)}), bf16[224,2,16,64]{0,1,3,2:T(2,128)(2,1)}, u32[]{:S(2)}, u32[]{:S(2)}) %all-to-all-start.8) | async-done | bytes 917536 | tf_op jit(solution)/shard_map/all_to_all | solution.py:148
  428.2 4.2 all-to-all-start.10
  432.6 1.9 fusion.17
  435.5 21.7 %all-to-all-done.10 = bf16[1,2,16,14336]{3,1,0,2:T(2,128)(2,1)} async-done(((bf16[1,2,16,14336]{3,1,0,2:T(2,128)(2,1)}), bf16[1,2,16,14336]{3,1,0,2:T(2,128)(2,1)}, u32[]{:S(2)}, u32[]{:S(2)}) %all-to-all-start.10) | async-done | bytes 917536 | tf_op jit(solution)/shard_map/all_to_all | solution.py:155
  457.2 3.5 all-to-all-start.7
  460.6 1.9 fusion.16
  463.5 14.3 %all-to-all-done.7 = bf16[224,16,64]{0,2,1:T(8,128)(2,1)S(1)} async-done(((bf16[224,16,64]{0,2,1:T(8,128)(2,1)}), bf16[224,16,64]{0,2,1:T(8,128)(2,1)S(1)}, u32[]{:S(2)}, u32[]{:S(2)}) %all-to-all-start.7) | async-done | bytes 458784 | tf_op jit(solution)/shard_map/all_to_all | solution.py:176
  477.8 4.1 all-to-all-start.9
  482.0 2.6 fusion.52
  486.8 4.2 reduce.3
  491.0 2.1 reshape.289
  493.2 5.0 all-to-all-done.9
  498.2 4.3 all-to-all-start.11
  502.5 1.7 fusion.19
  508.2 2.0 copy.288
  510.2 7.1 %all-to-all-done.11 = bf16[16,2,7168]{2,1,0:T(2,128)(2,1)} async-done(((bf16[16,2,7168]{2,1,0:T(2,128)(2,1)}), bf16[16,2,7168]{2,1,0:T(2,128)(2,1)}, u32[]{:S(2)}, u32[]{:S(2)}) %all-to-all-start.11) | async-done | bytes 458784 | tf_op jit(solution)/shard_map/all_to_all | solution.py:178
  517.3 2.9 reshape.290
  520.2 2.6 bitcast_reduce_fusion
  (108 shorter events, 34.6 us)
Async XLA Ops:
  10.1 16.5 %copy-start.8 = (bf16[1,224,1024]{2,1,0:T(8,128)(2,1)S(1)}, bf16[1,224,1024]{2,1,0:T(8,128)(2,1)}, u32[]{:S(2)}) copy-start(bf16[1,224,1024]{2,1,0:T(8,128)(2,1)} %param.16) | copy-start | bytes 1376260
  13.5 14.1 %copy-start.13 = (s32[16,16]{1,0:T(8,128)S(1)}, s32[16,16]{1,0:T(8,128)}, u32[]{:S(2)}) copy-start(s32[16,16]{1,0:T(8,128)} %param.20) | copy-start | bytes 3076
  14.7 31.4 %copy-start.15 = (s32[16]{0:T(128)S(1)}, s32[16]{0:T(128)}, u32[]{:S(2)}) copy-start(s32[16]{0:T(128)} %param.19) | copy-start | bytes 196
  14.7 32.2 %copy-start.9 = (bf16[1,224,1024]{2,1,0:T(8,128)(2,1)S(1)}, bf16[1,224,1024]{2,1,0:T(8,128)(2,1)}, u32[]{:S(2)}) copy-start(bf16[1,224,1024]{2,1,0:T(8,128)(2,1)} %param.17) | copy-start | bytes 1376260
  14.7 27.9 %all-to-all-start.4 = ((bf16[16,2,7168]{2,1,0:T(2,128)(2,1)}), bf16[16,2,7168]{2,1,0:T(2,128)(2,1)S(1)}, u32[]{:S(2)}, u32[]{:S(2)}) async-start(bf16[16,2,7168]{2,1,0:T(2,128)(2,1)} %reshape.287), calls=%async_computation.4 | async-start | bytes 917504 | tf_op jit(solution)/shard_map/all_to_all | solution.py:115
  42.6 20.1 %all-to-all-start = ((bf16[224,16,64]{0,2,1:T(8,128)(2,1)}), bf16[224,16,64]{0,2,1:T(8,128)(2,1)S(1)}, u32[]{:S(2)}, u32[]{:S(2)}) async-start(bf16[224,16,64]{0,2,1:T(8,128)(2,1)} %bitcast.9), calls=%async_computation | async-start | bytes 1048576 | tf_op jit(solution)/shard_map/all_to_all | solution.py:101
  62.7 20.2 %all-to-all-start.2 = ((bf16[224,16,64]{0,2,1:T(8,128)(2,1)}), bf16[224,16,64]{0,2,1:T(8,128)(2,1)S(1)}, u32[]{:S(2)}, u32[]{:S(2)}) async-start(bf16[224,16,64]{0,2,1:T(8,128)(2,1)} %bitcast.13), calls=%async_computation.2 | async-start | bytes 1048576 | tf_op jit(solution)/shard_map/all_to_all | solution.py:108
  82.9 28.4 %all-to-all-start.5 = ((bf16[1,2,16,14336]{3,1,0,2:T(2,128)(2,1)}), bf16[1,2,16,14336]{3,1,0,2:T(2,128)(2,1)}, u32[]{:S(2)}, u32[]{:S(2)}) async-start(bf16[1,2,16,14336]{3,1,0,2:T(2,128)(2,1)} %broadcast_select_fusion), calls=%async_computation.5 | async-start | bytes 1835008 | tf_op jit(solution)/shard_map/all_to_all | solution.py:130
  89.8 25.1 %copy-start.14 = (s32[1,16,10]{1,0,2:T(1,128)S(1)}, s32[1,16,10]{1,0,2:T(1,128)}, u32[]{:S(2)}) copy-start(s32[1,16,10]{1,0,2:T(1,128)} %param.21) | copy-start | bytes 1924
  111.3 31.4 %all-to-all-start.3 = ((bf16[224,2,16,64]{0,3,1,2:T(8,128)(2,1)}), bf16[224,2,16,64]{0,3,1,2:T(8,128)(2,1)S(1)}, u32[]{:S(2)}, u32[]{:S(2)}) async-start(bf16[224,2,16,64]{0,3,1,2:T(8,128)(2,1)} %copy.252), calls=%async_computation.3 | async-start | bytes 2097152 | tf_op jit(solution)/shard_map/all_to_all | solution.py:129
  116.5 30.5 %copy-start.12 = (bf16[512,16]{0,1:T(8,128)(2,1)S(1)}, bf16[512,16]{0,1:T(8,128)(2,1)}, u32[]{:S(2)}) copy-start(bf16[512,16]{0,1:T(8,128)(2,1)} %param.15) | copy-start | bytes 49156
  116.5 31.6 %copy-start.10 = (bf16[512,224]{0,1:T(8,128)(2,1)S(1)}, bf16[512,224]{0,1:T(8,128)(2,1)}, u32[]{:S(2)}) copy-start(bf16[512,224]{0,1:T(8,128)(2,1)} %param.13) | copy-start | bytes 688132
  116.5 31.8 %copy-start.11 = (bf16[512,224]{0,1:T(8,128)(2,1)S(1)}, bf16[512,224]{0,1:T(8,128)(2,1)}, u32[]{:S(2)}) copy-start(bf16[512,224]{0,1:T(8,128)(2,1)} %param.14) | copy-start | bytes 688132
  142.7 31.5 %all-to-all-start.1 = ((bf16[224,2,16,64]{0,3,1,2:T(8,128)(2,1)}), bf16[224,2,16,64]{0,3,1,2:T(8,128)(2,1)S(1)}, u32[]{:S(2)}, u32[]{:S(2)}) async-start(bf16[224,2,16,64]{0,3,1,2:T(8,128)(2,1)} %copy.246), calls=%async_computation.1 | async-start | bytes 2097152 | tf_op jit(solution)/shard_map/all_to_all | solution.py:128
  146.3 199.4 %all-reduce.3.cloned.1.call-start = ((), (), s32[]{:S(2)}) async-start(), calls=%async_computation.12 | async-start | bytes 7864320 | tf_op jit(solution)/shard_map/psum | solution.py:21
  155.8 1.0 copy-start
  174.3 1.7 copy-start.2
  174.3 1.9 copy-start.4
  357.8 38.7 %all-to-all-start.6 = ((bf16[224,2,16,64]{0,1,3,2:T(2,128)(2,1)}), bf16[224,2,16,64]{0,1,3,2:T(2,128)(2,1)}, u32[]{:S(2)}, u32[]{:S(2)}) async-start(bf16[224,2,16,64]{0,1,3,2:T(2,128)(2,1)} %copy.274), calls=%async_computation.6 | async-start | bytes 2097152 | tf_op jit(solution)/shard_map/all_to_all | solution.py:141
  396.5 31.7 %all-to-all-start.8 = ((bf16[224,2,16,64]{0,1,3,2:T(2,128)(2,1)}), bf16[224,2,16,64]{0,1,3,2:T(2,128)(2,1)}, u32[]{:S(2)}, u32[]{:S(2)}) async-start(bf16[224,2,16,64]{0,1,3,2:T(2,128)(2,1)} %copy.278), calls=%async_computation.8 | async-start | bytes 2097152 | tf_op jit(solution)/shard_map/all_to_all | solution.py:148
  428.2 28.9 %all-to-all-start.10 = ((bf16[1,2,16,14336]{3,1,0,2:T(2,128)(2,1)}), bf16[1,2,16,14336]{3,1,0,2:T(2,128)(2,1)}, u32[]{:S(2)}, u32[]{:S(2)}) async-start(bf16[1,2,16,14336]{3,1,0,2:T(2,128)(2,1)} %copy.282), calls=%async_computation.10 | async-start | bytes 1835008 | tf_op jit(solution)/shard_map/all_to_all | solution.py:155
  457.2 20.7 %all-to-all-start.7 = ((bf16[224,16,64]{0,2,1:T(8,128)(2,1)}), bf16[224,16,64]{0,2,1:T(8,128)(2,1)S(1)}, u32[]{:S(2)}, u32[]{:S(2)}) async-start(bf16[224,16,64]{0,2,1:T(8,128)(2,1)} %copy.276), calls=%async_computation.7 | async-start | bytes 1048576 | tf_op jit(solution)/shard_map/all_to_all | solution.py:176
  477.8 6.7 %copy-start.6 = (bf16[224,16,64]{0,2,1:T(8,128)(2,1)}, bf16[224,16,64]{0,2,1:T(8,128)(2,1)S(1)}, u32[]{:S(2)}) copy-start(bf16[224,16,64]{0,2,1:T(8,128)(2,1)S(1)} %all-to-all-done.7) | copy-start | bytes 1376260
  477.8 20.3 %all-to-all-start.9 = ((bf16[224,16,64]{0,2,1:T(8,128)(2,1)}), bf16[224,16,64]{0,2,1:T(8,128)(2,1)}, u32[]{:S(2)}, u32[]{:S(2)}) async-start(bf16[224,16,64]{0,2,1:T(8,128)(2,1)} %copy.280), calls=%async_computation.9 | async-start | bytes 1048576 | tf_op jit(solution)/shard_map/all_to_all | solution.py:177
  486.8 15.7 %copy-start.1 = (bf16[224,2,16,64]{0,3,2,1:T(8,128)(2,1)S(1)}, bf16[224,2,16,64]{0,3,2,1:T(8,128)(2,1)}, u32[]{:S(2)}) copy-start(bf16[224,2,16,64]{0,3,2,1:T(8,128)(2,1)} %copy-done) | copy-start | bytes 2752516
  498.2 19.2 %all-to-all-start.11 = ((bf16[16,2,7168]{2,1,0:T(2,128)(2,1)}), bf16[16,2,7168]{2,1,0:T(2,128)(2,1)}, u32[]{:S(2)}, u32[]{:S(2)}) async-start(bf16[16,2,7168]{2,1,0:T(2,128)(2,1)} %reshape.289), calls=%async_computation.11 | async-start | bytes 917504 | tf_op jit(solution)/shard_map/all_to_all | solution.py:178
  502.5 2.9 copy-start.5
  504.2 1.3 copy-start.3
  506.0 1.2 copy-start.7
Sparse Core Ops, SparseCore 0:
  177.9 167.7 all-reduce.2
where the time goes:
time: 540 us; the launch traced here: 532 us
  waiting for transfers between devices  358 us (66%)
  starting transfers between devices  61.9 us (11%)
  local copies, waits for them, and re-layouts  58.1 us (11%)
  matrix products  21.8 us (4%)
  other arithmetic  17.1 us (3%)
  between operations  14.8 us (3%)
    psum x1, waiting for transfers between devices, expert_pass(): lax.psum(part_up.astype(jnp.bfloat16), 'member').astype(jnp.float32)  168 us
    all_to_all x1, waiting for transfers between devices, body(): lax.all_to_all(up_sent, 'group', split_axis=2, concat_axis=2, tiled=True)  26.2 us
    all_to_all x1, waiting for transfers between devices, body(): lax.all_to_all(weight_down.reshape(1, MAXE, group_total, piece_size * wid...  21.7 us
    all_to_all x1, waiting for transfers between devices, body(): lax.all_to_all(down_sent, 'group', split_axis=2, concat_axis=2, tiled=True)  21.5 us
    all_to_all x1, waiting for transfers between devices, body(): lax.all_to_all(weight_gate.reshape(width_share, MAXE, group_total, piece_...  20.9 us
    unnamed x49, local copies, waits for them, and re-layouts  17.7 us
    all_to_all x1, waiting for transfers between devices, body(): lax.all_to_all(gate_sent, 'group', split_axis=2, concat_axis=2, tiled=True)  15.8 us
    all_to_all x1, waiting for transfers between devices, body(): lax.all_to_all(weight_up.reshape(width_share, MAXE, group_total, piece_si...  15.6 us
  transfers between devices with their start and end apart: 13, of which 13 were waited for; matrix products, arithmetic and copies ran while one was open for 12% of the time, Pallas kernels for 0%

commit v1 on v0

v1 whole, which is shorter than its diff:
```python
import jax
import jax.numpy as jnp
from jax import lax
from jax.experimental import pallas as pl
from jax.experimental.pallas import tpu as pltpu
from jax.sharding import Mesh, PartitionSpec as P

BLK = 32
USERS = 2
LANES = 512
P_LANE = 224
DY_LANE = 256
LIST_LANE = 480
GROUP = ("z", "core")
F32 = jnp.float32
BF16 = jnp.bfloat16
VMEM_LIMIT = 56 * 1024 * 1024


def dot(a, b, ca, cb):
    return lax.dot_general(a, b, (((ca,), (cb,)), ((), ())), preferred_element_type=F32)


def call(kernel, out_shape, args, **kw):
    return pl.pallas_call(
        kernel,
        out_shape=out_shape,
        compiler_params=pltpu.CompilerParams(vmem_limit_bytes=VMEM_LIMIT),
        **kw,
    )(*args)


def token_permutation(rows):
    o = lax.broadcasted_iota(jnp.int32, (rows, rows), 0)
    t = lax.broadcasted_iota(jnp.int32, (rows, rows), 1)
    source = ((o >> 1) & 15) * BLK + (o >> 5) * 2 + (o & 1)
    return (t == source).astype(BF16)


def pack_kernel(tok_ref, dy_ref, prob_ref, list_ref, out_ref, all_ref):
    width = tok_ref.shape[0]
    all_ref[...] = jnp.zeros_like(all_ref)
    all_ref[0:width] = tok_ref[...]
    all_ref[P_LANE : P_LANE + 16] = prob_ref[...]
    all_ref[DY_LANE : DY_LANE + width] = dy_ref[...]
    packed = dot(token_permutation(LANES), all_ref[...], 1, 1)
    packed = packed.reshape(out_ref.shape) + list_ref[...].astype(F32)[None]
    out_ref[...] = packed.astype(BF16)


def select_kernel(rows_ref, info_ref, out_ref, pick_ref):
    rows = rows_ref[...]
    total = info_ref.shape[0]
    columns = lax.broadcasted_iota(jnp.int32, (total, rows.shape[0]), 1)
    list_rows = (columns == info_ref[:, 0:1]).astype(BF16)
    lists = dot(list_rows, rows[:, 384:512], 1, 0)
    lanes = lax.broadcasted_iota(jnp.int32, lists.shape, 1) + 384
    block = jnp.sum(jnp.where(lanes == info_ref[:, 2:3], lists, 0.0), axis=1, keepdims=True)
    column = info_ref[:, 1:2] + 2 * block.astype(jnp.int32)
    pick = (columns == column).astype(BF16)
    pick_ref[...] = pick
    out_ref[...] = dot(pick, rows, 1, 0).astype(BF16)


def row_prob(rows, mark):
    return jnp.sum(rows[:, 0:256].astype(F32) * mark, axis=1, keepdims=True)


def hidden_kernel(rows_ref, panel_ref, mark_ref, out_ref, acc_ref):
    step = pl.program_id(0)
    rows = rows_ref[0]
    count = rows.shape[0]
    hid = panel_ref.shape[2]
    x = rows[:, 0:P_LANE]
    prob = row_prob(rows, mark_ref[...])
    grad = (prob * rows[:, DY_LANE : DY_LANE + P_LANE].astype(F32)).astype(BF16)

    @pl.when(step == 0)
    def _():
        acc_ref[...] = jnp.zeros_like(acc_ref)

    acc_ref[0] += dot(x, panel_ref[0, 0:224], 1, 0)
    acc_ref[1] += dot(x, panel_ref[0, 224:448], 1, 0)
    acc_ref[2] += dot(grad, panel_ref[0, 448:672], 1, 0)

    @pl.when(step == pl.num_programs(0) - 1)
    def _():
        for part in range(3):
            for piece in range(hid // 128):
                out_ref[piece, part * count : (part + 1) * count] = acc_ref[
                    part, :, piece * 128 : (piece + 1) * 128
                ].astype(BF16)


def point_kernel(parts_ref, out_ref):
    count = out_ref.shape[0] // 3
    total = jnp.sum(parts_ref[...].astype(F32), axis=0)
    gate, up, grad = total[0:count], total[count : 2 * count], total[2 * count :]
    sigma = jax.nn.sigmoid(gate)
    out_ref[0:count] = (gate * sigma * up).astype(BF16)
    out_ref[count : 2 * count] = (grad * up * sigma * (1.0 + gate * (1.0 - sigma))).astype(BF16)
    out_ref[2 * count :] = (grad * gate * sigma).astype(BF16)


def hidden_parts(act_ref):
    count = act_ref.shape[1] // 3
    return [
        jnp.concatenate(
            [act_ref[k, i * count : (i + 1) * count] for k in range(act_ref.shape[0])], axis=1
        )
        for i in range(3)
    ]


def result_kernel(act_ref, panel_ref, rows_ref, mark_ref, out_ref):
    hidden, gate_grad, up_grad = hidden_parts(act_ref)
    prob = row_prob(rows_ref[0], mark_ref[...])
    outcome = prob * dot(hidden, panel_ref[0, 448:672], 1, 1)
    dx = dot(gate_grad, panel_ref[0, 0:224], 1, 1) + dot(up_grad, panel_ref[0, 224:448], 1, 1)
    out_ref[0] = jnp.zeros_like(out_ref[0])
    out_ref[0, :, 0:P_LANE] = outcome.astype(BF16)
    out_ref[0, :, DY_LANE : DY_LANE + P_LANE] = dx.astype(BF16)


def weight_kernel(act_ref, rows_ref, mark_ref, out_ref):
    hidden, gate_grad, up_grad = hidden_parts(act_ref)
    rows = rows_ref[0]
    x = rows[:, 0:P_LANE]
    prob = row_prob(rows, mark_ref[...])
    grad = (prob * rows[:, DY_LANE : DY_LANE + P_LANE].astype(F32)).astype(BF16)
    out_ref[0, 0:224] = dot(x, gate_grad, 0, 0).astype(BF16)
    out_ref[0, 224:448] = dot(x, up_grad, 0, 0).astype(BF16)
    out_ref[0, 448:672] = dot(grad, hidden, 0, 0).astype(BF16)


def combine_kernel(pick_ref, rows_ref, out_ref):
    out_ref[...] = dot(pick_ref[...], rows_ref[...], 0, 0).astype(BF16)


def unpack_kernel(rows_ref, out_ref, dx_ref):
    result = dot(rows_ref[...], token_permutation(LANES), 0, 0).astype(BF16)
    out_ref[...] = result[0:P_LANE]
    dx_ref[...] = result[DY_LANE : DY_LANE + P_LANE]


def routing_info(expert_slot, block_counts, entries):
    groups, experts = block_counts.shape
    ids = jnp.arange(experts, dtype=jnp.int32)
    slot_is = (expert_slot[:, None] == ids[None, :]).astype(jnp.int32)
    slot_expert = jnp.sum(slot_is * ids[:, None], axis=0)
    counts = jnp.sum(block_counts[:, :, None] * slot_is[None], axis=1)
    used = (counts > 0).astype(jnp.int32)
    before = (ids[:, None] < ids[None, :]).astype(jnp.int32)
    rank = jnp.sum(used[:, None, :] * before[:, :, None], axis=0)
    user_ids = jnp.arange(USERS, dtype=jnp.int32)
    chosen = used[:, :, None] * (rank[:, :, None] == user_ids).astype(jnp.int32)
    user_group = jnp.sum(chosen * ids[:, None, None], axis=0)
    user_count = jnp.sum(chosen * counts[:, :, None], axis=0)
    shape = (groups, USERS, entries, 2)
    entry = lax.broadcasted_iota(jnp.int32, shape, 2)
    row = lax.broadcasted_iota(jnp.int32, shape, 3)
    group = user_group[:, :, None, None]
    list_row = jnp.broadcast_to(group * BLK + slot_expert[:, None, None, None], shape)
    base = jnp.where(entry < user_count[:, :, None, None], group * BLK + row, -100000)
    info = jnp.stack([list_row, base, entry + LIST_LANE], axis=-1)
    return info.reshape(-1, 3), slot_expert


def exchange(array, axis):
    return lax.all_to_all(array, axis, split_axis=0, concat_axis=0, tiled=True)


def body(
    tokens, grad_output, gate_prob, w_gate, w_up, w_down, expert_slot, block_counts, block_lists
):
    groups = lax.axis_size(GROUP)
    share_y = lax.axis_size("y")
    share_x = lax.axis_size("x")
    width = tokens.shape[1]
    hid = w_gate.shape[2]
    entries = block_lists.shape[2]
    picked = USERS * entries * 2
    total = groups * picked
    count = total // share_x

    panels = jnp.concatenate([w_gate[0], w_up[0], w_down[0].T], axis=0)
    panels = lax.all_gather(panels, "x", axis=0, tiled=False)

    lists = lax.pad(
        block_lists[0].astype(BF16),
        jnp.zeros((), BF16),
        ((0, BLK - 16, 0), (LIST_LANE, LANES - LIST_LANE - entries, 0)),
    )
    packed = call(
        pack_kernel,
        jax.ShapeDtypeStruct((groups, BLK, LANES), BF16),
        (tokens.T, grad_output.T, gate_prob.T, lists),
        scratch_shapes=[pltpu.VMEM((LANES, LANES), BF16)],
    )
    info, slot_expert = routing_info(expert_slot, block_counts, entries)
    expert = lax.dynamic_index_in_dim(slot_expert, lax.axis_index(GROUP), 0, keepdims=False)
    mark = (jnp.arange(256, dtype=jnp.int32) == P_LANE + expert).astype(F32)[None]
    spread = exchange(packed, GROUP).reshape(groups * BLK, LANES)
    sent, pick = call(
        select_kernel,
        (
            jax.ShapeDtypeStruct((total, LANES), BF16),
            jax.ShapeDtypeStruct((total, groups * BLK), BF16),
        ),
        (spread, info),
    )
    got = exchange(sent.reshape(groups, picked, LANES), GROUP)
    rows = exchange(got.reshape(share_x, count, LANES), "x")

    row_spec = pl.BlockSpec((1, count, LANES), lambda i: (i, 0, 0))
    panel_spec = pl.BlockSpec((1, 3 * width, hid), lambda i: (i, 0, 0))
    mark_spec = pl.BlockSpec((1, 256), lambda i: (0, 0))
    act_shape = (share_y, 3 * count, hid // share_y)
    act_spec = pl.BlockSpec(act_shape, lambda i: (0, 0, 0))
    parts = call(
        hidden_kernel,
        jax.ShapeDtypeStruct(act_shape, BF16),
        (rows, panels, mark),
        grid=(share_x,),
        in_specs=[row_spec, panel_spec, mark_spec],
        out_specs=act_spec,
        scratch_shapes=[pltpu.VMEM((3, count, hid), F32)],
    )
    parts = exchange(parts, "y")
    act = call(point_kernel, jax.ShapeDtypeStruct(act_shape[1:], BF16), (parts,))
    act = lax.all_gather(act, "y", axis=0, tiled=False)
    results = call(
        result_kernel,
        jax.ShapeDtypeStruct((share_x, count, LANES), BF16),
        (act, panels, rows, mark),
        grid=(share_x,),
        in_specs=[act_spec, panel_spec, row_spec, mark_spec],
        out_specs=row_spec,
    )
    weights = call(
        weight_kernel,
        jax.ShapeDtypeStruct((share_x, 3 * width, hid), BF16),
        (act, rows, mark),
        grid=(share_x,),
        in_specs=[act_spec, row_spec, mark_spec],
        out_specs=panel_spec,
    )
    weights = lax.psum_scatter(weights, "x", scatter_dimension=0, tiled=False)
    back = exchange(results, "x").reshape(groups, picked, LANES)
    back = exchange(back, GROUP).reshape(total, LANES)
    summed = call(combine_kernel, jax.ShapeDtypeStruct((groups * BLK, LANES), BF16), (pick, back))
    home = exchange(summed.reshape(groups, BLK, LANES), GROUP).reshape(groups * BLK, LANES)
    out, dx = call(
        unpack_kernel,
        (jax.ShapeDtypeStruct((width, groups * BLK), BF16),) * 2,
        (home,),
    )
    return (
        out.T,
        dx.T,
        weights[None, 0:width],
        weights[None, width : 2 * width],
        weights[2 * width :].T[None],
    )


def solution(mesh):
    devices = mesh.devices.reshape(8, 2, 8, 4)
    inner = Mesh(devices, ("z", "core", "y", "x"))
    member = ("y", "x")
    in_specs = (
        P(GROUP, member),
        P(GROUP, member),
        P(GROUP, None),
        P(GROUP, member, None),
        P(GROUP, member, None),
        P(GROUP, None, member),
        P(),
        P(),
        P(GROUP, None, None),
    )
    out_specs = (
        P(GROUP, member),
        P(GROUP, member),
        P(GROUP, member, None),
        P(GROUP, member, None),
        P(GROUP, None, member),
    )
    return jax.shard_map(body, mesh=inner, in_specs=in_specs, out_specs=out_specs, check_vma=False)
```

time: 540 us -> 253 us (0.47); the launches traced: 532 us -> 252 us
  waiting for transfers between devices: 358 us -> 26.8 us
  blocking collectives: 0 us -> 154 us
  local copies, waits for them, and re-layouts: 58.1 us -> 7.15 us
  starting transfers between devices: 61.9 us -> 15.9 us
  Pallas kernels: 0 us -> 29.7 us
  matrix products: 21.8 us -> 0 us
  other arithmetic: 17.1 us -> 3.67 us
    psum x1 -> x0, waiting for transfers between devices: 168 us -> none  [expert_pass(): lax.psum(part_up.astype(jnp.bfloat16), 'member').astype(jnp.float32)]
    all_to_all x12 -> x2, waiting for transfers between devices: 190 us -> 26.8 us  [exchange(): return lax.all_to_all(array, axis, split_axis=0, concat_axis=0, tiled=True)]
    all_to_all x0 -> x5, blocking collectives: none -> 131 us  [exchange(): return lax.all_to_all(array, axis, split_axis=0, concat_axis=0, tiled=True)]
    all_to_all x12 -> x2, starting transfers between devices: 61.4 us -> 15.9 us  [exchange(): return lax.all_to_all(array, axis, split_axis=0, concat_axis=0, tiled=True)]
    pallas_call x0 -> x8, Pallas kernels: none -> 29.7 us  [call(): pl.pallas_call(kernel, out_shape=out_shape, compiler_params=pltpu.Compile...]
    all_gather x0 -> x1, blocking collectives: none -> 23.5 us  [body(): act = lax.all_gather(act, 'y', axis=0, tiled=False)]
    dot_general x14 -> x0, matrix products: 21.8 us -> none  [the longest x1 2.95 us: expert_pass(): jnp.einsum('sui,sug->sig', hidden_state, gradient_rows, preferred_element...]
    reshape x9 -> x0, local copies, waits for them, and re-layouts: 18.5 us -> none  [the longest x2 6.47 us: body(): weight_down.reshape(1, MAXE, group_total, piece_size * width_share)]
  transfers between devices with their start and end apart: 13 -> 4, of which waited for: 13 -> 2; matrix products, arithmetic and copies ran while one was open for 12% -> 2% of each run, Pallas kernels for 0% -> 6%
where the time goes in v1:
time: 253 us; the launch traced here: 252 us
  blocking collectives  154 us (61%)
  Pallas kernels  29.7 us (12%)
  waiting for transfers between devices  26.8 us (11%)
  starting transfers between devices  15.9 us (6%)
  between operations  14.8 us (6%)
  local copies, waits for them, and re-layouts  7.15 us (3%)
  other arithmetic  3.67 us (1%)
    all_to_all x5, blocking collectives, exchange(): return lax.all_to_all(array, axis, split_axis=0, concat_axis=0, tiled=True)  131 us
    pallas_call x8, Pallas kernels, call(): pl.pallas_call(kernel, out_shape=out_shape, compiler_params=pltpu.Compile...  29.7 us
    all_to_all x2, waiting for transfers between devices, exchange(): return lax.all_to_all(array, axis, split_axis=0, concat_axis=0, tiled=True)  26.8 us
    all_gather x1, blocking collectives, body(): act = lax.all_gather(act, 'y', axis=0, tiled=False)  23.5 us
    all_to_all x2, starting transfers between devices, exchange(): return lax.all_to_all(array, axis, split_axis=0, concat_axis=0, tiled=True)  15.9 us
  transfers between devices with their start and end apart: 4, of which 2 were waited for; matrix products, arithmetic and copies ran while one was open for 2% of the time, Pallas kernels for 6%

profile of v1, /device:TPU:1, one launch (start us, length us, event | category | flops | bytes accessed | tf_op | source)
XLA Modules:
  0.0 252.1 jit_solution(3327425270447383599)
XLA Ops:
  7.2 0.0 copy-start.3
  7.2 0.0 all-gather.4.cloned.1.call-start
  7.2 0.0 copy-start.4
  7.2 0.0 copy-start.2
  7.2 2.5 %pad_maximum_fusion = bf16[672,1024]{1,0:T(8,128)(2,1)} fusion(bf16[224,1024]{1,0:T(8,128)(2,1)} %bitcast.38, bf16[224,1024]{1,0:T(8,128)(2,1)} %bitcast.39, bf16[224,1024]{1,0:T(8,128)(2,1)} %bitcast.40), kind=kLoop, calls=%fused_computation | loop fusion | flops 4128768 | bytes 2752512 | tf_op jit(solution)/shard_map/concatenate | solution.py:186
  9.8 0.0 all-gather.4.cloned.1.call-update
  9.8 0.0 copy-done.3
  9.8 0.1 copy.21
  9.9 0.7 pad.3.list_ref
  10.6 2.3 shard_map.128
  12.9 11.8 %all-to-all-start = ((bf16[16,32,512]{2,1,0:T(8,128)(2,1)}), bf16[16,32,512]{2,1,0:T(8,128)(2,1)S(1)}, u32[]{:S(2)}, u32[]{:S(2)}) async-start(bf16[16,32,512]{2,1,0:T(8,128)(2,1)} %shard_map.128), calls=%async_computation | async-start | bytes 1048576 | tf_op jit(solution)/shard_map/all_to_all | solution.py:170
  24.8 0.1 fusion.2
  24.8 0.0 copy-done.2
  24.8 0.1 multiply_reduce_fusion.1
  25.0 0.1 multiply_reduce_fusion
  25.1 0.1 select_reduce_fusion
  25.2 0.1 copy.22
  25.3 0.1 copy.23
  25.4 0.1 copy.24
  25.5 0.1 add_select_fusion
  25.6 0.1 select_n.20
  25.7 0.1 stack_broadcast_in_dim.7
  25.8 0.1 stack_broadcast_in_dim.8
  26.0 0.1 stack.9
  26.1 0.1 stack.10
  26.3 0.9 copy.25.info_ref
  27.2 14.9 %all-to-all-done = bf16[16,32,512]{2,1,0:T(8,128)(2,1)S(1)} async-done(((bf16[16,32,512]{2,1,0:T(8,128)(2,1)}), bf16[16,32,512]{2,1,0:T(8,128)(2,1)S(1)}, u32[]{:S(2)}, u32[]{:S(2)}) %all-to-all-start) | async-done | bytes 524320 | tf_op jit(solution)/shard_map/all_to_all | solution.py:170
  42.1 0.8 copy-done.1
  42.9 3.4 %shard_map.129 = (bf16[640,512]{1,0:T(8,128)(2,1)}, bf16[640,512]{1,0:T(8,128)(2,1)}) custom-call(bf16[512,512]{1,0:T(8,128)(2,1)} %bitcast.35, s32[640,3]{1,0:T(8,128)} %copy.25.info_ref), custom_call_target="tpu_custom_call" | custom-call | tf_op jit(solution)/shard_map/pallas_call | solution.py:25
  46.3 23.2 %all_to_all.35 = bf16[16,40,512]{2,1,0:T(8,128)(2,1)} all-to-all(bf16[16,40,512]{2,1,0:T(8,128)(2,1)} %bitcast.37), channel_id=1, replica_groups=mesh['z'=8,'core'=2,'y'=8,'x'=4] {'z','core'}, dimensions={0} | all-to-all | bytes 1310720 | tf_op jit(solution)/shard_map/all_to_all | solution.py:170
  69.5 4.0 %all-to-all-start.2 = ((bf16[4,160,512]{2,1,0:T(8,128)(2,1)}), bf16[4,160,512]{2,1,0:T(8,128)(2,1)S(1)}, u32[]{:S(2)}, u32[]{:S(2)}) async-start(bf16[4,160,512]{2,1,0:T(8,128)(2,1)} %bitcast.6), calls=%async_computation.2 | async-start | bytes 1310720 | tf_op jit(solution)/shard_map/all_to_all | solution.py:170
  73.5 0.6 dynamic_slice.4
  74.8 0.6 compare_convert_fusion.1.mark_ref
  75.3 11.8 %all-to-all-done.2.rows_ref = bf16[4,160,512]{2,1,0:T(8,128)(2,1)S(1)} async-done(((bf16[4,160,512]{2,1,0:T(8,128)(2,1)}), bf16[4,160,512]{2,1,0:T(8,128)(2,1)S(1)}, u32[]{:S(2)}, u32[]{:S(2)}) %all-to-all-start.2) | async-done | bytes 655392 | tf_op jit(solution)/shard_map/all_to_all | solution.py:170
  87.2 0.8 copy-done
  88.0 5.7 %shard_map.130 = bf16[8,480,128]{2,1,0:T(8,128)(2,1)} custom-call(bf16[4,160,512]{2,1,0:T(8,128)(2,1)} %copy-done, bf16[4,672,1024]{2,1,0:T(8,128)(2,1)} %bitcast.28, f32[1,256]{1,0:T(1,128)} %compare_convert_fusion.1.mark_ref), custom_call_target="tpu_custom_call" | custom-call | tf_op jit(solution)/shard_map/pallas_call | solution.py:25
  93.7 32.8 %all_to_all.36.parts_ref = bf16[8,480,128]{2,1,0:T(8,128)(2,1)} all-to-all(bf16[8,480,128]{2,1,0:T(8,128)(2,1)} %shard_map.130), channel_id=1, replica_groups=mesh['z'=8,'core'=2,'y'=8,'x'=4] {'y'}, dimensions={0} | all-to-all | bytes 1966080 | tf_op jit(solution)/shard_map/all_to_all | solution.py:170
  126.5 2.0 shard_map.131
  128.5 23.5 %all-gather.1 = bf16[3840,128]{1,0:T(8,128)(2,1)} all-gather(bf16[480,128]{1,0:T(8,128)(2,1)} %shard_map.131), channel_id=3, replica_groups=mesh['z'=8,'core'=2,'y'=8,'x'=4] {'y'}, dimensions={0}, use_global_device_ids=true | all-gather | bytes 1105920 | tf_op jit(solution)/shard_map/all_gather | solution.py:231
  152.1 5.6 %shard_map.135 = bf16[4,672,1024]{2,1,0:T(8,128)(2,1)} custom-call(bf16[8,480,128]{2,1,0:T(8,128)(2,1)} %bitcast.30, bf16[4,160,512]{2,1,0:T(8,128)(2,1)} %copy-done, f32[1,256]{1,0:T(1,128)} %compare_convert_fusion.1.mark_ref), custom_call_target="tpu_custom_call" | custom-call | tf_op jit(solution)/shard_map/pallas_call | solution.py:25
  157.6 0.0 reduce-scatter.2.cloned.1.call-update
  157.6 5.8 %shard_map.132 = bf16[4,160,512]{2,1,0:T(8,128)(2,1)} custom-call(bf16[8,480,128]{2,1,0:T(8,128)(2,1)} %bitcast.31, bf16[4,672,1024]{2,1,0:T(8,128)(2,1)} %bitcast.29, bf16[4,160,512]{2,1,0:T(8,128)(2,1)} %copy-done, f32[1,256]{1,0:T(1,128)} %compare_convert_fusion.1.mark_ref), custom_call_target="tpu_custom_call" | custom-call | tf_op jit(solution)/shard_map/pallas_call | solution.py:25
  163.4 11.1 %all_to_all.37 = bf16[4,160,512]{2,1,0:T(8,128)(2,1)S(1)} all-to-all(bf16[4,160,512]{2,1,0:T(8,128)(2,1)} %shard_map.132), channel_id=1, replica_groups=mesh['z'=8,'core'=2,'y'=8,'x'=4] {'x'}, dimensions={0} | all-to-all | bytes 1310720 | tf_op jit(solution)/shard_map/all_to_all | solution.py:170
  174.5 42.2 %all_to_all.38 = bf16[16,40,512]{2,1,0:T(8,128)(2,1)} all-to-all(bf16[16,40,512]{2,1,0:T(8,128)(2,1)S(1)} %bitcast.33), channel_id=1, replica_groups=mesh['z'=8,'core'=2,'y'=8,'x'=4] {'z','core'}, dimensions={0} | all-to-all | bytes 1310720 | tf_op jit(solution)/shard_map/all_to_all | solution.py:170
  216.7 2.7 %shard_map.133 = bf16[512,512]{1,0:T(8,128)(2,1)} custom-call(bf16[640,512]{1,0:T(8,128)(2,1)} %get-tuple-element.9.pick_ref, bf16[640,512]{1,0:T(8,128)(2,1)} %bitcast.32), custom_call_target="tpu_custom_call" | custom-call | tf_op jit(solution)/shard_map/pallas_call | solution.py:25
  219.4 21.2 %all_to_all.39 = bf16[16,32,512]{2,1,0:T(8,128)(2,1)} all-to-all(bf16[16,32,512]{2,1,0:T(8,128)(2,1)} %bitcast.34), channel_id=1, replica_groups=mesh['z'=8,'core'=2,'y'=8,'x'=4] {'z','core'}, dimensions={0} | all-to-all | bytes 1048576 | tf_op jit(solution)/shard_map/all_to_all | solution.py:170
  240.6 2.2 shard_map.134
  242.8 2.4 slice_bitcast_fusion
  (12 shorter events, 0.1 us)
Async XLA Ops:
  7.2 2.6 %copy-start.3 = (s32[1,16,10]{1,0,2:T(1,128)S(1)}, s32[1,16,10]{1,0,2:T(1,128)}, u32[]{:S(2)}) copy-start(s32[1,16,10]{1,0,2:T(1,128)} %param.17) | copy-start | bytes 1924
  7.2 80.0 %all-gather.4.cloned.1.call-start = ((), (), s32[]{:S(2)}) async-start(), calls=%async_computation.9 | async-start | bytes 6881280 | tf_op jit(solution)/shard_map/all_gather | solution.py:187
  7.2 17.5 %copy-start.4 = (s32[16]{0:T(128)S(1)}, s32[16]{0:T(128)}, u32[]{:S(2)}) copy-start(s32[16]{0:T(128)} %param.15) | copy-start | bytes 196
  7.2 17.6 %copy-start.2 = (s32[16,16]{1,0:T(8,128)S(1)}, s32[16,16]{1,0:T(8,128)}, u32[]{:S(2)}) copy-start(s32[16,16]{1,0:T(8,128)} %param.16) | copy-start | bytes 3076
  12.9 29.2 %all-to-all-start = ((bf16[16,32,512]{2,1,0:T(8,128)(2,1)}), bf16[16,32,512]{2,1,0:T(8,128)(2,1)S(1)}, u32[]{:S(2)}, u32[]{:S(2)}) async-start(bf16[16,32,512]{2,1,0:T(8,128)(2,1)} %shard_map.128), calls=%async_computation | async-start | bytes 1048576 | tf_op jit(solution)/shard_map/all_to_all | solution.py:170
  42.1 0.8 copy-start.1
  69.5 17.7 %all-to-all-start.2 = ((bf16[4,160,512]{2,1,0:T(8,128)(2,1)}), bf16[4,160,512]{2,1,0:T(8,128)(2,1)S(1)}, u32[]{:S(2)}, u32[]{:S(2)}) async-start(bf16[4,160,512]{2,1,0:T(8,128)(2,1)} %bitcast.6), calls=%async_computation.2 | async-start | bytes 1310720 | tf_op jit(solution)/shard_map/all_to_all | solution.py:170
  73.5 169.3 %reduce-scatter.2.cloned.1.call-start = ((), (), s32[]{:S(2)}) async-start(), calls=%async_computation.8 | async-start | bytes 6881280 | tf_op jit(solution)/shard_map/reduce_scatter | solution.py:248
  87.2 0.8 copy-start
Sparse Core Ops, SparseCore 0:
  10.1 72.3 all-gather.3
  157.8 68.7 reduce-scatter.1

commit v2 on v1

v2 whole, which is shorter than its diff:
```python
import jax
import jax.numpy as jnp
from jax import lax
from jax.experimental import pallas as pl
from jax.experimental.pallas import tpu as pltpu
from jax.sharding import Mesh, PartitionSpec as P

BLK = 32
USERS = 2
LANES = 512
P_LANE = 224
DY_LANE = 256
LIST_LANE = 480
GROUP = ("z", "core")
OWNERS = ("x", "z", "core")
F32 = jnp.float32
BF16 = jnp.bfloat16
VMEM_LIMIT = 24 * 1024 * 1024
VMEM_LARGE = 56 * 1024 * 1024


def dot(a, b, ca, cb):
    return lax.dot_general(a, b, (((ca,), (cb,)), ((), ())), preferred_element_type=F32)


def call(kernel, out_shape, args, limit=VMEM_LIMIT, **kw):
    return pl.pallas_call(
        kernel,
        out_shape=out_shape,
        compiler_params=pltpu.CompilerParams(vmem_limit_bytes=limit),
        **kw,
    )(*args)


def token_permutation(rows):
    o = lax.broadcasted_iota(jnp.int32, (rows, rows), 0)
    t = lax.broadcasted_iota(jnp.int32, (rows, rows), 1)
    source = ((o >> 1) & 15) * BLK + (o >> 5) * 2 + (o & 1)
    return (t == source).astype(BF16)


def pack_kernel(tok_ref, dy_ref, prob_ref, list_ref, out_ref, all_ref):
    width = tok_ref.shape[0]
    all_ref[...] = jnp.zeros_like(all_ref)
    all_ref[0:width] = tok_ref[...]
    all_ref[P_LANE : P_LANE + 16] = prob_ref[...]
    all_ref[DY_LANE : DY_LANE + width] = dy_ref[...]
    packed = dot(token_permutation(LANES), all_ref[...], 1, 1)
    packed = packed.reshape(out_ref.shape) + list_ref[...].astype(F32)[None]
    out_ref[...] = packed.astype(BF16)


def split_lanes(tmp_ref, rows):
    count = rows.shape[0]
    for c in range(4):
        tmp_ref[pl.ds(c, count, stride=4), :] = rows[:, c * 128 : (c + 1) * 128]
    return tmp_ref[...].astype(BF16)


def join_lanes(tmp_ref, tiles):
    tmp_ref[...] = tiles.astype(F32)
    count = tmp_ref.shape[0] // 4
    return jnp.concatenate([tmp_ref[pl.ds(c, count, stride=4), :] for c in range(4)], axis=1)


def select_kernel(rows_ref, info_ref, out_ref, pick_ref, tmp_ref):
    rows = rows_ref[...]
    total = info_ref.shape[0]
    columns = lax.broadcasted_iota(jnp.int32, (total, rows.shape[0]), 1)
    list_rows = (columns == info_ref[:, 0:1]).astype(BF16)
    lists = dot(list_rows, rows[:, 384:512], 1, 0)
    lanes = lax.broadcasted_iota(jnp.int32, lists.shape, 1) + 384
    block = jnp.sum(jnp.where(lanes == info_ref[:, 2:3], lists, 0.0), axis=1, keepdims=True)
    column = info_ref[:, 1:2] + 2 * block.astype(jnp.int32)
    pick = (columns == column).astype(BF16)
    pick_ref[...] = pick
    out_ref[...] = split_lanes(tmp_ref, dot(pick, rows, 1, 0))


def hidden_kernel(x_ref, tiles_ref, mark_ref, gate_ref, *refs):
    down_refs, (out_ref, rows_ref, prob_ref, acc_ref, tmp_ref) = refs[:4], refs[4:]
    step = pl.program_id(0)
    rows = join_lanes(tmp_ref, tiles_ref[0])
    count = rows.shape[0]
    hid = gate_ref.shape[2]
    width = gate_ref.shape[1] // 2
    prob = jnp.sum(rows[:, 0:256] * mark_ref[...], axis=1, keepdims=True)
    x = rows[:, 0:256].astype(BF16)
    grad = (prob * rows[:, DY_LANE:LANES]).astype(BF16)
    rows_ref[0, :, 0:DY_LANE] = x
    rows_ref[0, :, DY_LANE:LANES] = grad
    prob_ref[...] = jnp.broadcast_to(prob, prob_ref.shape)
    x = x[:, 0:width]
    grad = grad[:, 0:width]

    @pl.when(step == 0)
    def _():
        acc_ref[...] = jnp.zeros_like(acc_ref)

    acc_ref[0] += dot(x, gate_ref[0, 0:width], 1, 0)
    acc_ref[1] += dot(x, gate_ref[0, width : 2 * width], 1, 0)
    for d in range(4):

        @pl.when(step == d)
        def _():
            acc_ref[2] += dot(grad, down_refs[d][...], 1, 0)

    @pl.when(step == pl.num_programs(0) - 1)
    def _():
        for part in range(3):
            for piece in range(hid // 128):
                out_ref[piece, part * count : (part + 1) * count] = acc_ref[
                    part, :, piece * 128 : (piece + 1) * 128
                ].astype(BF16)


def point_kernel(parts_ref, out_ref):
    count = out_ref.shape[0] // 3
    total = jnp.sum(parts_ref[...].astype(F32), axis=0)
    gate, up, grad = total[0:count], total[count : 2 * count], total[2 * count :]
    sigma = jax.nn.sigmoid(gate)
    out_ref[0:count] = (gate * sigma * up).astype(BF16)
    out_ref[count : 2 * count] = (grad * up * sigma * (1.0 + gate * (1.0 - sigma))).astype(BF16)
    out_ref[2 * count :] = (grad * gate * sigma).astype(BF16)


def hidden_parts(act_ref):
    count = act_ref.shape[1] // 3
    return [
        jnp.concatenate(
            [act_ref[k, i * count : (i + 1) * count] for k in range(act_ref.shape[0])], axis=1
        )
        for i in range(3)
    ]


def result_kernel(x_ref, act_ref, prob_ref, gate_ref, *refs):
    down_refs, (out_ref, res_ref, tmp_ref) = refs[:4], refs[4:]
    step = pl.program_id(0)
    width = gate_ref.shape[1] // 2
    hidden, gate_grad, up_grad = hidden_parts(act_ref)

    @pl.when(step == 0)
    def _():
        res_ref[...] = jnp.zeros_like(res_ref)

    for d in range(4):

        @pl.when(step == d)
        def _():
            outcome = prob_ref[:, 0:1] * dot(hidden, down_refs[d][...], 1, 1)
            res_ref[:, 0:width] = outcome

    dx = dot(gate_grad, gate_ref[0, 0:width], 1, 1)
    dx += dot(up_grad, gate_ref[0, width : 2 * width], 1, 1)
    res_ref[:, DY_LANE : DY_LANE + width] = dx
    out_ref[0] = split_lanes(tmp_ref, res_ref[...])


def gate_grad_kernel(act_ref, rows_ref, out_ref):
    _, gate_grad, up_grad = hidden_parts(act_ref)
    width = out_ref.shape[1] // 2
    x = rows_ref[0, :, 0:width]
    out_ref[0, 0:width] = dot(x, gate_grad, 0, 0).astype(BF16)
    out_ref[0, width : 2 * width] = dot(x, up_grad, 0, 0).astype(BF16)


def down_grad_kernel(x_ref, act_ref, rows_ref, *out_refs):
    hidden = hidden_parts(act_ref)[0]
    width = out_refs[0].shape[0]
    grad = rows_ref[0, :, DY_LANE : DY_LANE + width]
    for d in range(4):

        @pl.when(pl.program_id(0) == d)
        def _():
            out_refs[d][...] = dot(grad, hidden, 0, 0).astype(BF16)


def sum_kernel(*refs):
    total = refs[0][...].astype(F32)
    for ref in refs[1:-1]:
        total += ref[...].astype(F32)
    refs[-1][...] = total.astype(BF16)


def combine_kernel(pick_ref, tiles_ref, out_ref, tmp_ref):
    rows = join_lanes(tmp_ref, tiles_ref[...]).astype(BF16)
    out_ref[...] = dot(pick_ref[...], rows, 0, 0).astype(BF16)


def unpack_kernel(rows_ref, out_ref, dx_ref):
    result = dot(rows_ref[...], token_permutation(LANES), 0, 0).astype(BF16)
    out_ref[...] = result[0:P_LANE]
    dx_ref[...] = result[DY_LANE : DY_LANE + P_LANE]


def routing_info(expert_slot, block_counts, entries, share_x):
    groups, experts = block_counts.shape
    ids = jnp.arange(experts, dtype=jnp.int32)
    slot_is = (expert_slot[:, None] == ids[None, :]).astype(jnp.int32)
    slot_expert = jnp.sum(slot_is * ids[:, None], axis=0)
    counts = jnp.sum(block_counts[:, :, None] * slot_is[None], axis=1)
    used = (counts > 0).astype(jnp.int32)
    before = (ids[:, None] < ids[None, :]).astype(jnp.int32)
    rank = jnp.sum(used[:, None, :] * before[:, :, None], axis=0)
    user_ids = jnp.arange(USERS, dtype=jnp.int32)[:, None, None]
    chosen = used[None] * (rank[None] == user_ids).astype(jnp.int32)
    user_group = jnp.sum(chosen * ids[None, :, None], axis=1)
    user_count = jnp.sum(chosen * counts[None], axis=1)
    per_x = USERS * entries * 2 // share_x
    shape = (share_x, groups, per_x)
    member = lax.broadcasted_iota(jnp.int32, shape, 0) * per_x
    member = member + lax.broadcasted_iota(jnp.int32, shape, 2)
    first = member < entries * 2
    entry = (member >> 1) - jnp.where(first, 0, entries)
    group = jnp.where(first, user_group[0][None, :, None], user_group[1][None, :, None])
    limit = jnp.where(first, user_count[0][None, :, None], user_count[1][None, :, None])
    list_row = group * BLK + slot_expert[None, :, None]
    base = jnp.where(entry < limit, group * BLK + (member & 1), -100000)
    info = jnp.stack([list_row, base, entry + LIST_LANE], axis=-1)
    return info.reshape(-1, 3)


def exchange(array, axis):
    return lax.all_to_all(array, axis, split_axis=0, concat_axis=0, tiled=True)


def body(
    tokens, grad_output, gate_prob, w_gate, w_up, w_down, expert_slot, block_counts, block_lists
):
    groups = lax.axis_size(GROUP)
    share_y = lax.axis_size("y")
    share_x = lax.axis_size("x")
    width = tokens.shape[1]
    hid = w_gate.shape[2]
    entries = block_lists.shape[2]
    picked = USERS * entries * 2
    total = groups * picked
    count = total // share_x

    me_x = lax.axis_index("x")
    order = me_x[None].astype(jnp.int32)
    shifts = [[(i, (i + d) % share_x) for i in range(share_x)] for d in range(share_x)]

    gates = jnp.concatenate([w_gate[0], w_up[0]], axis=0)
    gates = lax.all_gather(gates, "x", axis=0, tiled=False)
    down = w_down[0].T
    downs = [down] + [lax.ppermute(down, "x", shifts[d]) for d in range(1, share_x)]

    lists = lax.pad(
        block_lists[0].astype(BF16),
        jnp.zeros((), BF16),
        ((0, BLK - 16, 0), (LIST_LANE, LANES - LIST_LANE - entries, 0)),
    )
    packed = call(
        pack_kernel,
        jax.ShapeDtypeStruct((groups, BLK, LANES), BF16),
        (tokens.T, grad_output.T, gate_prob.T, lists),
        scratch_shapes=[pltpu.VMEM((LANES, LANES), BF16)],
    )
    info = routing_info(expert_slot, block_counts, entries, share_x)
    mine = (expert_slot == lax.axis_index(GROUP)).astype(F32)
    mark = lax.pad(mine, jnp.zeros((), F32), ((P_LANE, 16, 0),))[None]
    spread = exchange(packed, GROUP).reshape(groups * BLK, LANES)
    sent, pick = call(
        select_kernel,
        (
            jax.ShapeDtypeStruct((4 * total, 128), BF16),
            jax.ShapeDtypeStruct((total, groups * BLK), BF16),
        ),
        (spread, info),
        scratch_shapes=[pltpu.VMEM((4 * total, 128), F32)],
    )
    pieces = (share_x * groups, 4 * picked // share_x, 128)
    tiles = exchange(sent.reshape(pieces), OWNERS).reshape(share_x, 4 * count, 128)

    def before(d, x):
        return (lax.rem(x[0] + share_x - d, share_x), 0, 0)

    def after(d, x):
        return (lax.rem(x[0] + d, share_x), 0, 0)

    def whole(*shape):
        return pl.BlockSpec(shape, lambda *_: (0,) * len(shape))

    tile_block = (1, 4 * count, 128)
    row_block = (1, count, LANES)
    gate_block = (1, 2 * width, hid)
    act_shape = (share_y, 3 * count, hid // share_y)
    parts, rows, prob = call(
        hidden_kernel,
        (
            jax.ShapeDtypeStruct(act_shape, BF16),
            jax.ShapeDtypeStruct((share_x, count, LANES), BF16),
            jax.ShapeDtypeStruct((count, 128), F32),
        ),
        (order, tiles, mark, gates, *downs),
        VMEM_LARGE,
        grid_spec=pltpu.PrefetchScalarGridSpec(
            num_scalar_prefetch=1,
            grid=(share_x,),
            in_specs=[
                pl.BlockSpec(tile_block, before),
                whole(1, 256),
                pl.BlockSpec(gate_block, before),
            ]
            + [whole(width, hid)] * 4,
            out_specs=[whole(*act_shape), pl.BlockSpec(row_block, before), whole(count, 128)],
            scratch_shapes=[
                pltpu.VMEM((3, count, hid), F32),
                pltpu.VMEM((4 * count, 128), F32),
            ],
        ),
    )
    parts = exchange(parts, "y")
    act = call(point_kernel, jax.ShapeDtypeStruct(act_shape[1:], BF16), (parts,))
    act = lax.all_gather(act, "y", axis=0, tiled=False)
    results = call(
        result_kernel,
        jax.ShapeDtypeStruct((share_x, 4 * count, 128), BF16),
        (order, act, prob, gates, *downs),
        VMEM_LARGE,
        grid_spec=pltpu.PrefetchScalarGridSpec(
            num_scalar_prefetch=1,
            grid=(share_x,),
            in_specs=[whole(*act_shape), whole(count, 128), pl.BlockSpec(gate_block, before)]
            + [whole(width, hid)] * 4,
            out_specs=pl.BlockSpec(tile_block, before),
            scratch_shapes=[pltpu.VMEM((count, LANES), F32), pltpu.VMEM((4 * count, 128), F32)],
        ),
    )
    late_act, results = lax.optimization_barrier((act, results))
    gate_grads = call(
        gate_grad_kernel,
        jax.ShapeDtypeStruct((share_x, 2 * width, hid), BF16),
        (late_act, rows),
        VMEM_LARGE,
        grid=(share_x,),
        in_specs=[whole(*act_shape), pl.BlockSpec(row_block, lambda i: (i, 0, 0))],
        out_specs=pl.BlockSpec(gate_block, lambda i: (i, 0, 0)),
    )
    gate_grads = lax.psum_scatter(gate_grads, "x", scatter_dimension=0, tiled=False)
    down_grads = call(
        down_grad_kernel,
        (jax.ShapeDtypeStruct((width, hid), BF16),) * 4,
        (order, late_act, rows),
        grid_spec=pltpu.PrefetchScalarGridSpec(
            num_scalar_prefetch=1,
            grid=(share_x,),
            in_specs=[whole(*act_shape), pl.BlockSpec(row_block, after)],
            out_specs=[whole(width, hid)] * 4,
        ),
    )
    down_grads = [down_grads[0]] + [
        lax.ppermute(down_grads[d], "x", shifts[d]) for d in range(1, share_x)
    ]
    down_grad = call(sum_kernel, jax.ShapeDtypeStruct((width, hid), BF16), down_grads)
    back = exchange(results.reshape(pieces), OWNERS).reshape(4 * total, 128)
    summed = call(
        combine_kernel,
        jax.ShapeDtypeStruct((groups * BLK, LANES), BF16),
        (pick, back),
        scratch_shapes=[pltpu.VMEM((4 * total, 128), F32)],
    )
    home = exchange(summed.reshape(groups, BLK, LANES), GROUP).reshape(groups * BLK, LANES)
    out, dx = call(
        unpack_kernel,
        (jax.ShapeDtypeStruct((width, groups * BLK), BF16),) * 2,
        (home,),
    )
    return (
        out.T,
        dx.T,
        gate_grads[None, 0:width],
        gate_grads[None, width:],
        down_grad.T[None],
    )


def solution(mesh):
    devices = mesh.devices.reshape(8, 2, 8, 4)
    inner = Mesh(devices, ("z", "core", "y", "x"))
    member = ("y", "x")
    in_specs = (
        P(GROUP, member),
        P(GROUP, member),
        P(GROUP, None),
        P(GROUP, member, None),
        P(GROUP, member, None),
        P(GROUP, None, member),
        P(),
        P(),
        P(GROUP, None, None),
    )
    out_specs = (
        P(GROUP, member),
        P(GROUP, member),
        P(GROUP, member, None),
        P(GROUP, member, None),
        P(GROUP, None, member),
    )
    return jax.shard_map(body, mesh=inner, in_specs=in_specs, out_specs=out_specs, check_vma=False)
```

time: 253 us -> 255 us (level)
  blocking collectives: 154 us -> 92.3 us
  waiting for transfers between devices: 26.8 us -> 70.9 us
  starting transfers between devices: 15.9 us -> 41.6 us
  Pallas kernels: 29.7 us -> 26.9 us
    all_to_all x5 -> x2, blocking collectives: 131 us -> 68.5 us  [exchange(): return lax.all_to_all(array, axis, split_axis=0, concat_axis=0, tiled=True)]
    ppermute x0 -> x6, waiting for transfers between devices: none -> 54.7 us  [the longest x3 32.6 us: body(): lax.ppermute(down, 'x', shifts[d])]
    ppermute x0 -> x6, starting transfers between devices: none -> 18.9 us  [the longest x3 9.58 us: body(): lax.ppermute(down, 'x', shifts[d])]
    all_to_all x2 -> x3, waiting for transfers between devices: 26.8 us -> 16.1 us  [exchange(): return lax.all_to_all(array, axis, split_axis=0, concat_axis=0, tiled=True)]
    all_to_all x2 -> x3, starting transfers between devices: 15.9 us -> 22.7 us  [exchange(): return lax.all_to_all(array, axis, split_axis=0, concat_axis=0, tiled=True)]
    pallas_call x8 -> x10, Pallas kernels: 29.7 us -> 26.9 us  [call(): pl.pallas_call(kernel, out_shape=out_shape, compiler_params=pltpu.Compile...]
  transfers between devices with their start and end apart: 4 -> 11, of which waited for: 2 -> 6; matrix products, arithmetic and copies ran while one was open for 2% -> 1% of each run, Pallas kernels for 6% -> 3%
where the time goes in v2:
time: 255 us; the launch traced here: 254 us
  blocking collectives  92.3 us (36%)
  waiting for transfers between devices  70.9 us (28%)
  starting transfers between devices  41.6 us (16%)
  Pallas kernels  26.9 us (11%)
  between operations  14.3 us (6%)
  local copies, waits for them, and re-layouts  4.83 us (2%)
  other arithmetic  3.4 us (1%)
    all_to_all x2, blocking collectives, exchange(): return lax.all_to_all(array, axis, split_axis=0, concat_axis=0, tiled=True)  68.5 us
    ppermute x3, waiting for transfers between devices, body(): lax.ppermute(down, 'x', shifts[d])  32.6 us
    pallas_call x10, Pallas kernels, call(): pl.pallas_call(kernel, out_shape=out_shape, compiler_params=pltpu.Compile...  26.9 us
    all_gather x1, blocking collectives, body(): act = lax.all_gather(act, 'y', axis=0, tiled=False)  23.8 us
    all_to_all x3, starting transfers between devices, exchange(): return lax.all_to_all(array, axis, split_axis=0, concat_axis=0, tiled=True)  22.7 us
    ppermute x3, waiting for transfers between devices, body(): lax.ppermute(down_grads[d], 'x', shifts[d])  22.1 us
    all_to_all x3, waiting for transfers between devices, exchange(): return lax.all_to_all(array, axis, split_axis=0, concat_axis=0, tiled=True)  16.1 us
    ppermute x3, starting transfers between devices, body(): lax.ppermute(down, 'x', shifts[d])  9.58 us
  transfers between devices with their start and end apart: 11, of which 6 were waited for; matrix products, arithmetic and copies ran while one was open for 1% of the time, Pallas kernels for 3%

profile of v2, /device:TPU:1, one launch (start us, length us, event | category | flops | bytes accessed | tf_op | source)
XLA Modules:
  0.0 254.3 jit_solution(304571037321443810)
XLA Ops:
  7.2 0.0 all-gather.4.cloned.1.call-start
  7.3 2.2 pad_maximum_fusion
  9.5 0.0 all-gather.4.cloned.1.call-update
  9.5 0.1 copy.21
  9.6 0.1 pad.7.list_ref
  9.7 1.3 shard_map.128
  11.0 12.0 %all-to-all-start = ((bf16[16,32,512]{2,1,0:T(8,128)(2,1)}), bf16[16,32,512]{2,1,0:T(8,128)(2,1)S(1)}, u32[]{:S(2)}, u32[]{:S(2)}) async-start(bf16[16,32,512]{2,1,0:T(8,128)(2,1)} %shard_map.128), calls=%async_computation | async-start | bytes 1048576 | tf_op jit(solution)/shard_map/all_to_all | solution.py:225
  23.0 0.1 fusion.5
  23.1 0.1 multiply_reduce_fusion.1
  23.2 0.1 multiply_reduce_fusion
  23.3 0.1 select_reduce_fusion
  23.4 0.1 fusion
  23.5 0.1 reshape.248
  23.7 0.1 reshape.255
  23.8 0.1 reshape.252
  24.0 0.2 copy.22.info_ref
  24.2 16.1 %all-to-all-done = bf16[16,32,512]{2,1,0:T(8,128)(2,1)S(1)} async-done(((bf16[16,32,512]{2,1,0:T(8,128)(2,1)}), bf16[16,32,512]{2,1,0:T(8,128)(2,1)S(1)}, u32[]{:S(2)}, u32[]{:S(2)}) %all-to-all-start) | async-done | bytes 524320 | tf_op jit(solution)/shard_map/all_to_all | solution.py:225
  40.3 2.3 shard_map.129
  42.6 5.9 %all-to-all-start.1 = ((bf16[64,40,128]{2,1,0:T(8,128)(2,1)}), bf16[64,40,128]{2,1,0:T(8,128)(2,1)S(1)}, u32[]{:S(2)}, u32[]{:S(2)}) async-start(bf16[64,40,128]{2,1,0:T(8,128)(2,1)} %bitcast.10), calls=%async_computation.1 | async-start | bytes 1310720 | tf_op jit(solution)/shard_map/all_to_all | solution.py:225
  48.5 0.0 reduce-scatter.2.cloned.1.call-start
  48.6 4.7 %collective-permute-start.2 = (bf16[224,1024]{1,0:T(8,128)(2,1)S(1)}, bf16[224,1024]{1,0:T(8,128)(2,1)S(1)}, u32[]{:S(2)}, u32[]{:S(2)}) collective-permute-start(bf16[224,1024]{1,0:T(8,128)(2,1)S(1)} %bitcast.49), channel_id=1, source_target_pairs={{0,3},{1,0},{2,1},{3,2},{4,7},{5,4},{6,5},{7,6},{8,11},{9,8},{10,9... | collective-permute-start | bytes 1376264 | tf_op jit(solution)/shard_map/ppermute | solution.py:248
  53.3 2.3 collective-permute-start.1
  55.6 2.6 %collective-permute-start = (bf16[224,1024]{1,0:T(8,128)(2,1)S(1)}, bf16[224,1024]{1,0:T(8,128)(2,1)}, u32[]{:S(2)}, u32[]{:S(2)}) collective-permute-start(bf16[224,1024]{1,0:T(8,128)(2,1)S(1)} %bitcast.51), channel_id=1, source_target_pairs={{0,1},{1,2},{2,3},{3,0},{4,5},{5,6},{6,7},{7,4},{8,9},{9,10},{10,1... | collective-permute-start | bytes 1376264 | tf_op jit(solution)/shard_map/ppermute | solution.py:248
  58.2 0.6 pad_convert_fusion
  58.9 19.9 %collective-permute-done.2.refs_3_ = bf16[224,1024]{1,0:T(8,128)(2,1)S(1)} collective-permute-done((bf16[224,1024]{1,0:T(8,128)(2,1)S(1)}, bf16[224,1024]{1,0:T(8,128)(2,1)S(1)}, u32[]{:S(2)}, u32[]{:S(2)}) %collective-permute-start.2) | collective-permute-done | bytes 458784 | tf_op jit(solution)/shard_map/ppermute | solution.py:248
  78.7 3.0 %collective-permute-done.1.refs_2_ = bf16[224,1024]{1,0:T(8,128)(2,1)S(1)} collective-permute-done((bf16[224,1024]{1,0:T(8,128)(2,1)S(1)}, bf16[224,1024]{1,0:T(8,128)(2,1)S(1)}, u32[]{:S(2)}, u32[]{:S(2)}) %collective-permute-start.1) | collective-permute-done | bytes 458784 | tf_op jit(solution)/shard_map/ppermute | solution.py:248
  81.8 9.7 %collective-permute-done.refs_1_ = bf16[224,1024]{1,0:T(8,128)(2,1)} collective-permute-done((bf16[224,1024]{1,0:T(8,128)(2,1)S(1)}, bf16[224,1024]{1,0:T(8,128)(2,1)}, u32[]{:S(2)}, u32[]{:S(2)}) %collective-permute-start) | collective-permute-done | bytes 458784 | tf_op jit(solution)/shard_map/ppermute | solution.py:248
  91.5 0.8 copy-done.6
  92.3 6.6 %shard_map.130 = (bf16[8,480,128]{2,1,0:T(8,128)(2,1)}, bf16[4,160,512]{2,1,0:T(8,128)(2,1)}, f32[160,128]{1,0:T(8,128)}) custom-call(s32[1]{0:T(128)} %bitcast.9.x_ref, bf16[4,640,128]{2,1,0:T(8,128)(2,1)} %bitcast.46, f32[1,256]{1,0:T(1,128)} %bitcast.55, bf16[4,448,1024]{2,1,0:T(8,128)(2,1)} %bitcast.43, bf16[224,1024]{1,0:T(8,128)(2,1)} %bitcast.47, ...), custom_call_target="tpu_custom_call" | custom-call | tf_op jit(solution)/shard_map/pallas_call | solution.py:27
  98.9 32.8 %all_to_all.25.parts_ref = bf16[8,480,128]{2,1,0:T(8,128)(2,1)S(1)} all-to-all(bf16[8,480,128]{2,1,0:T(8,128)(2,1)} %get-tuple-element.20), channel_id=1, replica_groups=mesh['z'=8,'core'=2,'y'=8,'x'=4] {'y'}, dimensions={0} | all-to-all | bytes 1966080 | tf_op jit(solution)/shard_map/all_to_all | solution.py:225
  131.7 0.2 shard_map.131
  131.8 23.8 %all-gather.1 = bf16[3840,128]{1,0:T(8,128)(2,1)} all-gather(bf16[480,128]{1,0:T(8,128)(2,1)S(1)} %shard_map.131), channel_id=3, replica_groups=mesh['z'=8,'core'=2,'y'=8,'x'=4] {'y'}, dimensions={0}, use_global_device_ids=true | all-gather | bytes 1105920 | tf_op jit(solution)/shard_map/all_gather | solution.py:317
  155.6 6.6 %shard_map.132 = bf16[4,640,128]{2,1,0:T(8,128)(2,1)} custom-call(s32[1]{0:T(128)} %bitcast.9.x_ref, bf16[8,480,128]{2,1,0:T(8,128)(2,1)} %bitcast.34, f32[160,128]{1,0:T(8,128)} %get-tuple-element.21.prob_ref, bf16[4,448,1024]{2,1,0:T(8,128)(2,1)} %bitcast.44, bf16[224,1024]{1,0:T(8,128)(2,1)} %bitcast.48, bf16[224,1024]{1,0:T(8,128)(2,1)} %collective-permute-done.refs_1_, ...), custom_call_target="tpu_custom_call" | custom-call | tf_op jit(solution)/shard_map/pallas_call | solution.py:27
  162.3 4.9 %shard_map.135 = bf16[4,448,1024]{2,1,0:T(8,128)(2,1)} custom-call(bf16[8,480,128]{2,1,0:T(8,128)(2,1)} %bitcast.35, bf16[4,160,512]{2,1,0:T(8,128)(2,1)} %get-tuple-element.26.rows_ref), custom_call_target="tpu_custom_call" | custom-call | tf_op jit(solution)/shard_map/pallas_call | solution.py:27
  167.2 0.0 reduce-scatter.2.cloned.1.call-update
  167.2 1.1 copy-done.5
  168.3 35.8 %all_to_all.26 = bf16[64,40,128]{2,1,0:T(8,128)(2,1)S(1)} all-to-all(bf16[64,40,128]{2,1,0:T(8,128)(2,1)S(1)} %bitcast.45), channel_id=1, replica_groups=mesh['z'=8,'core'=2,'y'=8,'x'=4] {'x','z','core'}, dimensions={0} | all-to-all | bytes 1310720 | tf_op jit(solution)/shard_map/all_to_all | solution.py:225
  204.0 1.4 shard_map.133
  205.5 4.8 %all-to-all-start.4 = ((bf16[16,32,512]{2,1,0:T(8,128)(2,1)}), bf16[16,32,512]{2,1,0:T(8,128)(2,1)S(1)}, u32[]{:S(2)}, u32[]{:S(2)}) async-start(bf16[16,32,512]{2,1,0:T(8,128)(2,1)} %bitcast.22), calls=%async_computation.4 | async-start | bytes 1048576 | tf_op jit(solution)/shard_map/all_to_all | solution.py:225
  210.3 1.4 shard_map.136
  211.7 1.9 collective-permute-start.3
  213.6 4.4 %collective-permute-start.4 = (bf16[224,1024]{1,0:T(8,128)(2,1)S(1)}, bf16[224,1024]{1,0:T(8,128)(2,1)S(1)}, u32[]{:S(2)}, u32[]{:S(2)}) collective-permute-start(bf16[224,1024]{1,0:T(8,128)(2,1)S(1)} %get-tuple-element.29), channel_id=1, source_target_pairs={{0,2},{1,3},{2,0},{3,1},{4,6},{5,7},{6,4},{7,5},{8,10},{9,11},{10,... | collective-permute-start | bytes 1376264 | tf_op jit(solution)/shard_map/ppermute | solution.py:355
  218.0 3.0 %collective-permute-start.5 = (bf16[224,1024]{1,0:T(8,128)(2,1)S(1)}, bf16[224,1024]{1,0:T(8,128)(2,1)S(1)}, u32[]{:S(2)}, u32[]{:S(2)}) collective-permute-start(bf16[224,1024]{1,0:T(8,128)(2,1)S(1)} %get-tuple-element.30), channel_id=1, source_target_pairs={{0,3},{1,0},{2,1},{3,2},{4,7},{5,4},{6,5},{7,6},{8,11},{9,8},{10,9... | collective-permute-start | bytes 1376264 | tf_op jit(solution)/shard_map/ppermute | solution.py:355
  221.0 11.9 %collective-permute-done.3.refs_1_ = bf16[224,1024]{1,0:T(8,128)(2,1)S(1)} collective-permute-done((bf16[224,1024]{1,0:T(8,128)(2,1)S(1)}, bf16[224,1024]{1,0:T(8,128)(2,1)S(1)}, u32[]{:S(2)}, u32[]{:S(2)}) %collective-permute-start.3) | collective-permute-done | bytes 458784 | tf_op jit(solution)/shard_map/ppermute | solution.py:355
  232.9 10.2 %collective-permute-done.4.refs_2_ = bf16[224,1024]{1,0:T(8,128)(2,1)S(1)} collective-permute-done((bf16[224,1024]{1,0:T(8,128)(2,1)S(1)}, bf16[224,1024]{1,0:T(8,128)(2,1)S(1)}, u32[]{:S(2)}, u32[]{:S(2)}) %collective-permute-start.4) | collective-permute-done | bytes 458784 | tf_op jit(solution)/shard_map/ppermute | solution.py:355
  243.2 1.0 shard_map.137
  244.2 1.2 shard_map.134
  245.3 2.1 fusion.7
  (37 shorter events, 0.1 us)
Async XLA Ops:
  7.2 2.4 copy-start.11
  7.2 2.5 copy-start.4
  7.2 2.5 copy-start.3
  7.2 2.5 copy-start.2
  7.2 84.3 %all-gather.4.cloned.1.call-start = ((), (), s32[]{:S(2)}) async-start(), calls=%async_computation.7 | async-start | bytes 4587520 | tf_op jit(solution)/shard_map/all_gather | solution.py:246
  9.5 13.5 %copy-start.12 = (s32[16]{0:T(128)S(1)}, s32[16]{0:T(128)}, u32[]{:S(2)}) copy-start(s32[16]{0:T(128)} %param.15) | copy-start | bytes 196
  9.5 13.5 %copy-start.10 = (s32[16,16]{1,0:T(8,128)S(1)}, s32[16,16]{1,0:T(8,128)}, u32[]{:S(2)}) copy-start(s32[16,16]{1,0:T(8,128)} %param.16) | copy-start | bytes 3076
  11.0 37.6 %copy-start.7 = (bf16[1,1024,224]{1,2,0:T(8,128)(2,1)S(1)}, bf16[1,1024,224]{1,2,0:T(8,128)(2,1)}, u32[]{:S(2)}) copy-start(bf16[1,1024,224]{1,2,0:T(8,128)(2,1)} %param.14) | copy-start | bytes 1376260
  11.0 29.3 %all-to-all-start = ((bf16[16,32,512]{2,1,0:T(8,128)(2,1)}), bf16[16,32,512]{2,1,0:T(8,128)(2,1)S(1)}, u32[]{:S(2)}, u32[]{:S(2)}) async-start(bf16[16,32,512]{2,1,0:T(8,128)(2,1)} %shard_map.128), calls=%async_computation | async-start | bytes 1048576 | tf_op jit(solution)/shard_map/all_to_all | solution.py:225
  42.6 48.9 %all-to-all-start.1 = ((bf16[64,40,128]{2,1,0:T(8,128)(2,1)}), bf16[64,40,128]{2,1,0:T(8,128)(2,1)S(1)}, u32[]{:S(2)}, u32[]{:S(2)}) async-start(bf16[64,40,128]{2,1,0:T(8,128)(2,1)} %bitcast.10), calls=%async_computation.1 | async-start | bytes 1310720 | tf_op jit(solution)/shard_map/all_to_all | solution.py:225
  48.5 196.8 %reduce-scatter.2.cloned.1.call-start = ((), (), s32[]{:S(2)}) async-start(), calls=%async_computation.6 | async-start | bytes 4587520 | tf_op jit(solution)/shard_map/reduce_scatter | solution.py:342
  48.6 30.1 %collective-permute-start.2 = (bf16[224,1024]{1,0:T(8,128)(2,1)S(1)}, bf16[224,1024]{1,0:T(8,128)(2,1)S(1)}, u32[]{:S(2)}, u32[]{:S(2)}) collective-permute-start(bf16[224,1024]{1,0:T(8,128)(2,1)S(1)} %bitcast.49), channel_id=1, source_target_pairs={{0,3},{1,0},{2,1},{3,2},{4,7},{5,4},{6,5},{7,6},{8,11},{9,8},{10,9... | collective-permute-start | bytes 1376264 | tf_op jit(solution)/shard_map/ppermute | solution.py:248
  53.3 28.4 %collective-permute-start.1 = (bf16[224,1024]{1,0:T(8,128)(2,1)S(1)}, bf16[224,1024]{1,0:T(8,128)(2,1)S(1)}, u32[]{:S(2)}, u32[]{:S(2)}) collective-permute-start(bf16[224,1024]{1,0:T(8,128)(2,1)S(1)} %bitcast.50), channel_id=1, source_target_pairs={{0,2},{1,3},{2,0},{3,1},{4,6},{5,7},{6,4},{7,5},{8,10},{9,11},{10,... | collective-permute-start | bytes 1376264 | tf_op jit(solution)/shard_map/ppermute | solution.py:248
  55.6 35.9 %collective-permute-start = (bf16[224,1024]{1,0:T(8,128)(2,1)S(1)}, bf16[224,1024]{1,0:T(8,128)(2,1)}, u32[]{:S(2)}, u32[]{:S(2)}) collective-permute-start(bf16[224,1024]{1,0:T(8,128)(2,1)S(1)} %bitcast.51), channel_id=1, source_target_pairs={{0,1},{1,2},{2,3},{3,0},{4,5},{5,6},{6,7},{7,4},{8,9},{9,10},{10,1... | collective-permute-start | bytes 1376264 | tf_op jit(solution)/shard_map/ppermute | solution.py:248
  78.7 12.8 %copy-start.8 = (bf16[224,1024]{1,0:T(8,128)(2,1)}, bf16[224,1024]{1,0:T(8,128)(2,1)S(1)}, u32[]{:S(2)}) copy-start(bf16[224,1024]{1,0:T(8,128)(2,1)S(1)} %collective-permute-done.2.refs_3_) | copy-start | bytes 1376260
  81.8 9.7 %copy-start.9 = (bf16[224,1024]{1,0:T(8,128)(2,1)}, bf16[224,1024]{1,0:T(8,128)(2,1)S(1)}, u32[]{:S(2)}) copy-start(bf16[224,1024]{1,0:T(8,128)(2,1)S(1)} %collective-permute-done.1.refs_2_) | copy-start | bytes 1376260
  91.5 0.9 copy-start.6
  167.2 1.1 copy-start.5
  168.3 42.0 %copy-start = (bf16[3840,128]{1,0:T(8,128)(2,1)S(1)}, bf16[3840,128]{1,0:T(8,128)(2,1)}, u32[]{:S(2)}) copy-start(bf16[3840,128]{1,0:T(8,128)(2,1)} %all-gather.1) | copy-start | bytes 2949124
  168.3 42.0 %copy-start.1 = (bf16[4,160,512]{2,1,0:T(8,128)(2,1)S(1)}, bf16[4,160,512]{2,1,0:T(8,128)(2,1)}, u32[]{:S(2)}) copy-start(bf16[4,160,512]{2,1,0:T(8,128)(2,1)} %get-tuple-element.26.rows_ref) | copy-start | bytes 1966084
  205.5 38.7 %all-to-all-start.4 = ((bf16[16,32,512]{2,1,0:T(8,128)(2,1)}), bf16[16,32,512]{2,1,0:T(8,128)(2,1)S(1)}, u32[]{:S(2)}, u32[]{:S(2)}) async-start(bf16[16,32,512]{2,1,0:T(8,128)(2,1)} %bitcast.22), calls=%async_computation.4 | async-start | bytes 1048576 | tf_op jit(solution)/shard_map/all_to_all | solution.py:225
  211.7 21.2 %collective-permute-start.3 = (bf16[224,1024]{1,0:T(8,128)(2,1)S(1)}, bf16[224,1024]{1,0:T(8,128)(2,1)S(1)}, u32[]{:S(2)}, u32[]{:S(2)}) collective-permute-start(bf16[224,1024]{1,0:T(8,128)(2,1)S(1)} %get-tuple-element.28), channel_id=1, source_target_pairs={{0,1},{1,2},{2,3},{3,0},{4,5},{5,6},{6,7},{7,4},{8,9},{9,10},{10,1... | collective-permute-start | bytes 1376264 | tf_op jit(solution)/shard_map/ppermute | solution.py:355
  213.6 29.5 %collective-permute-start.4 = (bf16[224,1024]{1,0:T(8,128)(2,1)S(1)}, bf16[224,1024]{1,0:T(8,128)(2,1)S(1)}, u32[]{:S(2)}, u32[]{:S(2)}) collective-permute-start(bf16[224,1024]{1,0:T(8,128)(2,1)S(1)} %get-tuple-element.29), channel_id=1, source_target_pairs={{0,2},{1,3},{2,0},{3,1},{4,6},{5,7},{6,4},{7,5},{8,10},{9,11},{10,... | collective-permute-start | bytes 1376264 | tf_op jit(solution)/shard_map/ppermute | solution.py:355
  218.0 25.1 %collective-permute-start.5 = (bf16[224,1024]{1,0:T(8,128)(2,1)S(1)}, bf16[224,1024]{1,0:T(8,128)(2,1)S(1)}, u32[]{:S(2)}, u32[]{:S(2)}) collective-permute-start(bf16[224,1024]{1,0:T(8,128)(2,1)S(1)} %get-tuple-element.30), channel_id=1, source_target_pairs={{0,3},{1,0},{2,1},{3,2},{4,7},{5,4},{6,5},{7,6},{8,11},{9,8},{10,9... | collective-permute-start | bytes 1376264 | tf_op jit(solution)/shard_map/ppermute | solution.py:355
Sparse Core Ops, SparseCore 0:
  10.1 78.7 all-gather.3
  167.3 62.0 reduce-scatter.1

commit v3 on v2

--- a/solution.py
+++ b/solution.py
@@ -78,32 +78,30 @@
 
 
 def hidden_kernel(x_ref, tiles_ref, mark_ref, gate_ref, *refs):
-    down_refs, (out_ref, rows_ref, prob_ref, acc_ref, tmp_ref) = refs[:4], refs[4:]
+    up_refs, down_refs, refs = refs[:4], refs[4:8], refs[8:]
+    row_refs, (out_ref, prob_ref, acc_ref, tmp_ref) = refs[:4], refs[4:]
     step = pl.program_id(0)
     rows = join_lanes(tmp_ref, tiles_ref[0])
     count = rows.shape[0]
-    hid = gate_ref.shape[2]
-    width = gate_ref.shape[1] // 2
+    width, hid = gate_ref.shape[1:]
     prob = jnp.sum(rows[:, 0:256] * mark_ref[...], axis=1, keepdims=True)
     x = rows[:, 0:256].astype(BF16)
     grad = (prob * rows[:, DY_LANE:LANES]).astype(BF16)
-    rows_ref[0, :, 0:DY_LANE] = x
-    rows_ref[0, :, DY_LANE:LANES] = grad
     prob_ref[...] = jnp.broadcast_to(prob, prob_ref.shape)
-    x = x[:, 0:width]
-    grad = grad[:, 0:width]
 
     @pl.when(step == 0)
     def _():
         acc_ref[...] = jnp.zeros_like(acc_ref)
 
-    acc_ref[0] += dot(x, gate_ref[0, 0:width], 1, 0)
-    acc_ref[1] += dot(x, gate_ref[0, width : 2 * width], 1, 0)
+    acc_ref[0] += dot(x[:, 0:width], gate_ref[0], 1, 0)
     for d in range(4):
 
         @pl.when(step == d)
         def _():
-            acc_ref[2] += dot(grad, down_refs[d][...], 1, 0)
+            row_refs[d][:, 0:DY_LANE] = x
+            row_refs[d][:, DY_LANE:LANES] = grad
+            acc_ref[1] += dot(x[:, 0:width], up_refs[d][...], 1, 0)
+            acc_ref[2] += dot(grad[:, 0:width], down_refs[d][...], 1, 0)
 
     @pl.when(step == pl.num_programs(0) - 1)
     def _():
@@ -124,63 +122,59 @@
     out_ref[2 * count :] = (grad * gate * sigma).astype(BF16)
 
 
-def hidden_parts(act_ref):
-    count = act_ref.shape[1] // 3
+def hidden_parts(act):
+    count = act.shape[1] // 3
     return [
-        jnp.concatenate(
-            [act_ref[k, i * count : (i + 1) * count] for k in range(act_ref.shape[0])], axis=1
-        )
+        jnp.concatenate([act[k, i * count : (i + 1) * count] for k in range(act.shape[0])], axis=1)
         for i in range(3)
     ]
 
 
 def result_kernel(x_ref, act_ref, prob_ref, gate_ref, *refs):
-    down_refs, (out_ref, res_ref, tmp_ref) = refs[:4], refs[4:]
+    up_refs, down_refs, (out_ref, res_ref, tmp_ref) = refs[:4], refs[4:8], refs[8:]
     step = pl.program_id(0)
-    width = gate_ref.shape[1] // 2
+    width = gate_ref.shape[1]
     hidden, gate_grad, up_grad = hidden_parts(act_ref)
 
     @pl.when(step == 0)
     def _():
         res_ref[...] = jnp.zeros_like(res_ref)
 
+    dx = dot(gate_grad, gate_ref[0], 1, 1)
     for d in range(4):
 
         @pl.when(step == d)
         def _():
-            outcome = prob_ref[:, 0:1] * dot(hidden, down_refs[d][...], 1, 1)
-            res_ref[:, 0:width] = outcome
-
-    dx = dot(gate_grad, gate_ref[0, 0:width], 1, 1)
-    dx += dot(up_grad, gate_ref[0, width : 2 * width], 1, 1)
-    res_ref[:, DY_LANE : DY_LANE + width] = dx
+            res_ref[:, 0:width] = prob_ref[:, 0:1] * dot(hidden, down_refs[d][...], 1, 1)
+            res_ref[:, DY_LANE : DY_LANE + width] = dx + dot(up_grad, up_refs[d][...], 1, 1)
+
     out_ref[0] = split_lanes(tmp_ref, res_ref[...])
 
 
-def gate_grad_kernel(act_ref, rows_ref, out_ref):
-    _, gate_grad, up_grad = hidden_parts(act_ref)
-    width = out_ref.shape[1] // 2
-    x = rows_ref[0, :, 0:width]
-    out_ref[0, 0:width] = dot(x, gate_grad, 0, 0).astype(BF16)
-    out_ref[0, width : 2 * width] = dot(x, up_grad, 0, 0).astype(BF16)
-
-
-def down_grad_kernel(x_ref, act_ref, rows_ref, *out_refs):
-    hidden = hidden_parts(act_ref)[0]
+def weight_kernel(x_ref, act_ref, *refs):
+    row_refs, out_refs, acc_ref = refs[:4], refs[4:7], refs[7]
+    step = pl.program_id(0)
     width = out_refs[0].shape[0]
-    grad = rows_ref[0, :, DY_LANE : DY_LANE + width]
+    hidden, gate_grad, up_grad = hidden_parts(act_ref.at[0])
+
+    @pl.when(step == 0)
+    def _():
+        acc_ref[...] = jnp.zeros_like(acc_ref)
+
     for d in range(4):
 
-        @pl.when(pl.program_id(0) == d)
+        @pl.when(step == d)
         def _():
-            out_refs[d][...] = dot(grad, hidden, 0, 0).astype(BF16)
-
-
-def sum_kernel(*refs):
-    total = refs[0][...].astype(F32)
-    for ref in refs[1:-1]:
-        total += ref[...].astype(F32)
-    refs[-1][...] = total.astype(BF16)
+            x = row_refs[d][:, 0:width]
+            grad = row_refs[d][:, DY_LANE : DY_LANE + width]
+            acc_ref[0] += dot(x, gate_grad, 0, 0)
+            acc_ref[1] += dot(x, up_grad, 0, 0)
+            acc_ref[2] += dot(grad, hidden, 0, 0)
+
+    @pl.when(step == pl.num_programs(0) - 1)
+    def _():
+        for part in range(3):
+            out_refs[part][...] = acc_ref[part].astype(BF16)
 
 
 def combine_kernel(pick_ref, tiles_ref, out_ref, tmp_ref):
@@ -242,10 +236,12 @@
     order = me_x[None].astype(jnp.int32)
     shifts = [[(i, (i + d) % share_x) for i in range(share_x)] for d in range(share_x)]
 
-    gates = jnp.concatenate([w_gate[0], w_up[0]], axis=0)
-    gates = lax.all_gather(gates, "x", axis=0, tiled=False)
-    down = w_down[0].T
-    downs = [down] + [lax.ppermute(down, "x", shifts[d]) for d in range(1, share_x)]
+    def shift(array, d):
+        return lax.ppermute(array, "x", shifts[d])
+
+    gates = lax.all_gather(w_gate[0], "x", axis=0, tiled=False)
+    up, down = w_up[0], w_down[0].T
+    up_right, down_left = shift(up, 1), shift(down, 3)
 
     lists = lax.pad(
         block_lists[0].astype(BF16),
@@ -256,12 +252,14 @@
         pack_kernel,
         jax.ShapeDtypeStruct((groups, BLK, LANES), BF16),
         (tokens.T, grad_output.T, gate_prob.T, lists),
+        VMEM_LARGE,
         scratch_shapes=[pltpu.VMEM((LANES, LANES), BF16)],
     )
     info = routing_info(expert_slot, block_counts, entries, share_x)
     mine = (expert_slot == lax.axis_index(GROUP)).astype(F32)
     mark = lax.pad(mine, jnp.zeros((), F32), ((P_LANE, 16, 0),))[None]
     spread = exchange(packed, GROUP).reshape(groups * BLK, LANES)
+    spread, up_right, down_left = lax.optimization_barrier((spread, up_right, down_left))
     sent, pick = call(
         select_kernel,
         (
@@ -271,6 +269,8 @@
         (spread, info),
         scratch_shapes=[pltpu.VMEM((4 * total, 128), F32)],
     )
+    ups = [up, up_right, shift(up_right, 1), shift(up, 3)]
+    downs = [down, shift(down, 1), shift(down_left, 3), down_left]
     pieces = (share_x * groups, 4 * picked // share_x, 128)
     tiles = exchange(sent.reshape(pieces), OWNERS).reshape(share_x, 4 * count, 128)
 
@@ -284,17 +284,13 @@
         return pl.BlockSpec(shape, lambda *_: (0,) * len(shape))
 
     tile_block = (1, 4 * count, 128)
-    row_block = (1, count, LANES)
-    gate_block = (1, 2 * width, hid)
+    gate_block = (1, width, hid)
     act_shape = (share_y, 3 * count, hid // share_y)
-    parts, rows, prob = call(
+    *rows, parts, prob = call(
         hidden_kernel,
-        (
-            jax.ShapeDtypeStruct(act_shape, BF16),
-            jax.ShapeDtypeStruct((share_x, count, LANES), BF16),
-            jax.ShapeDtypeStruct((count, 128), F32),
-        ),
-        (order, tiles, mark, gates, *downs),
+        (jax.ShapeDtypeStruct((count, LANES), BF16),) * 4
+        + (jax.ShapeDtypeStruct(act_shape, BF16), jax.ShapeDtypeStruct((count, 128), F32)),
+        (order, tiles, mark, gates, *ups, *downs),
         VMEM_LARGE,
         grid_spec=pltpu.PrefetchScalarGridSpec(
             num_scalar_prefetch=1,
@@ -304,8 +300,8 @@
                 whole(1, 256),
                 pl.BlockSpec(gate_block, before),
             ]
-            + [whole(width, hid)] * 4,
-            out_specs=[whole(*act_shape), pl.BlockSpec(row_block, before), whole(count, 128)],
+            + [whole(width, hid)] * 8,
+            out_specs=[whole(count, LANES)] * 4 + [whole(*act_shape), whole(count, 128)],
             scratch_shapes=[
                 pltpu.VMEM((3, count, hid), F32),
                 pltpu.VMEM((4 * count, 128), F32),
@@ -313,48 +309,39 @@
         ),
     )
     parts = exchange(parts, "y")
+    rows = [rows[0]] + [shift(rows[d], share_x - d) for d in range(1, share_x)]
+    parts, *rows = lax.optimization_barrier((parts, *rows))
     act = call(point_kernel, jax.ShapeDtypeStruct(act_shape[1:], BF16), (parts,))
     act = lax.all_gather(act, "y", axis=0, tiled=False)
+    all_act = lax.all_gather(act, "x", axis=0, tiled=False)
     results = call(
         result_kernel,
         jax.ShapeDtypeStruct((share_x, 4 * count, 128), BF16),
-        (order, act, prob, gates, *downs),
+        (order, act, prob, gates, *ups, *downs),
         VMEM_LARGE,
         grid_spec=pltpu.PrefetchScalarGridSpec(
             num_scalar_prefetch=1,
             grid=(share_x,),
             in_specs=[whole(*act_shape), whole(count, 128), pl.BlockSpec(gate_block, before)]
-            + [whole(width, hid)] * 4,
+            + [whole(width, hid)] * 8,
             out_specs=pl.BlockSpec(tile_block, before),
             scratch_shapes=[pltpu.VMEM((count, LANES), F32), pltpu.VMEM((4 * count, 128), F32)],
         ),
     )
-    late_act, results = lax.optimization_barrier((act, results))
-    gate_grads = call(
-        gate_grad_kernel,
-        jax.ShapeDtypeStruct((share_x, 2 * width, hid), BF16),
-        (late_act, rows),
+    weights = call(
+        weight_kernel,
+        (jax.ShapeDtypeStruct((width, hid), BF16),) * 3,
+        (order, all_act, *rows),
         VMEM_LARGE,
-        grid=(share_x,),
-        in_specs=[whole(*act_shape), pl.BlockSpec(row_block, lambda i: (i, 0, 0))],
-        out_specs=pl.BlockSpec(gate_block, lambda i: (i, 0, 0)),
-    )
-    gate_grads = lax.psum_scatter(gate_grads, "x", scatter_dimension=0, tiled=False)
-    down_grads = call(
-        down_grad_kernel,
-        (jax.ShapeDtypeStruct((width, hid), BF16),) * 4,
-        (order, late_act, rows),
         grid_spec=pltpu.PrefetchScalarGridSpec(
             num_scalar_prefetch=1,
             grid=(share_x,),
-            in_specs=[whole(*act_shape), pl.BlockSpec(row_block, after)],
-            out_specs=[whole(width, hid)] * 4,
+            in_specs=[pl.BlockSpec((1,) + act_shape, lambda d, x: after(d, x) + (0,))]
+            + [whole(count, LANES)] * 4,
+            out_specs=[whole(width, hid)] * 3,
+            scratch_shapes=[pltpu.VMEM((3, width, hid), F32)],
         ),
     )
-    down_grads = [down_grads[0]] + [
-        lax.ppermute(down_grads[d], "x", shifts[d]) for d in range(1, share_x)
-    ]
-    down_grad = call(sum_kernel, jax.ShapeDtypeStruct((width, hid), BF16), down_grads)
     back = exchange(results.reshape(pieces), OWNERS).reshape(4 * total, 128)
     summed = call(
         combine_kernel,
@@ -371,9 +358,9 @@
     return (
         out.T,
         dx.T,
-        gate_grads[None, 0:width],
-        gate_grads[None, width:],
-        down_grad.T[None],
+        weights[0][None],
+        weights[1][None],
+        weights[2].T[None],
     )
 
 

time: 255 us -> 231 us (0.906)
  blocking collectives: 92.3 us -> 77.1 us
  waiting for transfers between devices: 70.9 us -> 55.8 us
  starting transfers between devices: 41.6 us -> 50.8 us
    ppermute x6 -> x9, waiting for transfers between devices: 54.7 us -> 27.2 us  [shift(): return lax.ppermute(array, 'x', shifts[d])]
    all_to_all x2, blocking collectives: 68.5 us -> 53.6 us  [exchange(): return lax.all_to_all(array, axis, split_axis=0, concat_axis=0, tiled=True)]
    all_to_all x3, waiting for transfers between devices: 16.1 us -> 27.9 us  [exchange(): return lax.all_to_all(array, axis, split_axis=0, concat_axis=0, tiled=True)]
    ppermute x6 -> x9, starting transfers between devices: 18.9 us -> 27.5 us  [shift(): return lax.ppermute(array, 'x', shifts[d])]
    pallas_call x10 -> x8, Pallas kernels: 26.9 us -> 26.2 us  [call(): pl.pallas_call(kernel, out_shape=out_shape, compiler_params=pltpu.Compile...]
  transfers between devices with their start and end apart: 11 -> 14, of which waited for: 6 -> 7; matrix products, arithmetic and copies ran while one was open for 1% -> 2% of each run, Pallas kernels for 3% -> 6%
where the time goes in v3:
time: 231 us; the launch traced here: 230 us
  blocking collectives  77.1 us (33%)
  waiting for transfers between devices  55.8 us (24%)
  starting transfers between devices  50.8 us (22%)
  Pallas kernels  26.2 us (11%)
  between operations  14.4 us (6%)
  other arithmetic  3.16 us (1%)
  local copies, waits for them, and re-layouts  2.91 us (1%)
    all_to_all x2, blocking collectives, exchange(): return lax.all_to_all(array, axis, split_axis=0, concat_axis=0, tiled=True)  53.6 us
    all_to_all x3, waiting for transfers between devices, exchange(): return lax.all_to_all(array, axis, split_axis=0, concat_axis=0, tiled=True)  27.9 us
    ppermute x9, starting transfers between devices, shift(): return lax.ppermute(array, 'x', shifts[d])  27.5 us
    ppermute x9, waiting for transfers between devices, shift(): return lax.ppermute(array, 'x', shifts[d])  27.2 us
    pallas_call x8, Pallas kernels, call(): pl.pallas_call(kernel, out_shape=out_shape, compiler_params=pltpu.Compile...  26.2 us
    all_gather x1, blocking collectives, body(): act = lax.all_gather(act, 'y', axis=0, tiled=False)  23.4 us
    all_to_all x3, starting transfers between devices, exchange(): return lax.all_to_all(array, axis, split_axis=0, concat_axis=0, tiled=True)  23.3 us
  transfers between devices with their start and end apart: 14, of which 7 were waited for; matrix products, arithmetic and copies ran while one was open for 2% of the time, Pallas kernels for 6%

profile of v3, /device:TPU:1, one launch (start us, length us, event | category | flops | bytes accessed | tf_op | source)
XLA Modules:
  0.0 230.2 jit_solution(16912162332824617473)
XLA Ops:
  7.2 0.0 all-gather.5.cloned.1.call-start
  7.2 0.7 all-gather.5.cloned.1.call-update
  7.9 4.0 %collective-permute-start = (bf16[224,1024]{1,0:T(8,128)(2,1)}, bf16[224,1024]{1,0:T(8,128)(2,1)S(1)}, u32[]{:S(2)}, u32[]{:S(2)}) collective-permute-start(bf16[224,1024]{1,0:T(8,128)(2,1)} %bitcast.44), channel_id=1, source_target_pairs={{0,1},{1,2},{2,3},{3,0},{4,5},{5,6},{6,7},{7,4},{8,9},{9,10},{10,1... | collective-permute-start | bytes 1376264 | tf_op jit(solution)/shard_map/ppermute | solution.py:240
  11.9 3.2 %collective-permute-start.1 = (bf16[224,1024]{1,0:T(8,128)(2,1)}, bf16[224,1024]{1,0:T(8,128)(2,1)S(1)}, u32[]{:S(2)}, u32[]{:S(2)}) collective-permute-start(bf16[224,1024]{1,0:T(8,128)(2,1)} %bitcast.48), channel_id=1, source_target_pairs={{0,3},{1,0},{2,1},{3,2},{4,7},{5,4},{6,5},{7,6},{8,11},{9,8},{10,9... | collective-permute-start | bytes 1376264 | tf_op jit(solution)/shard_map/ppermute | solution.py:240
  15.1 0.8 copy.21
  15.9 0.7 pad.7.list_ref
  16.6 2.3 %shard_map.128 = bf16[16,32,512]{2,1,0:T(8,128)(2,1)} custom-call(bf16[224,512]{1,0:T(8,128)(2,1)} %bitcast.52, bf16[224,512]{1,0:T(8,128)(2,1)} %bitcast.53, bf16[16,512]{1,0:T(8,128)(2,1)} %bitcast.54, bf16[32,512]{1,0:T(8,128)(2,1)} %pad.7.list_ref), custom_call_target="tpu_custom_call" | custom-call | tf_op jit(solution)/shard_map/pallas_call | solution.py:27
  18.9 11.7 %all-to-all-start = ((bf16[16,32,512]{2,1,0:T(8,128)(2,1)}), bf16[16,32,512]{2,1,0:T(8,128)(2,1)S(1)}, u32[]{:S(2)}, u32[]{:S(2)}) async-start(bf16[16,32,512]{2,1,0:T(8,128)(2,1)} %shard_map.128), calls=%async_computation | async-start | bytes 1048576 | tf_op jit(solution)/shard_map/all_to_all | solution.py:219
  30.6 0.7 fusion.5
  31.4 0.8 multiply_reduce_fusion.1
  32.2 0.1 multiply_reduce_fusion
  32.4 0.7 select_reduce_fusion
  33.1 0.1 fusion
  33.2 0.1 reshape.244
  33.3 0.1 reshape.251
  33.5 0.1 reshape.248
  33.7 0.2 copy.22.info_ref
  33.9 14.1 %all-to-all-done = bf16[16,32,512]{2,1,0:T(8,128)(2,1)S(1)} async-done(((bf16[16,32,512]{2,1,0:T(8,128)(2,1)}), bf16[16,32,512]{2,1,0:T(8,128)(2,1)S(1)}, u32[]{:S(2)}, u32[]{:S(2)}) %all-to-all-start) | async-done | bytes 524320 | tf_op jit(solution)/shard_map/all_to_all | solution.py:219
  48.0 2.3 %shard_map.129 = (bf16[2560,128]{1,0:T(8,128)(2,1)}, bf16[640,512]{1,0:T(8,128)(2,1)S(1)}) custom-call(bf16[512,512]{1,0:T(8,128)(2,1)S(1)} %bitcast.37, s32[640,3]{1,0:T(8,128)S(1)} %copy.22.info_ref), custom_call_target="tpu_custom_call" | custom-call | tf_op jit(solution)/shard_map/pallas_call | solution.py:27
  50.3 4.7 %all-to-all-start.1 = ((bf16[64,40,128]{2,1,0:T(8,128)(2,1)}), bf16[64,40,128]{2,1,0:T(8,128)(2,1)S(1)}, u32[]{:S(2)}, u32[]{:S(2)}) async-start(bf16[64,40,128]{2,1,0:T(8,128)(2,1)} %bitcast.13), calls=%async_computation.1 | async-start | bytes 1310720 | tf_op jit(solution)/shard_map/all_to_all | solution.py:219
  55.0 4.7 %collective-permute-start.3 = (bf16[224,1024]{1,0:T(8,128)(2,1)S(1)}, bf16[224,1024]{1,0:T(8,128)(2,1)}, u32[]{:S(2)}, u32[]{:S(2)}) collective-permute-start(bf16[224,1024]{1,0:T(8,128)(2,1)S(1)} %bitcast.47), channel_id=1, source_target_pairs={{0,3},{1,0},{2,1},{3,2},{4,7},{5,4},{6,5},{7,6},{8,11},{9,8},{10,9... | collective-permute-start | bytes 1376264 | tf_op jit(solution)/shard_map/ppermute | solution.py:240
  59.8 1.9 collective-permute-start.4
  61.7 2.0 collective-permute-start.2
  63.6 4.5 %collective-permute-start.5 = (bf16[224,1024]{1,0:T(8,128)(2,1)S(1)}, bf16[224,1024]{1,0:T(8,128)(2,1)}, u32[]{:S(2)}, u32[]{:S(2)}) collective-permute-start(bf16[224,1024]{1,0:T(8,128)(2,1)S(1)} %collective-permute-done.1.refs_7_), channel_id=1, source_target_pairs={{0,3},{1,0},{2,1},{3,2},{4,7},{5,4},{6,5},{7,6},{8,11},{9,8},{10,9... | collective-permute-start | bytes 1376264 | tf_op jit(solution)/shard_map/ppermute | solution.py:240
  68.2 0.6 pad_convert_fusion
  68.9 6.2 %collective-permute-done.3.refs_3_ = bf16[224,1024]{1,0:T(8,128)(2,1)} collective-permute-done((bf16[224,1024]{1,0:T(8,128)(2,1)S(1)}, bf16[224,1024]{1,0:T(8,128)(2,1)}, u32[]{:S(2)}, u32[]{:S(2)}) %collective-permute-start.3) | collective-permute-done | bytes 458784 | tf_op jit(solution)/shard_map/ppermute | solution.py:240
  75.1 4.4 %collective-permute-done.4.refs_5_ = bf16[224,1024]{1,0:T(8,128)(2,1)} collective-permute-done((bf16[224,1024]{1,0:T(8,128)(2,1)S(1)}, bf16[224,1024]{1,0:T(8,128)(2,1)}, u32[]{:S(2)}, u32[]{:S(2)}) %collective-permute-start.4) | collective-permute-done | bytes 458784 | tf_op jit(solution)/shard_map/ppermute | solution.py:240
  79.5 9.8 %collective-permute-done.2.refs_2_ = bf16[224,1024]{1,0:T(8,128)(2,1)} collective-permute-done((bf16[224,1024]{1,0:T(8,128)(2,1)S(1)}, bf16[224,1024]{1,0:T(8,128)(2,1)}, u32[]{:S(2)}, u32[]{:S(2)}) %collective-permute-start.2) | collective-permute-done | bytes 458784 | tf_op jit(solution)/shard_map/ppermute | solution.py:240
  89.3 0.0 all-gather.5.cloned.1.call-done.gate_ref
  89.4 0.8 copy-done
  90.2 6.9 %shard_map.130 = (bf16[160,512]{1,0:T(8,128)(2,1)}, bf16[160,512]{1,0:T(8,128)(2,1)}, bf16[160,512]{1,0:T(8,128)(2,1)}, bf16[160,512]{1,0:T(8,128)(2,1)}, bf16[8...) custom-call(s32[1]{0:T(128)} %bitcast.12.x_ref, bf16[4,640,128]{2,1,0:T(8,128)(2,1)} %bitcast.43, f32[1,256]{1,0:T(1,128)} %bitcast.55, ...), custom_call_target="tpu_custom_call" | custom-call | tf_op jit(solution)/shard_map/pallas_call | solution.py:27
  97.1 6.8 %all-to-all-start.2 = ((bf16[8,480,128]{2,1,0:T(8,128)(2,1)}), bf16[8,480,128]{2,1,0:T(8,128)(2,1)S(1)}, u32[]{:S(2)}, u32[]{:S(2)}) async-start(bf16[8,480,128]{2,1,0:T(8,128)(2,1)} %get-tuple-element.31), calls=%async_computation.2 | async-start | bytes 1966080 | tf_op jit(solution)/shard_map/all_to_all | solution.py:219
  103.9 0.0 all-gather.7.cloned.1.call-start
  104.0 1.9 collective-permute-start.6
  105.9 2.6 %collective-permute-start.7 = (bf16[160,512]{1,0:T(8,128)(2,1)}, bf16[160,512]{1,0:T(8,128)(2,1)S(1)}, u32[]{:S(2)}, u32[]{:S(2)}) collective-permute-start(bf16[160,512]{1,0:T(8,128)(2,1)} %get-tuple-element.34), channel_id=1, source_target_pairs={{0,2},{1,3},{2,0},{3,1},{4,6},{5,7},{6,4},{7,5},{8,10},{9,11},{10,... | collective-permute-start | bytes 491528 | tf_op jit(solution)/shard_map/ppermute | solution.py:240
  108.5 2.7 %collective-permute-start.8 = (bf16[160,512]{1,0:T(8,128)(2,1)}, bf16[160,512]{1,0:T(8,128)(2,1)S(1)}, u32[]{:S(2)}, u32[]{:S(2)}) collective-permute-start(bf16[160,512]{1,0:T(8,128)(2,1)} %get-tuple-element.35), channel_id=1, source_target_pairs={{0,1},{1,2},{2,3},{3,0},{4,5},{5,6},{6,7},{7,4},{8,9},{9,10},{10,1... | collective-permute-start | bytes 491528 | tf_op jit(solution)/shard_map/ppermute | solution.py:240
  111.2 2.8 %collective-permute-done.7.refs_2_ = bf16[160,512]{1,0:T(8,128)(2,1)S(1)} collective-permute-done((bf16[160,512]{1,0:T(8,128)(2,1)}, bf16[160,512]{1,0:T(8,128)(2,1)S(1)}, u32[]{:S(2)}, u32[]{:S(2)}) %collective-permute-start.7) | collective-permute-done | bytes 163872 | tf_op jit(solution)/shard_map/ppermute | solution.py:240
  114.0 3.9 %collective-permute-done.8.refs_3_ = bf16[160,512]{1,0:T(8,128)(2,1)S(1)} collective-permute-done((bf16[160,512]{1,0:T(8,128)(2,1)}, bf16[160,512]{1,0:T(8,128)(2,1)S(1)}, u32[]{:S(2)}, u32[]{:S(2)}) %collective-permute-start.8) | collective-permute-done | bytes 163872 | tf_op jit(solution)/shard_map/ppermute | solution.py:240
  118.0 13.8 %all-to-all-done.2.parts_ref = bf16[8,480,128]{2,1,0:T(8,128)(2,1)S(1)} async-done(((bf16[8,480,128]{2,1,0:T(8,128)(2,1)}), bf16[8,480,128]{2,1,0:T(8,128)(2,1)S(1)}, u32[]{:S(2)}, u32[]{:S(2)}) %all-to-all-start.2) | async-done | bytes 983072 | tf_op jit(solution)/shard_map/all_to_all | solution.py:219
  131.7 0.2 shard_map.131
  131.9 23.4 %all-gather = bf16[3840,128]{1,0:T(8,128)(2,1)} all-gather(bf16[480,128]{1,0:T(8,128)(2,1)S(1)} %shard_map.131), channel_id=2, replica_groups=mesh['z'=8,'core'=2,'y'=8,'x'=4] {'y'}, dimensions={0}, use_global_device_ids=true | all-gather | bytes 1105920 | tf_op jit(solution)/shard_map/all_gather | solution.py:315
  155.3 0.0 all-gather.7.cloned.1.call-update
  155.4 7.0 %shard_map.132 = bf16[4,640,128]{2,1,0:T(8,128)(2,1)} custom-call(s32[1]{0:T(128)} %bitcast.12.x_ref, bf16[8,480,128]{2,1,0:T(8,128)(2,1)} %bitcast.40, f32[160,128]{1,0:T(8,128)} %get-tuple-element.37.prob_ref, bf16[4,224,1024]{2,1,0:T(8,128)(2,1)} %all-gather.5.cloned.1.call-done.gate_ref, bf16[224,1024]{1,0:T(8,128)(2,1)} %bitcast.46, ...), custom_call_target="tpu_custom_call" | custom-call | tf_op jit(solution)/shard_map/pallas_call | solution.py:27
  162.3 31.7 %all_to_all.25 = bf16[64,40,128]{2,1,0:T(8,128)(2,1)S(1)} all-to-all(bf16[64,40,128]{2,1,0:T(8,128)(2,1)} %bitcast.42), channel_id=1, replica_groups=mesh['z'=8,'core'=2,'y'=8,'x'=4] {'x','z','core'}, dimensions={0} | all-to-all | bytes 1310720 | tf_op jit(solution)/shard_map/all_to_all | solution.py:219
  194.0 0.6 shard_map.133
  194.7 21.9 %all_to_all.26 = bf16[16,32,512]{2,1,0:T(8,128)(2,1)S(1)} all-to-all(bf16[16,32,512]{2,1,0:T(8,128)(2,1)S(1)} %bitcast.36), channel_id=1, replica_groups=mesh['z'=8,'core'=2,'y'=8,'x'=4] {'z','core'}, dimensions={0} | all-to-all | bytes 1048576 | tf_op jit(solution)/shard_map/all_to_all | solution.py:219
  216.6 1.2 shard_map.134
  217.8 5.6 %shard_map.135 = (bf16[224,1024]{1,0:T(8,128)(2,1)}, bf16[224,1024]{1,0:T(8,128)(2,1)}, bf16[224,1024]{1,0:T(8,128)(2,1)}) custom-call(s32[1]{0:T(128)} %bitcast.12.x_ref, bf16[4,8,480,128]{3,2,1,0:T(8,128)(2,1)} %bitcast.41, bf16[160,512]{1,0:T(8,128)(2,1)} %get-tuple-element.40.refs_0_, bf16[160,512]{1,0:T(8,128)(2,1)} %copy-done.5, ...), custom_call_target="tpu_custom_call" | custom-call | tf_op jit(solution)/shard_map/pallas_call | solution.py:27
  (31 shorter events, 0.1 us)
Async XLA Ops:
  7.2 47.9 %copy-start.1 = (bf16[1,224,1024]{2,1,0:T(8,128)(2,1)S(1)}, bf16[1,224,1024]{2,1,0:T(8,128)(2,1)}, u32[]{:S(2)}) copy-start(bf16[1,224,1024]{2,1,0:T(8,128)(2,1)} %param.13) | copy-start | bytes 1376260
  7.2 52.6 %copy-start.2 = (bf16[1,1024,224]{1,2,0:T(8,128)(2,1)S(1)}, bf16[1,1024,224]{1,2,0:T(8,128)(2,1)}, u32[]{:S(2)}) copy-start(bf16[1,1024,224]{1,2,0:T(8,128)(2,1)} %param.14) | copy-start | bytes 1376260
  7.2 61.0 %copy-start.8 = (s32[16]{0:T(128)S(1)}, s32[16]{0:T(128)}, u32[]{:S(2)}) copy-start(s32[16]{0:T(128)} %param.15) | copy-start | bytes 196
  7.2 82.1 %all-gather.5.cloned.1.call-start = ((), (), s32[]{:S(2)}) async-start(), calls=%async_computation.5 | async-start | bytes 2293760 | tf_op jit(solution)/shard_map/all_gather | solution.py:242
  7.9 25.9 %collective-permute-start = (bf16[224,1024]{1,0:T(8,128)(2,1)}, bf16[224,1024]{1,0:T(8,128)(2,1)S(1)}, u32[]{:S(2)}, u32[]{:S(2)}) collective-permute-start(bf16[224,1024]{1,0:T(8,128)(2,1)} %bitcast.44), channel_id=1, source_target_pairs={{0,1},{1,2},{2,3},{3,0},{4,5},{5,6},{6,7},{7,4},{8,9},{9,10},{10,1... | collective-permute-start | bytes 1376264 | tf_op jit(solution)/shard_map/ppermute | solution.py:240
  11.9 22.0 %collective-permute-start.1 = (bf16[224,1024]{1,0:T(8,128)(2,1)}, bf16[224,1024]{1,0:T(8,128)(2,1)S(1)}, u32[]{:S(2)}, u32[]{:S(2)}) collective-permute-start(bf16[224,1024]{1,0:T(8,128)(2,1)} %bitcast.48), channel_id=1, source_target_pairs={{0,3},{1,0},{2,1},{3,2},{4,7},{5,4},{6,5},{7,6},{8,11},{9,8},{10,9... | collective-permute-start | bytes 1376264 | tf_op jit(solution)/shard_map/ppermute | solution.py:240
  18.9 29.1 %all-to-all-start = ((bf16[16,32,512]{2,1,0:T(8,128)(2,1)}), bf16[16,32,512]{2,1,0:T(8,128)(2,1)S(1)}, u32[]{:S(2)}, u32[]{:S(2)}) async-start(bf16[16,32,512]{2,1,0:T(8,128)(2,1)} %shard_map.128), calls=%async_computation | async-start | bytes 1048576 | tf_op jit(solution)/shard_map/all_to_all | solution.py:219
  33.8 55.5 %copy-start.3 = (bf16[224,1024]{1,0:T(8,128)(2,1)}, bf16[224,1024]{1,0:T(8,128)(2,1)S(1)}, u32[]{:S(2)}) copy-start(bf16[224,1024]{1,0:T(8,128)(2,1)S(1)} %collective-permute-done.refs_1_) | copy-start | bytes 1376260
  33.9 55.5 %copy-start.4 = (bf16[224,1024]{1,0:T(8,128)(2,1)}, bf16[224,1024]{1,0:T(8,128)(2,1)S(1)}, u32[]{:S(2)}) copy-start(bf16[224,1024]{1,0:T(8,128)(2,1)S(1)} %collective-permute-done.1.refs_7_) | copy-start | bytes 1376260
  50.3 39.0 %all-to-all-start.1 = ((bf16[64,40,128]{2,1,0:T(8,128)(2,1)}), bf16[64,40,128]{2,1,0:T(8,128)(2,1)S(1)}, u32[]{:S(2)}, u32[]{:S(2)}) async-start(bf16[64,40,128]{2,1,0:T(8,128)(2,1)} %bitcast.13), calls=%async_computation.1 | async-start | bytes 1310720 | tf_op jit(solution)/shard_map/all_to_all | solution.py:219
  55.0 20.1 %collective-permute-start.3 = (bf16[224,1024]{1,0:T(8,128)(2,1)S(1)}, bf16[224,1024]{1,0:T(8,128)(2,1)}, u32[]{:S(2)}, u32[]{:S(2)}) collective-permute-start(bf16[224,1024]{1,0:T(8,128)(2,1)S(1)} %bitcast.47), channel_id=1, source_target_pairs={{0,3},{1,0},{2,1},{3,2},{4,7},{5,4},{6,5},{7,6},{8,11},{9,8},{10,9... | collective-permute-start | bytes 1376264 | tf_op jit(solution)/shard_map/ppermute | solution.py:240
  59.8 19.7 %collective-permute-start.4 = (bf16[224,1024]{1,0:T(8,128)(2,1)S(1)}, bf16[224,1024]{1,0:T(8,128)(2,1)}, u32[]{:S(2)}, u32[]{:S(2)}) collective-permute-start(bf16[224,1024]{1,0:T(8,128)(2,1)S(1)} %bitcast.51), channel_id=1, source_target_pairs={{0,1},{1,2},{2,3},{3,0},{4,5},{5,6},{6,7},{7,4},{8,9},{9,10},{10,1... | collective-permute-start | bytes 1376264 | tf_op jit(solution)/shard_map/ppermute | solution.py:240
  61.7 27.6 %collective-permute-start.2 = (bf16[224,1024]{1,0:T(8,128)(2,1)S(1)}, bf16[224,1024]{1,0:T(8,128)(2,1)}, u32[]{:S(2)}, u32[]{:S(2)}) collective-permute-start(bf16[224,1024]{1,0:T(8,128)(2,1)S(1)} %collective-permute-done.refs_1_), channel_id=1, source_target_pairs={{0,1},{1,2},{2,3},{3,0},{4,5},{5,6},{6,7},{7,4},{8,9},{9,10},{10,1... | collective-permute-start | bytes 1376264 | tf_op jit(solution)/shard_map/ppermute | solution.py:240
  63.6 25.7 %collective-permute-start.5 = (bf16[224,1024]{1,0:T(8,128)(2,1)S(1)}, bf16[224,1024]{1,0:T(8,128)(2,1)}, u32[]{:S(2)}, u32[]{:S(2)}) collective-permute-start(bf16[224,1024]{1,0:T(8,128)(2,1)S(1)} %collective-permute-done.1.refs_7_), channel_id=1, source_target_pairs={{0,3},{1,0},{2,1},{3,2},{4,7},{5,4},{6,5},{7,6},{8,11},{9,8},{10,9... | collective-permute-start | bytes 1376264 | tf_op jit(solution)/shard_map/ppermute | solution.py:240
  89.3 0.9 copy-start
  97.1 34.6 %all-to-all-start.2 = ((bf16[8,480,128]{2,1,0:T(8,128)(2,1)}), bf16[8,480,128]{2,1,0:T(8,128)(2,1)S(1)}, u32[]{:S(2)}, u32[]{:S(2)}) async-start(bf16[8,480,128]{2,1,0:T(8,128)(2,1)} %get-tuple-element.31), calls=%async_computation.2 | async-start | bytes 1966080 | tf_op jit(solution)/shard_map/all_to_all | solution.py:219
  103.9 113.8 %all-gather.7.cloned.1.call-start = ((), (), s32[]{:S(2)}) async-start(), calls=%async_computation.6 | async-start | bytes 4915200 | tf_op jit(solution)/shard_map/all_gather | solution.py:316
  104.0 7.2 %collective-permute-start.6 = (bf16[160,512]{1,0:T(8,128)(2,1)}, bf16[160,512]{1,0:T(8,128)(2,1)S(1)}, u32[]{:S(2)}, u32[]{:S(2)}) collective-permute-start(bf16[160,512]{1,0:T(8,128)(2,1)} %get-tuple-element.33), channel_id=1, source_target_pairs={{0,3},{1,0},{2,1},{3,2},{4,7},{5,4},{6,5},{7,6},{8,11},{9,8},{10,9... | collective-permute-start | bytes 491528 | tf_op jit(solution)/shard_map/ppermute | solution.py:240
  105.9 8.1 %collective-permute-start.7 = (bf16[160,512]{1,0:T(8,128)(2,1)}, bf16[160,512]{1,0:T(8,128)(2,1)S(1)}, u32[]{:S(2)}, u32[]{:S(2)}) collective-permute-start(bf16[160,512]{1,0:T(8,128)(2,1)} %get-tuple-element.34), channel_id=1, source_target_pairs={{0,2},{1,3},{2,0},{3,1},{4,6},{5,7},{6,4},{7,5},{8,10},{9,11},{10,... | collective-permute-start | bytes 491528 | tf_op jit(solution)/shard_map/ppermute | solution.py:240
  108.5 9.5 %collective-permute-start.8 = (bf16[160,512]{1,0:T(8,128)(2,1)}, bf16[160,512]{1,0:T(8,128)(2,1)S(1)}, u32[]{:S(2)}, u32[]{:S(2)}) collective-permute-start(bf16[160,512]{1,0:T(8,128)(2,1)} %get-tuple-element.35), channel_id=1, source_target_pairs={{0,1},{1,2},{2,3},{3,0},{4,5},{5,6},{6,7},{7,4},{8,9},{9,10},{10,1... | collective-permute-start | bytes 491528 | tf_op jit(solution)/shard_map/ppermute | solution.py:240
  111.2 51.1 %copy-start.5 = (bf16[160,512]{1,0:T(8,128)(2,1)}, bf16[160,512]{1,0:T(8,128)(2,1)S(1)}, u32[]{:S(2)}) copy-start(bf16[160,512]{1,0:T(8,128)(2,1)S(1)} %collective-permute-done.6.refs_1_) | copy-start | bytes 491524
  114.0 48.3 %copy-start.6 = (bf16[160,512]{1,0:T(8,128)(2,1)}, bf16[160,512]{1,0:T(8,128)(2,1)S(1)}, u32[]{:S(2)}) copy-start(bf16[160,512]{1,0:T(8,128)(2,1)S(1)} %collective-permute-done.7.refs_2_) | copy-start | bytes 491524
  118.0 44.4 %copy-start.7 = (bf16[160,512]{1,0:T(8,128)(2,1)}, bf16[160,512]{1,0:T(8,128)(2,1)S(1)}, u32[]{:S(2)}) copy-start(bf16[160,512]{1,0:T(8,128)(2,1)S(1)} %collective-permute-done.8.refs_3_) | copy-start | bytes 491524
Sparse Core Ops, SparseCore 0:
  10.1 39.4 all-gather.4
  155.5 56.2 all-gather.6

commit v4 on v3

--- a/solution.py
+++ b/solution.py
@@ -46,8 +46,12 @@
     all_ref[P_LANE : P_LANE + 16] = prob_ref[...]
     all_ref[DY_LANE : DY_LANE + width] = dy_ref[...]
     packed = dot(token_permutation(LANES), all_ref[...], 1, 1)
-    packed = packed.reshape(out_ref.shape) + list_ref[...].astype(F32)[None]
-    out_ref[...] = packed.astype(BF16)
+    lists = list_ref[:, 0, :].astype(F32).astype(BF16)
+    entry = lax.broadcasted_iota(jnp.int32, (lists.shape[0], LANES), 0)
+    lane = lax.broadcasted_iota(jnp.int32, (lists.shape[0], LANES), 1)
+    lists = dot(lists, (lane == entry + LIST_LANE).astype(BF16), 0, 0)
+    lists = jnp.concatenate([lists, jnp.zeros((BLK - lists.shape[0], LANES), F32)], axis=0)
+    out_ref[...] = (packed.reshape(out_ref.shape) + lists[None]).astype(BF16)
 
 
 def split_lanes(tmp_ref, rows):
@@ -122,11 +126,11 @@
     out_ref[2 * count :] = (grad * gate * sigma).astype(BF16)
 
 
-def hidden_parts(act):
-    count = act.shape[1] // 3
+def hidden_parts(act, parts):
+    count = act.shape[1] // parts
     return [
         jnp.concatenate([act[k, i * count : (i + 1) * count] for k in range(act.shape[0])], axis=1)
-        for i in range(3)
+        for i in range(parts)
     ]
 
 
@@ -134,7 +138,7 @@
     up_refs, down_refs, (out_ref, res_ref, tmp_ref) = refs[:4], refs[4:8], refs[8:]
     step = pl.program_id(0)
     width = gate_ref.shape[1]
-    hidden, gate_grad, up_grad = hidden_parts(act_ref)
+    hidden, gate_grad, up_grad = hidden_parts(act_ref, 3)
 
     @pl.when(step == 0)
     def _():
@@ -151,11 +155,11 @@
     out_ref[0] = split_lanes(tmp_ref, res_ref[...])
 
 
-def weight_kernel(x_ref, act_ref, *refs):
-    row_refs, out_refs, acc_ref = refs[:4], refs[4:7], refs[7]
+def gate_grad_kernel(x_ref, act_ref, *refs):
+    row_refs, out_refs, acc_ref = refs[:4], refs[4:6], refs[6]
     step = pl.program_id(0)
     width = out_refs[0].shape[0]
-    hidden, gate_grad, up_grad = hidden_parts(act_ref.at[0])
+    grads = hidden_parts(act_ref.at[0], 2)
 
     @pl.when(step == 0)
     def _():
@@ -166,15 +170,23 @@
         @pl.when(step == d)
         def _():
             x = row_refs[d][:, 0:width]
-            grad = row_refs[d][:, DY_LANE : DY_LANE + width]
-            acc_ref[0] += dot(x, gate_grad, 0, 0)
-            acc_ref[1] += dot(x, up_grad, 0, 0)
-            acc_ref[2] += dot(grad, hidden, 0, 0)
+            for part in range(2):
+                acc_ref[part] += dot(x, grads[part], 0, 0)
 
     @pl.when(step == pl.num_programs(0) - 1)
     def _():
-        for part in range(3):
+        for part in range(2):
             out_refs[part][...] = acc_ref[part].astype(BF16)
+
+
+def down_grad_kernel(*refs):
+    act_refs, row_refs, out_ref = refs[:4], refs[4:8], refs[8]
+    width = out_ref.shape[0]
+    total = 0.0
+    for d in range(4):
+        grad = row_refs[d][:, DY_LANE : DY_LANE + width]
+        total += dot(grad, hidden_parts(act_refs[d], 1)[0], 0, 0)
+    out_ref[...] = total.astype(BF16)
 
 
 def combine_kernel(pick_ref, tiles_ref, out_ref, tmp_ref):
@@ -241,17 +253,10 @@
 
     gates = lax.all_gather(w_gate[0], "x", axis=0, tiled=False)
     up, down = w_up[0], w_down[0].T
-    up_right, down_left = shift(up, 1), shift(down, 3)
-
-    lists = lax.pad(
-        block_lists[0].astype(BF16),
-        jnp.zeros((), BF16),
-        ((0, BLK - 16, 0), (LIST_LANE, LANES - LIST_LANE - entries, 0)),
-    )
     packed = call(
         pack_kernel,
         jax.ShapeDtypeStruct((groups, BLK, LANES), BF16),
-        (tokens.T, grad_output.T, gate_prob.T, lists),
+        (tokens.T, grad_output.T, gate_prob.T, block_lists.transpose(2, 0, 1)),
         VMEM_LARGE,
         scratch_shapes=[pltpu.VMEM((LANES, LANES), BF16)],
     )
@@ -259,6 +264,9 @@
     mine = (expert_slot == lax.axis_index(GROUP)).astype(F32)
     mark = lax.pad(mine, jnp.zeros((), F32), ((P_LANE, 16, 0),))[None]
     spread = exchange(packed, GROUP).reshape(groups * BLK, LANES)
+    info, up_late, down_late = lax.optimization_barrier((info, up, down))
+    up_right, down_left = shift(up_late, 1), shift(down_late, 3)
+    down_right, up_left = shift(down_late, 1), shift(up_late, 3)
     spread, up_right, down_left = lax.optimization_barrier((spread, up_right, down_left))
     sent, pick = call(
         select_kernel,
@@ -269,8 +277,9 @@
         (spread, info),
         scratch_shapes=[pltpu.VMEM((4 * total, 128), F32)],
     )
-    ups = [up, up_right, shift(up_right, 1), shift(up, 3)]
-    downs = [down, shift(down, 1), shift(down_left, 3), down_left]
+    sent, down_right, up_left = lax.optimization_barrier((sent, down_right, up_left))
+    ups = [up, up_right, shift(up_right, 1), up_left]
+    downs = [down, down_right, shift(down_left, 3), down_left]
     pieces = (share_x * groups, 4 * picked // share_x, 128)
     tiles = exchange(sent.reshape(pieces), OWNERS).reshape(share_x, 4 * count, 128)
 
@@ -313,7 +322,7 @@
     parts, *rows = lax.optimization_barrier((parts, *rows))
     act = call(point_kernel, jax.ShapeDtypeStruct(act_shape[1:], BF16), (parts,))
     act = lax.all_gather(act, "y", axis=0, tiled=False)
-    all_act = lax.all_gather(act, "x", axis=0, tiled=False)
+    grads = lax.all_gather(act[:, count:], "x", axis=0, tiled=False)
     results = call(
         result_kernel,
         jax.ShapeDtypeStruct((share_x, 4 * count, 128), BF16),
@@ -328,21 +337,26 @@
             scratch_shapes=[pltpu.VMEM((count, LANES), F32), pltpu.VMEM((4 * count, 128), F32)],
         ),
     )
-    weights = call(
-        weight_kernel,
-        (jax.ShapeDtypeStruct((width, hid), BF16),) * 3,
-        (order, all_act, *rows),
+    back = exchange(results.reshape(pieces), OWNERS).reshape(4 * total, 128)
+    own = act[:, 0:count]
+    hidden = [own] + [shift(own, share_x - d) for d in range(1, share_x)]
+    back, *hidden = lax.optimization_barrier((back, *hidden))
+    down_grad = call(down_grad_kernel, jax.ShapeDtypeStruct((width, hid), BF16), (*hidden, *rows))
+    grad_block = (1, share_y, 2 * count, hid // share_y)
+    gate_grad, up_grad = call(
+        gate_grad_kernel,
+        (jax.ShapeDtypeStruct((width, hid), BF16),) * 2,
+        (order, grads, *rows),
         VMEM_LARGE,
         grid_spec=pltpu.PrefetchScalarGridSpec(
             num_scalar_prefetch=1,
             grid=(share_x,),
-            in_specs=[pl.BlockSpec((1,) + act_shape, lambda d, x: after(d, x) + (0,))]
+            in_specs=[pl.BlockSpec(grad_block, lambda d, x: after(d, x) + (0,))]
             + [whole(count, LANES)] * 4,
-            out_specs=[whole(width, hid)] * 3,
-            scratch_shapes=[pltpu.VMEM((3, width, hid), F32)],
+            out_specs=[whole(width, hid)] * 2,
+            scratch_shapes=[pltpu.VMEM((2, width, hid), F32)],
         ),
     )
-    back = exchange(results.reshape(pieces), OWNERS).reshape(4 * total, 128)
     summed = call(
         combine_kernel,
         jax.ShapeDtypeStruct((groups * BLK, LANES), BF16),
@@ -350,6 +364,9 @@
         scratch_shapes=[pltpu.VMEM((4 * total, 128), F32)],
     )
     home = exchange(summed.reshape(groups, BLK, LANES), GROUP).reshape(groups * BLK, LANES)
+    home, gate_grad, up_grad, down_grad = lax.optimization_barrier(
+        (home, gate_grad, up_grad, down_grad)
+    )
     out, dx = call(
         unpack_kernel,
         (jax.ShapeDtypeStruct((width, groups * BLK), BF16),) * 2,
@@ -358,9 +375,9 @@
     return (
         out.T,
         dx.T,
-        weights[0][None],
-        weights[1][None],
-        weights[2].T[None],
+        gate_grad[None],
+        up_grad[None],
+        down_grad.T[None],
     )
 
 

time: 231 us -> 262 us (1.13)
  blocking collectives: 77.1 us -> 20.9 us
  waiting for transfers between devices: 55.8 us -> 101 us
  starting transfers between devices: 50.8 us -> 91.2 us
    all_to_all x2 -> x0, blocking collectives: 53.6 us -> none  [exchange(): return lax.all_to_all(array, axis, split_axis=0, concat_axis=0, tiled=True)]
    ppermute x9 -> x12, waiting for transfers between devices: 27.2 us -> 78 us  [shift(): return lax.ppermute(array, 'x', shifts[d])]
    all_to_all x3 -> x5, starting transfers between devices: 23.3 us -> 52.8 us  [exchange(): return lax.all_to_all(array, axis, split_axis=0, concat_axis=0, tiled=True)]
    ppermute x9 -> x12, starting transfers between devices: 27.5 us -> 38.4 us  [shift(): return lax.ppermute(array, 'x', shifts[d])]
    all_to_all x3 -> x5, waiting for transfers between devices: 27.9 us -> 21.9 us  [exchange(): return lax.all_to_all(array, axis, split_axis=0, concat_axis=0, tiled=True)]
    pallas_call x8 -> x9, Pallas kernels: 26.2 us -> 27.5 us  [call(): pl.pallas_call(kernel, out_shape=out_shape, compiler_params=pltpu.Compile...]
  transfers between devices with their start and end apart: 14 -> 19, of which waited for: 7 -> 11; matrix products, arithmetic and copies ran while one was open for 2% -> 2% of each run, Pallas kernels for 6% -> 7%
where the time goes in v4:
time: 262 us; the launch traced here: 261 us
  waiting for transfers between devices  101 us (39%)
  starting transfers between devices  91.2 us (35%)
  Pallas kernels  27.5 us (10%)
  blocking collectives  20.9 us (8%)
  between operations  14.4 us (5%)
  local copies, waits for them, and re-layouts  3.79 us (1%)
    ppermute x12, waiting for transfers between devices, shift(): return lax.ppermute(array, 'x', shifts[d])  78 us
    all_to_all x5, starting transfers between devices, exchange(): return lax.all_to_all(array, axis, split_axis=0, concat_axis=0, tiled=True)  52.8 us
    ppermute x12, starting transfers between devices, shift(): return lax.ppermute(array, 'x', shifts[d])  38.4 us
    pallas_call x9, Pallas kernels, call(): pl.pallas_call(kernel, out_shape=out_shape, compiler_params=pltpu.Compile...  27.5 us
    all_to_all x5, waiting for transfers between devices, exchange(): return lax.all_to_all(array, axis, split_axis=0, concat_axis=0, tiled=True)  21.9 us
    all_gather x1, blocking collectives, body(): act = lax.all_gather(act, 'y', axis=0, tiled=False)  20.9 us
  transfers between devices with their start and end apart: 19, of which 11 were waited for; matrix products, arithmetic and copies ran while one was open for 2% of the time, Pallas kernels for 7%

profile of v4, /device:TPU:1, one launch (start us, length us, event | category | flops | bytes accessed | tf_op | source)
XLA Modules:
  0.0 260.9 jit_solution(4991931211505975616)
XLA Ops:
  7.2 0.7 all-gather.5.cloned.1.call-update
  7.9 2.4 shard_map.128
  10.3 11.8 %all-to-all-start = ((bf16[16,32,512]{2,1,0:T(8,128)(2,1)}), bf16[16,32,512]{2,1,0:T(8,128)(2,1)S(1)}, u32[]{:S(2)}, u32[]{:S(2)}) async-start(bf16[16,32,512]{2,1,0:T(8,128)(2,1)} %shard_map.128), calls=%async_computation | async-start | bytes 1048576 | tf_op jit(solution)/shard_map/all_to_all | solution.py:231
  22.1 0.7 fusion.5
  22.9 0.8 multiply_reduce_fusion.1
  24.5 3.1 %collective-permute-start = (bf16[224,1024]{1,0:T(8,128)(2,1)S(1)}, bf16[224,1024]{1,0:T(8,128)(2,1)S(1)}, u32[]{:S(2)}, u32[]{:S(2)}) collective-permute-start(bf16[224,1024]{1,0:T(8,128)(2,1)S(1)} %bitcast.45), channel_id=1, source_target_pairs={{0,1},{1,2},{2,3},{3,0},{4,5},{5,6},{6,7},{7,4},{8,9},{9,10},{10,1... | collective-permute-start | bytes 1376264 | tf_op jit(solution)/shard_map/ppermute | solution.py:252
  27.6 3.4 %collective-permute-start.1 = (bf16[224,1024]{1,0:T(8,128)(2,1)S(1)}, bf16[224,1024]{1,0:T(8,128)(2,1)S(1)}, u32[]{:S(2)}, u32[]{:S(2)}) collective-permute-start(bf16[224,1024]{1,0:T(8,128)(2,1)S(1)} %bitcast.49), channel_id=1, source_target_pairs={{0,3},{1,0},{2,1},{3,2},{4,7},{5,4},{6,5},{7,6},{8,11},{9,8},{10,9... | collective-permute-start | bytes 1376264 | tf_op jit(solution)/shard_map/ppermute | solution.py:252
  31.0 3.2 %collective-permute-start.3 = (bf16[224,1024]{1,0:T(8,128)(2,1)S(1)}, bf16[224,1024]{1,0:T(8,128)(2,1)}, u32[]{:S(2)}, u32[]{:S(2)}) collective-permute-start(bf16[224,1024]{1,0:T(8,128)(2,1)S(1)} %bitcast.46), channel_id=1, source_target_pairs={{0,3},{1,0},{2,1},{3,2},{4,7},{5,4},{6,5},{7,6},{8,11},{9,8},{10,9... | collective-permute-start | bytes 1376264 | tf_op jit(solution)/shard_map/ppermute | solution.py:252
  34.2 2.1 collective-permute-start.2
  36.5 8.0 %collective-permute-done.refs_1_ = bf16[224,1024]{1,0:T(8,128)(2,1)S(1)} collective-permute-done((bf16[224,1024]{1,0:T(8,128)(2,1)S(1)}, bf16[224,1024]{1,0:T(8,128)(2,1)S(1)}, u32[]{:S(2)}, u32[]{:S(2)}) %collective-permute-start) | collective-permute-done | bytes 458784 | tf_op jit(solution)/shard_map/ppermute | solution.py:252
  44.5 5.4 %collective-permute-done.1.refs_7_ = bf16[224,1024]{1,0:T(8,128)(2,1)S(1)} collective-permute-done((bf16[224,1024]{1,0:T(8,128)(2,1)S(1)}, bf16[224,1024]{1,0:T(8,128)(2,1)S(1)}, u32[]{:S(2)}, u32[]{:S(2)}) %collective-permute-start.1) | collective-permute-done | bytes 458784 | tf_op jit(solution)/shard_map/ppermute | solution.py:252
  49.9 2.3 shard_map.129
  52.3 13.7 %collective-permute-done.3.refs_3_ = bf16[224,1024]{1,0:T(8,128)(2,1)} collective-permute-done((bf16[224,1024]{1,0:T(8,128)(2,1)S(1)}, bf16[224,1024]{1,0:T(8,128)(2,1)}, u32[]{:S(2)}, u32[]{:S(2)}) %collective-permute-start.3) | collective-permute-done | bytes 458784 | tf_op jit(solution)/shard_map/ppermute | solution.py:252
  66.0 11.0 %all-to-all-start.1 = ((bf16[64,40,128]{2,1,0:T(8,128)(2,1)}), bf16[64,40,128]{2,1,0:T(8,128)(2,1)S(1)}, u32[]{:S(2)}, u32[]{:S(2)}) async-start(bf16[64,40,128]{2,1,0:T(8,128)(2,1)} %bitcast.13), calls=%async_computation.1 | async-start | bytes 1310720 | tf_op jit(solution)/shard_map/all_to_all | solution.py:231
  76.9 3.3 %collective-permute-start.4 = (bf16[224,1024]{1,0:T(8,128)(2,1)S(1)}, bf16[224,1024]{1,0:T(8,128)(2,1)S(1)}, u32[]{:S(2)}, u32[]{:S(2)}) collective-permute-start(bf16[224,1024]{1,0:T(8,128)(2,1)S(1)} %collective-permute-done.refs_1_), channel_id=1, source_target_pairs={{0,1},{1,2},{2,3},{3,0},{4,5},{5,6},{6,7},{7,4},{8,9},{9,10},{10,1... | collective-permute-start | bytes 1376264 | tf_op jit(solution)/shard_map/ppermute | solution.py:252
  80.3 3.3 %collective-permute-start.5 = (bf16[224,1024]{1,0:T(8,128)(2,1)S(1)}, bf16[224,1024]{1,0:T(8,128)(2,1)S(1)}, u32[]{:S(2)}, u32[]{:S(2)}) collective-permute-start(bf16[224,1024]{1,0:T(8,128)(2,1)S(1)} %collective-permute-done.1.refs_7_), channel_id=1, source_target_pairs={{0,3},{1,0},{2,1},{3,2},{4,7},{5,4},{6,5},{7,6},{8,11},{9,8},{10,9... | collective-permute-start | bytes 1376264 | tf_op jit(solution)/shard_map/ppermute | solution.py:252
  83.6 0.7 pad_convert_fusion
  84.3 13.9 %collective-permute-done.4.refs_2_ = bf16[224,1024]{1,0:T(8,128)(2,1)S(1)} collective-permute-done((bf16[224,1024]{1,0:T(8,128)(2,1)S(1)}, bf16[224,1024]{1,0:T(8,128)(2,1)S(1)}, u32[]{:S(2)}, u32[]{:S(2)}) %collective-permute-start.4) | collective-permute-done | bytes 458784 | tf_op jit(solution)/shard_map/ppermute | solution.py:252
  98.1 0.3 collective-permute-done.5.refs_6_
  98.5 0.4 copy-done.10
  98.9 0.3 copy-done.11
  99.2 0.2 copy-done.5
  99.4 6.9 %shard_map.130 = (bf16[160,512]{1,0:T(8,128)(2,1)}, bf16[160,512]{1,0:T(8,128)(2,1)}, bf16[160,512]{1,0:T(8,128)(2,1)}, bf16[160,512]{1,0:T(8,128)(2,1)}, bf16[8...) custom-call(s32[1]{0:T(128)} %bitcast.12.x_ref, bf16[4,640,128]{2,1,0:T(8,128)(2,1)} %bitcast.42, f32[1,256]{1,0:T(1,128)} %bitcast.56, ...), custom_call_target="tpu_custom_call" | custom-call | tf_op jit(solution)/shard_map/pallas_call | solution.py:27
  106.3 6.8 %all-to-all-start.2 = ((bf16[8,480,128]{2,1,0:T(8,128)(2,1)}), bf16[8,480,128]{2,1,0:T(8,128)(2,1)S(1)}, u32[]{:S(2)}, u32[]{:S(2)}) async-start(bf16[8,480,128]{2,1,0:T(8,128)(2,1)} %get-tuple-element.51), calls=%async_computation.2 | async-start | bytes 1966080 | tf_op jit(solution)/shard_map/all_to_all | solution.py:231
  113.2 4.4 %collective-permute-start.6 = (bf16[160,512]{1,0:T(8,128)(2,1)}, bf16[160,512]{1,0:T(8,128)(2,1)S(1)}, u32[]{:S(2)}, u32[]{:S(2)}) collective-permute-start(bf16[160,512]{1,0:T(8,128)(2,1)} %get-tuple-element.53), channel_id=1, source_target_pairs={{0,3},{1,0},{2,1},{3,2},{4,7},{5,4},{6,5},{7,6},{8,11},{9,8},{10,9... | collective-permute-start | bytes 491528 | tf_op jit(solution)/shard_map/ppermute | solution.py:252
  117.7 2.6 collective-permute-start.7
  120.3 2.1 collective-permute-start.8
  122.4 3.3 %collective-permute-done.7.refs_2_.refs_6_ = bf16[160,512]{1,0:T(8,128)(2,1)S(1)} collective-permute-done((bf16[160,512]{1,0:T(8,128)(2,1)}, bf16[160,512]{1,0:T(8,128)(2,1)S(1)}, u32[]{:S(2)}, u32[]{:S(2)}) %collective-permute-start.7) | collective-permute-done | bytes 163872 | tf_op jit(solution)/shard_map/ppermute | solution.py:252
  125.7 4.4 %collective-permute-done.8.refs_3_.refs_7_ = bf16[160,512]{1,0:T(8,128)(2,1)S(1)} collective-permute-done((bf16[160,512]{1,0:T(8,128)(2,1)}, bf16[160,512]{1,0:T(8,128)(2,1)S(1)}, u32[]{:S(2)}, u32[]{:S(2)}) %collective-permute-start.8) | collective-permute-done | bytes 163872 | tf_op jit(solution)/shard_map/ppermute | solution.py:252
  130.1 10.8 %all-to-all-done.2.parts_ref = bf16[8,480,128]{2,1,0:T(8,128)(2,1)S(1)} async-done(((bf16[8,480,128]{2,1,0:T(8,128)(2,1)}), bf16[8,480,128]{2,1,0:T(8,128)(2,1)S(1)}, u32[]{:S(2)}, u32[]{:S(2)}) %all-to-all-start.2) | async-done | bytes 983072 | tf_op jit(solution)/shard_map/all_to_all | solution.py:231
  140.9 0.2 shard_map.131
  141.1 20.9 %all-gather = bf16[3840,128]{1,0:T(8,128)(2,1)S(1)} all-gather(bf16[480,128]{1,0:T(8,128)(2,1)S(1)} %shard_map.131), channel_id=2, replica_groups=mesh['z'=8,'core'=2,'y'=8,'x'=4] {'y'}, dimensions={0}, use_global_device_ids=true | all-gather | bytes 1105920 | tf_op jit(solution)/shard_map/all_gather | solution.py:324
  162.0 0.9 slice.25
  163.0 0.2 copy-done.4
  163.3 6.9 %shard_map.132 = bf16[4,640,128]{2,1,0:T(8,128)(2,1)} custom-call(s32[1]{0:T(128)} %bitcast.12.x_ref, bf16[8,480,128]{2,1,0:T(8,128)(2,1)} %bitcast.38, f32[160,128]{1,0:T(8,128)} %get-tuple-element.57.prob_ref, bf16[4,224,1024]{2,1,0:T(8,128)(2,1)} %all-gather.5.cloned.1.call-done.gate_ref, bf16[224,1024]{1,0:T(8,128)(2,1)} %bitcast.44, ...), custom_call_target="tpu_custom_call" | custom-call | tf_op jit(solution)/shard_map/pallas_call | solution.py:27
  170.2 16.1 %all-to-all-start.3 = ((bf16[64,40,128]{2,1,0:T(8,128)(2,1)}), bf16[64,40,128]{2,1,0:T(8,128)(2,1)S(1)}, u32[]{:S(2)}, u32[]{:S(2)}) async-start(bf16[64,40,128]{2,1,0:T(8,128)(2,1)} %bitcast.40), calls=%async_computation.3 | async-start | bytes 1310720 | tf_op jit(solution)/shard_map/all_to_all | solution.py:231
  186.3 1.0 slice.24.refs_0_
  187.3 3.3 %collective-permute-start.11 = (bf16[8,160,128]{2,1,0:T(8,128)(2,1)S(1)}, bf16[8,160,128]{2,1,0:T(8,128)(2,1)S(1)}, u32[]{:S(2)}, u32[]{:S(2)}) collective-permute-start(bf16[8,160,128]{2,1,0:T(8,128)(2,1)S(1)} %slice.24.refs_0_), channel_id=1, source_target_pairs={{0,1},{1,2},{2,3},{3,0},{4,5},{5,6},{6,7},{7,4},{8,9},{9,10},{10,1... | collective-permute-start | bytes 983048 | tf_op jit(solution)/shard_map/ppermute | solution.py:252
  190.6 4.5 %collective-permute-start.10 = (bf16[8,160,128]{2,1,0:T(8,128)(2,1)S(1)}, bf16[8,160,128]{2,1,0:T(8,128)(2,1)S(1)}, u32[]{:S(2)}, u32[]{:S(2)}) collective-permute-start(bf16[8,160,128]{2,1,0:T(8,128)(2,1)S(1)} %slice.24.refs_0_), channel_id=1, source_target_pairs={{0,2},{1,3},{2,0},{3,1},{4,6},{5,7},{6,4},{7,5},{8,10},{9,11},{10,... | collective-permute-start | bytes 983048 | tf_op jit(solution)/shard_map/ppermute | solution.py:252
  195.1 3.0 %collective-permute-start.9 = (bf16[8,160,128]{2,1,0:T(8,128)(2,1)S(1)}, bf16[8,160,128]{2,1,0:T(8,128)(2,1)S(1)}, u32[]{:S(2)}, u32[]{:S(2)}) collective-permute-start(bf16[8,160,128]{2,1,0:T(8,128)(2,1)S(1)} %slice.24.refs_0_), channel_id=1, source_target_pairs={{0,3},{1,0},{2,1},{3,2},{4,7},{5,4},{6,5},{7,6},{8,11},{9,8},{10,9... | collective-permute-start | bytes 983048 | tf_op jit(solution)/shard_map/ppermute | solution.py:252
  198.1 15.2 %collective-permute-done.11.refs_3_ = bf16[8,160,128]{2,1,0:T(8,128)(2,1)S(1)} collective-permute-done((bf16[8,160,128]{2,1,0:T(8,128)(2,1)S(1)}, bf16[8,160,128]{2,1,0:T(8,128)(2,1)S(1)}, u32[]{:S(2)}, u32[]{:S(2)}) %collective-permute-start.11) | collective-permute-done | bytes 327712 | tf_op jit(solution)/shard_map/ppermute | solution.py:252
  213.3 13.8 %collective-permute-done.10.refs_2_ = bf16[8,160,128]{2,1,0:T(8,128)(2,1)S(1)} collective-permute-done((bf16[8,160,128]{2,1,0:T(8,128)(2,1)S(1)}, bf16[8,160,128]{2,1,0:T(8,128)(2,1)S(1)}, u32[]{:S(2)}, u32[]{:S(2)}) %collective-permute-start.10) | collective-permute-done | bytes 327712 | tf_op jit(solution)/shard_map/ppermute | solution.py:252
  227.1 1.4 shard_map.133
  228.5 7.1 %all-to-all-start.4 = ((bf16[16,32,512]{2,1,0:T(8,128)(2,1)}), bf16[16,32,512]{2,1,0:T(8,128)(2,1)S(1)}, u32[]{:S(2)}, u32[]{:S(2)}) async-start(bf16[16,32,512]{2,1,0:T(8,128)(2,1)} %bitcast.20), calls=%async_computation.4 | async-start | bytes 1048576 | tf_op jit(solution)/shard_map/all_to_all | solution.py:231
  235.6 1.4 shard_map.135
  237.0 4.8 %shard_map.134 = (bf16[224,1024]{1,0:T(8,128)(2,1)}, bf16[224,1024]{1,0:T(8,128)(2,1)}) custom-call(s32[1]{0:T(128)} %bitcast.12.x_ref, bf16[4,8,320,128]{3,2,1,0:T(8,128)(2,1)} %bitcast.41, bf16[160,512]{1,0:T(8,128)(2,1)} %get-tuple-element.59.refs_0_.refs_4_, bf16[160,512]{1,0:T(8,128)(2,1)} %copy-done.1, bf16[160,512]{1,0:T(8,128)(2,1)} %copy-done.2, ...), custom_call_target="tpu_custom_call" | custom-call | tf_op jit(solution)/shard_map/pallas_call | solution.py:27
  241.8 11.1 %all-to-all-done.4 = bf16[16,32,512]{2,1,0:T(8,128)(2,1)S(1)} async-done(((bf16[16,32,512]{2,1,0:T(8,128)(2,1)}), bf16[16,32,512]{2,1,0:T(8,128)(2,1)S(1)}, u32[]{:S(2)}, u32[]{:S(2)}) %all-to-all-start.4) | async-done | bytes 524320 | tf_op jit(solution)/shard_map/all_to_all | solution.py:231
  252.9 1.2 shard_map.136
  (47 shorter events, 1.1 us)
Async XLA Ops:
  7.2 16.7 %copy-start.12 = (s32[16]{0:T(128)S(1)}, s32[16]{0:T(128)}, u32[]{:S(2)}) copy-start(s32[16]{0:T(128)} %param.15) | copy-start | bytes 196
  7.2 20.5 %copy-start.7 = (bf16[1,1024,224]{1,2,0:T(8,128)(2,1)S(1)}, bf16[1,1024,224]{1,2,0:T(8,128)(2,1)}, u32[]{:S(2)}) copy-start(bf16[1,1024,224]{1,2,0:T(8,128)(2,1)} %param.14) | copy-start | bytes 1376260
  7.2 17.3 %copy-start.6 = (bf16[1,224,1024]{2,1,0:T(8,128)(2,1)S(1)}, bf16[1,224,1024]{2,1,0:T(8,128)(2,1)}, u32[]{:S(2)}) copy-start(bf16[1,224,1024]{2,1,0:T(8,128)(2,1)} %param.13) | copy-start | bytes 1376260
  7.2 91.2 %all-gather.5.cloned.1.call-start = ((), (), s32[]{:S(2)}) async-start(), calls=%async_computation.5 | async-start | bytes 2293760 | tf_op jit(solution)/shard_map/all_gather | solution.py:254
  10.3 39.6 %all-to-all-start = ((bf16[16,32,512]{2,1,0:T(8,128)(2,1)}), bf16[16,32,512]{2,1,0:T(8,128)(2,1)S(1)}, u32[]{:S(2)}, u32[]{:S(2)}) async-start(bf16[16,32,512]{2,1,0:T(8,128)(2,1)} %shard_map.128), calls=%async_computation | async-start | bytes 1048576 | tf_op jit(solution)/shard_map/all_to_all | solution.py:231
  24.5 20.0 %collective-permute-start = (bf16[224,1024]{1,0:T(8,128)(2,1)S(1)}, bf16[224,1024]{1,0:T(8,128)(2,1)S(1)}, u32[]{:S(2)}, u32[]{:S(2)}) collective-permute-start(bf16[224,1024]{1,0:T(8,128)(2,1)S(1)} %bitcast.45), channel_id=1, source_target_pairs={{0,1},{1,2},{2,3},{3,0},{4,5},{5,6},{6,7},{7,4},{8,9},{9,10},{10,1... | collective-permute-start | bytes 1376264 | tf_op jit(solution)/shard_map/ppermute | solution.py:252
  27.6 22.3 %collective-permute-start.1 = (bf16[224,1024]{1,0:T(8,128)(2,1)S(1)}, bf16[224,1024]{1,0:T(8,128)(2,1)S(1)}, u32[]{:S(2)}, u32[]{:S(2)}) collective-permute-start(bf16[224,1024]{1,0:T(8,128)(2,1)S(1)} %bitcast.49), channel_id=1, source_target_pairs={{0,3},{1,0},{2,1},{3,2},{4,7},{5,4},{6,5},{7,6},{8,11},{9,8},{10,9... | collective-permute-start | bytes 1376264 | tf_op jit(solution)/shard_map/ppermute | solution.py:252
  31.0 34.9 %collective-permute-start.3 = (bf16[224,1024]{1,0:T(8,128)(2,1)S(1)}, bf16[224,1024]{1,0:T(8,128)(2,1)}, u32[]{:S(2)}, u32[]{:S(2)}) collective-permute-start(bf16[224,1024]{1,0:T(8,128)(2,1)S(1)} %bitcast.46), channel_id=1, source_target_pairs={{0,3},{1,0},{2,1},{3,2},{4,7},{5,4},{6,5},{7,6},{8,11},{9,8},{10,9... | collective-permute-start | bytes 1376264 | tf_op jit(solution)/shard_map/ppermute | solution.py:252
  34.2 31.8 %collective-permute-start.2 = (bf16[224,1024]{1,0:T(8,128)(2,1)S(1)}, bf16[224,1024]{1,0:T(8,128)(2,1)}, u32[]{:S(2)}, u32[]{:S(2)}) collective-permute-start(bf16[224,1024]{1,0:T(8,128)(2,1)S(1)} %bitcast.50), channel_id=1, source_target_pairs={{0,1},{1,2},{2,3},{3,0},{4,5},{5,6},{6,7},{7,4},{8,9},{9,10},{10,1... | collective-permute-start | bytes 1376264 | tf_op jit(solution)/shard_map/ppermute | solution.py:252
  44.5 53.9 %copy-start.8 = (bf16[224,1024]{1,0:T(8,128)(2,1)}, bf16[224,1024]{1,0:T(8,128)(2,1)S(1)}, u32[]{:S(2)}) copy-start(bf16[224,1024]{1,0:T(8,128)(2,1)S(1)} %collective-permute-done.refs_1_) | copy-start | bytes 1376260
  49.9 48.5 %copy-start.9 = (bf16[224,1024]{1,0:T(8,128)(2,1)}, bf16[224,1024]{1,0:T(8,128)(2,1)S(1)}, u32[]{:S(2)}) copy-start(bf16[224,1024]{1,0:T(8,128)(2,1)S(1)} %collective-permute-done.1.refs_7_) | copy-start | bytes 1376260
  66.0 32.4 %all-to-all-start.1 = ((bf16[64,40,128]{2,1,0:T(8,128)(2,1)}), bf16[64,40,128]{2,1,0:T(8,128)(2,1)S(1)}, u32[]{:S(2)}, u32[]{:S(2)}) async-start(bf16[64,40,128]{2,1,0:T(8,128)(2,1)} %bitcast.13), calls=%async_computation.1 | async-start | bytes 1310720 | tf_op jit(solution)/shard_map/all_to_all | solution.py:231
  76.9 21.2 %collective-permute-start.4 = (bf16[224,1024]{1,0:T(8,128)(2,1)S(1)}, bf16[224,1024]{1,0:T(8,128)(2,1)S(1)}, u32[]{:S(2)}, u32[]{:S(2)}) collective-permute-start(bf16[224,1024]{1,0:T(8,128)(2,1)S(1)} %collective-permute-done.refs_1_), channel_id=1, source_target_pairs={{0,1},{1,2},{2,3},{3,0},{4,5},{5,6},{6,7},{7,4},{8,9},{9,10},{10,1... | collective-permute-start | bytes 1376264 | tf_op jit(solution)/shard_map/ppermute | solution.py:252
  80.3 18.1 %collective-permute-start.5 = (bf16[224,1024]{1,0:T(8,128)(2,1)S(1)}, bf16[224,1024]{1,0:T(8,128)(2,1)S(1)}, u32[]{:S(2)}, u32[]{:S(2)}) collective-permute-start(bf16[224,1024]{1,0:T(8,128)(2,1)S(1)} %collective-permute-done.1.refs_7_), channel_id=1, source_target_pairs={{0,3},{1,0},{2,1},{3,2},{4,7},{5,4},{6,5},{7,6},{8,11},{9,8},{10,9... | collective-permute-start | bytes 1376264 | tf_op jit(solution)/shard_map/ppermute | solution.py:252
  98.1 0.8 copy-start.10
  98.4 0.8 copy-start.11
  98.4 1.0 copy-start.5
  106.3 34.6 %all-to-all-start.2 = ((bf16[8,480,128]{2,1,0:T(8,128)(2,1)}), bf16[8,480,128]{2,1,0:T(8,128)(2,1)S(1)}, u32[]{:S(2)}, u32[]{:S(2)}) async-start(bf16[8,480,128]{2,1,0:T(8,128)(2,1)} %get-tuple-element.51), calls=%async_computation.2 | async-start | bytes 1966080 | tf_op jit(solution)/shard_map/all_to_all | solution.py:231
  113.2 123.9 %all-gather.7.cloned.1.call-start = ((), (), s32[]{:S(2)}) async-start(), calls=%async_computation.6 | async-start | bytes 3276800 | tf_op jit(solution)/shard_map/all_gather | solution.py:325
  113.2 9.2 %collective-permute-start.6 = (bf16[160,512]{1,0:T(8,128)(2,1)}, bf16[160,512]{1,0:T(8,128)(2,1)S(1)}, u32[]{:S(2)}, u32[]{:S(2)}) collective-permute-start(bf16[160,512]{1,0:T(8,128)(2,1)} %get-tuple-element.53), channel_id=1, source_target_pairs={{0,3},{1,0},{2,1},{3,2},{4,7},{5,4},{6,5},{7,6},{8,11},{9,8},{10,9... | collective-permute-start | bytes 491528 | tf_op jit(solution)/shard_map/ppermute | solution.py:252
  117.7 8.1 %collective-permute-start.7 = (bf16[160,512]{1,0:T(8,128)(2,1)}, bf16[160,512]{1,0:T(8,128)(2,1)S(1)}, u32[]{:S(2)}, u32[]{:S(2)}) collective-permute-start(bf16[160,512]{1,0:T(8,128)(2,1)} %get-tuple-element.54), channel_id=1, source_target_pairs={{0,2},{1,3},{2,0},{3,1},{4,6},{5,7},{6,4},{7,5},{8,10},{9,11},{10,... | collective-permute-start | bytes 491528 | tf_op jit(solution)/shard_map/ppermute | solution.py:252
  120.3 9.9 %collective-permute-start.8 = (bf16[160,512]{1,0:T(8,128)(2,1)}, bf16[160,512]{1,0:T(8,128)(2,1)S(1)}, u32[]{:S(2)}, u32[]{:S(2)}) collective-permute-start(bf16[160,512]{1,0:T(8,128)(2,1)} %get-tuple-element.55), channel_id=1, source_target_pairs={{0,1},{1,2},{2,3},{3,0},{4,5},{5,6},{6,7},{7,4},{8,9},{9,10},{10,1... | collective-permute-start | bytes 491528 | tf_op jit(solution)/shard_map/ppermute | solution.py:252
  122.4 113.2 %copy-start.1 = (bf16[160,512]{1,0:T(8,128)(2,1)}, bf16[160,512]{1,0:T(8,128)(2,1)S(1)}, u32[]{:S(2)}) copy-start(bf16[160,512]{1,0:T(8,128)(2,1)S(1)} %collective-permute-done.6.refs_1_.refs_5_) | copy-start | bytes 491524
  125.7 109.9 %copy-start.2 = (bf16[160,512]{1,0:T(8,128)(2,1)}, bf16[160,512]{1,0:T(8,128)(2,1)S(1)}, u32[]{:S(2)}) copy-start(bf16[160,512]{1,0:T(8,128)(2,1)S(1)} %collective-permute-done.7.refs_2_.refs_6_) | copy-start | bytes 491524
  130.1 105.5 %copy-start.3 = (bf16[160,512]{1,0:T(8,128)(2,1)}, bf16[160,512]{1,0:T(8,128)(2,1)S(1)}, u32[]{:S(2)}) copy-start(bf16[160,512]{1,0:T(8,128)(2,1)S(1)} %collective-permute-done.8.refs_3_.refs_7_) | copy-start | bytes 491524
  162.0 1.2 copy-start.4
  170.2 65.4 %copy-start = (bf16[160,512]{1,0:T(8,128)(2,1)S(1)}, bf16[160,512]{1,0:T(8,128)(2,1)}, u32[]{:S(2)}) copy-start(bf16[160,512]{1,0:T(8,128)(2,1)} %get-tuple-element.59.refs_0_.refs_4_) | copy-start | bytes 491524
  170.2 56.9 %all-to-all-start.3 = ((bf16[64,40,128]{2,1,0:T(8,128)(2,1)}), bf16[64,40,128]{2,1,0:T(8,128)(2,1)S(1)}, u32[]{:S(2)}, u32[]{:S(2)}) async-start(bf16[64,40,128]{2,1,0:T(8,128)(2,1)} %bitcast.40), calls=%async_computation.3 | async-start | bytes 1310720 | tf_op jit(solution)/shard_map/all_to_all | solution.py:231
  187.3 26.0 %collective-permute-start.11 = (bf16[8,160,128]{2,1,0:T(8,128)(2,1)S(1)}, bf16[8,160,128]{2,1,0:T(8,128)(2,1)S(1)}, u32[]{:S(2)}, u32[]{:S(2)}) collective-permute-start(bf16[8,160,128]{2,1,0:T(8,128)(2,1)S(1)} %slice.24.refs_0_), channel_id=1, source_target_pairs={{0,1},{1,2},{2,3},{3,0},{4,5},{5,6},{6,7},{7,4},{8,9},{9,10},{10,1... | collective-permute-start | bytes 983048 | tf_op jit(solution)/shard_map/ppermute | solution.py:252
  190.6 36.5 %collective-permute-start.10 = (bf16[8,160,128]{2,1,0:T(8,128)(2,1)S(1)}, bf16[8,160,128]{2,1,0:T(8,128)(2,1)S(1)}, u32[]{:S(2)}, u32[]{:S(2)}) collective-permute-start(bf16[8,160,128]{2,1,0:T(8,128)(2,1)S(1)} %slice.24.refs_0_), channel_id=1, source_target_pairs={{0,2},{1,3},{2,0},{3,1},{4,6},{5,7},{6,4},{7,5},{8,10},{9,11},{10,... | collective-permute-start | bytes 983048 | tf_op jit(solution)/shard_map/ppermute | solution.py:252
  195.1 32.0 %collective-permute-start.9 = (bf16[8,160,128]{2,1,0:T(8,128)(2,1)S(1)}, bf16[8,160,128]{2,1,0:T(8,128)(2,1)S(1)}, u32[]{:S(2)}, u32[]{:S(2)}) collective-permute-start(bf16[8,160,128]{2,1,0:T(8,128)(2,1)S(1)} %slice.24.refs_0_), channel_id=1, source_target_pairs={{0,3},{1,0},{2,1},{3,2},{4,7},{5,4},{6,5},{7,6},{8,11},{9,8},{10,9... | collective-permute-start | bytes 983048 | tf_op jit(solution)/shard_map/ppermute | solution.py:252
  228.5 24.4 %all-to-all-start.4 = ((bf16[16,32,512]{2,1,0:T(8,128)(2,1)}), bf16[16,32,512]{2,1,0:T(8,128)(2,1)S(1)}, u32[]{:S(2)}, u32[]{:S(2)}) async-start(bf16[16,32,512]{2,1,0:T(8,128)(2,1)} %bitcast.20), calls=%async_computation.4 | async-start | bytes 1048576 | tf_op jit(solution)/shard_map/all_to_all | solution.py:231
Sparse Core Ops, SparseCore 0:
  10.1 54.4 all-gather.4
  163.1 62.0 all-gather.6

commit v5 on v3

--- a/solution.py
+++ b/solution.py
@@ -46,8 +46,12 @@
     all_ref[P_LANE : P_LANE + 16] = prob_ref[...]
     all_ref[DY_LANE : DY_LANE + width] = dy_ref[...]
     packed = dot(token_permutation(LANES), all_ref[...], 1, 1)
-    packed = packed.reshape(out_ref.shape) + list_ref[...].astype(F32)[None]
-    out_ref[...] = packed.astype(BF16)
+    lists = list_ref[:, 0, :].astype(F32).astype(BF16)
+    entry = lax.broadcasted_iota(jnp.int32, (lists.shape[0], LANES), 0)
+    lane = lax.broadcasted_iota(jnp.int32, (lists.shape[0], LANES), 1)
+    lists = dot(lists, (lane == entry + LIST_LANE).astype(BF16), 0, 0)
+    lists = jnp.concatenate([lists, jnp.zeros((BLK - lists.shape[0], LANES), F32)], axis=0)
+    out_ref[...] = (packed.reshape(out_ref.shape) + lists[None]).astype(BF16)
 
 
 def split_lanes(tmp_ref, rows):
@@ -77,45 +81,69 @@
     out_ref[...] = split_lanes(tmp_ref, dot(pick, rows, 1, 0))
 
 
-def hidden_kernel(x_ref, tiles_ref, mark_ref, gate_ref, *refs):
-    up_refs, down_refs, refs = refs[:4], refs[4:8], refs[8:]
+def store_parts(out_ref, acc_ref):
+    parts, count = acc_ref.shape[:2]
+    for part in range(parts):
+        for piece in range(out_ref.shape[0]):
+            out_ref[piece, part * count : (part + 1) * count] = acc_ref[
+                part, :, piece * 128 : (piece + 1) * 128
+            ].astype(BF16)
+
+
+def gate_kernel(x_ref, tiles_ref, mark_ref, gate_ref, *refs):
     row_refs, (out_ref, prob_ref, acc_ref, tmp_ref) = refs[:4], refs[4:]
     step = pl.program_id(0)
     rows = join_lanes(tmp_ref, tiles_ref[0])
-    count = rows.shape[0]
-    width, hid = gate_ref.shape[1:]
+    width = gate_ref.shape[1] // 2
     prob = jnp.sum(rows[:, 0:256] * mark_ref[...], axis=1, keepdims=True)
     x = rows[:, 0:256].astype(BF16)
     grad = (prob * rows[:, DY_LANE:LANES]).astype(BF16)
     prob_ref[...] = jnp.broadcast_to(prob, prob_ref.shape)
-
-    @pl.when(step == 0)
-    def _():
-        acc_ref[...] = jnp.zeros_like(acc_ref)
-
-    acc_ref[0] += dot(x[:, 0:width], gate_ref[0], 1, 0)
     for d in range(4):
 
         @pl.when(step == d)
         def _():
             row_refs[d][:, 0:DY_LANE] = x
             row_refs[d][:, DY_LANE:LANES] = grad
-            acc_ref[1] += dot(x[:, 0:width], up_refs[d][...], 1, 0)
-            acc_ref[2] += dot(grad[:, 0:width], down_refs[d][...], 1, 0)
+
+    @pl.when(step == 0)
+    def _():
+        acc_ref[...] = jnp.zeros_like(acc_ref)
+
+    acc_ref[0] += dot(x[:, 0:width], gate_ref[0, 0:width], 1, 0)
+    acc_ref[1] += dot(x[:, 0:width], gate_ref[0, width : 2 * width], 1, 0)
 
     @pl.when(step == pl.num_programs(0) - 1)
     def _():
-        for part in range(3):
-            for piece in range(hid // 128):
-                out_ref[piece, part * count : (part + 1) * count] = acc_ref[
-                    part, :, piece * 128 : (piece + 1) * 128
-                ].astype(BF16)
-
-
-def point_kernel(parts_ref, out_ref):
+        store_parts(out_ref, acc_ref)
+
+
+def hidden_grad_kernel(x_ref, down_ref, *refs):
+    row_refs, (out_ref, acc_ref) = refs[:4], refs[4:]
+    step = pl.program_id(0)
+    width = down_ref.shape[1]
+
+    @pl.when(step == 0)
+    def _():
+        acc_ref[...] = jnp.zeros_like(acc_ref)
+
+    for d in range(4):
+
+        @pl.when(step == d)
+        def _():
+            grad = row_refs[d][:, DY_LANE : DY_LANE + width]
+            acc_ref[0] += dot(grad, down_ref[0], 1, 0)
+
+    @pl.when(step == pl.num_programs(0) - 1)
+    def _():
+        store_parts(out_ref, acc_ref)
+
+
+def point_kernel(parts_ref, grads_ref, out_ref):
     count = out_ref.shape[0] // 3
     total = jnp.sum(parts_ref[...].astype(F32), axis=0)
-    gate, up, grad = total[0:count], total[count : 2 * count], total[2 * count :]
+    grad = jnp.sum(grads_ref[...].astype(F32), axis=0)
+    gate, up = total[0:count], total[count : 2 * count]
     sigma = jax.nn.sigmoid(gate)
     out_ref[0:count] = (gate * sigma * up).astype(BF16)
     out_ref[count : 2 * count] = (grad * up * sigma * (1.0 + gate * (1.0 - sigma))).astype(BF16)
@@ -130,24 +158,18 @@
     ]
 
 
-def result_kernel(x_ref, act_ref, prob_ref, gate_ref, *refs):
-    up_refs, down_refs, (out_ref, res_ref, tmp_ref) = refs[:4], refs[4:8], refs[8:]
-    step = pl.program_id(0)
-    width = gate_ref.shape[1]
+def result_kernel(x_ref, act_ref, prob_ref, gate_ref, down_ref, out_ref, res_ref, tmp_ref):
+    width = down_ref.shape[1]
     hidden, gate_grad, up_grad = hidden_parts(act_ref)
 
-    @pl.when(step == 0)
+    @pl.when(pl.program_id(0) == 0)
     def _():
         res_ref[...] = jnp.zeros_like(res_ref)
 
-    dx = dot(gate_grad, gate_ref[0], 1, 1)
-    for d in range(4):
-
-        @pl.when(step == d)
-        def _():
-            res_ref[:, 0:width] = prob_ref[:, 0:1] * dot(hidden, down_refs[d][...], 1, 1)
-            res_ref[:, DY_LANE : DY_LANE + width] = dx + dot(up_grad, up_refs[d][...], 1, 1)
-
+    res_ref[:, 0:width] = prob_ref[:, 0:1] * dot(hidden, down_ref[0], 1, 1)
+    dx = dot(gate_grad, gate_ref[0, 0:width], 1, 1)
+    dx += dot(up_grad, gate_ref[0, width : 2 * width], 1, 1)
+    res_ref[:, DY_LANE : DY_LANE + width] = dx
     out_ref[0] = split_lanes(tmp_ref, res_ref[...])
 
 
@@ -239,19 +261,13 @@
     def shift(array, d):
         return lax.ppermute(array, "x", shifts[d])
 
-    gates = lax.all_gather(w_gate[0], "x", axis=0, tiled=False)
-    up, down = w_up[0], w_down[0].T
-    up_right, down_left = shift(up, 1), shift(down, 3)
-
-    lists = lax.pad(
-        block_lists[0].astype(BF16),
-        jnp.zeros((), BF16),
-        ((0, BLK - 16, 0), (LIST_LANE, LANES - LIST_LANE - entries, 0)),
-    )
+    gates = jnp.concatenate([w_gate[0], w_up[0]], axis=0)
+    gates = lax.all_gather(gates, "x", axis=0, tiled=False)
+
     packed = call(
         pack_kernel,
         jax.ShapeDtypeStruct((groups, BLK, LANES), BF16),
-        (tokens.T, grad_output.T, gate_prob.T, lists),
+        (tokens.T, grad_output.T, gate_prob.T, block_lists.transpose(2, 0, 1)),
         VMEM_LARGE,
         scratch_shapes=[pltpu.VMEM((LANES, LANES), BF16)],
     )
@@ -259,7 +275,8 @@
     mine = (expert_slot == lax.axis_index(GROUP)).astype(F32)
     mark = lax.pad(mine, jnp.zeros((), F32), ((P_LANE, 16, 0),))[None]
     spread = exchange(packed, GROUP).reshape(groups * BLK, LANES)
-    spread, up_right, down_left = lax.optimization_barrier((spread, up_right, down_left))
+    spread, info, down = lax.optimization_barrier((spread, info, w_down[0].T))
+    downs = lax.all_gather(down, "x", axis=0, tiled=False)
     sent, pick = call(
         select_kernel,
         (
@@ -269,8 +286,6 @@
         (spread, info),
         scratch_shapes=[pltpu.VMEM((4 * total, 128), F32)],
     )
-    ups = [up, up_right, shift(up_right, 1), shift(up, 3)]
-    downs = [down, shift(down, 1), shift(down_left, 3), down_left]
     pieces = (share_x * groups, 4 * picked // share_x, 128)
     tiles = exchange(sent.reshape(pieces), OWNERS).reshape(share_x, 4 * count, 128)
 
@@ -284,13 +299,16 @@
         return pl.BlockSpec(shape, lambda *_: (0,) * len(shape))
 
     tile_block = (1, 4 * count, 128)
-    gate_block = (1, width, hid)
+    gate_block = (1, 2 * width, hid)
+    down_block = (1, width, hid)
     act_shape = (share_y, 3 * count, hid // share_y)
+    gate_shape = (share_y, 2 * count, hid // share_y)
+    grad_shape = (share_y, count, hid // share_y)
     *rows, parts, prob = call(
-        hidden_kernel,
+        gate_kernel,
         (jax.ShapeDtypeStruct((count, LANES), BF16),) * 4
-        + (jax.ShapeDtypeStruct(act_shape, BF16), jax.ShapeDtypeStruct((count, 128), F32)),
-        (order, tiles, mark, gates, *ups, *downs),
+        + (jax.ShapeDtypeStruct(gate_shape, BF16), jax.ShapeDtypeStruct((count, 128), F32)),
+        (order, tiles, mark, gates),
         VMEM_LARGE,
         grid_spec=pltpu.PrefetchScalarGridSpec(
             num_scalar_prefetch=1,
@@ -299,31 +317,51 @@
                 pl.BlockSpec(tile_block, before),
                 whole(1, 256),
                 pl.BlockSpec(gate_block, before),
-            ]
-            + [whole(width, hid)] * 8,
-            out_specs=[whole(count, LANES)] * 4 + [whole(*act_shape), whole(count, 128)],
+            ],
+            out_specs=[whole(count, LANES)] * 4 + [whole(*gate_shape), whole(count, 128)],
             scratch_shapes=[
-                pltpu.VMEM((3, count, hid), F32),
+                pltpu.VMEM((2, count, hid), F32),
                 pltpu.VMEM((4 * count, 128), F32),
             ],
         ),
     )
     parts = exchange(parts, "y")
+    grad_parts = call(
+        hidden_grad_kernel,
+        jax.ShapeDtypeStruct(grad_shape, BF16),
+        (order, downs, *rows),
+        VMEM_LARGE,
+        grid_spec=pltpu.PrefetchScalarGridSpec(
+            num_scalar_prefetch=1,
+            grid=(share_x,),
+            in_specs=[pl.BlockSpec(down_block, before)] + [whole(count, LANES)] * 4,
+            out_specs=whole(*grad_shape),
+            scratch_shapes=[pltpu.VMEM((1, count, hid), F32)],
+        ),
+    )
+    parts, grad_parts = lax.optimization_barrier((parts, grad_parts))
+    grad_parts = exchange(grad_parts, "y")
     rows = [rows[0]] + [shift(rows[d], share_x - d) for d in range(1, share_x)]
-    parts, *rows = lax.optimization_barrier((parts, *rows))
-    act = call(point_kernel, jax.ShapeDtypeStruct(act_shape[1:], BF16), (parts,))
+    parts, grad_parts, *rows = lax.optimization_barrier((parts, grad_parts, *rows))
+    act = call(
+        point_kernel, jax.ShapeDtypeStruct(act_shape[1:], BF16), (parts, grad_parts)
+    )
     act = lax.all_gather(act, "y", axis=0, tiled=False)
     all_act = lax.all_gather(act, "x", axis=0, tiled=False)
     results = call(
         result_kernel,
         jax.ShapeDtypeStruct((share_x, 4 * count, 128), BF16),
-        (order, act, prob, gates, *ups, *downs),
+        (order, act, prob, gates, downs),
         VMEM_LARGE,
         grid_spec=pltpu.PrefetchScalarGridSpec(
             num_scalar_prefetch=1,
             grid=(share_x,),
-            in_specs=[whole(*act_shape), whole(count, 128), pl.BlockSpec(gate_block, before)]
-            + [whole(width, hid)] * 8,
+            in_specs=[
+                whole(*act_shape),
+                whole(count, 128),
+                pl.BlockSpec(gate_block, before),
+                pl.BlockSpec(down_block, before),
+            ],
             out_specs=pl.BlockSpec(tile_block, before),
             scratch_shapes=[pltpu.VMEM((count, LANES), F32), pltpu.VMEM((4 * count, 128), F32)],
         ),

time: 231 us -> 237 us (1.026)
  waiting for transfers between devices: 55.8 us -> 69 us
  starting transfers between devices: 50.8 us -> 38.8 us
  blocking collectives: 77.1 us -> 83 us
    all_gather x1 -> x2, waiting for transfers between devices: 0.02 us -> 27 us  [the longest x1 24.7 us: body(): downs = lax.all_gather(down, 'x', axis=0, tiled=False)]
    ppermute x9 -> x3, waiting for transfers between devices: 27.2 us -> 6.21 us  [shift(): return lax.ppermute(array, 'x', shifts[d])]
    ppermute x9 -> x3, starting transfers between devices: 27.5 us -> 7.99 us  [shift(): return lax.ppermute(array, 'x', shifts[d])]
    all_to_all x3 -> x4, waiting for transfers between devices: 27.9 us -> 35.7 us  [exchange(): return lax.all_to_all(array, axis, split_axis=0, concat_axis=0, tiled=True)]
    all_to_all x3 -> x4, starting transfers between devices: 23.3 us -> 30.7 us  [exchange(): return lax.all_to_all(array, axis, split_axis=0, concat_axis=0, tiled=True)]
    all_to_all x2, blocking collectives: 53.6 us -> 57.8 us  [exchange(): return lax.all_to_all(array, axis, split_axis=0, concat_axis=0, tiled=True)]
    pallas_call x8 -> x9, Pallas kernels: 26.2 us -> 27.4 us  [call(): pl.pallas_call(kernel, out_shape=out_shape, compiler_params=pltpu.Compile...]
  transfers between devices with their start and end apart: 14 -> 10, of which waited for: 7 -> 6; matrix products, arithmetic and copies ran while one was open for 2% -> 1% of each run, Pallas kernels for 6% -> 9%
where the time goes in v5:
time: 237 us; the launch traced here: 236 us
  blocking collectives  83 us (35%)
  waiting for transfers between devices  69 us (29%)
  starting transfers between devices  38.8 us (16%)
  Pallas kernels  27.4 us (12%)
  between operations  14 us (6%)
  other arithmetic  3.3 us (1%)
    all_to_all x2, blocking collectives, exchange(): return lax.all_to_all(array, axis, split_axis=0, concat_axis=0, tiled=True)  57.8 us
    all_to_all x4, waiting for transfers between devices, exchange(): return lax.all_to_all(array, axis, split_axis=0, concat_axis=0, tiled=True)  35.7 us
    all_to_all x4, starting transfers between devices, exchange(): return lax.all_to_all(array, axis, split_axis=0, concat_axis=0, tiled=True)  30.7 us
    pallas_call x9, Pallas kernels, call(): pl.pallas_call(kernel, out_shape=out_shape, compiler_params=pltpu.Compile...  27.4 us
    all_gather x1, blocking collectives, body(): act = lax.all_gather(act, 'y', axis=0, tiled=False)  25.1 us
    all_gather x1, waiting for transfers between devices, body(): downs = lax.all_gather(down, 'x', axis=0, tiled=False)  24.7 us
    ppermute x3, starting transfers between devices, shift(): return lax.ppermute(array, 'x', shifts[d])  7.99 us
    ppermute x3, waiting for transfers between devices, shift(): return lax.ppermute(array, 'x', shifts[d])  6.21 us
  transfers between devices with their start and end apart: 10, of which 6 were waited for; matrix products, arithmetic and copies ran while one was open for 1% of the time, Pallas kernels for 9%

profile of v5, /device:TPU:1, one launch (start us, length us, event | category | flops | bytes accessed | tf_op | source)
XLA Modules:
  0.0 236.0 jit_solution(17277127566681752885)
XLA Ops:
  7.2 0.0 all-gather.8.cloned.1.call-start
  7.2 2.2 pad_maximum_fusion
  9.4 0.0 all-gather.8.cloned.1.call-update
  9.4 2.4 %shard_map.128 = bf16[16,32,512]{2,1,0:T(8,128)(2,1)} custom-call(bf16[224,512]{1,0:T(8,128)(2,1)} %bitcast.53, bf16[224,512]{1,0:T(8,128)(2,1)} %bitcast.54, bf16[16,512]{1,0:T(8,128)(2,1)} %bitcast.55, s32[10,1,16]{2,1,0:T(1,128)} %bitcast.56), custom_call_target="tpu_custom_call" | custom-call | tf_op jit(solution)/shard_map/pallas_call | solution.py:27
  11.8 11.8 %all-to-all-start = ((bf16[16,32,512]{2,1,0:T(8,128)(2,1)}), bf16[16,32,512]{2,1,0:T(8,128)(2,1)S(1)}, u32[]{:S(2)}, u32[]{:S(2)}) async-start(bf16[16,32,512]{2,1,0:T(8,128)(2,1)} %shard_map.128), calls=%async_computation | async-start | bytes 1048576 | tf_op jit(solution)/shard_map/all_to_all | solution.py:241
  23.6 0.0 all-gather.10.cloned.1.call-start
  23.7 0.0 copy-done.8
  23.7 0.1 fusion.5
  23.8 0.1 multiply_reduce_fusion.1
  23.9 0.1 multiply_reduce_fusion
  24.0 0.1 select_reduce_fusion
  24.1 0.1 fusion
  24.2 0.1 reshape.243
  24.4 0.1 reshape.250
  24.5 0.1 reshape.247
  24.7 16.3 %all-to-all-done = bf16[16,32,512]{2,1,0:T(8,128)(2,1)S(1)} async-done(((bf16[16,32,512]{2,1,0:T(8,128)(2,1)}), bf16[16,32,512]{2,1,0:T(8,128)(2,1)S(1)}, u32[]{:S(2)}, u32[]{:S(2)}) %all-to-all-start) | async-done | bytes 524320 | tf_op jit(solution)/shard_map/all_to_all | solution.py:241
  41.0 0.0 all-gather.10.cloned.1.call-update
  41.0 0.2 copy.18.info_ref
  41.2 2.4 shard_map.129
  43.5 5.9 %all-to-all-start.1 = ((bf16[64,40,128]{2,1,0:T(8,128)(2,1)}), bf16[64,40,128]{2,1,0:T(8,128)(2,1)S(1)}, u32[]{:S(2)}, u32[]{:S(2)}) async-start(bf16[64,40,128]{2,1,0:T(8,128)(2,1)} %bitcast.12), calls=%async_computation.1 | async-start | bytes 1310720 | tf_op jit(solution)/shard_map/all_to_all | solution.py:241
  49.4 0.6 pad_convert_fusion
  50.1 19.5 %all-to-all-done.1 = bf16[64,40,128]{2,1,0:T(8,128)(2,1)S(1)} async-done(((bf16[64,40,128]{2,1,0:T(8,128)(2,1)}), bf16[64,40,128]{2,1,0:T(8,128)(2,1)S(1)}, u32[]{:S(2)}, u32[]{:S(2)}) %all-to-all-start.1) | async-done | bytes 655392 | tf_op jit(solution)/shard_map/all_to_all | solution.py:241
  69.6 2.3 all-gather.8.cloned.1.call-done
  71.8 5.3 %shard_map.130 = (bf16[160,512]{1,0:T(8,128)(2,1)}, bf16[160,512]{1,0:T(8,128)(2,1)}, bf16[160,512]{1,0:T(8,128)(2,1)}, bf16[160,512]{1,0:T(8,128)(2,1)}, bf16[8...) custom-call(s32[1]{0:T(128)} %bitcast.11.x_ref, bf16[4,640,128]{2,1,0:T(8,128)(2,1)} %bitcast.49, f32[1,256]{1,0:T(1,128)} %bitcast.57, ...), custom_call_target="tpu_custom_call" | custom-call | tf_op jit(solution)/shard_map/pallas_call | solution.py:27
  77.2 6.5 %all-to-all-start.2 = ((bf16[8,320,128]{2,1,0:T(8,128)(2,1)}), bf16[8,320,128]{2,1,0:T(8,128)(2,1)S(1)}, u32[]{:S(2)}, u32[]{:S(2)}) async-start(bf16[8,320,128]{2,1,0:T(8,128)(2,1)} %get-tuple-element.33), calls=%async_computation.2 | async-start | bytes 1310720 | tf_op jit(solution)/shard_map/all_to_all | solution.py:241
  83.6 0.0 copy-start.5
  83.6 0.0 copy-start.4
  83.7 24.7 %all-gather.10.cloned.1.call-done = bf16[896,1024]{1,0:T(8,128)(2,1)} async-done(((bf16[224,1024]{1,0:T(8,128)(2,1)}), bf16[896,1024]{1,0:T(8,128)(2,1)}) %all-gather.10.cloned.1.call-update) | async-done | bytes 1835024 | tf_op jit(solution)/shard_map/all_gather | solution.py:279
  108.3 3.8 %shard_map.131 = bf16[8,160,128]{2,1,0:T(8,128)(2,1)} custom-call(s32[1]{0:T(128)} %bitcast.11.x_ref, bf16[4,224,1024]{2,1,0:T(8,128)(2,1)} %bitcast.45, bf16[160,512]{1,0:T(8,128)(2,1)} %get-tuple-element.46.refs_0_, bf16[160,512]{1,0:T(8,128)(2,1)} %get-tuple-element.36.refs_1_, bf16[160,512]{1,0:T(8,128)(2,1)} %get-tuple-element.37.refs_2_, ...), custom_call_target="tpu_custom_call" | custom-call | tf_op jit(solution)/shard_map/pallas_call | solution.py:27
  112.1 0.0 all-to-all-done.2.parts_ref
  112.1 6.5 %all-to-all-start.3 = ((bf16[8,160,128]{2,1,0:T(8,128)(2,1)}), bf16[8,160,128]{2,1,0:T(8,128)(2,1)S(1)}, u32[]{:S(2)}, u32[]{:S(2)}) async-start(bf16[8,160,128]{2,1,0:T(8,128)(2,1)} %shard_map.131), calls=%async_computation.3 | async-start | bytes 655360 | tf_op jit(solution)/shard_map/all_to_all | solution.py:241
  118.6 0.0 all-gather.12.cloned.1.call-start
  118.7 2.5 %collective-permute-start = (bf16[160,512]{1,0:T(8,128)(2,1)S(1)}, bf16[160,512]{1,0:T(8,128)(2,1)S(1)}, u32[]{:S(2)}, u32[]{:S(2)}) collective-permute-start(bf16[160,512]{1,0:T(8,128)(2,1)S(1)} %copy-done.6), channel_id=1, source_target_pairs={{0,3},{1,0},{2,1},{3,2},{4,7},{5,4},{6,5},{7,6},{8,11},{9,8},{10,9... | collective-permute-start | bytes 491528 | tf_op jit(solution)/shard_map/ppermute | solution.py:262
  121.2 3.3 %collective-permute-start.1 = (bf16[160,512]{1,0:T(8,128)(2,1)S(1)}, bf16[160,512]{1,0:T(8,128)(2,1)S(1)}, u32[]{:S(2)}, u32[]{:S(2)}) collective-permute-start(bf16[160,512]{1,0:T(8,128)(2,1)S(1)} %copy-done.5), channel_id=1, source_target_pairs={{0,2},{1,3},{2,0},{3,1},{4,6},{5,7},{6,4},{7,5},{8,10},{9,11},{10,... | collective-permute-start | bytes 491528 | tf_op jit(solution)/shard_map/ppermute | solution.py:262
  124.5 2.2 collective-permute-start.2
  126.7 0.0 collective-permute-done.refs_1_
  126.7 2.2 collective-permute-done.1.refs_2_
  128.9 4.0 %collective-permute-done.2.refs_3_ = bf16[160,512]{1,0:T(8,128)(2,1)S(1)} collective-permute-done((bf16[160,512]{1,0:T(8,128)(2,1)S(1)}, bf16[160,512]{1,0:T(8,128)(2,1)S(1)}, u32[]{:S(2)}, u32[]{:S(2)}) %collective-permute-start.2) | collective-permute-done | bytes 163872 | tf_op jit(solution)/shard_map/ppermute | solution.py:262
  132.9 0.0 all-to-all-done.3.grads_ref
  132.9 0.2 shard_map.132
  133.1 25.1 %all-gather.2 = bf16[3840,128]{1,0:T(8,128)(2,1)} all-gather(bf16[480,128]{1,0:T(8,128)(2,1)S(1)} %shard_map.132), channel_id=4, replica_groups=mesh['z'=8,'core'=2,'y'=8,'x'=4] {'y'}, dimensions={0}, use_global_device_ids=true | all-gather | bytes 1105920 | tf_op jit(solution)/shard_map/all_gather | solution.py:349
  158.3 0.0 all-gather.12.cloned.1.call-update
  158.3 5.9 %shard_map.133 = bf16[4,640,128]{2,1,0:T(8,128)(2,1)} custom-call(s32[1]{0:T(128)} %bitcast.11.x_ref, bf16[8,480,128]{2,1,0:T(8,128)(2,1)} %bitcast.44, f32[160,128]{1,0:T(8,128)} %get-tuple-element.43.prob_ref, bf16[4,448,1024]{2,1,0:T(8,128)(2,1)} %bitcast.42, bf16[4,224,1024]{2,1,0:T(8,128)(2,1)} %bitcast.46), custom_call_target="tpu_custom_call" | custom-call | tf_op jit(solution)/shard_map/pallas_call | solution.py:27
  164.2 35.9 %all_to_all.30 = bf16[64,40,128]{2,1,0:T(8,128)(2,1)S(1)} all-to-all(bf16[64,40,128]{2,1,0:T(8,128)(2,1)} %bitcast.48), channel_id=1, replica_groups=mesh['z'=8,'core'=2,'y'=8,'x'=4] {'x','z','core'}, dimensions={0} | all-to-all | bytes 1310720 | tf_op jit(solution)/shard_map/all_to_all | solution.py:241
  200.1 0.6 shard_map.134
  200.8 21.9 %all_to_all.31 = bf16[16,32,512]{2,1,0:T(8,128)(2,1)S(1)} all-to-all(bf16[16,32,512]{2,1,0:T(8,128)(2,1)S(1)} %bitcast.38), channel_id=1, replica_groups=mesh['z'=8,'core'=2,'y'=8,'x'=4] {'z','core'}, dimensions={0} | all-to-all | bytes 1048576 | tf_op jit(solution)/shard_map/all_to_all | solution.py:241
  222.7 1.2 shard_map.135
  223.9 5.6 %shard_map.136 = (bf16[224,1024]{1,0:T(8,128)(2,1)}, bf16[224,1024]{1,0:T(8,128)(2,1)}, bf16[224,1024]{1,0:T(8,128)(2,1)}) custom-call(s32[1]{0:T(128)} %bitcast.11.x_ref, bf16[4,8,480,128]{3,2,1,0:T(8,128)(2,1)} %bitcast.47, bf16[160,512]{1,0:T(8,128)(2,1)} %get-tuple-element.46.refs_0_, bf16[160,512]{1,0:T(8,128)(2,1)} %copy-done.1, ...), custom_call_target="tpu_custom_call" | custom-call | tf_op jit(solution)/shard_map/pallas_call | solution.py:27
  (23 shorter events, 0.1 us)
Async XLA Ops:
  7.2 64.7 %all-gather.8.cloned.1.call-start = ((), (), s32[]{:S(2)}) async-start(), calls=%async_computation.6 | async-start | bytes 4587520 | tf_op jit(solution)/shard_map/all_gather | solution.py:265
  9.4 14.3 %copy-start.8 = (s32[16]{0:T(128)S(1)}, s32[16]{0:T(128)}, u32[]{:S(2)}) copy-start(s32[16]{0:T(128)} %param.15) | copy-start | bytes 196
  9.4 14.4 %copy-start.7 = (s32[16,16]{1,0:T(8,128)S(1)}, s32[16,16]{1,0:T(8,128)}, u32[]{:S(2)}) copy-start(s32[16,16]{1,0:T(8,128)} %param.16) | copy-start | bytes 3076
  11.8 29.2 %all-to-all-start = ((bf16[16,32,512]{2,1,0:T(8,128)(2,1)}), bf16[16,32,512]{2,1,0:T(8,128)(2,1)S(1)}, u32[]{:S(2)}, u32[]{:S(2)}) async-start(bf16[16,32,512]{2,1,0:T(8,128)(2,1)} %shard_map.128), calls=%async_computation | async-start | bytes 1048576 | tf_op jit(solution)/shard_map/all_to_all | solution.py:241
  23.6 84.7 %all-gather.10.cloned.1.call-start = ((), (), s32[]{:S(2)}) async-start(), calls=%async_computation.7 | async-start | bytes 2293760 | tf_op jit(solution)/shard_map/all_gather | solution.py:279
  43.5 26.0 %all-to-all-start.1 = ((bf16[64,40,128]{2,1,0:T(8,128)(2,1)}), bf16[64,40,128]{2,1,0:T(8,128)(2,1)S(1)}, u32[]{:S(2)}, u32[]{:S(2)}) async-start(bf16[64,40,128]{2,1,0:T(8,128)(2,1)} %bitcast.12), calls=%async_computation.1 | async-start | bytes 1310720 | tf_op jit(solution)/shard_map/all_to_all | solution.py:241
  69.6 2.3 copy-start
  77.2 35.0 %all-to-all-start.2 = ((bf16[8,320,128]{2,1,0:T(8,128)(2,1)}), bf16[8,320,128]{2,1,0:T(8,128)(2,1)S(1)}, u32[]{:S(2)}, u32[]{:S(2)}) async-start(bf16[8,320,128]{2,1,0:T(8,128)(2,1)} %get-tuple-element.33), calls=%async_computation.2 | async-start | bytes 1310720 | tf_op jit(solution)/shard_map/all_to_all | solution.py:241
  83.6 35.0 %copy-start.6 = (bf16[160,512]{1,0:T(8,128)(2,1)S(1)}, bf16[160,512]{1,0:T(8,128)(2,1)}, u32[]{:S(2)}) copy-start(bf16[160,512]{1,0:T(8,128)(2,1)} %get-tuple-element.36.refs_1_) | copy-start | bytes 491524
  83.6 37.5 %copy-start.5 = (bf16[160,512]{1,0:T(8,128)(2,1)S(1)}, bf16[160,512]{1,0:T(8,128)(2,1)}, u32[]{:S(2)}) copy-start(bf16[160,512]{1,0:T(8,128)(2,1)} %get-tuple-element.37.refs_2_) | copy-start | bytes 491524
  83.6 40.8 %copy-start.4 = (bf16[160,512]{1,0:T(8,128)(2,1)S(1)}, bf16[160,512]{1,0:T(8,128)(2,1)}, u32[]{:S(2)}) copy-start(bf16[160,512]{1,0:T(8,128)(2,1)} %get-tuple-element.38.refs_3_) | copy-start | bytes 491524
  112.1 20.8 %all-to-all-start.3 = ((bf16[8,160,128]{2,1,0:T(8,128)(2,1)}), bf16[8,160,128]{2,1,0:T(8,128)(2,1)S(1)}, u32[]{:S(2)}, u32[]{:S(2)}) async-start(bf16[8,160,128]{2,1,0:T(8,128)(2,1)} %shard_map.131), calls=%async_computation.3 | async-start | bytes 655360 | tf_op jit(solution)/shard_map/all_to_all | solution.py:241
  118.6 105.3 %all-gather.12.cloned.1.call-start = ((), (), s32[]{:S(2)}) async-start(), calls=%async_computation.8 | async-start | bytes 4915200 | tf_op jit(solution)/shard_map/all_gather | solution.py:350
  118.7 8.0 %collective-permute-start = (bf16[160,512]{1,0:T(8,128)(2,1)S(1)}, bf16[160,512]{1,0:T(8,128)(2,1)S(1)}, u32[]{:S(2)}, u32[]{:S(2)}) collective-permute-start(bf16[160,512]{1,0:T(8,128)(2,1)S(1)} %copy-done.6), channel_id=1, source_target_pairs={{0,3},{1,0},{2,1},{3,2},{4,7},{5,4},{6,5},{7,6},{8,11},{9,8},{10,9... | collective-permute-start | bytes 491528 | tf_op jit(solution)/shard_map/ppermute | solution.py:262
  121.2 7.7 %collective-permute-start.1 = (bf16[160,512]{1,0:T(8,128)(2,1)S(1)}, bf16[160,512]{1,0:T(8,128)(2,1)S(1)}, u32[]{:S(2)}, u32[]{:S(2)}) collective-permute-start(bf16[160,512]{1,0:T(8,128)(2,1)S(1)} %copy-done.5), channel_id=1, source_target_pairs={{0,2},{1,3},{2,0},{3,1},{4,6},{5,7},{6,4},{7,5},{8,10},{9,11},{10,... | collective-permute-start | bytes 491528 | tf_op jit(solution)/shard_map/ppermute | solution.py:262
  124.5 8.4 %collective-permute-start.2 = (bf16[160,512]{1,0:T(8,128)(2,1)S(1)}, bf16[160,512]{1,0:T(8,128)(2,1)S(1)}, u32[]{:S(2)}, u32[]{:S(2)}) collective-permute-start(bf16[160,512]{1,0:T(8,128)(2,1)S(1)} %copy-done.4), channel_id=1, source_target_pairs={{0,1},{1,2},{2,3},{3,0},{4,5},{5,6},{6,7},{7,4},{8,9},{9,10},{10,1... | collective-permute-start | bytes 491528 | tf_op jit(solution)/shard_map/ppermute | solution.py:262
  126.7 37.5 %copy-start.1 = (bf16[160,512]{1,0:T(8,128)(2,1)}, bf16[160,512]{1,0:T(8,128)(2,1)S(1)}, u32[]{:S(2)}) copy-start(bf16[160,512]{1,0:T(8,128)(2,1)S(1)} %collective-permute-done.refs_1_) | copy-start | bytes 491524
  128.9 35.3 %copy-start.2 = (bf16[160,512]{1,0:T(8,128)(2,1)}, bf16[160,512]{1,0:T(8,128)(2,1)S(1)}, u32[]{:S(2)}) copy-start(bf16[160,512]{1,0:T(8,128)(2,1)S(1)} %collective-permute-done.1.refs_2_) | copy-start | bytes 491524
  132.9 31.3 %copy-start.3 = (bf16[160,512]{1,0:T(8,128)(2,1)}, bf16[160,512]{1,0:T(8,128)(2,1)S(1)}, u32[]{:S(2)}) copy-start(bf16[160,512]{1,0:T(8,128)(2,1)S(1)} %collective-permute-done.2.refs_3_) | copy-start | bytes 491524
Sparse Core Ops, SparseCore 0:
  10.1 61.6 all-gather.7
  73.9 34.3 all-gather.9
  158.4 63.2 all-gather.11

commit v6 on v3

--- a/solution.py
+++ b/solution.py
@@ -8,6 +8,7 @@
 BLK = 32
 USERS = 2
 LANES = 512
+STEPS = (0, 3, 1, 2)
 P_LANE = 224
 DY_LANE = 256
 LIST_LANE = 480
@@ -46,8 +47,12 @@
     all_ref[P_LANE : P_LANE + 16] = prob_ref[...]
     all_ref[DY_LANE : DY_LANE + width] = dy_ref[...]
     packed = dot(token_permutation(LANES), all_ref[...], 1, 1)
-    packed = packed.reshape(out_ref.shape) + list_ref[...].astype(F32)[None]
-    out_ref[...] = packed.astype(BF16)
+    lists = list_ref[:, 0, :].astype(F32).astype(BF16)
+    entry = lax.broadcasted_iota(jnp.int32, (lists.shape[0], LANES), 0)
+    lane = lax.broadcasted_iota(jnp.int32, (lists.shape[0], LANES), 1)
+    lists = dot(lists, (lane == entry + LIST_LANE).astype(BF16), 0, 0)
+    lists = jnp.concatenate([lists, jnp.zeros((BLK - lists.shape[0], LANES), F32)], axis=0)
+    out_ref[...] = (packed.reshape(out_ref.shape) + lists[None]).astype(BF16)
 
 
 def split_lanes(tmp_ref, rows):
@@ -77,39 +82,49 @@
     out_ref[...] = split_lanes(tmp_ref, dot(pick, rows, 1, 0))
 
 
-def hidden_kernel(x_ref, tiles_ref, mark_ref, gate_ref, *refs):
-    up_refs, down_refs, refs = refs[:4], refs[4:8], refs[8:]
-    row_refs, (out_ref, prob_ref, acc_ref, tmp_ref) = refs[:4], refs[4:]
-    step = pl.program_id(0)
-    rows = join_lanes(tmp_ref, tiles_ref[0])
-    count = rows.shape[0]
-    width, hid = gate_ref.shape[1:]
-    prob = jnp.sum(rows[:, 0:256] * mark_ref[...], axis=1, keepdims=True)
-    x = rows[:, 0:256].astype(BF16)
-    grad = (prob * rows[:, DY_LANE:LANES]).astype(BF16)
-    prob_ref[...] = jnp.broadcast_to(prob, prob_ref.shape)
-
-    @pl.when(step == 0)
-    def _():
-        acc_ref[...] = jnp.zeros_like(acc_ref)
-
-    acc_ref[0] += dot(x[:, 0:width], gate_ref[0], 1, 0)
-    for d in range(4):
-
-        @pl.when(step == d)
-        def _():
-            row_refs[d][:, 0:DY_LANE] = x
-            row_refs[d][:, DY_LANE:LANES] = grad
-            acc_ref[1] += dot(x[:, 0:width], up_refs[d][...], 1, 0)
-            acc_ref[2] += dot(grad[:, 0:width], down_refs[d][...], 1, 0)
-
-    @pl.when(step == pl.num_programs(0) - 1)
-    def _():
-        for part in range(3):
-            for piece in range(hid // 128):
-                out_ref[piece, part * count : (part + 1) * count] = acc_ref[
-                    part, :, piece * 128 : (piece + 1) * 128
-                ].astype(BF16)
+def panel_copies(sources, panel_ref, sems):
+    half = panel_ref.shape[2] // 2
+    targets = [panel_ref.at[d] for d in range(3)]
+    targets += [panel_ref.at[3, :, pl.ds(i * half, half)] for i in range(2)]
+    copies = [
+        pltpu.make_async_copy(source, target, sems.at[i])
+        for i, (source, target) in enumerate(zip(sources, targets))
+    ]
+    for copy in copies:
+        copy.start()
+    return [copies[:1], copies[1:2], copies[2:3], copies[3:]]
+
+
+def hidden_kernel(x_ref, tiles_ref, mark_ref, *refs):
+    sources, row_refs = refs[:5], refs[5:9]
+    out_ref, prob_ref, acc_ref, tmp_ref, panel_ref, sems = refs[9:]
+    copies = panel_copies(sources, panel_ref, sems)
+    width = panel_ref.shape[1] // 3
+    parts = acc_ref.shape[0]
+    count = acc_ref.shape[1]
+    for d, step in enumerate(STEPS):
+        rows = join_lanes(tmp_ref, tiles_ref[lax.rem(x_ref[0] + step, 4)])
+        prob = jnp.sum(rows[:, 0:256] * mark_ref[...], axis=1, keepdims=True)
+        x = rows[:, 0:256].astype(BF16)
+        grad = (prob * rows[:, DY_LANE:LANES]).astype(BF16)
+        row_refs[d][:, 0:DY_LANE] = x
+        row_refs[d][:, DY_LANE:LANES] = grad
+        if d == 0:
+            prob_ref[...] = jnp.broadcast_to(prob, prob_ref.shape)
+        for copy in copies[d]:
+            copy.wait()
+        for part in range(parts):
+            left = grad if part == 2 else x
+            term = dot(left[:, 0:width], panel_ref[d, part * width : (part + 1) * width], 1, 0)
+            if d == 0:
+                acc_ref[part] = term
+            else:
+                acc_ref[part] += term
+    for part in range(parts):
+        for piece in range(out_ref.shape[0]):
+            out_ref[piece, part * count : (part + 1) * count] = acc_ref[
+                part, :, piece * 128 : (piece + 1) * 128
+            ].astype(BF16)
 
 
 def point_kernel(parts_ref, out_ref):
@@ -130,25 +145,21 @@
     ]
 
 
-def result_kernel(x_ref, act_ref, prob_ref, gate_ref, *refs):
-    up_refs, down_refs, (out_ref, res_ref, tmp_ref) = refs[:4], refs[4:8], refs[8:]
-    step = pl.program_id(0)
-    width = gate_ref.shape[1]
+def result_kernel(x_ref, act_ref, prob_ref, *refs):
+    sources, (out_ref, res_ref, tmp_ref, panel_ref, sems) = refs[:5], refs[5:]
+    copies = panel_copies(sources, panel_ref, sems)
+    width = panel_ref.shape[1] // 3
     hidden, gate_grad, up_grad = hidden_parts(act_ref)
-
-    @pl.when(step == 0)
-    def _():
-        res_ref[...] = jnp.zeros_like(res_ref)
-
-    dx = dot(gate_grad, gate_ref[0], 1, 1)
-    for d in range(4):
-
-        @pl.when(step == d)
-        def _():
-            res_ref[:, 0:width] = prob_ref[:, 0:1] * dot(hidden, down_refs[d][...], 1, 1)
-            res_ref[:, DY_LANE : DY_LANE + width] = dx + dot(up_grad, up_refs[d][...], 1, 1)
-
-    out_ref[0] = split_lanes(tmp_ref, res_ref[...])
+    res_ref[...] = jnp.zeros_like(res_ref)
+    for d, step in enumerate(STEPS):
+        for copy in copies[d]:
+            copy.wait()
+        outcome = prob_ref[:, 0:1] * dot(hidden, panel_ref[d, 2 * width :], 1, 1)
+        dx = dot(gate_grad, panel_ref[d, 0:width], 1, 1)
+        dx += dot(up_grad, panel_ref[d, width : 2 * width], 1, 1)
+        res_ref[:, 0:width] = outcome
+        res_ref[:, DY_LANE : DY_LANE + width] = dx
+        out_ref[lax.rem(x_ref[0] + step, 4)] = split_lanes(tmp_ref, res_ref[...])
 
 
 def weight_kernel(x_ref, act_ref, *refs):
@@ -239,19 +250,13 @@
     def shift(array, d):
         return lax.ppermute(array, "x", shifts[d])
 
-    gates = lax.all_gather(w_gate[0], "x", axis=0, tiled=False)
-    up, down = w_up[0], w_down[0].T
-    up_right, down_left = shift(up, 1), shift(down, 3)
-
-    lists = lax.pad(
-        block_lists[0].astype(BF16),
-        jnp.zeros((), BF16),
-        ((0, BLK - 16, 0), (LIST_LANE, LANES - LIST_LANE - entries, 0)),
-    )
+    panel = jnp.concatenate([w_gate[0], w_up[0], w_down[0].T], axis=0)
+    right, left = shift(panel, 1), shift(panel, 3)
+
     packed = call(
         pack_kernel,
         jax.ShapeDtypeStruct((groups, BLK, LANES), BF16),
-        (tokens.T, grad_output.T, gate_prob.T, lists),
+        (tokens.T, grad_output.T, gate_prob.T, block_lists.transpose(2, 0, 1)),
         VMEM_LARGE,
         scratch_shapes=[pltpu.VMEM((LANES, LANES), BF16)],
     )
@@ -259,7 +264,7 @@
     mine = (expert_slot == lax.axis_index(GROUP)).astype(F32)
     mark = lax.pad(mine, jnp.zeros((), F32), ((P_LANE, 16, 0),))[None]
     spread = exchange(packed, GROUP).reshape(groups * BLK, LANES)
-    spread, up_right, down_left = lax.optimization_barrier((spread, up_right, down_left))
+    spread, info = lax.optimization_barrier((spread, info))
     sent, pick = call(
         select_kernel,
         (
@@ -269,47 +274,36 @@
         (spread, info),
         scratch_shapes=[pltpu.VMEM((4 * total, 128), F32)],
     )
-    ups = [up, up_right, shift(up_right, 1), shift(up, 3)]
-    downs = [down, shift(down, 1), shift(down_left, 3), down_left]
+    sent, right, left = lax.optimization_barrier((sent, right, left))
+    half = hid // 2
+    panels = [panel, right, left, shift(right[:, 0:half], 1), shift(left[:, half:], 3)]
     pieces = (share_x * groups, 4 * picked // share_x, 128)
     tiles = exchange(sent.reshape(pieces), OWNERS).reshape(share_x, 4 * count, 128)
 
     def before(d, x):
         return (lax.rem(x[0] + share_x - d, share_x), 0, 0)
 
-    def after(d, x):
-        return (lax.rem(x[0] + d, share_x), 0, 0)
-
     def whole(*shape):
         return pl.BlockSpec(shape, lambda *_: (0,) * len(shape))
 
     tile_block = (1, 4 * count, 128)
-    gate_block = (1, width, hid)
     act_shape = (share_y, 3 * count, hid // share_y)
+    scalar_spec = pl.BlockSpec(memory_space=pltpu.SMEM)
+    vmem_spec = pl.BlockSpec(memory_space=pltpu.VMEM)
+    panel_specs = [pl.BlockSpec(memory_space=pl.ANY)] * 5
+    panel_scratch = [pltpu.VMEM((4, 3 * width, hid), BF16), pltpu.SemaphoreType.DMA((5,))]
     *rows, parts, prob = call(
         hidden_kernel,
         (jax.ShapeDtypeStruct((count, LANES), BF16),) * 4
         + (jax.ShapeDtypeStruct(act_shape, BF16), jax.ShapeDtypeStruct((count, 128), F32)),
-        (order, tiles, mark, gates, *ups, *downs),
+        (order, tiles, mark, *panels),
         VMEM_LARGE,
-        grid_spec=pltpu.PrefetchScalarGridSpec(
-            num_scalar_prefetch=1,
-            grid=(share_x,),
-            in_specs=[
-                pl.BlockSpec(tile_block, before),
-                whole(1, 256),
-                pl.BlockSpec(gate_block, before),
-            ]
-            + [whole(width, hid)] * 8,
-            out_specs=[whole(count, LANES)] * 4 + [whole(*act_shape), whole(count, 128)],
-            scratch_shapes=[
-                pltpu.VMEM((3, count, hid), F32),
-                pltpu.VMEM((4 * count, 128), F32),
-            ],
-        ),
+        in_specs=[scalar_spec, vmem_spec, vmem_spec] + panel_specs,
+        scratch_shapes=[pltpu.VMEM((3, count, hid), F32), pltpu.VMEM((4 * count, 128), F32)]
+        + panel_scratch,
     )
     parts = exchange(parts, "y")
-    rows = [rows[0]] + [shift(rows[d], share_x - d) for d in range(1, share_x)]
+    rows = [shift(rows[d], STEPS[d]) if STEPS[d] else rows[d] for d in range(share_x)]
     parts, *rows = lax.optimization_barrier((parts, *rows))
     act = call(point_kernel, jax.ShapeDtypeStruct(act_shape[1:], BF16), (parts,))
     act = lax.all_gather(act, "y", axis=0, tiled=False)
@@ -317,26 +311,21 @@
     results = call(
         result_kernel,
         jax.ShapeDtypeStruct((share_x, 4 * count, 128), BF16),
-        (order, act, prob, gates, *ups, *downs),
+        (order, act, prob, *panels),
+        VMEM_LARGE,
+        in_specs=[scalar_spec, vmem_spec, vmem_spec] + panel_specs,
+        scratch_shapes=[pltpu.VMEM((count, LANES), F32), pltpu.VMEM((4 * count, 128), F32)]
+        + panel_scratch,
+    )
+    weights = call(
+        weight_kernel,
+        (jax.ShapeDtypeStruct((width, hid), BF16),) * 3,
+        (order, all_act, *(rows[STEPS.index(d)] for d in range(share_x))),
         VMEM_LARGE,
         grid_spec=pltpu.PrefetchScalarGridSpec(
             num_scalar_prefetch=1,
             grid=(share_x,),
-            in_specs=[whole(*act_shape), whole(count, 128), pl.BlockSpec(gate_block, before)]
-            + [whole(width, hid)] * 8,
-            out_specs=pl.BlockSpec(tile_block, before),
-            scratch_shapes=[pltpu.VMEM((count, LANES), F32), pltpu.VMEM((4 * count, 128), F32)],
-        ),
-    )
-    weights = call(
-        weight_kernel,
-        (jax.ShapeDtypeStruct((width, hid), BF16),) * 3,
-        (order, all_act, *rows),
-        VMEM_LARGE,
-        grid_spec=pltpu.PrefetchScalarGridSpec(
-            num_scalar_prefetch=1,
-            grid=(share_x,),
-            in_specs=[pl.BlockSpec((1,) + act_shape, lambda d, x: after(d, x) + (0,))]
+            in_specs=[pl.BlockSpec((1,) + act_shape, lambda d, x: before(d, x) + (0,))]
             + [whole(count, LANES)] * 4,
             out_specs=[whole(width, hid)] * 3,
             scratch_shapes=[pltpu.VMEM((3, width, hid), F32)],

time: 231 us -> 233 us (level)
    ppermute x9 -> x7, starting transfers between devices: 27.5 us -> 21.1 us  [shift(): return lax.ppermute(array, 'x', shifts[d])]
    all_to_all x3, starting transfers between devices: 23.3 us -> 29.4 us  [exchange(): return lax.all_to_all(array, axis, split_axis=0, concat_axis=0, tiled=True)]
    slice x0 -> x2, local copies, waits for them, and re-layouts: none -> 3.16 us  [the longest x1 2.02 us: body(): left[:, half:]]
    all_to_all x3, waiting for transfers between devices: 27.9 us -> 30.9 us  [exchange(): return lax.all_to_all(array, axis, split_axis=0, concat_axis=0, tiled=True)]
    ppermute x9 -> x7, waiting for transfers between devices: 27.2 us -> 26 us  [shift(): return lax.ppermute(array, 'x', shifts[d])]
  transfers between devices with their start and end apart: 14 -> 11, of which waited for: 7 -> 6; matrix products, arithmetic and copies ran while one was open for 2% -> 2% of each run, Pallas kernels for 6% -> 6%
where the time goes in v6:
time: 233 us; the launch traced here: 232 us
  blocking collectives  77.9 us (33%)
  waiting for transfers between devices  56.9 us (24%)
  starting transfers between devices  50.5 us (22%)
  Pallas kernels  24.6 us (11%)
  between operations  14.4 us (6%)
  local copies, waits for them, and re-layouts  4.97 us (2%)
  other arithmetic  2.54 us (1%)
    all_to_all x2, blocking collectives, exchange(): return lax.all_to_all(array, axis, split_axis=0, concat_axis=0, tiled=True)  54.4 us
    all_to_all x3, waiting for transfers between devices, exchange(): return lax.all_to_all(array, axis, split_axis=0, concat_axis=0, tiled=True)  30.9 us
    all_to_all x3, starting transfers between devices, exchange(): return lax.all_to_all(array, axis, split_axis=0, concat_axis=0, tiled=True)  29.4 us
    ppermute x7, waiting for transfers between devices, shift(): return lax.ppermute(array, 'x', shifts[d])  26 us
    pallas_call x8, Pallas kernels, call(): pl.pallas_call(kernel, out_shape=out_shape, compiler_params=pltpu.Compile...  24.6 us
    all_gather x1, blocking collectives, body(): act = lax.all_gather(act, 'y', axis=0, tiled=False)  23.4 us
    ppermute x7, starting transfers between devices, shift(): return lax.ppermute(array, 'x', shifts[d])  21.1 us
  transfers between devices with their start and end apart: 11, of which 6 were waited for; matrix products, arithmetic and copies ran while one was open for 2% of the time, Pallas kernels for 6%

profile of v6, /device:TPU:1, one launch (start us, length us, event | category | flops | bytes accessed | tf_op | source)
XLA Modules:
  0.0 231.8 jit_solution(6481086261756167906)
XLA Ops:
  7.2 1.4 pad_maximum_fusion.refs_0_
  8.6 0.0 copy-start.8
  8.6 0.0 copy-start.7
  8.6 5.3 %collective-permute-start.1 = (bf16[672,1024]{1,0:T(8,128)(2,1)S(1)}, bf16[672,1024]{1,0:T(8,128)(2,1)}, u32[]{:S(2)}, u32[]{:S(2)}) collective-permute-start(bf16[672,1024]{1,0:T(8,128)(2,1)S(1)} %pad_maximum_fusion.refs_0_), channel_id=1, source_target_pairs={{0,3},{1,0},{2,1},{3,2},{4,7},{5,4},{6,5},{7,6},{8,11},{9,8},{10,9... | collective-permute-start | bytes 4128776 | tf_op jit(solution)/shard_map/ppermute | solution.py:251
  14.0 1.9 collective-permute-start
  15.9 2.4 %shard_map.128 = bf16[16,32,512]{2,1,0:T(8,128)(2,1)} custom-call(bf16[224,512]{1,0:T(8,128)(2,1)} %bitcast.47, bf16[224,512]{1,0:T(8,128)(2,1)} %bitcast.48, bf16[16,512]{1,0:T(8,128)(2,1)} %bitcast.49, s32[10,1,16]{2,1,0:T(1,128)} %bitcast.50), custom_call_target="tpu_custom_call" | custom-call | tf_op jit(solution)/shard_map/pallas_call | solution.py:28
  18.3 11.3 %all-to-all-start = ((bf16[16,32,512]{2,1,0:T(8,128)(2,1)}), bf16[16,32,512]{2,1,0:T(8,128)(2,1)S(1)}, u32[]{:S(2)}, u32[]{:S(2)}) async-start(bf16[16,32,512]{2,1,0:T(8,128)(2,1)} %shard_map.128), calls=%async_computation | async-start | bytes 1048576 | tf_op jit(solution)/shard_map/all_to_all | solution.py:230
  29.6 0.1 fusion.5
  29.6 0.1 multiply_reduce_fusion.1
  29.8 0.1 multiply_reduce_fusion
  29.9 0.1 select_reduce_fusion
  30.0 0.1 fusion
  30.1 0.1 reshape.243
  30.2 0.1 reshape.250
  30.4 0.1 reshape.247
  30.6 16.3 %all-to-all-done = bf16[16,32,512]{2,1,0:T(8,128)(2,1)S(1)} async-done(((bf16[16,32,512]{2,1,0:T(8,128)(2,1)}), bf16[16,32,512]{2,1,0:T(8,128)(2,1)S(1)}, u32[]{:S(2)}, u32[]{:S(2)}) %all-to-all-start) | async-done | bytes 524320 | tf_op jit(solution)/shard_map/all_to_all | solution.py:230
  46.9 0.2 copy.18.info_ref
  47.1 2.4 %shard_map.129 = (bf16[2560,128]{1,0:T(8,128)(2,1)}, bf16[640,512]{1,0:T(8,128)(2,1)S(1)}) custom-call(bf16[512,512]{1,0:T(8,128)(2,1)S(1)} %bitcast.37, s32[640,3]{1,0:T(8,128)S(1)} %copy.18.info_ref), custom_call_target="tpu_custom_call" | custom-call | tf_op jit(solution)/shard_map/pallas_call | solution.py:28
  49.5 11.2 %all-to-all-start.1 = ((bf16[64,40,128]{2,1,0:T(8,128)(2,1)}), bf16[64,40,128]{2,1,0:T(8,128)(2,1)S(1)}, u32[]{:S(2)}, u32[]{:S(2)}) async-start(bf16[64,40,128]{2,1,0:T(8,128)(2,1)} %bitcast.14), calls=%async_computation.1 | async-start | bytes 1310720 | tf_op jit(solution)/shard_map/all_to_all | solution.py:230
  60.6 1.1 slice.22
  61.8 2.0 slice.23
  63.8 4.7 %collective-permute-start.3 = (bf16[672,512]{1,0:T(8,128)(2,1)}, bf16[672,512]{1,0:T(8,128)(2,1)S(1)}, u32[]{:S(2)}, u32[]{:S(2)}) collective-permute-start(bf16[672,512]{1,0:T(8,128)(2,1)} %slice.23), channel_id=1, source_target_pairs={{0,3},{1,0},{2,1},{3,2},{4,7},{5,4},{6,5},{7,6},{8,11},{9,8},{10,9... | collective-permute-start | bytes 2064392 | tf_op jit(solution)/shard_map/ppermute | solution.py:251
  68.5 1.9 collective-permute-start.2
  70.5 0.6 pad_convert_fusion
  71.1 16.4 %collective-permute-done.3.refs_4_ = bf16[672,512]{1,0:T(8,128)(2,1)S(1)} collective-permute-done((bf16[672,512]{1,0:T(8,128)(2,1)}, bf16[672,512]{1,0:T(8,128)(2,1)S(1)}, u32[]{:S(2)}, u32[]{:S(2)}) %collective-permute-start.3) | collective-permute-done | bytes 688160 | tf_op jit(solution)/shard_map/ppermute | solution.py:251
  87.5 3.7 %collective-permute-done.2.refs_3_ = bf16[672,512]{1,0:T(8,128)(2,1)S(1)} collective-permute-done((bf16[672,512]{1,0:T(8,128)(2,1)S(1)}, bf16[672,512]{1,0:T(8,128)(2,1)S(1)}, u32[]{:S(2)}, u32[]{:S(2)}) %collective-permute-start.2) | collective-permute-done | bytes 688160 | tf_op jit(solution)/shard_map/ppermute | solution.py:251
  91.2 0.8 copy-done.2
  92.1 0.3 copy-done.3
  92.4 5.1 %shard_map.130 = (bf16[160,512]{1,0:T(8,128)(2,1)}, bf16[160,512]{1,0:T(8,128)(2,1)}, bf16[160,512]{1,0:T(8,128)(2,1)}, bf16[160,512]{1,0:T(8,128)(2,1)}, bf16[8...) custom-call(s32[1]{0:T(128)} %bitcast.9.x_ref, bf16[4,640,128]{2,1,0:T(8,128)(2,1)} %bitcast.43, f32[1,256]{1,0:T(1,128)} %bitcast.51, ...), custom_call_target="tpu_custom_call" | custom-call | tf_op jit(solution)/shard_map/pallas_call | solution.py:28
  97.5 0.0 copy-start.11
  97.5 0.0 copy-start.9
  97.5 7.0 %all-to-all-start.2 = ((bf16[8,480,128]{2,1,0:T(8,128)(2,1)}), bf16[8,480,128]{2,1,0:T(8,128)(2,1)S(1)}, u32[]{:S(2)}, u32[]{:S(2)}) async-start(bf16[8,480,128]{2,1,0:T(8,128)(2,1)} %get-tuple-element.35), calls=%async_computation.2 | async-start | bytes 1966080 | tf_op jit(solution)/shard_map/all_to_all | solution.py:230
  104.5 0.0 all-gather.4.cloned.1.call-start
  104.5 1.9 collective-permute-start.4
  106.5 3.4 %collective-permute-start.5 = (bf16[160,512]{1,0:T(8,128)(2,1)S(1)}, bf16[160,512]{1,0:T(8,128)(2,1)S(1)}, u32[]{:S(2)}, u32[]{:S(2)}) collective-permute-start(bf16[160,512]{1,0:T(8,128)(2,1)S(1)} %copy-done.10), channel_id=1, source_target_pairs={{0,1},{1,2},{2,3},{3,0},{4,5},{5,6},{6,7},{7,4},{8,9},{9,10},{10,1... | collective-permute-start | bytes 491528 | tf_op jit(solution)/shard_map/ppermute | solution.py:251
  109.8 1.9 collective-permute-start.6
  111.8 2.2 collective-permute-done.5.refs_1_
  114.0 3.7 %collective-permute-done.6.refs_2_ = bf16[160,512]{1,0:T(8,128)(2,1)S(1)} collective-permute-done((bf16[160,512]{1,0:T(8,128)(2,1)S(1)}, bf16[160,512]{1,0:T(8,128)(2,1)S(1)}, u32[]{:S(2)}, u32[]{:S(2)}) %collective-permute-start.6) | collective-permute-done | bytes 163872 | tf_op jit(solution)/shard_map/ppermute | solution.py:251
  117.7 14.6 %all-to-all-done.2.parts_ref = bf16[8,480,128]{2,1,0:T(8,128)(2,1)S(1)} async-done(((bf16[8,480,128]{2,1,0:T(8,128)(2,1)}), bf16[8,480,128]{2,1,0:T(8,128)(2,1)S(1)}, u32[]{:S(2)}, u32[]{:S(2)}) %all-to-all-start.2) | async-done | bytes 983072 | tf_op jit(solution)/shard_map/all_to_all | solution.py:230
  132.3 0.2 shard_map.131
  132.4 23.4 %all-gather = bf16[3840,128]{1,0:T(8,128)(2,1)} all-gather(bf16[480,128]{1,0:T(8,128)(2,1)S(1)} %shard_map.131), channel_id=2, replica_groups=mesh['z'=8,'core'=2,'y'=8,'x'=4] {'y'}, dimensions={0}, use_global_device_ids=true | all-gather | bytes 1105920 | tf_op jit(solution)/shard_map/all_gather | solution.py:309
  155.9 0.0 all-gather.4.cloned.1.call-update
  155.9 7.2 %shard_map.132 = bf16[4,640,128]{2,1,0:T(8,128)(2,1)} custom-call(s32[1]{0:T(128)} %bitcast.9.x_ref, bf16[8,480,128]{2,1,0:T(8,128)(2,1)} %bitcast.40, f32[160,128]{1,0:T(8,128)} %get-tuple-element.41.prob_ref, bf16[672,1024]{1,0:T(8,128)(2,1)} %copy-done, bf16[672,1024]{1,0:T(8,128)(2,1)} %collective-permute-done.refs_1_, ...), custom_call_target="tpu_custom_call" | custom-call | tf_op jit(solution)/shard_map/pallas_call | solution.py:28
  163.1 32.5 %all_to_all.25 = bf16[64,40,128]{2,1,0:T(8,128)(2,1)S(1)} all-to-all(bf16[64,40,128]{2,1,0:T(8,128)(2,1)} %bitcast.42), channel_id=1, replica_groups=mesh['z'=8,'core'=2,'y'=8,'x'=4] {'x','z','core'}, dimensions={0} | all-to-all | bytes 1310720 | tf_op jit(solution)/shard_map/all_to_all | solution.py:230
  195.6 0.6 shard_map.133
  196.2 21.9 %all_to_all.26 = bf16[16,32,512]{2,1,0:T(8,128)(2,1)S(1)} all-to-all(bf16[16,32,512]{2,1,0:T(8,128)(2,1)S(1)} %bitcast.36), channel_id=1, replica_groups=mesh['z'=8,'core'=2,'y'=8,'x'=4] {'z','core'}, dimensions={0} | all-to-all | bytes 1048576 | tf_op jit(solution)/shard_map/all_to_all | solution.py:230
  218.2 1.2 shard_map.134
  219.3 5.6 %shard_map.135 = (bf16[224,1024]{1,0:T(8,128)(2,1)}, bf16[224,1024]{1,0:T(8,128)(2,1)}, bf16[224,1024]{1,0:T(8,128)(2,1)}) custom-call(s32[1]{0:T(128)} %bitcast.9.x_ref, bf16[4,8,480,128]{3,2,1,0:T(8,128)(2,1)} %bitcast.41, bf16[160,512]{1,0:T(8,128)(2,1)} %get-tuple-element.44.refs_0_, bf16[160,512]{1,0:T(8,128)(2,1)} %copy-done.5, ...), custom_call_target="tpu_custom_call" | custom-call | tf_op jit(solution)/shard_map/pallas_call | solution.py:28
  (30 shorter events, 0.1 us)
Async XLA Ops:
  8.6 38.5 %copy-start = (bf16[672,1024]{1,0:T(8,128)(2,1)}, bf16[672,1024]{1,0:T(8,128)(2,1)S(1)}, u32[]{:S(2)}) copy-start(bf16[672,1024]{1,0:T(8,128)(2,1)S(1)} %pad_maximum_fusion.refs_0_) | copy-start | bytes 4128772
  8.6 21.0 %copy-start.8 = (s32[16]{0:T(128)S(1)}, s32[16]{0:T(128)}, u32[]{:S(2)}) copy-start(s32[16]{0:T(128)} %param.15) | copy-start | bytes 196
  8.6 21.0 %copy-start.7 = (s32[16,16]{1,0:T(8,128)S(1)}, s32[16,16]{1,0:T(8,128)}, u32[]{:S(2)}) copy-start(s32[16,16]{1,0:T(8,128)} %param.16) | copy-start | bytes 3076
  8.6 40.8 %collective-permute-start.1 = (bf16[672,1024]{1,0:T(8,128)(2,1)S(1)}, bf16[672,1024]{1,0:T(8,128)(2,1)}, u32[]{:S(2)}, u32[]{:S(2)}) collective-permute-start(bf16[672,1024]{1,0:T(8,128)(2,1)S(1)} %pad_maximum_fusion.refs_0_), channel_id=1, source_target_pairs={{0,3},{1,0},{2,1},{3,2},{4,7},{5,4},{6,5},{7,6},{8,11},{9,8},{10,9... | collective-permute-start | bytes 4128776 | tf_op jit(solution)/shard_map/ppermute | solution.py:251
  14.0 35.5 %collective-permute-start = (bf16[672,1024]{1,0:T(8,128)(2,1)S(1)}, bf16[672,1024]{1,0:T(8,128)(2,1)}, u32[]{:S(2)}, u32[]{:S(2)}) collective-permute-start(bf16[672,1024]{1,0:T(8,128)(2,1)S(1)} %pad_maximum_fusion.refs_0_), channel_id=1, source_target_pairs={{0,1},{1,2},{2,3},{3,0},{4,5},{5,6},{6,7},{7,4},{8,9},{9,10},{10,1... | collective-permute-start | bytes 4128776 | tf_op jit(solution)/shard_map/ppermute | solution.py:251
  18.3 28.6 %all-to-all-start = ((bf16[16,32,512]{2,1,0:T(8,128)(2,1)}), bf16[16,32,512]{2,1,0:T(8,128)(2,1)S(1)}, u32[]{:S(2)}, u32[]{:S(2)}) async-start(bf16[16,32,512]{2,1,0:T(8,128)(2,1)} %shard_map.128), calls=%async_computation | async-start | bytes 1048576 | tf_op jit(solution)/shard_map/all_to_all | solution.py:230
  49.5 41.8 %all-to-all-start.1 = ((bf16[64,40,128]{2,1,0:T(8,128)(2,1)}), bf16[64,40,128]{2,1,0:T(8,128)(2,1)S(1)}, u32[]{:S(2)}, u32[]{:S(2)}) async-start(bf16[64,40,128]{2,1,0:T(8,128)(2,1)} %bitcast.14), calls=%async_computation.1 | async-start | bytes 1310720 | tf_op jit(solution)/shard_map/all_to_all | solution.py:230
  63.8 23.7 %collective-permute-start.3 = (bf16[672,512]{1,0:T(8,128)(2,1)}, bf16[672,512]{1,0:T(8,128)(2,1)S(1)}, u32[]{:S(2)}, u32[]{:S(2)}) collective-permute-start(bf16[672,512]{1,0:T(8,128)(2,1)} %slice.23), channel_id=1, source_target_pairs={{0,3},{1,0},{2,1},{3,2},{4,7},{5,4},{6,5},{7,6},{8,11},{9,8},{10,9... | collective-permute-start | bytes 2064392 | tf_op jit(solution)/shard_map/ppermute | solution.py:251
  68.5 22.7 %collective-permute-start.2 = (bf16[672,512]{1,0:T(8,128)(2,1)S(1)}, bf16[672,512]{1,0:T(8,128)(2,1)S(1)}, u32[]{:S(2)}, u32[]{:S(2)}) collective-permute-start(bf16[672,512]{1,0:T(8,128)(2,1)S(1)} %slice.22), channel_id=1, source_target_pairs={{0,1},{1,2},{2,3},{3,0},{4,5},{5,6},{6,7},{7,4},{8,9},{9,10},{10,1... | collective-permute-start | bytes 2064392 | tf_op jit(solution)/shard_map/ppermute | solution.py:251
  87.5 3.8 %copy-start.1 = (bf16[672,512]{1,0:T(8,128)(2,1)}, bf16[672,512]{1,0:T(8,128)(2,1)S(1)}, u32[]{:S(2)}) copy-start(bf16[672,512]{1,0:T(8,128)(2,1)S(1)} %collective-permute-done.3.refs_4_) | copy-start | bytes 2064388
  91.2 0.9 copy-start.2
  91.2 1.2 copy-start.3
  97.5 7.0 %copy-start.11 = (bf16[160,512]{1,0:T(8,128)(2,1)S(1)}, bf16[160,512]{1,0:T(8,128)(2,1)}, u32[]{:S(2)}) copy-start(bf16[160,512]{1,0:T(8,128)(2,1)} %get-tuple-element.37) | copy-start | bytes 491524
  97.5 9.0 %copy-start.10 = (bf16[160,512]{1,0:T(8,128)(2,1)S(1)}, bf16[160,512]{1,0:T(8,128)(2,1)}, u32[]{:S(2)}) copy-start(bf16[160,512]{1,0:T(8,128)(2,1)} %get-tuple-element.38) | copy-start | bytes 491524
  97.5 12.3 %copy-start.9 = (bf16[160,512]{1,0:T(8,128)(2,1)S(1)}, bf16[160,512]{1,0:T(8,128)(2,1)}, u32[]{:S(2)}) copy-start(bf16[160,512]{1,0:T(8,128)(2,1)} %get-tuple-element.39) | copy-start | bytes 491524
  97.5 34.7 %all-to-all-start.2 = ((bf16[8,480,128]{2,1,0:T(8,128)(2,1)}), bf16[8,480,128]{2,1,0:T(8,128)(2,1)S(1)}, u32[]{:S(2)}, u32[]{:S(2)}) async-start(bf16[8,480,128]{2,1,0:T(8,128)(2,1)} %get-tuple-element.35), calls=%async_computation.2 | async-start | bytes 1966080 | tf_op jit(solution)/shard_map/all_to_all | solution.py:230
  104.5 114.9 %all-gather.4.cloned.1.call-start = ((), (), s32[]{:S(2)}) async-start(), calls=%async_computation.5 | async-start | bytes 4915200 | tf_op jit(solution)/shard_map/all_gather | solution.py:310
  104.5 7.2 %collective-permute-start.4 = (bf16[160,512]{1,0:T(8,128)(2,1)S(1)}, bf16[160,512]{1,0:T(8,128)(2,1)S(1)}, u32[]{:S(2)}, u32[]{:S(2)}) collective-permute-start(bf16[160,512]{1,0:T(8,128)(2,1)S(1)} %copy-done.11), channel_id=1, source_target_pairs={{0,3},{1,0},{2,1},{3,2},{4,7},{5,4},{6,5},{7,6},{8,11},{9,8},{10,9... | collective-permute-start | bytes 491528 | tf_op jit(solution)/shard_map/ppermute | solution.py:251
  106.5 7.6 %collective-permute-start.5 = (bf16[160,512]{1,0:T(8,128)(2,1)S(1)}, bf16[160,512]{1,0:T(8,128)(2,1)S(1)}, u32[]{:S(2)}, u32[]{:S(2)}) collective-permute-start(bf16[160,512]{1,0:T(8,128)(2,1)S(1)} %copy-done.10), channel_id=1, source_target_pairs={{0,1},{1,2},{2,3},{3,0},{4,5},{5,6},{6,7},{7,4},{8,9},{9,10},{10,1... | collective-permute-start | bytes 491528 | tf_op jit(solution)/shard_map/ppermute | solution.py:251
  109.8 7.9 %collective-permute-start.6 = (bf16[160,512]{1,0:T(8,128)(2,1)S(1)}, bf16[160,512]{1,0:T(8,128)(2,1)S(1)}, u32[]{:S(2)}, u32[]{:S(2)}) collective-permute-start(bf16[160,512]{1,0:T(8,128)(2,1)S(1)} %copy-done.9), channel_id=1, source_target_pairs={{0,2},{1,3},{2,0},{3,1},{4,6},{5,7},{6,4},{7,5},{8,10},{9,11},{10,... | collective-permute-start | bytes 491528 | tf_op jit(solution)/shard_map/ppermute | solution.py:251
  111.8 44.1 %copy-start.4 = (bf16[160,512]{1,0:T(8,128)(2,1)}, bf16[160,512]{1,0:T(8,128)(2,1)S(1)}, u32[]{:S(2)}) copy-start(bf16[160,512]{1,0:T(8,128)(2,1)S(1)} %collective-permute-done.4.refs_3_) | copy-start | bytes 491524
  114.0 41.9 %copy-start.5 = (bf16[160,512]{1,0:T(8,128)(2,1)}, bf16[160,512]{1,0:T(8,128)(2,1)S(1)}, u32[]{:S(2)}) copy-start(bf16[160,512]{1,0:T(8,128)(2,1)S(1)} %collective-permute-done.5.refs_1_) | copy-start | bytes 491524
  117.7 38.2 %copy-start.6 = (bf16[160,512]{1,0:T(8,128)(2,1)}, bf16[160,512]{1,0:T(8,128)(2,1)S(1)}, u32[]{:S(2)}) copy-start(bf16[160,512]{1,0:T(8,128)(2,1)S(1)} %collective-permute-done.6.refs_2_) | copy-start | bytes 491524
Sparse Core Ops, SparseCore 0:
  156.0 57.0 all-gather.3

commit v7 on v6

--- a/solution.py
+++ b/solution.py
@@ -82,26 +82,30 @@
     out_ref[...] = split_lanes(tmp_ref, dot(pick, rows, 1, 0))
 
 
-def panel_copies(sources, panel_ref, sems):
-    half = panel_ref.shape[2] // 2
-    targets = [panel_ref.at[d] for d in range(3)]
-    targets += [panel_ref.at[3, :, pl.ds(i * half, half)] for i in range(2)]
+def panel_copies(x_ref, sources, gate_ref, down_ref, sems):
+    half = down_ref.shape[2] // 2
+    pairs = []
+    for d, step in enumerate(STEPS):
+        pairs.append((sources[0].at[lax.rem(x_ref[0] + step, 4)], gate_ref.at[d]))
+        if d < 3:
+            pairs.append((sources[1 + d], down_ref.at[d]))
+    for i in range(2):
+        pairs.append((sources[4 + i], down_ref.at[3, :, pl.ds(i * half, half)]))
     copies = [
         pltpu.make_async_copy(source, target, sems.at[i])
-        for i, (source, target) in enumerate(zip(sources, targets))
+        for i, (source, target) in enumerate(pairs)
     ]
     for copy in copies:
         copy.start()
-    return [copies[:1], copies[1:2], copies[2:3], copies[3:]]
+    return [copies[0:2], copies[2:4], copies[4:6], copies[6:9]]
 
 
 def hidden_kernel(x_ref, tiles_ref, mark_ref, *refs):
-    sources, row_refs = refs[:5], refs[5:9]
-    out_ref, prob_ref, acc_ref, tmp_ref, panel_ref, sems = refs[9:]
-    copies = panel_copies(sources, panel_ref, sems)
-    width = panel_ref.shape[1] // 3
-    parts = acc_ref.shape[0]
-    count = acc_ref.shape[1]
+    sources, row_refs = refs[:6], refs[6:10]
+    out_ref, prob_ref, acc_ref, tmp_ref, gate_ref, down_ref, sems = refs[10:]
+    copies = panel_copies(x_ref, sources, gate_ref, down_ref, sems)
+    width = down_ref.shape[1]
+    parts, count = acc_ref.shape[:2]
     for d, step in enumerate(STEPS):
         rows = join_lanes(tmp_ref, tiles_ref[lax.rem(x_ref[0] + step, 4)])
         prob = jnp.sum(rows[:, 0:256] * mark_ref[...], axis=1, keepdims=True)
@@ -113,18 +117,22 @@
             prob_ref[...] = jnp.broadcast_to(prob, prob_ref.shape)
         for copy in copies[d]:
             copy.wait()
-        for part in range(parts):
-            left = grad if part == 2 else x
-            term = dot(left[:, 0:width], panel_ref[d, part * width : (part + 1) * width], 1, 0)
+        terms = [
+            dot(x[:, 0:width], gate_ref[d, 0:width], 1, 0),
+            dot(x[:, 0:width], gate_ref[d, width : 2 * width], 1, 0),
+            dot(grad[:, 0:width], down_ref[d], 1, 0),
+        ]
+        for part, term in enumerate(terms):
             if d == 0:
                 acc_ref[part] = term
+            elif d < 3:
+                acc_ref[part] += term
             else:
-                acc_ref[part] += term
-    for part in range(parts):
-        for piece in range(out_ref.shape[0]):
-            out_ref[piece, part * count : (part + 1) * count] = acc_ref[
-                part, :, piece * 128 : (piece + 1) * 128
-            ].astype(BF16)
+                total = (acc_ref[part] + term).astype(BF16)
+                for piece in range(out_ref.shape[0]):
+                    out_ref[piece, part * count : (part + 1) * count] = total[
+                        :, piece * 128 : (piece + 1) * 128
+                    ]
 
 
 def point_kernel(parts_ref, out_ref):
@@ -146,17 +154,17 @@
 
 
 def result_kernel(x_ref, act_ref, prob_ref, *refs):
-    sources, (out_ref, res_ref, tmp_ref, panel_ref, sems) = refs[:5], refs[5:]
-    copies = panel_copies(sources, panel_ref, sems)
-    width = panel_ref.shape[1] // 3
+    sources, (out_ref, res_ref, tmp_ref, gate_ref, down_ref, sems) = refs[:6], refs[6:]
+    copies = panel_copies(x_ref, sources, gate_ref, down_ref, sems)
+    width = down_ref.shape[1]
     hidden, gate_grad, up_grad = hidden_parts(act_ref)
     res_ref[...] = jnp.zeros_like(res_ref)
     for d, step in enumerate(STEPS):
         for copy in copies[d]:
             copy.wait()
-        outcome = prob_ref[:, 0:1] * dot(hidden, panel_ref[d, 2 * width :], 1, 1)
-        dx = dot(gate_grad, panel_ref[d, 0:width], 1, 1)
-        dx += dot(up_grad, panel_ref[d, width : 2 * width], 1, 1)
+        outcome = prob_ref[:, 0:1] * dot(hidden, down_ref[d], 1, 1)
+        dx = dot(gate_grad, gate_ref[d, 0:width], 1, 1)
+        dx += dot(up_grad, gate_ref[d, width : 2 * width], 1, 1)
         res_ref[:, 0:width] = outcome
         res_ref[:, DY_LANE : DY_LANE + width] = dx
         out_ref[lax.rem(x_ref[0] + step, 4)] = split_lanes(tmp_ref, res_ref[...])
@@ -250,8 +258,10 @@
     def shift(array, d):
         return lax.ppermute(array, "x", shifts[d])
 
-    panel = jnp.concatenate([w_gate[0], w_up[0], w_down[0].T], axis=0)
-    right, left = shift(panel, 1), shift(panel, 3)
+    gates = jnp.concatenate([w_gate[0], w_up[0]], axis=0)
+    gates = lax.all_gather(gates, "x", axis=0, tiled=False)
+    down = w_down[0].T
+    right, left = shift(down, 1), shift(down, 3)
 
     packed = call(
         pack_kernel,
@@ -264,7 +274,7 @@
     mine = (expert_slot == lax.axis_index(GROUP)).astype(F32)
     mark = lax.pad(mine, jnp.zeros((), F32), ((P_LANE, 16, 0),))[None]
     spread = exchange(packed, GROUP).reshape(groups * BLK, LANES)
-    spread, info = lax.optimization_barrier((spread, info))
+    spread, info, right, left = lax.optimization_barrier((spread, info, right, left))
     sent, pick = call(
         select_kernel,
         (
@@ -274,9 +284,8 @@
         (spread, info),
         scratch_shapes=[pltpu.VMEM((4 * total, 128), F32)],
     )
-    sent, right, left = lax.optimization_barrier((sent, right, left))
     half = hid // 2
-    panels = [panel, right, left, shift(right[:, 0:half], 1), shift(left[:, half:], 3)]
+    panels = [gates, down, right, left, shift(right[:, 0:half], 1), shift(left[:, half:], 3)]
     pieces = (share_x * groups, 4 * picked // share_x, 128)
     tiles = exchange(sent.reshape(pieces), OWNERS).reshape(share_x, 4 * count, 128)
 
@@ -290,8 +299,12 @@
     act_shape = (share_y, 3 * count, hid // share_y)
     scalar_spec = pl.BlockSpec(memory_space=pltpu.SMEM)
     vmem_spec = pl.BlockSpec(memory_space=pltpu.VMEM)
-    panel_specs = [pl.BlockSpec(memory_space=pl.ANY)] * 5
-    panel_scratch = [pltpu.VMEM((4, 3 * width, hid), BF16), pltpu.SemaphoreType.DMA((5,))]
+    panel_specs = [pl.BlockSpec(memory_space=pl.ANY)] * 6
+    panel_scratch = [
+        pltpu.VMEM((4, 2 * width, hid), BF16),
+        pltpu.VMEM((4, width, hid), BF16),
+        pltpu.SemaphoreType.DMA((9,)),
+    ]
     *rows, parts, prob = call(
         hidden_kernel,
         (jax.ShapeDtypeStruct((count, LANES), BF16),) * 4

time: 233 us -> 220 us (0.944)
  waiting for transfers between devices: 56.9 us -> 46.8 us
  local copies, waits for them, and re-layouts: 4.97 us -> 1.58 us
  blocking collectives: 77.9 us -> 80.4 us
  starting transfers between devices: 50.5 us -> 48.1 us
    ppermute x7, waiting for transfers between devices: 26 us -> 19.6 us  [shift(): return lax.ppermute(array, 'x', shifts[d])]
    all_to_all x3, starting transfers between devices: 29.4 us -> 24.2 us  [exchange(): return lax.all_to_all(array, axis, split_axis=0, concat_axis=0, tiled=True)]
    all_to_all x3, waiting for transfers between devices: 30.9 us -> 27.2 us  [exchange(): return lax.all_to_all(array, axis, split_axis=0, concat_axis=0, tiled=True)]
    ppermute x7, starting transfers between devices: 21.1 us -> 23.8 us  [shift(): return lax.ppermute(array, 'x', shifts[d])]
    all_to_all x2, blocking collectives: 54.4 us -> 57 us  [exchange(): return lax.all_to_all(array, axis, split_axis=0, concat_axis=0, tiled=True)]
  transfers between devices with their start and end apart: 11 -> 12, of which waited for: 6 -> 5; matrix products, arithmetic and copies ran while one was open for 2% -> 1% of each run, Pallas kernels for 6% -> 6%
where the time goes in v7:
time: 220 us; the launch traced here: 219 us
  blocking collectives  80.4 us (37%)
  starting transfers between devices  48.1 us (22%)
  waiting for transfers between devices  46.8 us (21%)
  Pallas kernels  24.6 us (11%)
  between operations  14.4 us (7%)
  other arithmetic  3.37 us (2%)
    all_to_all x2, blocking collectives, exchange(): return lax.all_to_all(array, axis, split_axis=0, concat_axis=0, tiled=True)  57 us
    all_to_all x3, waiting for transfers between devices, exchange(): return lax.all_to_all(array, axis, split_axis=0, concat_axis=0, tiled=True)  27.2 us
    pallas_call x8, Pallas kernels, call(): pl.pallas_call(kernel, out_shape=out_shape, compiler_params=pltpu.Compile...  24.6 us
    all_to_all x3, starting transfers between devices, exchange(): return lax.all_to_all(array, axis, split_axis=0, concat_axis=0, tiled=True)  24.2 us
    ppermute x7, starting transfers between devices, shift(): return lax.ppermute(array, 'x', shifts[d])  23.8 us
    all_gather x1, blocking collectives, body(): act = lax.all_gather(act, 'y', axis=0, tiled=False)  23.5 us
    ppermute x7, waiting for transfers between devices, shift(): return lax.ppermute(array, 'x', shifts[d])  19.6 us
  transfers between devices with their start and end apart: 12, of which 5 were waited for; matrix products, arithmetic and copies ran while one was open for 1% of the time, Pallas kernels for 6%

profile of v7, /device:TPU:1, one launch (start us, length us, event | category | flops | bytes accessed | tf_op | source)
XLA Modules:
  0.0 219.3 jit_solution(3788372314358310617)
XLA Ops:
  7.2 0.0 copy-start.3
  7.2 0.0 all-gather.6.cloned.1.call-start
  7.2 2.2 %pad_maximum_fusion = bf16[448,1024]{1,0:T(8,128)(2,1)} fusion(bf16[224,1024]{1,0:T(8,128)(2,1)} %bitcast.51, bf16[224,1024]{1,0:T(8,128)(2,1)} %bitcast.52), kind=kLoop, calls=%fused_computation | loop fusion | flops 1835008 | bytes 1835008 | tf_op jit(solution)/shard_map/concatenate | solution.py:261
  9.4 0.0 all-gather.6.cloned.1.call-update
  9.5 5.2 %collective-permute-start.1 = (bf16[224,1024]{1,0:T(8,128)(2,1)S(1)}, bf16[224,1024]{1,0:T(8,128)(2,1)S(1)}, u32[]{:S(2)}, u32[]{:S(2)}) collective-permute-start(bf16[224,1024]{1,0:T(8,128)(2,1)S(1)} %bitcast.49), channel_id=1, source_target_pairs={{0,3},{1,0},{2,1},{3,2},{4,7},{5,4},{6,5},{7,6},{8,11},{9,8},{10,9... | collective-permute-start | bytes 1376264 | tf_op jit(solution)/shard_map/ppermute | solution.py:259
  14.7 1.9 collective-permute-start
  16.6 2.4 %shard_map.128 = bf16[16,32,512]{2,1,0:T(8,128)(2,1)} custom-call(bf16[224,512]{1,0:T(8,128)(2,1)} %bitcast.53, bf16[224,512]{1,0:T(8,128)(2,1)} %bitcast.54, bf16[16,512]{1,0:T(8,128)(2,1)} %bitcast.55, s32[10,1,16]{2,1,0:T(1,128)} %bitcast.56), custom_call_target="tpu_custom_call" | custom-call | tf_op jit(solution)/shard_map/pallas_call | solution.py:28
  19.0 11.3 %all-to-all-start = ((bf16[16,32,512]{2,1,0:T(8,128)(2,1)}), bf16[16,32,512]{2,1,0:T(8,128)(2,1)S(1)}, u32[]{:S(2)}, u32[]{:S(2)}) async-start(bf16[16,32,512]{2,1,0:T(8,128)(2,1)} %shard_map.128), calls=%async_computation | async-start | bytes 1048576 | tf_op jit(solution)/shard_map/all_to_all | solution.py:238
  30.3 0.1 fusion.5
  30.4 0.1 multiply_reduce_fusion.1
  30.5 0.1 multiply_reduce_fusion
  30.7 0.1 select_reduce_fusion
  30.8 0.1 fusion
  30.8 0.1 reshape.243
  31.0 0.1 reshape.250
  31.1 0.1 reshape.247
  31.3 0.0 copy-start
  31.3 0.0 copy-start.1
  31.3 16.3 %all-to-all-done = bf16[16,32,512]{2,1,0:T(8,128)(2,1)S(1)} async-done(((bf16[16,32,512]{2,1,0:T(8,128)(2,1)}), bf16[16,32,512]{2,1,0:T(8,128)(2,1)S(1)}, u32[]{:S(2)}, u32[]{:S(2)}) %all-to-all-start) | async-done | bytes 524320 | tf_op jit(solution)/shard_map/all_to_all | solution.py:238
  47.6 0.2 copy.18.info_ref
  47.8 2.4 %shard_map.129 = (bf16[2560,128]{1,0:T(8,128)(2,1)}, bf16[640,512]{1,0:T(8,128)(2,1)S(1)}) custom-call(bf16[512,512]{1,0:T(8,128)(2,1)S(1)} %bitcast.38, s32[640,3]{1,0:T(8,128)S(1)} %copy.18.info_ref), custom_call_target="tpu_custom_call" | custom-call | tf_op jit(solution)/shard_map/pallas_call | solution.py:28
  50.2 6.1 %all-to-all-start.1 = ((bf16[64,40,128]{2,1,0:T(8,128)(2,1)}), bf16[64,40,128]{2,1,0:T(8,128)(2,1)S(1)}, u32[]{:S(2)}, u32[]{:S(2)}) async-start(bf16[64,40,128]{2,1,0:T(8,128)(2,1)} %bitcast.13), calls=%async_computation.1 | async-start | bytes 1310720 | tf_op jit(solution)/shard_map/all_to_all | solution.py:238
  56.3 4.7 %collective-permute-start.3 = (bf16[224,512]{1,0:T(8,128)(2,1)S(1)}, bf16[224,512]{1,0:T(8,128)(2,1)S(1)}, u32[]{:S(2)}, u32[]{:S(2)}) collective-permute-start(bf16[224,512]{1,0:T(8,128)(2,1)S(1)} %slice.23), channel_id=1, source_target_pairs={{0,3},{1,0},{2,1},{3,2},{4,7},{5,4},{6,5},{7,6},{8,11},{9,8},{10,9... | collective-permute-start | bytes 688136 | tf_op jit(solution)/shard_map/ppermute | solution.py:259
  61.0 1.9 collective-permute-start.2
  63.0 0.7 pad_convert_fusion
  63.7 12.2 %collective-permute-done.3.refs_5_ = bf16[224,512]{1,0:T(8,128)(2,1)S(1)} collective-permute-done((bf16[224,512]{1,0:T(8,128)(2,1)S(1)}, bf16[224,512]{1,0:T(8,128)(2,1)S(1)}, u32[]{:S(2)}, u32[]{:S(2)}) %collective-permute-start.3) | collective-permute-done | bytes 229408 | tf_op jit(solution)/shard_map/ppermute | solution.py:259
  75.8 0.7 collective-permute-done.2.refs_4_
  76.5 0.0 all-gather.6.cloned.1.call-done
  76.6 0.6 copy-done.5
  77.2 0.3 copy-done.2
  77.5 5.1 %shard_map.130 = (bf16[160,512]{1,0:T(8,128)(2,1)}, bf16[160,512]{1,0:T(8,128)(2,1)}, bf16[160,512]{1,0:T(8,128)(2,1)}, bf16[160,512]{1,0:T(8,128)(2,1)}, bf16[8...) custom-call(s32[1]{0:T(128)} %bitcast.12.x_ref, bf16[4,640,128]{2,1,0:T(8,128)(2,1)} %bitcast.46, f32[1,256]{1,0:T(1,128)} %bitcast.57, ...), custom_call_target="tpu_custom_call" | custom-call | tf_op jit(solution)/shard_map/pallas_call | solution.py:28
  82.6 0.0 copy-start.13
  82.6 6.8 %all-to-all-start.2 = ((bf16[8,480,128]{2,1,0:T(8,128)(2,1)}), bf16[8,480,128]{2,1,0:T(8,128)(2,1)S(1)}, u32[]{:S(2)}, u32[]{:S(2)}) async-start(bf16[8,480,128]{2,1,0:T(8,128)(2,1)} %get-tuple-element.33), calls=%async_computation.2 | async-start | bytes 1966080 | tf_op jit(solution)/shard_map/all_to_all | solution.py:238
  89.4 0.0 all-gather.8.cloned.1.call-start
  89.4 4.6 %collective-permute-start.4 = (bf16[160,512]{1,0:T(8,128)(2,1)S(1)}, bf16[160,512]{1,0:T(8,128)(2,1)S(1)}, u32[]{:S(2)}, u32[]{:S(2)}) collective-permute-start(bf16[160,512]{1,0:T(8,128)(2,1)S(1)} %copy-done.13), channel_id=1, source_target_pairs={{0,3},{1,0},{2,1},{3,2},{4,7},{5,4},{6,5},{7,6},{8,11},{9,8},{10,9... | collective-permute-start | bytes 491528 | tf_op jit(solution)/shard_map/ppermute | solution.py:259
  94.0 1.9 collective-permute-start.5
  96.0 3.5 %collective-permute-start.6 = (bf16[160,512]{1,0:T(8,128)(2,1)S(1)}, bf16[160,512]{1,0:T(8,128)(2,1)S(1)}, u32[]{:S(2)}, u32[]{:S(2)}) collective-permute-start(bf16[160,512]{1,0:T(8,128)(2,1)S(1)} %copy-done.11), channel_id=1, source_target_pairs={{0,2},{1,3},{2,0},{3,1},{4,6},{5,7},{6,4},{7,5},{8,10},{9,11},{10,... | collective-permute-start | bytes 491528 | tf_op jit(solution)/shard_map/ppermute | solution.py:259
  99.5 6.7 %collective-permute-done.5.refs_1_ = bf16[160,512]{1,0:T(8,128)(2,1)S(1)} collective-permute-done((bf16[160,512]{1,0:T(8,128)(2,1)S(1)}, bf16[160,512]{1,0:T(8,128)(2,1)S(1)}, u32[]{:S(2)}, u32[]{:S(2)}) %collective-permute-start.5) | collective-permute-done | bytes 163872 | tf_op jit(solution)/shard_map/ppermute | solution.py:259
  106.3 10.9 %all-to-all-done.2.parts_ref = bf16[8,480,128]{2,1,0:T(8,128)(2,1)S(1)} async-done(((bf16[8,480,128]{2,1,0:T(8,128)(2,1)}), bf16[8,480,128]{2,1,0:T(8,128)(2,1)S(1)}, u32[]{:S(2)}, u32[]{:S(2)}) %all-to-all-start.2) | async-done | bytes 983072 | tf_op jit(solution)/shard_map/all_to_all | solution.py:238
  117.2 0.2 shard_map.131
  117.4 23.5 %all-gather.1 = bf16[3840,128]{1,0:T(8,128)(2,1)} all-gather(bf16[480,128]{1,0:T(8,128)(2,1)S(1)} %shard_map.131), channel_id=3, replica_groups=mesh['z'=8,'core'=2,'y'=8,'x'=4] {'y'}, dimensions={0}, use_global_device_ids=true | all-gather | bytes 1105920 | tf_op jit(solution)/shard_map/all_gather | solution.py:322
  140.8 0.0 all-gather.8.cloned.1.call-update
  140.9 7.2 %shard_map.132 = bf16[4,640,128]{2,1,0:T(8,128)(2,1)} custom-call(s32[1]{0:T(128)} %bitcast.12.x_ref, bf16[8,480,128]{2,1,0:T(8,128)(2,1)} %bitcast.43, f32[160,128]{1,0:T(8,128)} %get-tuple-element.39.prob_ref, bf16[4,448,1024]{2,1,0:T(8,128)(2,1)} %bitcast.41, bf16[224,1024]{1,0:T(8,128)(2,1)} %bitcast.48, bf16[224,1024]{1,0:T(8,128)(2,1)} %copy-done.1, ...), custom_call_target="tpu_custom_call" | custom-call | tf_op jit(solution)/shard_map/pallas_call | solution.py:28
  148.1 35.0 %all_to_all.25 = bf16[64,40,128]{2,1,0:T(8,128)(2,1)S(1)} all-to-all(bf16[64,40,128]{2,1,0:T(8,128)(2,1)} %bitcast.45), channel_id=1, replica_groups=mesh['z'=8,'core'=2,'y'=8,'x'=4] {'x','z','core'}, dimensions={0} | all-to-all | bytes 1310720 | tf_op jit(solution)/shard_map/all_to_all | solution.py:238
  183.1 0.6 shard_map.133
  183.8 21.9 %all_to_all.26 = bf16[16,32,512]{2,1,0:T(8,128)(2,1)S(1)} all-to-all(bf16[16,32,512]{2,1,0:T(8,128)(2,1)S(1)} %bitcast.37), channel_id=1, replica_groups=mesh['z'=8,'core'=2,'y'=8,'x'=4] {'z','core'}, dimensions={0} | all-to-all | bytes 1048576 | tf_op jit(solution)/shard_map/all_to_all | solution.py:238
  205.7 1.2 shard_map.134
  206.9 5.6 %shard_map.135 = (bf16[224,1024]{1,0:T(8,128)(2,1)}, bf16[224,1024]{1,0:T(8,128)(2,1)}, bf16[224,1024]{1,0:T(8,128)(2,1)}) custom-call(s32[1]{0:T(128)} %bitcast.12.x_ref, bf16[4,8,480,128]{3,2,1,0:T(8,128)(2,1)} %bitcast.44, bf16[160,512]{1,0:T(8,128)(2,1)} %get-tuple-element.42.refs_0_, bf16[160,512]{1,0:T(8,128)(2,1)} %copy-done.7, ...), custom_call_target="tpu_custom_call" | custom-call | tf_op jit(solution)/shard_map/pallas_call | solution.py:28
  (37 shorter events, 0.2 us)
Async XLA Ops:
  7.2 2.3 %copy-start.3 = (bf16[1,1024,224]{1,2,0:T(8,128)(2,1)S(1)}, bf16[1,1024,224]{1,2,0:T(8,128)(2,1)}, u32[]{:S(2)}) copy-start(bf16[1,1024,224]{1,2,0:T(8,128)(2,1)} %param.14) | copy-start | bytes 1376260
  7.2 69.3 %all-gather.6.cloned.1.call-start = ((), (), s32[]{:S(2)}) async-start(), calls=%async_computation.5 | async-start | bytes 4587520 | tf_op jit(solution)/shard_map/all_gather | solution.py:262
  9.4 20.9 %copy-start.10 = (s32[16]{0:T(128)S(1)}, s32[16]{0:T(128)}, u32[]{:S(2)}) copy-start(s32[16]{0:T(128)} %param.15) | copy-start | bytes 196
  9.4 20.9 %copy-start.9 = (s32[16,16]{1,0:T(8,128)S(1)}, s32[16,16]{1,0:T(8,128)}, u32[]{:S(2)}) copy-start(s32[16,16]{1,0:T(8,128)} %param.16) | copy-start | bytes 3076
  9.5 21.8 %collective-permute-start.1 = (bf16[224,1024]{1,0:T(8,128)(2,1)S(1)}, bf16[224,1024]{1,0:T(8,128)(2,1)S(1)}, u32[]{:S(2)}, u32[]{:S(2)}) collective-permute-start(bf16[224,1024]{1,0:T(8,128)(2,1)S(1)} %bitcast.49), channel_id=1, source_target_pairs={{0,3},{1,0},{2,1},{3,2},{4,7},{5,4},{6,5},{7,6},{8,11},{9,8},{10,9... | collective-permute-start | bytes 1376264 | tf_op jit(solution)/shard_map/ppermute | solution.py:259
  14.7 16.6 %collective-permute-start = (bf16[224,1024]{1,0:T(8,128)(2,1)S(1)}, bf16[224,1024]{1,0:T(8,128)(2,1)S(1)}, u32[]{:S(2)}, u32[]{:S(2)}) collective-permute-start(bf16[224,1024]{1,0:T(8,128)(2,1)S(1)} %bitcast.50), channel_id=1, source_target_pairs={{0,1},{1,2},{2,3},{3,0},{4,5},{5,6},{6,7},{7,4},{8,9},{9,10},{10,1... | collective-permute-start | bytes 1376264 | tf_op jit(solution)/shard_map/ppermute | solution.py:259
  19.0 28.6 %all-to-all-start = ((bf16[16,32,512]{2,1,0:T(8,128)(2,1)}), bf16[16,32,512]{2,1,0:T(8,128)(2,1)S(1)}, u32[]{:S(2)}, u32[]{:S(2)}) async-start(bf16[16,32,512]{2,1,0:T(8,128)(2,1)} %shard_map.128), calls=%async_computation | async-start | bytes 1048576 | tf_op jit(solution)/shard_map/all_to_all | solution.py:238
  31.3 45.2 %copy-start = (bf16[224,1024]{1,0:T(8,128)(2,1)}, bf16[224,1024]{1,0:T(8,128)(2,1)S(1)}, u32[]{:S(2)}) copy-start(bf16[224,1024]{1,0:T(8,128)(2,1)S(1)} %collective-permute-done.1.refs_3_) | copy-start | bytes 1376260
  31.3 45.2 %copy-start.1 = (bf16[224,1024]{1,0:T(8,128)(2,1)}, bf16[224,1024]{1,0:T(8,128)(2,1)S(1)}, u32[]{:S(2)}) copy-start(bf16[224,1024]{1,0:T(8,128)(2,1)S(1)} %collective-permute-done.refs_2_) | copy-start | bytes 1376260
  50.2 26.4 %all-to-all-start.1 = ((bf16[64,40,128]{2,1,0:T(8,128)(2,1)}), bf16[64,40,128]{2,1,0:T(8,128)(2,1)S(1)}, u32[]{:S(2)}, u32[]{:S(2)}) async-start(bf16[64,40,128]{2,1,0:T(8,128)(2,1)} %bitcast.13), calls=%async_computation.1 | async-start | bytes 1310720 | tf_op jit(solution)/shard_map/all_to_all | solution.py:238
  56.3 19.5 %collective-permute-start.3 = (bf16[224,512]{1,0:T(8,128)(2,1)S(1)}, bf16[224,512]{1,0:T(8,128)(2,1)S(1)}, u32[]{:S(2)}, u32[]{:S(2)}) collective-permute-start(bf16[224,512]{1,0:T(8,128)(2,1)S(1)} %slice.23), channel_id=1, source_target_pairs={{0,3},{1,0},{2,1},{3,2},{4,7},{5,4},{6,5},{7,6},{8,11},{9,8},{10,9... | collective-permute-start | bytes 688136 | tf_op jit(solution)/shard_map/ppermute | solution.py:259
  61.0 15.5 %collective-permute-start.2 = (bf16[224,512]{1,0:T(8,128)(2,1)S(1)}, bf16[224,512]{1,0:T(8,128)(2,1)S(1)}, u32[]{:S(2)}, u32[]{:S(2)}) collective-permute-start(bf16[224,512]{1,0:T(8,128)(2,1)S(1)} %slice.22), channel_id=1, source_target_pairs={{0,1},{1,2},{2,3},{3,0},{4,5},{5,6},{6,7},{7,4},{8,9},{9,10},{10,1... | collective-permute-start | bytes 688136 | tf_op jit(solution)/shard_map/ppermute | solution.py:259
  75.8 0.7 copy-start.4
  76.5 0.7 copy-start.5
  76.5 0.9 copy-start.2
  82.6 6.9 %copy-start.13 = (bf16[160,512]{1,0:T(8,128)(2,1)S(1)}, bf16[160,512]{1,0:T(8,128)(2,1)}, u32[]{:S(2)}) copy-start(bf16[160,512]{1,0:T(8,128)(2,1)} %get-tuple-element.35) | copy-start | bytes 491524
  82.6 11.4 %copy-start.12 = (bf16[160,512]{1,0:T(8,128)(2,1)S(1)}, bf16[160,512]{1,0:T(8,128)(2,1)}, u32[]{:S(2)}) copy-start(bf16[160,512]{1,0:T(8,128)(2,1)} %get-tuple-element.36) | copy-start | bytes 491524
  82.6 13.4 %copy-start.11 = (bf16[160,512]{1,0:T(8,128)(2,1)S(1)}, bf16[160,512]{1,0:T(8,128)(2,1)}, u32[]{:S(2)}) copy-start(bf16[160,512]{1,0:T(8,128)(2,1)} %get-tuple-element.37) | copy-start | bytes 491524
  82.6 34.6 %all-to-all-start.2 = ((bf16[8,480,128]{2,1,0:T(8,128)(2,1)}), bf16[8,480,128]{2,1,0:T(8,128)(2,1)S(1)}, u32[]{:S(2)}, u32[]{:S(2)}) async-start(bf16[8,480,128]{2,1,0:T(8,128)(2,1)} %get-tuple-element.33), calls=%async_computation.2 | async-start | bytes 1966080 | tf_op jit(solution)/shard_map/all_to_all | solution.py:238
  89.4 117.5 %all-gather.8.cloned.1.call-start = ((), (), s32[]{:S(2)}) async-start(), calls=%async_computation.6 | async-start | bytes 4915200 | tf_op jit(solution)/shard_map/all_gather | solution.py:323
  89.4 10.1 %collective-permute-start.4 = (bf16[160,512]{1,0:T(8,128)(2,1)S(1)}, bf16[160,512]{1,0:T(8,128)(2,1)S(1)}, u32[]{:S(2)}, u32[]{:S(2)}) collective-permute-start(bf16[160,512]{1,0:T(8,128)(2,1)S(1)} %copy-done.13), channel_id=1, source_target_pairs={{0,3},{1,0},{2,1},{3,2},{4,7},{5,4},{6,5},{7,6},{8,11},{9,8},{10,9... | collective-permute-start | bytes 491528 | tf_op jit(solution)/shard_map/ppermute | solution.py:259
  94.0 12.2 %collective-permute-start.5 = (bf16[160,512]{1,0:T(8,128)(2,1)S(1)}, bf16[160,512]{1,0:T(8,128)(2,1)S(1)}, u32[]{:S(2)}, u32[]{:S(2)}) collective-permute-start(bf16[160,512]{1,0:T(8,128)(2,1)S(1)} %copy-done.12), channel_id=1, source_target_pairs={{0,1},{1,2},{2,3},{3,0},{4,5},{5,6},{6,7},{7,4},{8,9},{9,10},{10,1... | collective-permute-start | bytes 491528 | tf_op jit(solution)/shard_map/ppermute | solution.py:259
  96.0 10.3 %collective-permute-start.6 = (bf16[160,512]{1,0:T(8,128)(2,1)S(1)}, bf16[160,512]{1,0:T(8,128)(2,1)S(1)}, u32[]{:S(2)}, u32[]{:S(2)}) collective-permute-start(bf16[160,512]{1,0:T(8,128)(2,1)S(1)} %copy-done.11), channel_id=1, source_target_pairs={{0,2},{1,3},{2,0},{3,1},{4,6},{5,7},{6,4},{7,5},{8,10},{9,11},{10,... | collective-permute-start | bytes 491528 | tf_op jit(solution)/shard_map/ppermute | solution.py:259
  99.5 48.5 %copy-start.6 = (bf16[160,512]{1,0:T(8,128)(2,1)}, bf16[160,512]{1,0:T(8,128)(2,1)S(1)}, u32[]{:S(2)}) copy-start(bf16[160,512]{1,0:T(8,128)(2,1)S(1)} %collective-permute-done.4.refs_3_) | copy-start | bytes 491524
  106.2 41.8 %copy-start.7 = (bf16[160,512]{1,0:T(8,128)(2,1)}, bf16[160,512]{1,0:T(8,128)(2,1)S(1)}, u32[]{:S(2)}) copy-start(bf16[160,512]{1,0:T(8,128)(2,1)S(1)} %collective-permute-done.5.refs_1_) | copy-start | bytes 491524
  106.3 41.8 %copy-start.8 = (bf16[160,512]{1,0:T(8,128)(2,1)}, bf16[160,512]{1,0:T(8,128)(2,1)S(1)}, u32[]{:S(2)}) copy-start(bf16[160,512]{1,0:T(8,128)(2,1)S(1)} %collective-permute-done.6.refs_2_) | copy-start | bytes 491524
Sparse Core Ops, SparseCore 0:
  10.1 64.8 all-gather.5
  141.0 59.5 all-gather.7

commit v8 on v7

--- a/solution.py
+++ b/solution.py
@@ -40,8 +40,26 @@
     return (t == source).astype(BF16)
 
 
-def pack_kernel(tok_ref, dy_ref, prob_ref, list_ref, out_ref, all_ref):
+def pack_kernel(
+    tok_ref, dy_ref, prob_ref, list_ref, gate_ref, up_ref, down_ref, out_ref, a_ref, b_ref, *refs
+):
+    all_ref, sems = refs
     width = tok_ref.shape[0]
+    hid = gate_ref.shape[1]
+    half = hid // 2
+    copies = [
+        pltpu.make_async_copy(source, target, sems.at[i])
+        for i, (source, target) in enumerate(
+            (
+                (gate_ref, a_ref.at[:, pl.ds(0, hid)]),
+                (up_ref.at[:, pl.ds(0, half)], a_ref.at[:, pl.ds(hid, half)]),
+                (down_ref, b_ref.at[:, pl.ds(0, hid)]),
+                (up_ref.at[:, pl.ds(half, half)], b_ref.at[:, pl.ds(hid, half)]),
+            )
+        )
+    ]
+    for copy in copies:
+        copy.start()
     all_ref[...] = jnp.zeros_like(all_ref)
     all_ref[0:width] = tok_ref[...]
     all_ref[P_LANE : P_LANE + 16] = prob_ref[...]
@@ -53,6 +71,8 @@
     lists = dot(lists, (lane == entry + LIST_LANE).astype(BF16), 0, 0)
     lists = jnp.concatenate([lists, jnp.zeros((BLK - lists.shape[0], LANES), F32)], axis=0)
     out_ref[...] = (packed.reshape(out_ref.shape) + lists[None]).astype(BF16)
+    for copy in copies:
+        copy.wait()
 
 
 def split_lanes(tmp_ref, rows):
@@ -82,15 +102,15 @@
     out_ref[...] = split_lanes(tmp_ref, dot(pick, rows, 1, 0))
 
 
-def panel_copies(x_ref, sources, gate_ref, down_ref, sems):
-    half = down_ref.shape[2] // 2
+def panel_copies(x_ref, sources, a_ref, b_ref, sems):
+    half = b_ref.shape[2] // 2
     pairs = []
     for d, step in enumerate(STEPS):
-        pairs.append((sources[0].at[lax.rem(x_ref[0] + step, 4)], gate_ref.at[d]))
+        pairs.append((sources[0].at[lax.rem(x_ref[0] + step, 4)], a_ref.at[d]))
         if d < 3:
-            pairs.append((sources[1 + d], down_ref.at[d]))
+            pairs.append((sources[1 + d], b_ref.at[d]))
     for i in range(2):
-        pairs.append((sources[4 + i], down_ref.at[3, :, pl.ds(i * half, half)]))
+        pairs.append((sources[4 + i], b_ref.at[3, :, pl.ds(i * half, half)]))
     copies = [
         pltpu.make_async_copy(source, target, sems.at[i])
         for i, (source, target) in enumerate(pairs)
@@ -102,10 +122,11 @@
 
 def hidden_kernel(x_ref, tiles_ref, mark_ref, *refs):
     sources, row_refs = refs[:6], refs[6:10]
-    out_ref, prob_ref, acc_ref, tmp_ref, gate_ref, down_ref, sems = refs[10:]
-    copies = panel_copies(x_ref, sources, gate_ref, down_ref, sems)
-    width = down_ref.shape[1]
-    parts, count = acc_ref.shape[:2]
+    out_ref, prob_ref, acc_ref, tmp_ref, a_ref, b_ref, sems = refs[10:]
+    copies = panel_copies(x_ref, sources, a_ref, b_ref, sems)
+    width = a_ref.shape[1]
+    parts, count, hid = acc_ref.shape
+    half = hid // 2
     for d, step in enumerate(STEPS):
         rows = join_lanes(tmp_ref, tiles_ref[lax.rem(x_ref[0] + step, 4)])
         prob = jnp.sum(rows[:, 0:256] * mark_ref[...], axis=1, keepdims=True)
@@ -117,22 +138,23 @@
             prob_ref[...] = jnp.broadcast_to(prob, prob_ref.shape)
         for copy in copies[d]:
             copy.wait()
+        x, grad = x[:, 0:width], grad[:, 0:width]
         terms = [
-            dot(x[:, 0:width], gate_ref[d, 0:width], 1, 0),
-            dot(x[:, 0:width], gate_ref[d, width : 2 * width], 1, 0),
-            dot(grad[:, 0:width], down_ref[d], 1, 0),
+            (0, 0, hid, dot(x, a_ref[d, :, 0:hid], 1, 0)),
+            (1, 0, half, dot(x, a_ref[d, :, hid:], 1, 0)),
+            (1, half, hid, dot(x, b_ref[d, :, hid:], 1, 0)),
+            (2, 0, hid, dot(grad, b_ref[d, :, 0:hid], 1, 0)),
         ]
-        for part, term in enumerate(terms):
+        for part, low, high, term in terms:
             if d == 0:
-                acc_ref[part] = term
+                acc_ref[part, :, low:high] = term
             elif d < 3:
-                acc_ref[part] += term
+                acc_ref[part, :, low:high] += term
             else:
-                total = (acc_ref[part] + term).astype(BF16)
-                for piece in range(out_ref.shape[0]):
-                    out_ref[piece, part * count : (part + 1) * count] = total[
-                        :, piece * 128 : (piece + 1) * 128
-                    ]
+                total = (acc_ref[part, :, low:high] + term).astype(BF16)
+                for piece in range(low // 128, high // 128):
+                    lane = piece * 128 - low
+                    out_ref[piece, part * count : (part + 1) * count] = total[:, lane : lane + 128]
 
 
 def point_kernel(parts_ref, out_ref):
@@ -154,17 +176,19 @@
 
 
 def result_kernel(x_ref, act_ref, prob_ref, *refs):
-    sources, (out_ref, res_ref, tmp_ref, gate_ref, down_ref, sems) = refs[:6], refs[6:]
-    copies = panel_copies(x_ref, sources, gate_ref, down_ref, sems)
-    width = down_ref.shape[1]
+    sources, (out_ref, res_ref, tmp_ref, a_ref, b_ref, sems) = refs[:6], refs[6:]
+    copies = panel_copies(x_ref, sources, a_ref, b_ref, sems)
+    width = a_ref.shape[1]
     hidden, gate_grad, up_grad = hidden_parts(act_ref)
+    hid = hidden.shape[1]
+    half = hid // 2
+    first = jnp.concatenate([gate_grad, up_grad[:, 0:half]], axis=1)
     res_ref[...] = jnp.zeros_like(res_ref)
     for d, step in enumerate(STEPS):
         for copy in copies[d]:
             copy.wait()
-        outcome = prob_ref[:, 0:1] * dot(hidden, down_ref[d], 1, 1)
-        dx = dot(gate_grad, gate_ref[d, 0:width], 1, 1)
-        dx += dot(up_grad, gate_ref[d, width : 2 * width], 1, 1)
+        outcome = prob_ref[:, 0:1] * dot(hidden, b_ref[d, :, 0:hid], 1, 1)
+        dx = dot(first, a_ref[d], 1, 1) + dot(up_grad[:, half:], b_ref[d, :, hid:], 1, 1)
         res_ref[:, 0:width] = outcome
         res_ref[:, DY_LANE : DY_LANE + width] = dx
         out_ref[lax.rem(x_ref[0] + step, 4)] = split_lanes(tmp_ref, res_ref[...])
@@ -258,18 +282,28 @@
     def shift(array, d):
         return lax.ppermute(array, "x", shifts[d])
 
-    gates = jnp.concatenate([w_gate[0], w_up[0]], axis=0)
-    gates = lax.all_gather(gates, "x", axis=0, tiled=False)
-    down = w_down[0].T
-    right, left = shift(down, 1), shift(down, 3)
-
-    packed = call(
+    vmem_spec = pl.BlockSpec(memory_space=pltpu.VMEM)
+    any_spec = pl.BlockSpec(memory_space=pl.ANY)
+    both = jax.ShapeDtypeStruct((width, 3 * hid // 2), BF16)
+    packed, panel_a, panel_b = call(
         pack_kernel,
-        jax.ShapeDtypeStruct((groups, BLK, LANES), BF16),
-        (tokens.T, grad_output.T, gate_prob.T, block_lists.transpose(2, 0, 1)),
+        (jax.ShapeDtypeStruct((groups, BLK, LANES), BF16), both, both),
+        (
+            tokens.T,
+            grad_output.T,
+            gate_prob.T,
+            block_lists.transpose(2, 0, 1),
+            w_gate[0],
+            w_up[0],
+            w_down[0].T,
+        ),
         VMEM_LARGE,
-        scratch_shapes=[pltpu.VMEM((LANES, LANES), BF16)],
-    )
+        in_specs=[vmem_spec] * 4 + [any_spec] * 3,
+        out_specs=[vmem_spec, any_spec, any_spec],
+        scratch_shapes=[pltpu.VMEM((LANES, LANES), BF16), pltpu.SemaphoreType.DMA((4,))],
+    )
+    all_a = lax.all_gather(panel_a, "x", axis=0, tiled=False)
+    right, left = shift(panel_b, 1), shift(panel_b, 3)
     info = routing_info(expert_slot, block_counts, entries, share_x)
     mine = (expert_slot == lax.axis_index(GROUP)).astype(F32)
     mark = lax.pad(mine, jnp.zeros((), F32), ((P_LANE, 16, 0),))[None]
@@ -284,8 +318,8 @@
         (spread, info),
         scratch_shapes=[pltpu.VMEM((4 * total, 128), F32)],
     )
-    half = hid // 2
-    panels = [gates, down, right, left, shift(right[:, 0:half], 1), shift(left[:, half:], 3)]
+    half = 3 * hid // 4
+    panels = [all_a, panel_b, right, left, shift(right[:, 0:half], 1), shift(left[:, half:], 3)]
     pieces = (share_x * groups, 4 * picked // share_x, 128)
     tiles = exchange(sent.reshape(pieces), OWNERS).reshape(share_x, 4 * count, 128)
 
@@ -298,13 +332,8 @@
     tile_block = (1, 4 * count, 128)
     act_shape = (share_y, 3 * count, hid // share_y)
     scalar_spec = pl.BlockSpec(memory_space=pltpu.SMEM)
-    vmem_spec = pl.BlockSpec(memory_space=pltpu.VMEM)
-    panel_specs = [pl.BlockSpec(memory_space=pl.ANY)] * 6
-    panel_scratch = [
-        pltpu.VMEM((4, 2 * width, hid), BF16),
-        pltpu.VMEM((4, width, hid), BF16),
-        pltpu.SemaphoreType.DMA((9,)),
-    ]
+    panel_specs = [any_spec] * 6
+    panel_scratch = [pltpu.VMEM((4,) + both.shape, BF16)] * 2 + [pltpu.SemaphoreType.DMA((9,))]
     *rows, parts, prob = call(
         hidden_kernel,
         (jax.ShapeDtypeStruct((count, LANES), BF16),) * 4

time: 220 us -> 262 us (1.19)
  Pallas kernels: 24.6 us -> 67 us
  blocking collectives: 80.4 us -> 77.1 us
    pallas_call x8, Pallas kernels: 24.6 us -> 67 us  [call(): pl.pallas_call(kernel, out_shape=out_shape, compiler_params=pltpu.Compile...]
    all_to_all x2, blocking collectives: 57 us -> 53.7 us  [exchange(): return lax.all_to_all(array, axis, split_axis=0, concat_axis=0, tiled=True)]
    all_to_all x3, starting transfers between devices: 24.2 us -> 27.4 us  [exchange(): return lax.all_to_all(array, axis, split_axis=0, concat_axis=0, tiled=True)]
  transfers between devices with their start and end apart: 12 -> 12, of which waited for: 5 -> 7; matrix products, arithmetic and copies ran while one was open for 1% -> 2% of each run, Pallas kernels for 6% -> 4%
where the time goes in v8:
time: 262 us; the launch traced here: 261 us
  blocking collectives  77.1 us (29%)
  Pallas kernels  67 us (26%)
  starting transfers between devices  49 us (19%)
  waiting for transfers between devices  48.6 us (19%)
  between operations  14.3 us (5%)
  other arithmetic  3.17 us (1%)
    pallas_call x8, Pallas kernels, call(): pl.pallas_call(kernel, out_shape=out_shape, compiler_params=pltpu.Compile...  67 us
    all_to_all x2, blocking collectives, exchange(): return lax.all_to_all(array, axis, split_axis=0, concat_axis=0, tiled=True)  53.7 us
    all_to_all x3, waiting for transfers between devices, exchange(): return lax.all_to_all(array, axis, split_axis=0, concat_axis=0, tiled=True)  28.4 us
    all_to_all x3, starting transfers between devices, exchange(): return lax.all_to_all(array, axis, split_axis=0, concat_axis=0, tiled=True)  27.4 us
    all_gather x1, blocking collectives, body(): act = lax.all_gather(act, 'y', axis=0, tiled=False)  23.4 us
    ppermute x7, starting transfers between devices, shift(): return lax.ppermute(array, 'x', shifts[d])  21.5 us
    ppermute x7, waiting for transfers between devices, shift(): return lax.ppermute(array, 'x', shifts[d])  20.1 us
  transfers between devices with their start and end apart: 12, of which 7 were waited for; matrix products, arithmetic and copies ran while one was open for 2% of the time, Pallas kernels for 4%

profile of v8, /device:TPU:1, one launch (start us, length us, event | category | flops | bytes accessed | tf_op | source)
XLA Modules:
  0.0 261.4 jit_solution(11388088474438603195)
XLA Ops:
  7.2 0.0 all-gather.6.cloned.1.call-start
  7.2 0.0 copy-start.7
  7.2 44.7 %shard_map.128 = (bf16[16,32,512]{2,1,0:T(8,128)(2,1)}, bf16[224,1536]{1,0:T(8,128)(2,1)}, bf16[224,1536]{1,0:T(8,128)(2,1)}) custom-call(bf16[224,512]{1,0:T(8,128)(2,1)} %bitcast.50, bf16[224,512]{1,0:T(8,128)(2,1)} %bitcast.51, bf16[16,512]{1,0:T(8,128)(2,1)} %bitcast.52, s32[10,1,16]{2,1,0:T(1,128)} %bitcast.53, bf16[224,1024]{1,0:T(8,128)(2,1)} %bitcast.47, ...), custom_call_target="tpu_custom_call" | custom-call | tf_op jit(solution)/shard_map/pallas_call | solution.py:28
  51.9 0.0 all-gather.6.cloned.1.call-update
  51.9 5.2 %collective-permute-start.1 = (bf16[224,1536]{1,0:T(8,128)(2,1)}, bf16[224,1536]{1,0:T(8,128)(2,1)S(1)}, u32[]{:S(2)}, u32[]{:S(2)}) collective-permute-start(bf16[224,1536]{1,0:T(8,128)(2,1)} %get-tuple-element.31.refs_1_), channel_id=1, source_target_pairs={{0,3},{1,0},{2,1},{3,2},{4,7},{5,4},{6,5},{7,6},{8,11},{9,8},{10,9... | collective-permute-start | bytes 2064392 | tf_op jit(solution)/shard_map/ppermute | solution.py:283
  57.2 1.9 collective-permute-start
  59.1 11.3 %all-to-all-start = ((bf16[16,32,512]{2,1,0:T(8,128)(2,1)}), bf16[16,32,512]{2,1,0:T(8,128)(2,1)S(1)}, u32[]{:S(2)}, u32[]{:S(2)}) async-start(bf16[16,32,512]{2,1,0:T(8,128)(2,1)} %get-tuple-element.30), calls=%async_computation | async-start | bytes 1048576 | tf_op jit(solution)/shard_map/all_to_all | solution.py:262
  70.4 0.7 fusion.5
  71.1 0.8 multiply_reduce_fusion.1
  72.0 0.1 multiply_reduce_fusion
  72.1 0.7 select_reduce_fusion
  72.9 0.1 fusion
  73.0 0.1 reshape.243
  73.1 0.1 reshape.250
  73.2 0.1 reshape.247
  73.4 0.0 collective-permute-done.1.refs_3_
  73.4 0.5 collective-permute-done.refs_2_
  73.9 13.8 %all-to-all-done = bf16[16,32,512]{2,1,0:T(8,128)(2,1)S(1)} async-done(((bf16[16,32,512]{2,1,0:T(8,128)(2,1)}), bf16[16,32,512]{2,1,0:T(8,128)(2,1)S(1)}, u32[]{:S(2)}, u32[]{:S(2)}) %all-to-all-start) | async-done | bytes 524320 | tf_op jit(solution)/shard_map/all_to_all | solution.py:262
  87.7 0.2 copy.18.info_ref
  87.9 2.4 shard_map.129
  90.3 8.9 %all-to-all-start.1 = ((bf16[64,40,128]{2,1,0:T(8,128)(2,1)}), bf16[64,40,128]{2,1,0:T(8,128)(2,1)S(1)}, u32[]{:S(2)}, u32[]{:S(2)}) async-start(bf16[64,40,128]{2,1,0:T(8,128)(2,1)} %bitcast.14), calls=%async_computation.1 | async-start | bytes 1310720 | tf_op jit(solution)/shard_map/all_to_all | solution.py:262
  99.2 0.8 slice.23
  100.0 4.7 %collective-permute-start.3 = (bf16[224,768]{1,0:T(8,128)(2,1)}, bf16[224,768]{1,0:T(8,128)(2,1)S(1)}, u32[]{:S(2)}, u32[]{:S(2)}) collective-permute-start(bf16[224,768]{1,0:T(8,128)(2,1)} %slice.23), channel_id=1, source_target_pairs={{0,3},{1,0},{2,1},{3,2},{4,7},{5,4},{6,5},{7,6},{8,11},{9,8},{10,9... | collective-permute-start | bytes 1032200 | tf_op jit(solution)/shard_map/ppermute | solution.py:283
  104.7 1.9 collective-permute-start.2
  106.6 0.6 pad_convert_fusion
  107.3 9.9 %collective-permute-done.3.refs_5_ = bf16[224,768]{1,0:T(8,128)(2,1)S(1)} collective-permute-done((bf16[224,768]{1,0:T(8,128)(2,1)}, bf16[224,768]{1,0:T(8,128)(2,1)S(1)}, u32[]{:S(2)}, u32[]{:S(2)}) %collective-permute-start.3) | collective-permute-done | bytes 344096 | tf_op jit(solution)/shard_map/ppermute | solution.py:283
  117.1 4.4 %collective-permute-done.2.refs_4_ = bf16[224,768]{1,0:T(8,128)(2,1)} collective-permute-done((bf16[224,768]{1,0:T(8,128)(2,1)S(1)}, bf16[224,768]{1,0:T(8,128)(2,1)}, u32[]{:S(2)}, u32[]{:S(2)}) %collective-permute-start.2) | collective-permute-done | bytes 344096 | tf_op jit(solution)/shard_map/ppermute | solution.py:283
  121.6 0.0 all-to-all-done.1
  121.6 0.9 copy-done.2
  122.5 5.1 %shard_map.130 = (bf16[160,512]{1,0:T(8,128)(2,1)}, bf16[160,512]{1,0:T(8,128)(2,1)}, bf16[160,512]{1,0:T(8,128)(2,1)}, bf16[160,512]{1,0:T(8,128)(2,1)}, bf16[8...) custom-call(s32[1]{0:T(128)} %bitcast.13.x_ref, bf16[4,640,128]{2,1,0:T(8,128)(2,1)} %bitcast.46, f32[1,256]{1,0:T(1,128)} %bitcast.54, ...), custom_call_target="tpu_custom_call" | custom-call | tf_op jit(solution)/shard_map/pallas_call | solution.py:28
  127.6 7.2 %all-to-all-start.2 = ((bf16[8,480,128]{2,1,0:T(8,128)(2,1)}), bf16[8,480,128]{2,1,0:T(8,128)(2,1)S(1)}, u32[]{:S(2)}, u32[]{:S(2)}) async-start(bf16[8,480,128]{2,1,0:T(8,128)(2,1)} %get-tuple-element.39), calls=%async_computation.2 | async-start | bytes 1966080 | tf_op jit(solution)/shard_map/all_to_all | solution.py:262
  134.8 0.0 all-gather.8.cloned.1.call-start
  134.8 2.3 collective-permute-start.4
  137.1 3.0 %collective-permute-start.5 = (bf16[160,512]{1,0:T(8,128)(2,1)}, bf16[160,512]{1,0:T(8,128)(2,1)S(1)}, u32[]{:S(2)}, u32[]{:S(2)}) collective-permute-start(bf16[160,512]{1,0:T(8,128)(2,1)} %get-tuple-element.42), channel_id=1, source_target_pairs={{0,1},{1,2},{2,3},{3,0},{4,5},{5,6},{6,7},{7,4},{8,9},{9,10},{10,1... | collective-permute-start | bytes 491528 | tf_op jit(solution)/shard_map/ppermute | solution.py:283
  140.1 2.5 collective-permute-start.6
  142.6 0.0 collective-permute-done.4.refs_3_
  142.7 2.6 %collective-permute-done.5.refs_1_ = bf16[160,512]{1,0:T(8,128)(2,1)S(1)} collective-permute-done((bf16[160,512]{1,0:T(8,128)(2,1)}, bf16[160,512]{1,0:T(8,128)(2,1)S(1)}, u32[]{:S(2)}, u32[]{:S(2)}) %collective-permute-start.5) | collective-permute-done | bytes 163872 | tf_op jit(solution)/shard_map/ppermute | solution.py:283
  145.3 2.8 %collective-permute-done.6.refs_2_ = bf16[160,512]{1,0:T(8,128)(2,1)S(1)} collective-permute-done((bf16[160,512]{1,0:T(8,128)(2,1)}, bf16[160,512]{1,0:T(8,128)(2,1)S(1)}, u32[]{:S(2)}, u32[]{:S(2)}) %collective-permute-start.6) | collective-permute-done | bytes 163872 | tf_op jit(solution)/shard_map/ppermute | solution.py:283
  148.0 14.6 %all-to-all-done.2.parts_ref = bf16[8,480,128]{2,1,0:T(8,128)(2,1)S(1)} async-done(((bf16[8,480,128]{2,1,0:T(8,128)(2,1)}), bf16[8,480,128]{2,1,0:T(8,128)(2,1)S(1)}, u32[]{:S(2)}, u32[]{:S(2)}) %all-to-all-start.2) | async-done | bytes 983072 | tf_op jit(solution)/shard_map/all_to_all | solution.py:262
  162.6 0.2 shard_map.131
  162.8 23.4 %all-gather.1 = bf16[3840,128]{1,0:T(8,128)(2,1)} all-gather(bf16[480,128]{1,0:T(8,128)(2,1)S(1)} %shard_map.131), channel_id=3, replica_groups=mesh['z'=8,'core'=2,'y'=8,'x'=4] {'y'}, dimensions={0}, use_global_device_ids=true | all-gather | bytes 1105920 | tf_op jit(solution)/shard_map/all_gather | solution.py:351
  186.2 0.0 all-gather.8.cloned.1.call-update
  186.2 7.2 %shard_map.132 = bf16[4,640,128]{2,1,0:T(8,128)(2,1)} custom-call(s32[1]{0:T(128)} %bitcast.13.x_ref, bf16[8,480,128]{2,1,0:T(8,128)(2,1)} %bitcast.43, f32[160,128]{1,0:T(8,128)} %get-tuple-element.45.prob_ref, bf16[4,224,1536]{2,1,0:T(8,128)(2,1)} %bitcast.41, bf16[224,1536]{1,0:T(8,128)(2,1)} %get-tuple-element.31.refs_1_, bf16[224,1536]{1,0:T(8,128)(2,1)} %copy-done.1, ...), custom_call_target="tpu_custom_call" | custom-call | tf_op jit(solution)/shard_map/pallas_call | solution.py:28
  193.5 31.7 %all_to_all.25 = bf16[64,40,128]{2,1,0:T(8,128)(2,1)S(1)} all-to-all(bf16[64,40,128]{2,1,0:T(8,128)(2,1)} %bitcast.45), channel_id=1, replica_groups=mesh['z'=8,'core'=2,'y'=8,'x'=4] {'x','z','core'}, dimensions={0} | all-to-all | bytes 1310720 | tf_op jit(solution)/shard_map/all_to_all | solution.py:262
  225.2 0.6 shard_map.133
  225.8 21.9 %all_to_all.26 = bf16[16,32,512]{2,1,0:T(8,128)(2,1)S(1)} all-to-all(bf16[16,32,512]{2,1,0:T(8,128)(2,1)S(1)} %bitcast.37), channel_id=1, replica_groups=mesh['z'=8,'core'=2,'y'=8,'x'=4] {'z','core'}, dimensions={0} | all-to-all | bytes 1048576 | tf_op jit(solution)/shard_map/all_to_all | solution.py:262
  247.8 1.2 shard_map.134
  249.0 5.6 %shard_map.135 = (bf16[224,1024]{1,0:T(8,128)(2,1)}, bf16[224,1024]{1,0:T(8,128)(2,1)}, bf16[224,1024]{1,0:T(8,128)(2,1)}) custom-call(s32[1]{0:T(128)} %bitcast.13.x_ref, bf16[4,8,480,128]{3,2,1,0:T(8,128)(2,1)} %bitcast.44, bf16[160,512]{1,0:T(8,128)(2,1)} %get-tuple-element.48.refs_0_, bf16[160,512]{1,0:T(8,128)(2,1)} %copy-done.5, ...), custom_call_target="tpu_custom_call" | custom-call | tf_op jit(solution)/shard_map/pallas_call | solution.py:28
  (24 shorter events, 0.1 us)
Async XLA Ops:
  7.2 114.4 %all-gather.6.cloned.1.call-start = ((), (), s32[]{:S(2)}) async-start(), calls=%async_computation.5 | async-start | bytes 3440640 | tf_op jit(solution)/shard_map/all_gather | solution.py:305
  7.2 99.4 %copy-start.7 = (s32[16]{0:T(128)S(1)}, s32[16]{0:T(128)}, u32[]{:S(2)}) copy-start(s32[16]{0:T(128)} %param.15) | copy-start | bytes 196
  51.9 21.5 %collective-permute-start.1 = (bf16[224,1536]{1,0:T(8,128)(2,1)}, bf16[224,1536]{1,0:T(8,128)(2,1)S(1)}, u32[]{:S(2)}, u32[]{:S(2)}) collective-permute-start(bf16[224,1536]{1,0:T(8,128)(2,1)} %get-tuple-element.31.refs_1_), channel_id=1, source_target_pairs={{0,3},{1,0},{2,1},{3,2},{4,7},{5,4},{6,5},{7,6},{8,11},{9,8},{10,9... | collective-permute-start | bytes 2064392 | tf_op jit(solution)/shard_map/ppermute | solution.py:283
  57.2 16.7 %collective-permute-start = (bf16[224,1536]{1,0:T(8,128)(2,1)}, bf16[224,1536]{1,0:T(8,128)(2,1)S(1)}, u32[]{:S(2)}, u32[]{:S(2)}) collective-permute-start(bf16[224,1536]{1,0:T(8,128)(2,1)} %get-tuple-element.31.refs_1_), channel_id=1, source_target_pairs={{0,1},{1,2},{2,3},{3,0},{4,5},{5,6},{6,7},{7,4},{8,9},{9,10},{10,1... | collective-permute-start | bytes 2064392 | tf_op jit(solution)/shard_map/ppermute | solution.py:283
  59.1 28.6 %all-to-all-start = ((bf16[16,32,512]{2,1,0:T(8,128)(2,1)}), bf16[16,32,512]{2,1,0:T(8,128)(2,1)S(1)}, u32[]{:S(2)}, u32[]{:S(2)}) async-start(bf16[16,32,512]{2,1,0:T(8,128)(2,1)} %get-tuple-element.30), calls=%async_computation | async-start | bytes 1048576 | tf_op jit(solution)/shard_map/all_to_all | solution.py:262
  73.4 48.2 %copy-start = (bf16[224,1536]{1,0:T(8,128)(2,1)}, bf16[224,1536]{1,0:T(8,128)(2,1)S(1)}, u32[]{:S(2)}) copy-start(bf16[224,1536]{1,0:T(8,128)(2,1)S(1)} %collective-permute-done.1.refs_3_) | copy-start | bytes 2064388
  73.9 47.7 %copy-start.1 = (bf16[224,1536]{1,0:T(8,128)(2,1)}, bf16[224,1536]{1,0:T(8,128)(2,1)S(1)}, u32[]{:S(2)}) copy-start(bf16[224,1536]{1,0:T(8,128)(2,1)S(1)} %collective-permute-done.refs_2_) | copy-start | bytes 2064388
  90.3 31.3 %all-to-all-start.1 = ((bf16[64,40,128]{2,1,0:T(8,128)(2,1)}), bf16[64,40,128]{2,1,0:T(8,128)(2,1)S(1)}, u32[]{:S(2)}, u32[]{:S(2)}) async-start(bf16[64,40,128]{2,1,0:T(8,128)(2,1)} %bitcast.14), calls=%async_computation.1 | async-start | bytes 1310720 | tf_op jit(solution)/shard_map/all_to_all | solution.py:262
  100.0 17.2 %collective-permute-start.3 = (bf16[224,768]{1,0:T(8,128)(2,1)}, bf16[224,768]{1,0:T(8,128)(2,1)S(1)}, u32[]{:S(2)}, u32[]{:S(2)}) collective-permute-start(bf16[224,768]{1,0:T(8,128)(2,1)} %slice.23), channel_id=1, source_target_pairs={{0,3},{1,0},{2,1},{3,2},{4,7},{5,4},{6,5},{7,6},{8,11},{9,8},{10,9... | collective-permute-start | bytes 1032200 | tf_op jit(solution)/shard_map/ppermute | solution.py:283
  104.7 16.9 %collective-permute-start.2 = (bf16[224,768]{1,0:T(8,128)(2,1)S(1)}, bf16[224,768]{1,0:T(8,128)(2,1)}, u32[]{:S(2)}, u32[]{:S(2)}) collective-permute-start(bf16[224,768]{1,0:T(8,128)(2,1)S(1)} %slice.22), channel_id=1, source_target_pairs={{0,1},{1,2},{2,3},{3,0},{4,5},{5,6},{6,7},{7,4},{8,9},{9,10},{10,1... | collective-permute-start | bytes 1032200 | tf_op jit(solution)/shard_map/ppermute | solution.py:283
  117.1 4.4 %copy-start.3 = (bf16[224,768]{1,0:T(8,128)(2,1)}, bf16[224,768]{1,0:T(8,128)(2,1)S(1)}, u32[]{:S(2)}) copy-start(bf16[224,768]{1,0:T(8,128)(2,1)S(1)} %collective-permute-done.3.refs_5_) | copy-start | bytes 1032196
  121.6 0.9 copy-start.2
  127.6 35.0 %all-to-all-start.2 = ((bf16[8,480,128]{2,1,0:T(8,128)(2,1)}), bf16[8,480,128]{2,1,0:T(8,128)(2,1)S(1)}, u32[]{:S(2)}, u32[]{:S(2)}) async-start(bf16[8,480,128]{2,1,0:T(8,128)(2,1)} %get-tuple-element.39), calls=%async_computation.2 | async-start | bytes 1966080 | tf_op jit(solution)/shard_map/all_to_all | solution.py:262
  134.8 114.2 %all-gather.8.cloned.1.call-start = ((), (), s32[]{:S(2)}) async-start(), calls=%async_computation.6 | async-start | bytes 4915200 | tf_op jit(solution)/shard_map/all_gather | solution.py:352
  134.8 7.8 %collective-permute-start.4 = (bf16[160,512]{1,0:T(8,128)(2,1)}, bf16[160,512]{1,0:T(8,128)(2,1)S(1)}, u32[]{:S(2)}, u32[]{:S(2)}) collective-permute-start(bf16[160,512]{1,0:T(8,128)(2,1)} %get-tuple-element.41), channel_id=1, source_target_pairs={{0,3},{1,0},{2,1},{3,2},{4,7},{5,4},{6,5},{7,6},{8,11},{9,8},{10,9... | collective-permute-start | bytes 491528 | tf_op jit(solution)/shard_map/ppermute | solution.py:283
  137.1 8.1 %collective-permute-start.5 = (bf16[160,512]{1,0:T(8,128)(2,1)}, bf16[160,512]{1,0:T(8,128)(2,1)S(1)}, u32[]{:S(2)}, u32[]{:S(2)}) collective-permute-start(bf16[160,512]{1,0:T(8,128)(2,1)} %get-tuple-element.42), channel_id=1, source_target_pairs={{0,1},{1,2},{2,3},{3,0},{4,5},{5,6},{6,7},{7,4},{8,9},{9,10},{10,1... | collective-permute-start | bytes 491528 | tf_op jit(solution)/shard_map/ppermute | solution.py:283
  140.1 7.9 %collective-permute-start.6 = (bf16[160,512]{1,0:T(8,128)(2,1)}, bf16[160,512]{1,0:T(8,128)(2,1)S(1)}, u32[]{:S(2)}, u32[]{:S(2)}) collective-permute-start(bf16[160,512]{1,0:T(8,128)(2,1)} %get-tuple-element.43), channel_id=1, source_target_pairs={{0,2},{1,3},{2,0},{3,1},{4,6},{5,7},{6,4},{7,5},{8,10},{9,11},{10,... | collective-permute-start | bytes 491528 | tf_op jit(solution)/shard_map/ppermute | solution.py:283
  142.6 50.8 %copy-start.4 = (bf16[160,512]{1,0:T(8,128)(2,1)}, bf16[160,512]{1,0:T(8,128)(2,1)S(1)}, u32[]{:S(2)}) copy-start(bf16[160,512]{1,0:T(8,128)(2,1)S(1)} %collective-permute-done.4.refs_3_) | copy-start | bytes 491524
  145.3 48.2 %copy-start.5 = (bf16[160,512]{1,0:T(8,128)(2,1)}, bf16[160,512]{1,0:T(8,128)(2,1)S(1)}, u32[]{:S(2)}) copy-start(bf16[160,512]{1,0:T(8,128)(2,1)S(1)} %collective-permute-done.5.refs_1_) | copy-start | bytes 491524
  148.0 45.4 %copy-start.6 = (bf16[160,512]{1,0:T(8,128)(2,1)}, bf16[160,512]{1,0:T(8,128)(2,1)S(1)}, u32[]{:S(2)}) copy-start(bf16[160,512]{1,0:T(8,128)(2,1)S(1)} %collective-permute-done.6.refs_2_) | copy-start | bytes 491524
Sparse Core Ops, SparseCore 0:
  52.1 48.3 all-gather.5
  186.4 56.3 all-gather.7

commit v9 on v7

--- a/solution.py
+++ b/solution.py
@@ -171,29 +171,39 @@
 
 
 def weight_kernel(x_ref, act_ref, *refs):
-    row_refs, out_refs, acc_ref = refs[:4], refs[4:7], refs[7]
-    step = pl.program_id(0)
+    row_refs, out_refs, (buf_ref, sems) = refs[:4], refs[4:7], refs[7:]
     width = out_refs[0].shape[0]
-    hidden, gate_grad, up_grad = hidden_parts(act_ref.at[0])
-
-    @pl.when(step == 0)
-    def _():
-        acc_ref[...] = jnp.zeros_like(acc_ref)
-
-    for d in range(4):
-
-        @pl.when(step == d)
-        def _():
-            x = row_refs[d][:, 0:width]
-            grad = row_refs[d][:, DY_LANE : DY_LANE + width]
-            acc_ref[0] += dot(x, gate_grad, 0, 0)
-            acc_ref[1] += dot(x, up_grad, 0, 0)
-            acc_ref[2] += dot(grad, hidden, 0, 0)
-
-    @pl.when(step == pl.num_programs(0) - 1)
-    def _():
-        for part in range(3):
-            out_refs[part][...] = acc_ref[part].astype(BF16)
+    count = row_refs[0].shape[0]
+    parts = (1, 2, 0)
+    copies = [
+        [
+            pltpu.make_async_copy(
+                act_ref.at[lax.rem(x_ref[0] + 4 - d, 4), :, pl.ds(part * count, count)],
+                buf_ref.at[part, d],
+                sems.at[part, d],
+            )
+            for d in range(4)
+        ]
+        for part in parts
+    ]
+    for group in copies:
+        for copy in group:
+            copy.start()
+    x, grad = (
+        jnp.concatenate([ref[:, lane : lane + width] for ref in row_refs], axis=0)
+        for lane in (0, DY_LANE)
+    )
+    for i, part in enumerate(parts):
+        for copy in copies[i]:
+            copy.wait()
+        right = jnp.concatenate(
+            [
+                jnp.concatenate([buf_ref[part, d, k] for k in range(buf_ref.shape[2])], axis=1)
+                for d in range(4)
+            ],
+            axis=0,
+        )
+        out_refs[i][...] = dot(grad if part == 0 else x, right, 0, 0).astype(BF16)
 
 
 def combine_kernel(pick_ref, tiles_ref, out_ref, tmp_ref):
@@ -261,7 +271,6 @@
     gates = jnp.concatenate([w_gate[0], w_up[0]], axis=0)
     gates = lax.all_gather(gates, "x", axis=0, tiled=False)
     down = w_down[0].T
-    right, left = shift(down, 1), shift(down, 3)
 
     packed = call(
         pack_kernel,
@@ -274,7 +283,9 @@
     mine = (expert_slot == lax.axis_index(GROUP)).astype(F32)
     mark = lax.pad(mine, jnp.zeros((), F32), ((P_LANE, 16, 0),))[None]
     spread = exchange(packed, GROUP).reshape(groups * BLK, LANES)
-    spread, info, right, left = lax.optimization_barrier((spread, info, right, left))
+    info, down_late = lax.optimization_barrier((info, down))
+    right, left = shift(down_late, 1), shift(down_late, 3)
+    spread, info = lax.optimization_barrier((spread, info))
     sent, pick = call(
         select_kernel,
         (
@@ -284,18 +295,12 @@
         (spread, info),
         scratch_shapes=[pltpu.VMEM((4 * total, 128), F32)],
     )
+    sent, right, left = lax.optimization_barrier((sent, right, left))
     half = hid // 2
     panels = [gates, down, right, left, shift(right[:, 0:half], 1), shift(left[:, half:], 3)]
     pieces = (share_x * groups, 4 * picked // share_x, 128)
     tiles = exchange(sent.reshape(pieces), OWNERS).reshape(share_x, 4 * count, 128)
 
-    def before(d, x):
-        return (lax.rem(x[0] + share_x - d, share_x), 0, 0)
-
-    def whole(*shape):
-        return pl.BlockSpec(shape, lambda *_: (0,) * len(shape))
-
-    tile_block = (1, 4 * count, 128)
     act_shape = (share_y, 3 * count, hid // share_y)
     scalar_spec = pl.BlockSpec(memory_space=pltpu.SMEM)
     vmem_spec = pl.BlockSpec(memory_space=pltpu.VMEM)
@@ -335,14 +340,11 @@
         (jax.ShapeDtypeStruct((width, hid), BF16),) * 3,
         (order, all_act, *(rows[STEPS.index(d)] for d in range(share_x))),
         VMEM_LARGE,
-        grid_spec=pltpu.PrefetchScalarGridSpec(
-            num_scalar_prefetch=1,
-            grid=(share_x,),
-            in_specs=[pl.BlockSpec((1,) + act_shape, lambda d, x: before(d, x) + (0,))]
-            + [whole(count, LANES)] * 4,
-            out_specs=[whole(width, hid)] * 3,
-            scratch_shapes=[pltpu.VMEM((3, width, hid), F32)],
-        ),
+        in_specs=[scalar_spec, panel_specs[0]] + [vmem_spec] * 4,
+        scratch_shapes=[
+            pltpu.VMEM((3, share_x, share_y, count, hid // share_y), BF16),
+            pltpu.SemaphoreType.DMA((3, share_x)),
+        ],
     )
     back = exchange(results.reshape(pieces), OWNERS).reshape(4 * total, 128)
     summed = call(

time: 220 us -> 227 us (1.032)
  waiting for transfers between devices: 46.8 us -> 56.9 us
    ppermute x7, waiting for transfers between devices: 19.6 us -> 32.3 us  [shift(): return lax.ppermute(array, 'x', shifts[d])]
    ppermute x7, starting transfers between devices: 23.8 us -> 20.2 us  [shift(): return lax.ppermute(array, 'x', shifts[d])]
    all_to_all x3, starting transfers between devices: 24.2 us -> 27.4 us  [exchange(): return lax.all_to_all(array, axis, split_axis=0, concat_axis=0, tiled=True)]
    all_to_all x3, waiting for transfers between devices: 27.2 us -> 24.5 us  [exchange(): return lax.all_to_all(array, axis, split_axis=0, concat_axis=0, tiled=True)]
  transfers between devices with their start and end apart: 12 -> 12, of which waited for: 5 -> 8; matrix products, arithmetic and copies ran while one was open for 1% -> 1% of each run, Pallas kernels for 6% -> 6%
where the time goes in v9:
time: 227 us; the launch traced here: 226 us
  blocking collectives  78.2 us (34%)
  waiting for transfers between devices  56.9 us (25%)
  starting transfers between devices  47.7 us (21%)
  Pallas kernels  24 us (11%)
  between operations  14.4 us (6%)
  other arithmetic  3.33 us (1%)
    all_to_all x2, blocking collectives, exchange(): return lax.all_to_all(array, axis, split_axis=0, concat_axis=0, tiled=True)  54.7 us
    ppermute x7, waiting for transfers between devices, shift(): return lax.ppermute(array, 'x', shifts[d])  32.3 us
    all_to_all x3, starting transfers between devices, exchange(): return lax.all_to_all(array, axis, split_axis=0, concat_axis=0, tiled=True)  27.4 us
    all_to_all x3, waiting for transfers between devices, exchange(): return lax.all_to_all(array, axis, split_axis=0, concat_axis=0, tiled=True)  24.5 us
    pallas_call x8, Pallas kernels, call(): pl.pallas_call(kernel, out_shape=out_shape, compiler_params=pltpu.Compile...  24 us
    all_gather x1, blocking collectives, body(): act = lax.all_gather(act, 'y', axis=0, tiled=False)  23.5 us
    ppermute x7, starting transfers between devices, shift(): return lax.ppermute(array, 'x', shifts[d])  20.2 us
  transfers between devices with their start and end apart: 12, of which 8 were waited for; matrix products, arithmetic and copies ran while one was open for 1% of the time, Pallas kernels for 6%

profile of v9, /device:TPU:1, one launch (start us, length us, event | category | flops | bytes accessed | tf_op | source)
XLA Modules:
  0.0 226.0 jit_solution(13796420155339117427)
XLA Ops:
  7.2 0.0 all-gather.6.cloned.1.call-start
  7.2 2.2 pad_maximum_fusion
  9.4 0.0 all-gather.6.cloned.1.call-update
  9.4 2.4 %shard_map.128 = bf16[16,32,512]{2,1,0:T(8,128)(2,1)} custom-call(bf16[224,512]{1,0:T(8,128)(2,1)} %bitcast.53, bf16[224,512]{1,0:T(8,128)(2,1)} %bitcast.54, bf16[16,512]{1,0:T(8,128)(2,1)} %bitcast.55, s32[10,1,16]{2,1,0:T(1,128)} %bitcast.56), custom_call_target="tpu_custom_call" | custom-call | tf_op jit(solution)/shard_map/pallas_call | solution.py:28
  11.8 11.8 %all-to-all-start = ((bf16[16,32,512]{2,1,0:T(8,128)(2,1)}), bf16[16,32,512]{2,1,0:T(8,128)(2,1)S(1)}, u32[]{:S(2)}, u32[]{:S(2)}) async-start(bf16[16,32,512]{2,1,0:T(8,128)(2,1)} %shard_map.128), calls=%async_computation | async-start | bytes 1048576 | tf_op jit(solution)/shard_map/all_to_all | solution.py:248
  23.7 0.1 fusion.5
  23.8 0.1 multiply_reduce_fusion.1
  23.9 0.1 multiply_reduce_fusion
  24.0 0.1 select_reduce_fusion
  24.1 0.1 fusion
  24.2 0.1 reshape.243
  24.4 0.1 reshape.250
  24.5 0.1 reshape.247
  24.7 4.4 %collective-permute-start.1 = (bf16[224,1024]{1,0:T(8,128)(2,1)S(1)}, bf16[224,1024]{1,0:T(8,128)(2,1)S(1)}, u32[]{:S(2)}, u32[]{:S(2)}) collective-permute-start(bf16[224,1024]{1,0:T(8,128)(2,1)S(1)} %bitcast.49), channel_id=1, source_target_pairs={{0,3},{1,0},{2,1},{3,2},{4,7},{5,4},{6,5},{7,6},{8,11},{9,8},{10,9... | collective-permute-start | bytes 1376264 | tf_op jit(solution)/shard_map/ppermute | solution.py:269
  29.1 1.9 collective-permute-start
  31.0 10.0 %all-to-all-done = bf16[16,32,512]{2,1,0:T(8,128)(2,1)S(1)} async-done(((bf16[16,32,512]{2,1,0:T(8,128)(2,1)}), bf16[16,32,512]{2,1,0:T(8,128)(2,1)S(1)}, u32[]{:S(2)}, u32[]{:S(2)}) %all-to-all-start) | async-done | bytes 524320 | tf_op jit(solution)/shard_map/all_to_all | solution.py:248
  41.0 0.2 copy.18.info_ref
  41.2 2.4 %shard_map.129 = (bf16[2560,128]{1,0:T(8,128)(2,1)}, bf16[640,512]{1,0:T(8,128)(2,1)S(1)}) custom-call(bf16[512,512]{1,0:T(8,128)(2,1)S(1)} %bitcast.38, s32[640,3]{1,0:T(8,128)S(1)} %copy.18.info_ref), custom_call_target="tpu_custom_call" | custom-call | tf_op jit(solution)/shard_map/pallas_call | solution.py:28
  43.5 1.3 collective-permute-done.1.refs_3_
  44.9 8.8 %collective-permute-done.refs_2_ = bf16[224,1024]{1,0:T(8,128)(2,1)S(1)} collective-permute-done((bf16[224,1024]{1,0:T(8,128)(2,1)S(1)}, bf16[224,1024]{1,0:T(8,128)(2,1)S(1)}, u32[]{:S(2)}, u32[]{:S(2)}) %collective-permute-start) | collective-permute-done | bytes 458784 | tf_op jit(solution)/shard_map/ppermute | solution.py:269
  53.7 8.7 %all-to-all-start.1 = ((bf16[64,40,128]{2,1,0:T(8,128)(2,1)}), bf16[64,40,128]{2,1,0:T(8,128)(2,1)S(1)}, u32[]{:S(2)}, u32[]{:S(2)}) async-start(bf16[64,40,128]{2,1,0:T(8,128)(2,1)} %bitcast.12), calls=%async_computation.1 | async-start | bytes 1310720 | tf_op jit(solution)/shard_map/all_to_all | solution.py:248
  62.4 4.7 %collective-permute-start.3 = (bf16[224,512]{1,0:T(8,128)(2,1)S(1)}, bf16[224,512]{1,0:T(8,128)(2,1)S(1)}, u32[]{:S(2)}, u32[]{:S(2)}) collective-permute-start(bf16[224,512]{1,0:T(8,128)(2,1)S(1)} %slice.23), channel_id=1, source_target_pairs={{0,3},{1,0},{2,1},{3,2},{4,7},{5,4},{6,5},{7,6},{8,11},{9,8},{10,9... | collective-permute-start | bytes 688136 | tf_op jit(solution)/shard_map/ppermute | solution.py:269
  67.1 1.9 collective-permute-start.2
  69.1 0.7 pad_convert_fusion
  69.8 10.9 %collective-permute-done.3.refs_5_ = bf16[224,512]{1,0:T(8,128)(2,1)S(1)} collective-permute-done((bf16[224,512]{1,0:T(8,128)(2,1)S(1)}, bf16[224,512]{1,0:T(8,128)(2,1)S(1)}, u32[]{:S(2)}, u32[]{:S(2)}) %collective-permute-start.3) | collective-permute-done | bytes 229408 | tf_op jit(solution)/shard_map/ppermute | solution.py:269
  80.6 5.4 %collective-permute-done.2.refs_4_ = bf16[224,512]{1,0:T(8,128)(2,1)S(1)} collective-permute-done((bf16[224,512]{1,0:T(8,128)(2,1)S(1)}, bf16[224,512]{1,0:T(8,128)(2,1)S(1)}, u32[]{:S(2)}, u32[]{:S(2)}) %collective-permute-start.2) | collective-permute-done | bytes 229408 | tf_op jit(solution)/shard_map/ppermute | solution.py:269
  86.0 0.0 all-gather.6.cloned.1.call-done
  86.1 0.6 copy-done.5
  86.7 0.3 copy-done.2
  87.0 5.1 %shard_map.130 = (bf16[160,512]{1,0:T(8,128)(2,1)}, bf16[160,512]{1,0:T(8,128)(2,1)}, bf16[160,512]{1,0:T(8,128)(2,1)}, bf16[160,512]{1,0:T(8,128)(2,1)}, bf16[8...) custom-call(s32[1]{0:T(128)} %bitcast.11.x_ref, bf16[4,640,128]{2,1,0:T(8,128)(2,1)} %bitcast.46, f32[1,256]{1,0:T(1,128)} %bitcast.57, ...), custom_call_target="tpu_custom_call" | custom-call | tf_op jit(solution)/shard_map/pallas_call | solution.py:28
  92.1 0.0 copy-start.13
  92.1 6.9 %all-to-all-start.2 = ((bf16[8,480,128]{2,1,0:T(8,128)(2,1)}), bf16[8,480,128]{2,1,0:T(8,128)(2,1)S(1)}, u32[]{:S(2)}, u32[]{:S(2)}) async-start(bf16[8,480,128]{2,1,0:T(8,128)(2,1)} %get-tuple-element.39), calls=%async_computation.2 | async-start | bytes 1966080 | tf_op jit(solution)/shard_map/all_to_all | solution.py:248
  99.0 0.0 all-gather.8.cloned.1.call-start
  99.1 1.9 collective-permute-start.4
  101.0 3.4 %collective-permute-start.5 = (bf16[160,512]{1,0:T(8,128)(2,1)S(1)}, bf16[160,512]{1,0:T(8,128)(2,1)S(1)}, u32[]{:S(2)}, u32[]{:S(2)}) collective-permute-start(bf16[160,512]{1,0:T(8,128)(2,1)S(1)} %copy-done.12), channel_id=1, source_target_pairs={{0,1},{1,2},{2,3},{3,0},{4,5},{5,6},{6,7},{7,4},{8,9},{9,10},{10,1... | collective-permute-start | bytes 491528 | tf_op jit(solution)/shard_map/ppermute | solution.py:269
  104.4 1.9 collective-permute-start.6
  106.4 2.6 %collective-permute-done.5.refs_1_ = bf16[160,512]{1,0:T(8,128)(2,1)S(1)} collective-permute-done((bf16[160,512]{1,0:T(8,128)(2,1)S(1)}, bf16[160,512]{1,0:T(8,128)(2,1)S(1)}, u32[]{:S(2)}, u32[]{:S(2)}) %collective-permute-start.5) | collective-permute-done | bytes 163872 | tf_op jit(solution)/shard_map/ppermute | solution.py:269
  109.0 3.3 %collective-permute-done.6.refs_2_ = bf16[160,512]{1,0:T(8,128)(2,1)S(1)} collective-permute-done((bf16[160,512]{1,0:T(8,128)(2,1)S(1)}, bf16[160,512]{1,0:T(8,128)(2,1)S(1)}, u32[]{:S(2)}, u32[]{:S(2)}) %collective-permute-start.6) | collective-permute-done | bytes 163872 | tf_op jit(solution)/shard_map/ppermute | solution.py:269
  112.3 14.6 %all-to-all-done.2.parts_ref = bf16[8,480,128]{2,1,0:T(8,128)(2,1)S(1)} async-done(((bf16[8,480,128]{2,1,0:T(8,128)(2,1)}), bf16[8,480,128]{2,1,0:T(8,128)(2,1)S(1)}, u32[]{:S(2)}, u32[]{:S(2)}) %all-to-all-start.2) | async-done | bytes 983072 | tf_op jit(solution)/shard_map/all_to_all | solution.py:248
  126.8 0.2 shard_map.131
  127.0 23.5 %all-gather.1 = bf16[3840,128]{1,0:T(8,128)(2,1)} all-gather(bf16[480,128]{1,0:T(8,128)(2,1)S(1)} %shard_map.131), channel_id=3, replica_groups=mesh['z'=8,'core'=2,'y'=8,'x'=4] {'y'}, dimensions={0}, use_global_device_ids=true | all-gather | bytes 1105920 | tf_op jit(solution)/shard_map/all_gather | solution.py:327
  150.5 0.0 all-gather.8.cloned.1.call-update
  150.5 7.2 %shard_map.132 = bf16[4,640,128]{2,1,0:T(8,128)(2,1)} custom-call(s32[1]{0:T(128)} %bitcast.11.x_ref, bf16[8,480,128]{2,1,0:T(8,128)(2,1)} %bitcast.43, f32[160,128]{1,0:T(8,128)} %get-tuple-element.45.prob_ref, bf16[4,448,1024]{2,1,0:T(8,128)(2,1)} %bitcast.41, bf16[224,1024]{1,0:T(8,128)(2,1)} %bitcast.48, bf16[224,1024]{1,0:T(8,128)(2,1)} %copy-done.1, ...), custom_call_target="tpu_custom_call" | custom-call | tf_op jit(solution)/shard_map/pallas_call | solution.py:28
  157.8 32.8 %all_to_all.25 = bf16[64,40,128]{2,1,0:T(8,128)(2,1)S(1)} all-to-all(bf16[64,40,128]{2,1,0:T(8,128)(2,1)} %bitcast.45), channel_id=1, replica_groups=mesh['z'=8,'core'=2,'y'=8,'x'=4] {'x','z','core'}, dimensions={0} | all-to-all | bytes 1310720 | tf_op jit(solution)/shard_map/all_to_all | solution.py:248
  190.5 0.6 shard_map.133
  191.1 21.9 %all_to_all.26 = bf16[16,32,512]{2,1,0:T(8,128)(2,1)S(1)} all-to-all(bf16[16,32,512]{2,1,0:T(8,128)(2,1)S(1)} %bitcast.37), channel_id=1, replica_groups=mesh['z'=8,'core'=2,'y'=8,'x'=4] {'z','core'}, dimensions={0} | all-to-all | bytes 1048576 | tf_op jit(solution)/shard_map/all_to_all | solution.py:248
  213.1 1.2 shard_map.134
  214.2 4.9 %shard_map.135 = (bf16[224,1024]{1,0:T(8,128)(2,1)}, bf16[224,1024]{1,0:T(8,128)(2,1)}, bf16[224,1024]{1,0:T(8,128)(2,1)}) custom-call(s32[1]{0:T(128)} %bitcast.11.x_ref, bf16[4,8,480,128]{3,2,1,0:T(8,128)(2,1)} %bitcast.44, bf16[160,512]{1,0:T(8,128)(2,1)} %get-tuple-element.48.refs_0_, bf16[160,512]{1,0:T(8,128)(2,1)} %copy-done.7, ...), custom_call_target="tpu_custom_call" | custom-call | tf_op jit(solution)/shard_map/pallas_call | solution.py:28
  (37 shorter events, 0.1 us)
Async XLA Ops:
  7.2 78.9 %all-gather.6.cloned.1.call-start = ((), (), s32[]{:S(2)}) async-start(), calls=%async_computation.5 | async-start | bytes 4587520 | tf_op jit(solution)/shard_map/all_gather | solution.py:272
  9.4 14.3 %copy-start.10 = (s32[16]{0:T(128)S(1)}, s32[16]{0:T(128)}, u32[]{:S(2)}) copy-start(s32[16]{0:T(128)} %param.15) | copy-start | bytes 196
  9.4 14.4 %copy-start.9 = (s32[16,16]{1,0:T(8,128)S(1)}, s32[16,16]{1,0:T(8,128)}, u32[]{:S(2)}) copy-start(s32[16,16]{1,0:T(8,128)} %param.16) | copy-start | bytes 3076
  9.4 15.3 %copy-start.3 = (bf16[1,1024,224]{1,2,0:T(8,128)(2,1)S(1)}, bf16[1,1024,224]{1,2,0:T(8,128)(2,1)}, u32[]{:S(2)}) copy-start(bf16[1,1024,224]{1,2,0:T(8,128)(2,1)} %param.14) | copy-start | bytes 1376260
  11.8 29.2 %all-to-all-start = ((bf16[16,32,512]{2,1,0:T(8,128)(2,1)}), bf16[16,32,512]{2,1,0:T(8,128)(2,1)S(1)}, u32[]{:S(2)}, u32[]{:S(2)}) async-start(bf16[16,32,512]{2,1,0:T(8,128)(2,1)} %shard_map.128), calls=%async_computation | async-start | bytes 1048576 | tf_op jit(solution)/shard_map/all_to_all | solution.py:248
  24.7 20.2 %collective-permute-start.1 = (bf16[224,1024]{1,0:T(8,128)(2,1)S(1)}, bf16[224,1024]{1,0:T(8,128)(2,1)S(1)}, u32[]{:S(2)}, u32[]{:S(2)}) collective-permute-start(bf16[224,1024]{1,0:T(8,128)(2,1)S(1)} %bitcast.49), channel_id=1, source_target_pairs={{0,3},{1,0},{2,1},{3,2},{4,7},{5,4},{6,5},{7,6},{8,11},{9,8},{10,9... | collective-permute-start | bytes 1376264 | tf_op jit(solution)/shard_map/ppermute | solution.py:269
  29.1 24.5 %collective-permute-start = (bf16[224,1024]{1,0:T(8,128)(2,1)S(1)}, bf16[224,1024]{1,0:T(8,128)(2,1)S(1)}, u32[]{:S(2)}, u32[]{:S(2)}) collective-permute-start(bf16[224,1024]{1,0:T(8,128)(2,1)S(1)} %bitcast.50), channel_id=1, source_target_pairs={{0,1},{1,2},{2,3},{3,0},{4,5},{5,6},{6,7},{7,4},{8,9},{9,10},{10,1... | collective-permute-start | bytes 1376264 | tf_op jit(solution)/shard_map/ppermute | solution.py:269
  44.9 41.2 %copy-start = (bf16[224,1024]{1,0:T(8,128)(2,1)}, bf16[224,1024]{1,0:T(8,128)(2,1)S(1)}, u32[]{:S(2)}) copy-start(bf16[224,1024]{1,0:T(8,128)(2,1)S(1)} %collective-permute-done.1.refs_3_) | copy-start | bytes 1376260
  53.7 32.4 %copy-start.1 = (bf16[224,1024]{1,0:T(8,128)(2,1)}, bf16[224,1024]{1,0:T(8,128)(2,1)S(1)}, u32[]{:S(2)}) copy-start(bf16[224,1024]{1,0:T(8,128)(2,1)S(1)} %collective-permute-done.refs_2_) | copy-start | bytes 1376260
  53.7 32.4 %all-to-all-start.1 = ((bf16[64,40,128]{2,1,0:T(8,128)(2,1)}), bf16[64,40,128]{2,1,0:T(8,128)(2,1)S(1)}, u32[]{:S(2)}, u32[]{:S(2)}) async-start(bf16[64,40,128]{2,1,0:T(8,128)(2,1)} %bitcast.12), calls=%async_computation.1 | async-start | bytes 1310720 | tf_op jit(solution)/shard_map/all_to_all | solution.py:248
  62.4 18.2 %collective-permute-start.3 = (bf16[224,512]{1,0:T(8,128)(2,1)S(1)}, bf16[224,512]{1,0:T(8,128)(2,1)S(1)}, u32[]{:S(2)}, u32[]{:S(2)}) collective-permute-start(bf16[224,512]{1,0:T(8,128)(2,1)S(1)} %slice.23), channel_id=1, source_target_pairs={{0,3},{1,0},{2,1},{3,2},{4,7},{5,4},{6,5},{7,6},{8,11},{9,8},{10,9... | collective-permute-start | bytes 688136 | tf_op jit(solution)/shard_map/ppermute | solution.py:269
  67.1 18.9 %collective-permute-start.2 = (bf16[224,512]{1,0:T(8,128)(2,1)S(1)}, bf16[224,512]{1,0:T(8,128)(2,1)S(1)}, u32[]{:S(2)}, u32[]{:S(2)}) collective-permute-start(bf16[224,512]{1,0:T(8,128)(2,1)S(1)} %slice.22), channel_id=1, source_target_pairs={{0,1},{1,2},{2,3},{3,0},{4,5},{5,6},{6,7},{7,4},{8,9},{9,10},{10,1... | collective-permute-start | bytes 688136 | tf_op jit(solution)/shard_map/ppermute | solution.py:269
  80.6 5.4 %copy-start.4 = (bf16[224,512]{1,0:T(8,128)(2,1)}, bf16[224,512]{1,0:T(8,128)(2,1)S(1)}, u32[]{:S(2)}) copy-start(bf16[224,512]{1,0:T(8,128)(2,1)S(1)} %collective-permute-done.3.refs_5_) | copy-start | bytes 688132
  86.0 0.7 copy-start.5
  86.0 0.9 copy-start.2
  92.1 7.0 %copy-start.13 = (bf16[160,512]{1,0:T(8,128)(2,1)S(1)}, bf16[160,512]{1,0:T(8,128)(2,1)}, u32[]{:S(2)}) copy-start(bf16[160,512]{1,0:T(8,128)(2,1)} %get-tuple-element.41) | copy-start | bytes 491524
  92.1 8.9 %copy-start.12 = (bf16[160,512]{1,0:T(8,128)(2,1)S(1)}, bf16[160,512]{1,0:T(8,128)(2,1)}, u32[]{:S(2)}) copy-start(bf16[160,512]{1,0:T(8,128)(2,1)} %get-tuple-element.42) | copy-start | bytes 491524
  92.1 12.3 %copy-start.11 = (bf16[160,512]{1,0:T(8,128)(2,1)S(1)}, bf16[160,512]{1,0:T(8,128)(2,1)}, u32[]{:S(2)}) copy-start(bf16[160,512]{1,0:T(8,128)(2,1)} %get-tuple-element.43) | copy-start | bytes 491524
  92.1 34.7 %all-to-all-start.2 = ((bf16[8,480,128]{2,1,0:T(8,128)(2,1)}), bf16[8,480,128]{2,1,0:T(8,128)(2,1)S(1)}, u32[]{:S(2)}, u32[]{:S(2)}) async-start(bf16[8,480,128]{2,1,0:T(8,128)(2,1)} %get-tuple-element.39), calls=%async_computation.2 | async-start | bytes 1966080 | tf_op jit(solution)/shard_map/all_to_all | solution.py:248
  99.0 115.2 %all-gather.8.cloned.1.call-start = ((), (), s32[]{:S(2)}) async-start(), calls=%async_computation.6 | async-start | bytes 4915200 | tf_op jit(solution)/shard_map/all_gather | solution.py:328
  99.1 7.2 %collective-permute-start.4 = (bf16[160,512]{1,0:T(8,128)(2,1)S(1)}, bf16[160,512]{1,0:T(8,128)(2,1)S(1)}, u32[]{:S(2)}, u32[]{:S(2)}) collective-permute-start(bf16[160,512]{1,0:T(8,128)(2,1)S(1)} %copy-done.13), channel_id=1, source_target_pairs={{0,3},{1,0},{2,1},{3,2},{4,7},{5,4},{6,5},{7,6},{8,11},{9,8},{10,9... | collective-permute-start | bytes 491528 | tf_op jit(solution)/shard_map/ppermute | solution.py:269
  101.0 8.0 %collective-permute-start.5 = (bf16[160,512]{1,0:T(8,128)(2,1)S(1)}, bf16[160,512]{1,0:T(8,128)(2,1)S(1)}, u32[]{:S(2)}, u32[]{:S(2)}) collective-permute-start(bf16[160,512]{1,0:T(8,128)(2,1)S(1)} %copy-done.12), channel_id=1, source_target_pairs={{0,1},{1,2},{2,3},{3,0},{4,5},{5,6},{6,7},{7,4},{8,9},{9,10},{10,1... | collective-permute-start | bytes 491528 | tf_op jit(solution)/shard_map/ppermute | solution.py:269
  104.4 7.9 %collective-permute-start.6 = (bf16[160,512]{1,0:T(8,128)(2,1)S(1)}, bf16[160,512]{1,0:T(8,128)(2,1)S(1)}, u32[]{:S(2)}, u32[]{:S(2)}) collective-permute-start(bf16[160,512]{1,0:T(8,128)(2,1)S(1)} %copy-done.11), channel_id=1, source_target_pairs={{0,2},{1,3},{2,0},{3,1},{4,6},{5,7},{6,4},{7,5},{8,10},{9,11},{10,... | collective-permute-start | bytes 491528 | tf_op jit(solution)/shard_map/ppermute | solution.py:269
  106.3 51.4 %copy-start.6 = (bf16[160,512]{1,0:T(8,128)(2,1)}, bf16[160,512]{1,0:T(8,128)(2,1)S(1)}, u32[]{:S(2)}) copy-start(bf16[160,512]{1,0:T(8,128)(2,1)S(1)} %collective-permute-done.4.refs_3_) | copy-start | bytes 491524
  109.0 48.7 %copy-start.7 = (bf16[160,512]{1,0:T(8,128)(2,1)}, bf16[160,512]{1,0:T(8,128)(2,1)S(1)}, u32[]{:S(2)}) copy-start(bf16[160,512]{1,0:T(8,128)(2,1)S(1)} %collective-permute-done.5.refs_1_) | copy-start | bytes 491524
  112.3 45.5 %copy-start.8 = (bf16[160,512]{1,0:T(8,128)(2,1)}, bf16[160,512]{1,0:T(8,128)(2,1)S(1)}, u32[]{:S(2)}) copy-start(bf16[160,512]{1,0:T(8,128)(2,1)S(1)} %collective-permute-done.6.refs_2_) | copy-start | bytes 491524
Sparse Core Ops, SparseCore 0:
  10.1 75.1 all-gather.5
  150.6 57.3 all-gather.7

commit v10 on v9

--- a/solution.py
+++ b/solution.py
@@ -271,6 +271,7 @@
     gates = jnp.concatenate([w_gate[0], w_up[0]], axis=0)
     gates = lax.all_gather(gates, "x", axis=0, tiled=False)
     down = w_down[0].T
+    right, left = shift(down, 1), shift(down, 3)
 
     packed = call(
         pack_kernel,
@@ -283,9 +284,7 @@
     mine = (expert_slot == lax.axis_index(GROUP)).astype(F32)
     mark = lax.pad(mine, jnp.zeros((), F32), ((P_LANE, 16, 0),))[None]
     spread = exchange(packed, GROUP).reshape(groups * BLK, LANES)
-    info, down_late = lax.optimization_barrier((info, down))
-    right, left = shift(down_late, 1), shift(down_late, 3)
-    spread, info = lax.optimization_barrier((spread, info))
+    spread, info, right, left = lax.optimization_barrier((spread, info, right, left))
     sent, pick = call(
         select_kernel,
         (
@@ -295,7 +294,6 @@
         (spread, info),
         scratch_shapes=[pltpu.VMEM((4 * total, 128), F32)],
     )
-    sent, right, left = lax.optimization_barrier((sent, right, left))
     half = hid // 2
     panels = [gates, down, right, left, shift(right[:, 0:half], 1), shift(left[:, half:], 3)]
     pieces = (share_x * groups, 4 * picked // share_x, 128)
@@ -354,6 +352,7 @@
         scratch_shapes=[pltpu.VMEM((4 * total, 128), F32)],
     )
     home = exchange(summed.reshape(groups, BLK, LANES), GROUP).reshape(groups * BLK, LANES)
+    home, *weights = lax.optimization_barrier((home, *weights))
     out, dx = call(
         unpack_kernel,
         (jax.ShapeDtypeStruct((width, groups * BLK), BF16),) * 2,

time: 227 us -> 216 us (0.952)
  blocking collectives: 78.2 us -> 58.5 us
  starting transfers between devices: 47.7 us -> 52.9 us
  waiting for transfers between devices: 56.9 us -> 59.2 us
    all_to_all x2 -> x1, blocking collectives: 54.7 us -> 35.1 us  [exchange(): return lax.all_to_all(array, axis, split_axis=0, concat_axis=0, tiled=True)]
    ppermute x7, waiting for transfers between devices: 32.3 us -> 19.6 us  [shift(): return lax.ppermute(array, 'x', shifts[d])]
    all_gather x1, waiting for transfers between devices: 0.01 us -> 11.3 us  [body(): all_act = lax.all_gather(act, 'x', axis=0, tiled=False)]
    all_to_all x3 -> x4, waiting for transfers between devices: 24.5 us -> 28.3 us  [exchange(): return lax.all_to_all(array, axis, split_axis=0, concat_axis=0, tiled=True)]
    ppermute x7, starting transfers between devices: 20.2 us -> 23.8 us  [shift(): return lax.ppermute(array, 'x', shifts[d])]
    all_to_all x3 -> x4, starting transfers between devices: 27.4 us -> 29 us  [exchange(): return lax.all_to_all(array, axis, split_axis=0, concat_axis=0, tiled=True)]
  transfers between devices with their start and end apart: 12 -> 13, of which waited for: 8 -> 7; matrix products, arithmetic and copies ran while one was open for 1% -> 1% of each run, Pallas kernels for 6% -> 9%
where the time goes in v10:
time: 216 us; the launch traced here: 215 us
  waiting for transfers between devices  59.2 us (27%)
  blocking collectives  58.5 us (27%)
  starting transfers between devices  52.9 us (24%)
  Pallas kernels  24.7 us (11%)
  between operations  14.4 us (7%)
  other arithmetic  3.36 us (2%)
    all_to_all x1, blocking collectives, exchange(): return lax.all_to_all(array, axis, split_axis=0, concat_axis=0, tiled=True)  35.1 us
    all_to_all x4, starting transfers between devices, exchange(): return lax.all_to_all(array, axis, split_axis=0, concat_axis=0, tiled=True)  29 us
    all_to_all x4, waiting for transfers between devices, exchange(): return lax.all_to_all(array, axis, split_axis=0, concat_axis=0, tiled=True)  28.3 us
    pallas_call x8, Pallas kernels, call(): pl.pallas_call(kernel, out_shape=out_shape, compiler_params=pltpu.Compile...  24.7 us
    ppermute x7, starting transfers between devices, shift(): return lax.ppermute(array, 'x', shifts[d])  23.8 us
    all_gather x1, blocking collectives, body(): act = lax.all_gather(act, 'y', axis=0, tiled=False)  23.5 us
    ppermute x7, waiting for transfers between devices, shift(): return lax.ppermute(array, 'x', shifts[d])  19.6 us
    all_gather x1, waiting for transfers between devices, body(): all_act = lax.all_gather(act, 'x', axis=0, tiled=False)  11.3 us
  transfers between devices with their start and end apart: 13, of which 7 were waited for; matrix products, arithmetic and copies ran while one was open for 1% of the time, Pallas kernels for 9%

profile of v10, /device:TPU:1, one launch (start us, length us, event | category | flops | bytes accessed | tf_op | source)
XLA Modules:
  0.0 214.7 jit_solution(7698728952607255134)
XLA Ops:
  7.2 0.0 copy-start.3
  7.2 0.0 all-gather.6.cloned.1.call-start
  7.2 2.2 %pad_maximum_fusion = bf16[448,1024]{1,0:T(8,128)(2,1)} fusion(bf16[224,1024]{1,0:T(8,128)(2,1)} %bitcast.50, bf16[224,1024]{1,0:T(8,128)(2,1)} %bitcast.51), kind=kLoop, calls=%fused_computation | loop fusion | flops 1835008 | bytes 1835008 | tf_op jit(solution)/shard_map/concatenate | solution.py:271
  9.4 0.0 all-gather.6.cloned.1.call-update
  9.5 5.2 %collective-permute-start.1 = (bf16[224,1024]{1,0:T(8,128)(2,1)S(1)}, bf16[224,1024]{1,0:T(8,128)(2,1)S(1)}, u32[]{:S(2)}, u32[]{:S(2)}) collective-permute-start(bf16[224,1024]{1,0:T(8,128)(2,1)S(1)} %bitcast.48), channel_id=1, source_target_pairs={{0,3},{1,0},{2,1},{3,2},{4,7},{5,4},{6,5},{7,6},{8,11},{9,8},{10,9... | collective-permute-start | bytes 1376264 | tf_op jit(solution)/shard_map/ppermute | solution.py:269
  14.7 1.9 collective-permute-start
  16.6 2.4 %shard_map.128 = bf16[16,32,512]{2,1,0:T(8,128)(2,1)} custom-call(bf16[224,512]{1,0:T(8,128)(2,1)} %bitcast.52, bf16[224,512]{1,0:T(8,128)(2,1)} %bitcast.53, bf16[16,512]{1,0:T(8,128)(2,1)} %bitcast.54, s32[10,1,16]{2,1,0:T(1,128)} %bitcast.55), custom_call_target="tpu_custom_call" | custom-call | tf_op jit(solution)/shard_map/pallas_call | solution.py:28
  19.0 11.3 %all-to-all-start = ((bf16[16,32,512]{2,1,0:T(8,128)(2,1)}), bf16[16,32,512]{2,1,0:T(8,128)(2,1)S(1)}, u32[]{:S(2)}, u32[]{:S(2)}) async-start(bf16[16,32,512]{2,1,0:T(8,128)(2,1)} %shard_map.128), calls=%async_computation | async-start | bytes 1048576 | tf_op jit(solution)/shard_map/all_to_all | solution.py:248
  30.3 0.1 fusion.5
  30.3 0.1 multiply_reduce_fusion.1
  30.5 0.1 multiply_reduce_fusion
  30.6 0.1 select_reduce_fusion
  30.7 0.1 fusion
  30.8 0.1 reshape.243
  31.0 0.1 reshape.250
  31.1 0.1 reshape.247
  31.3 0.0 copy-start.1
  31.3 16.3 %all-to-all-done = bf16[16,32,512]{2,1,0:T(8,128)(2,1)S(1)} async-done(((bf16[16,32,512]{2,1,0:T(8,128)(2,1)}), bf16[16,32,512]{2,1,0:T(8,128)(2,1)S(1)}, u32[]{:S(2)}, u32[]{:S(2)}) %all-to-all-start) | async-done | bytes 524320 | tf_op jit(solution)/shard_map/all_to_all | solution.py:248
  47.6 0.2 copy.18.info_ref
  47.8 2.4 %shard_map.129 = (bf16[2560,128]{1,0:T(8,128)(2,1)}, bf16[640,512]{1,0:T(8,128)(2,1)S(1)}) custom-call(bf16[512,512]{1,0:T(8,128)(2,1)S(1)} %bitcast.37, s32[640,3]{1,0:T(8,128)S(1)} %copy.18.info_ref), custom_call_target="tpu_custom_call" | custom-call | tf_op jit(solution)/shard_map/pallas_call | solution.py:28
  50.1 6.1 %all-to-all-start.1 = ((bf16[64,40,128]{2,1,0:T(8,128)(2,1)}), bf16[64,40,128]{2,1,0:T(8,128)(2,1)S(1)}, u32[]{:S(2)}, u32[]{:S(2)}) async-start(bf16[64,40,128]{2,1,0:T(8,128)(2,1)} %bitcast.13), calls=%async_computation.1 | async-start | bytes 1310720 | tf_op jit(solution)/shard_map/all_to_all | solution.py:248
  56.3 4.7 %collective-permute-start.3 = (bf16[224,512]{1,0:T(8,128)(2,1)S(1)}, bf16[224,512]{1,0:T(8,128)(2,1)S(1)}, u32[]{:S(2)}, u32[]{:S(2)}) collective-permute-start(bf16[224,512]{1,0:T(8,128)(2,1)S(1)} %slice.23), channel_id=1, source_target_pairs={{0,3},{1,0},{2,1},{3,2},{4,7},{5,4},{6,5},{7,6},{8,11},{9,8},{10,9... | collective-permute-start | bytes 688136 | tf_op jit(solution)/shard_map/ppermute | solution.py:269
  61.0 1.9 collective-permute-start.2
  63.0 0.7 pad_convert_fusion
  63.6 12.2 %collective-permute-done.3.refs_5_ = bf16[224,512]{1,0:T(8,128)(2,1)S(1)} collective-permute-done((bf16[224,512]{1,0:T(8,128)(2,1)S(1)}, bf16[224,512]{1,0:T(8,128)(2,1)S(1)}, u32[]{:S(2)}, u32[]{:S(2)}) %collective-permute-start.3) | collective-permute-done | bytes 229408 | tf_op jit(solution)/shard_map/ppermute | solution.py:269
  75.8 0.7 collective-permute-done.2.refs_4_
  76.5 0.0 all-gather.6.cloned.1.call-done
  76.6 0.6 copy-done.5
  77.2 0.2 copy-done.2
  77.4 5.1 %shard_map.130 = (bf16[160,512]{1,0:T(8,128)(2,1)}, bf16[160,512]{1,0:T(8,128)(2,1)}, bf16[160,512]{1,0:T(8,128)(2,1)}, bf16[160,512]{1,0:T(8,128)(2,1)}, bf16[8...) custom-call(s32[1]{0:T(128)} %bitcast.12.x_ref, bf16[4,640,128]{2,1,0:T(8,128)(2,1)} %bitcast.45, f32[1,256]{1,0:T(1,128)} %bitcast.56, ...), custom_call_target="tpu_custom_call" | custom-call | tf_op jit(solution)/shard_map/pallas_call | solution.py:28
  82.6 6.8 %all-to-all-start.2 = ((bf16[8,480,128]{2,1,0:T(8,128)(2,1)}), bf16[8,480,128]{2,1,0:T(8,128)(2,1)S(1)}, u32[]{:S(2)}, u32[]{:S(2)}) async-start(bf16[8,480,128]{2,1,0:T(8,128)(2,1)} %get-tuple-element.37), calls=%async_computation.2 | async-start | bytes 1966080 | tf_op jit(solution)/shard_map/all_to_all | solution.py:248
  89.3 0.0 all-gather.8.cloned.1.call-start
  89.4 4.6 %collective-permute-start.4 = (bf16[160,512]{1,0:T(8,128)(2,1)S(1)}, bf16[160,512]{1,0:T(8,128)(2,1)S(1)}, u32[]{:S(2)}, u32[]{:S(2)}) collective-permute-start(bf16[160,512]{1,0:T(8,128)(2,1)S(1)} %copy-done.13), channel_id=1, source_target_pairs={{0,3},{1,0},{2,1},{3,2},{4,7},{5,4},{6,5},{7,6},{8,11},{9,8},{10,9... | collective-permute-start | bytes 491528 | tf_op jit(solution)/shard_map/ppermute | solution.py:269
  94.0 1.9 collective-permute-start.5
  95.9 3.5 %collective-permute-start.6 = (bf16[160,512]{1,0:T(8,128)(2,1)S(1)}, bf16[160,512]{1,0:T(8,128)(2,1)S(1)}, u32[]{:S(2)}, u32[]{:S(2)}) collective-permute-start(bf16[160,512]{1,0:T(8,128)(2,1)S(1)} %copy-done.11), channel_id=1, source_target_pairs={{0,2},{1,3},{2,0},{3,1},{4,6},{5,7},{6,4},{7,5},{8,10},{9,11},{10,... | collective-permute-start | bytes 491528 | tf_op jit(solution)/shard_map/ppermute | solution.py:269
  99.5 6.7 %collective-permute-done.5.refs_1_ = bf16[160,512]{1,0:T(8,128)(2,1)S(1)} collective-permute-done((bf16[160,512]{1,0:T(8,128)(2,1)S(1)}, bf16[160,512]{1,0:T(8,128)(2,1)S(1)}, u32[]{:S(2)}, u32[]{:S(2)}) %collective-permute-start.5) | collective-permute-done | bytes 163872 | tf_op jit(solution)/shard_map/ppermute | solution.py:269
  106.2 10.9 %all-to-all-done.2.parts_ref = bf16[8,480,128]{2,1,0:T(8,128)(2,1)S(1)} async-done(((bf16[8,480,128]{2,1,0:T(8,128)(2,1)}), bf16[8,480,128]{2,1,0:T(8,128)(2,1)S(1)}, u32[]{:S(2)}, u32[]{:S(2)}) %all-to-all-start.2) | async-done | bytes 983072 | tf_op jit(solution)/shard_map/all_to_all | solution.py:248
  117.1 0.2 shard_map.131
  117.3 23.5 %all-gather.1 = bf16[3840,128]{1,0:T(8,128)(2,1)} all-gather(bf16[480,128]{1,0:T(8,128)(2,1)S(1)} %shard_map.131), channel_id=3, replica_groups=mesh['z'=8,'core'=2,'y'=8,'x'=4] {'y'}, dimensions={0}, use_global_device_ids=true | all-gather | bytes 1105920 | tf_op jit(solution)/shard_map/all_gather | solution.py:325
  140.8 0.0 all-gather.8.cloned.1.call-update
  140.8 7.2 %shard_map.132 = bf16[4,640,128]{2,1,0:T(8,128)(2,1)} custom-call(s32[1]{0:T(128)} %bitcast.12.x_ref, bf16[8,480,128]{2,1,0:T(8,128)(2,1)} %bitcast.42, f32[160,128]{1,0:T(8,128)} %get-tuple-element.43.prob_ref, bf16[4,448,1024]{2,1,0:T(8,128)(2,1)} %bitcast.40, bf16[224,1024]{1,0:T(8,128)(2,1)} %bitcast.47, bf16[224,1024]{1,0:T(8,128)(2,1)} %copy-done.1, ...), custom_call_target="tpu_custom_call" | custom-call | tf_op jit(solution)/shard_map/pallas_call | solution.py:28
  148.0 35.1 %all_to_all.25 = bf16[64,40,128]{2,1,0:T(8,128)(2,1)S(1)} all-to-all(bf16[64,40,128]{2,1,0:T(8,128)(2,1)} %bitcast.44), channel_id=1, replica_groups=mesh['z'=8,'core'=2,'y'=8,'x'=4] {'x','z','core'}, dimensions={0} | all-to-all | bytes 1310720 | tf_op jit(solution)/shard_map/all_to_all | solution.py:248
  183.1 1.4 shard_map.133
  184.5 4.8 %all-to-all-start.4 = ((bf16[16,32,512]{2,1,0:T(8,128)(2,1)}), bf16[16,32,512]{2,1,0:T(8,128)(2,1)S(1)}, u32[]{:S(2)}, u32[]{:S(2)}) async-start(bf16[16,32,512]{2,1,0:T(8,128)(2,1)} %bitcast.22), calls=%async_computation.4 | async-start | bytes 1048576 | tf_op jit(solution)/shard_map/all_to_all | solution.py:248
  189.3 11.3 %all-gather.8.cloned.1.call-done = bf16[32,480,128]{2,1,0:T(8,128)(2,1)} async-done(((bf16[8,480,128]{2,1,0:T(8,128)(2,1)}), bf16[32,480,128]{2,1,0:T(8,128)(2,1)}) %all-gather.8.cloned.1.call-update) | async-done | bytes 3932176 | tf_op jit(solution)/shard_map/all_gather | solution.py:326
  200.6 4.9 %shard_map.134 = (bf16[224,1024]{1,0:T(8,128)(2,1)}, bf16[224,1024]{1,0:T(8,128)(2,1)}, bf16[224,1024]{1,0:T(8,128)(2,1)}) custom-call(s32[1]{0:T(128)} %bitcast.12.x_ref, bf16[4,8,480,128]{3,2,1,0:T(8,128)(2,1)} %bitcast.43, bf16[160,512]{1,0:T(8,128)(2,1)} %get-tuple-element.44.refs_0_, bf16[160,512]{1,0:T(8,128)(2,1)} %copy-done.7, ...), custom_call_target="tpu_custom_call" | custom-call | tf_op jit(solution)/shard_map/pallas_call | solution.py:28
  205.5 1.1 all-to-all-done.4
  206.7 1.2 shard_map.135
  (38 shorter events, 0.2 us)
Async XLA Ops:
  7.2 2.3 %copy-start.3 = (bf16[1,1024,224]{1,2,0:T(8,128)(2,1)S(1)}, bf16[1,1024,224]{1,2,0:T(8,128)(2,1)}, u32[]{:S(2)}) copy-start(bf16[1,1024,224]{1,2,0:T(8,128)(2,1)} %param.14) | copy-start | bytes 1376260
  7.2 69.4 %all-gather.6.cloned.1.call-start = ((), (), s32[]{:S(2)}) async-start(), calls=%async_computation.5 | async-start | bytes 4587520 | tf_op jit(solution)/shard_map/all_gather | solution.py:272
  9.4 20.9 %copy-start.10 = (s32[16]{0:T(128)S(1)}, s32[16]{0:T(128)}, u32[]{:S(2)}) copy-start(s32[16]{0:T(128)} %param.15) | copy-start | bytes 196
  9.4 20.9 %copy-start.9 = (s32[16,16]{1,0:T(8,128)S(1)}, s32[16,16]{1,0:T(8,128)}, u32[]{:S(2)}) copy-start(s32[16,16]{1,0:T(8,128)} %param.16) | copy-start | bytes 3076
  9.5 21.8 %collective-permute-start.1 = (bf16[224,1024]{1,0:T(8,128)(2,1)S(1)}, bf16[224,1024]{1,0:T(8,128)(2,1)S(1)}, u32[]{:S(2)}, u32[]{:S(2)}) collective-permute-start(bf16[224,1024]{1,0:T(8,128)(2,1)S(1)} %bitcast.48), channel_id=1, source_target_pairs={{0,3},{1,0},{2,1},{3,2},{4,7},{5,4},{6,5},{7,6},{8,11},{9,8},{10,9... | collective-permute-start | bytes 1376264 | tf_op jit(solution)/shard_map/ppermute | solution.py:269
  14.7 16.6 %collective-permute-start = (bf16[224,1024]{1,0:T(8,128)(2,1)S(1)}, bf16[224,1024]{1,0:T(8,128)(2,1)S(1)}, u32[]{:S(2)}, u32[]{:S(2)}) collective-permute-start(bf16[224,1024]{1,0:T(8,128)(2,1)S(1)} %bitcast.49), channel_id=1, source_target_pairs={{0,1},{1,2},{2,3},{3,0},{4,5},{5,6},{6,7},{7,4},{8,9},{9,10},{10,1... | collective-permute-start | bytes 1376264 | tf_op jit(solution)/shard_map/ppermute | solution.py:269
  19.0 28.6 %all-to-all-start = ((bf16[16,32,512]{2,1,0:T(8,128)(2,1)}), bf16[16,32,512]{2,1,0:T(8,128)(2,1)S(1)}, u32[]{:S(2)}, u32[]{:S(2)}) async-start(bf16[16,32,512]{2,1,0:T(8,128)(2,1)} %shard_map.128), calls=%async_computation | async-start | bytes 1048576 | tf_op jit(solution)/shard_map/all_to_all | solution.py:248
  31.3 45.3 %copy-start = (bf16[224,1024]{1,0:T(8,128)(2,1)}, bf16[224,1024]{1,0:T(8,128)(2,1)S(1)}, u32[]{:S(2)}) copy-start(bf16[224,1024]{1,0:T(8,128)(2,1)S(1)} %collective-permute-done.1.refs_3_) | copy-start | bytes 1376260
  31.3 45.2 %copy-start.1 = (bf16[224,1024]{1,0:T(8,128)(2,1)}, bf16[224,1024]{1,0:T(8,128)(2,1)S(1)}, u32[]{:S(2)}) copy-start(bf16[224,1024]{1,0:T(8,128)(2,1)S(1)} %collective-permute-done.refs_2_) | copy-start | bytes 1376260
  50.1 26.4 %all-to-all-start.1 = ((bf16[64,40,128]{2,1,0:T(8,128)(2,1)}), bf16[64,40,128]{2,1,0:T(8,128)(2,1)S(1)}, u32[]{:S(2)}, u32[]{:S(2)}) async-start(bf16[64,40,128]{2,1,0:T(8,128)(2,1)} %bitcast.13), calls=%async_computation.1 | async-start | bytes 1310720 | tf_op jit(solution)/shard_map/all_to_all | solution.py:248
  56.3 19.5 %collective-permute-start.3 = (bf16[224,512]{1,0:T(8,128)(2,1)S(1)}, bf16[224,512]{1,0:T(8,128)(2,1)S(1)}, u32[]{:S(2)}, u32[]{:S(2)}) collective-permute-start(bf16[224,512]{1,0:T(8,128)(2,1)S(1)} %slice.23), channel_id=1, source_target_pairs={{0,3},{1,0},{2,1},{3,2},{4,7},{5,4},{6,5},{7,6},{8,11},{9,8},{10,9... | collective-permute-start | bytes 688136 | tf_op jit(solution)/shard_map/ppermute | solution.py:269
  61.0 15.5 %collective-permute-start.2 = (bf16[224,512]{1,0:T(8,128)(2,1)S(1)}, bf16[224,512]{1,0:T(8,128)(2,1)S(1)}, u32[]{:S(2)}, u32[]{:S(2)}) collective-permute-start(bf16[224,512]{1,0:T(8,128)(2,1)S(1)} %slice.22), channel_id=1, source_target_pairs={{0,1},{1,2},{2,3},{3,0},{4,5},{5,6},{6,7},{7,4},{8,9},{9,10},{10,1... | collective-permute-start | bytes 688136 | tf_op jit(solution)/shard_map/ppermute | solution.py:269
  75.8 0.7 copy-start.4
  76.5 0.7 copy-start.5
  76.5 0.9 copy-start.2
  82.5 6.8 %copy-start.13 = (bf16[160,512]{1,0:T(8,128)(2,1)S(1)}, bf16[160,512]{1,0:T(8,128)(2,1)}, u32[]{:S(2)}) copy-start(bf16[160,512]{1,0:T(8,128)(2,1)} %get-tuple-element.39) | copy-start | bytes 491524
  82.6 11.4 %copy-start.12 = (bf16[160,512]{1,0:T(8,128)(2,1)S(1)}, bf16[160,512]{1,0:T(8,128)(2,1)}, u32[]{:S(2)}) copy-start(bf16[160,512]{1,0:T(8,128)(2,1)} %get-tuple-element.40) | copy-start | bytes 491524
  82.6 13.3 %copy-start.11 = (bf16[160,512]{1,0:T(8,128)(2,1)S(1)}, bf16[160,512]{1,0:T(8,128)(2,1)}, u32[]{:S(2)}) copy-start(bf16[160,512]{1,0:T(8,128)(2,1)} %get-tuple-element.41) | copy-start | bytes 491524
  82.6 34.5 %all-to-all-start.2 = ((bf16[8,480,128]{2,1,0:T(8,128)(2,1)}), bf16[8,480,128]{2,1,0:T(8,128)(2,1)S(1)}, u32[]{:S(2)}, u32[]{:S(2)}) async-start(bf16[8,480,128]{2,1,0:T(8,128)(2,1)} %get-tuple-element.37), calls=%async_computation.2 | async-start | bytes 1966080 | tf_op jit(solution)/shard_map/all_to_all | solution.py:248
  89.3 111.2 %all-gather.8.cloned.1.call-start = ((), (), s32[]{:S(2)}) async-start(), calls=%async_computation.6 | async-start | bytes 4915200 | tf_op jit(solution)/shard_map/all_gather | solution.py:326
  89.4 10.1 %collective-permute-start.4 = (bf16[160,512]{1,0:T(8,128)(2,1)S(1)}, bf16[160,512]{1,0:T(8,128)(2,1)S(1)}, u32[]{:S(2)}, u32[]{:S(2)}) collective-permute-start(bf16[160,512]{1,0:T(8,128)(2,1)S(1)} %copy-done.13), channel_id=1, source_target_pairs={{0,3},{1,0},{2,1},{3,2},{4,7},{5,4},{6,5},{7,6},{8,11},{9,8},{10,9... | collective-permute-start | bytes 491528 | tf_op jit(solution)/shard_map/ppermute | solution.py:269
  94.0 12.2 %collective-permute-start.5 = (bf16[160,512]{1,0:T(8,128)(2,1)S(1)}, bf16[160,512]{1,0:T(8,128)(2,1)S(1)}, u32[]{:S(2)}, u32[]{:S(2)}) collective-permute-start(bf16[160,512]{1,0:T(8,128)(2,1)S(1)} %copy-done.12), channel_id=1, source_target_pairs={{0,1},{1,2},{2,3},{3,0},{4,5},{5,6},{6,7},{7,4},{8,9},{9,10},{10,1... | collective-permute-start | bytes 491528 | tf_op jit(solution)/shard_map/ppermute | solution.py:269
  95.9 10.3 %collective-permute-start.6 = (bf16[160,512]{1,0:T(8,128)(2,1)S(1)}, bf16[160,512]{1,0:T(8,128)(2,1)S(1)}, u32[]{:S(2)}, u32[]{:S(2)}) collective-permute-start(bf16[160,512]{1,0:T(8,128)(2,1)S(1)} %copy-done.11), channel_id=1, source_target_pairs={{0,2},{1,3},{2,0},{3,1},{4,6},{5,7},{6,4},{7,5},{8,10},{9,11},{10,... | collective-permute-start | bytes 491528 | tf_op jit(solution)/shard_map/ppermute | solution.py:269
  99.5 48.5 %copy-start.6 = (bf16[160,512]{1,0:T(8,128)(2,1)}, bf16[160,512]{1,0:T(8,128)(2,1)S(1)}, u32[]{:S(2)}) copy-start(bf16[160,512]{1,0:T(8,128)(2,1)S(1)} %collective-permute-done.4.refs_3_) | copy-start | bytes 491524
  106.2 41.8 %copy-start.7 = (bf16[160,512]{1,0:T(8,128)(2,1)}, bf16[160,512]{1,0:T(8,128)(2,1)S(1)}, u32[]{:S(2)}) copy-start(bf16[160,512]{1,0:T(8,128)(2,1)S(1)} %collective-permute-done.5.refs_1_) | copy-start | bytes 491524
  106.2 41.8 %copy-start.8 = (bf16[160,512]{1,0:T(8,128)(2,1)}, bf16[160,512]{1,0:T(8,128)(2,1)S(1)}, u32[]{:S(2)}) copy-start(bf16[160,512]{1,0:T(8,128)(2,1)S(1)} %collective-permute-done.6.refs_2_) | copy-start | bytes 491524
  184.5 22.2 %all-to-all-start.4 = ((bf16[16,32,512]{2,1,0:T(8,128)(2,1)}), bf16[16,32,512]{2,1,0:T(8,128)(2,1)S(1)}, u32[]{:S(2)}, u32[]{:S(2)}) async-start(bf16[16,32,512]{2,1,0:T(8,128)(2,1)} %bitcast.22), calls=%async_computation.4 | async-start | bytes 1048576 | tf_op jit(solution)/shard_map/all_to_all | solution.py:248
Sparse Core Ops, SparseCore 0:
  10.1 64.8 all-gather.5
  140.9 59.6 all-gather.7

commit v11 on v10

--- a/solution.py
+++ b/solution.py
@@ -80,6 +80,24 @@
     pick = (columns == column).astype(BF16)
     pick_ref[...] = pick
     out_ref[...] = split_lanes(tmp_ref, dot(pick, rows, 1, 0))
+
+
+def join_kernel(gate_ref, up_ref, out_ref, buf_ref, sems):
+    width = gate_ref.shape[0]
+    half = width // 2
+    loads, stores = [], []
+    for i in range(4):
+        source = (gate_ref, up_ref)[i // 2].at[pl.ds(i % 2 * half, half)]
+        rows = pl.ds(i * half, half)
+        loads.append(pltpu.make_async_copy(source, buf_ref.at[rows], sems.at[0, i]))
+        stores.append(pltpu.make_async_copy(buf_ref.at[rows], out_ref.at[rows], sems.at[1, i]))
+    for load in loads:
+        load.start()
+    for load, store in zip(loads, stores):
+        load.wait()
+        store.start()
+    for store in stores:
+        store.wait()
 
 
 def panel_copies(x_ref, sources, gate_ref, down_ref, sems):
@@ -268,7 +286,16 @@
     def shift(array, d):
         return lax.ppermute(array, "x", shifts[d])
 
-    gates = jnp.concatenate([w_gate[0], w_up[0]], axis=0)
+    any_spec = pl.BlockSpec(memory_space=pl.ANY)
+    gates = call(
+        join_kernel,
+        jax.ShapeDtypeStruct((2 * width, hid), BF16),
+        (w_gate[0], w_up[0]),
+        VMEM_LARGE,
+        in_specs=[any_spec] * 2,
+        out_specs=any_spec,
+        scratch_shapes=[pltpu.VMEM((2 * width, hid), BF16), pltpu.SemaphoreType.DMA((2, 4))],
+    )
     gates = lax.all_gather(gates, "x", axis=0, tiled=False)
     down = w_down[0].T
     right, left = shift(down, 1), shift(down, 3)

time: 216 us -> 216 us (level)
  other arithmetic: 3.36 us -> 1.11 us
    concatenate x1 -> x0, other arithmetic: 2.2 us -> none  [body(): gates = jnp.concatenate([w_gate[0], w_up[0]], axis=0)]
    pallas_call x8 -> x9, Pallas kernels: 24.7 us -> 26.8 us  [call(): pl.pallas_call(kernel, out_shape=out_shape, compiler_params=pltpu.Compile...]
where the time goes in v11:
time: 216 us; the launch traced here: 215 us
  waiting for transfers between devices  59.5 us (28%)
  blocking collectives  58.8 us (27%)
  starting transfers between devices  52.6 us (24%)
  Pallas kernels  26.8 us (12%)
  between operations  14.4 us (7%)
    all_to_all x1, blocking collectives, exchange(): return lax.all_to_all(array, axis, split_axis=0, concat_axis=0, tiled=True)  35.3 us
    all_to_all x4, starting transfers between devices, exchange(): return lax.all_to_all(array, axis, split_axis=0, concat_axis=0, tiled=True)  28.7 us
    all_to_all x4, waiting for transfers between devices, exchange(): return lax.all_to_all(array, axis, split_axis=0, concat_axis=0, tiled=True)  28.2 us
    pallas_call x9, Pallas kernels, call(): pl.pallas_call(kernel, out_shape=out_shape, compiler_params=pltpu.Compile...  26.8 us
    ppermute x7, starting transfers between devices, shift(): return lax.ppermute(array, 'x', shifts[d])  23.8 us
    all_gather x1, blocking collectives, body(): act = lax.all_gather(act, 'y', axis=0, tiled=False)  23.5 us
    ppermute x7, waiting for transfers between devices, shift(): return lax.ppermute(array, 'x', shifts[d])  20 us
    all_gather x1, waiting for transfers between devices, body(): all_act = lax.all_gather(act, 'x', axis=0, tiled=False)  11.2 us
  transfers between devices with their start and end apart: 13, of which 7 were waited for; matrix products, arithmetic and copies ran while one was open for 1% of the time, Pallas kernels for 9%

profile of v11, /device:TPU:1, one launch (start us, length us, event | category | flops | bytes accessed | tf_op | source)
XLA Modules:
  0.0 214.7 jit_solution(1662358329880576077)
XLA Ops:
  7.2 0.0 all-gather.6.cloned.1.call-start
  7.2 2.0 shard_map.130
  9.3 0.0 all-gather.6.cloned.1.call-update
  9.3 5.2 %collective-permute-start.1 = (bf16[224,1024]{1,0:T(8,128)(2,1)}, bf16[224,1024]{1,0:T(8,128)(2,1)S(1)}, u32[]{:S(2)}, u32[]{:S(2)}) collective-permute-start(bf16[224,1024]{1,0:T(8,128)(2,1)} %bitcast.46), channel_id=1, source_target_pairs={{0,3},{1,0},{2,1},{3,2},{4,7},{5,4},{6,5},{7,6},{8,11},{9,8},{10,9... | collective-permute-start | bytes 1376264 | tf_op jit(solution)/shard_map/ppermute | solution.py:287
  14.5 1.9 collective-permute-start
  16.5 2.4 %shard_map.128 = bf16[16,32,512]{2,1,0:T(8,128)(2,1)} custom-call(bf16[224,512]{1,0:T(8,128)(2,1)} %bitcast.52, bf16[224,512]{1,0:T(8,128)(2,1)} %bitcast.53, bf16[16,512]{1,0:T(8,128)(2,1)} %bitcast.54, s32[10,1,16]{2,1,0:T(1,128)} %bitcast.55), custom_call_target="tpu_custom_call" | custom-call | tf_op jit(solution)/shard_map/pallas_call | solution.py:28
  18.9 11.3 %all-to-all-start = ((bf16[16,32,512]{2,1,0:T(8,128)(2,1)}), bf16[16,32,512]{2,1,0:T(8,128)(2,1)S(1)}, u32[]{:S(2)}, u32[]{:S(2)}) async-start(bf16[16,32,512]{2,1,0:T(8,128)(2,1)} %shard_map.128), calls=%async_computation | async-start | bytes 1048576 | tf_op jit(solution)/shard_map/all_to_all | solution.py:266
  30.1 0.1 fusion.5
  30.2 0.1 multiply_reduce_fusion.1
  30.4 0.1 multiply_reduce_fusion
  30.5 0.1 select_reduce_fusion
  30.6 0.1 fusion
  30.7 0.1 reshape.243
  30.8 0.1 reshape.250
  31.0 0.1 reshape.247
  31.2 0.0 copy-start
  31.2 0.0 copy-start.1
  31.2 16.3 %all-to-all-done = bf16[16,32,512]{2,1,0:T(8,128)(2,1)S(1)} async-done(((bf16[16,32,512]{2,1,0:T(8,128)(2,1)}), bf16[16,32,512]{2,1,0:T(8,128)(2,1)S(1)}, u32[]{:S(2)}, u32[]{:S(2)}) %all-to-all-start) | async-done | bytes 524320 | tf_op jit(solution)/shard_map/all_to_all | solution.py:266
  47.5 0.2 copy.18.info_ref
  47.6 2.4 %shard_map.129 = (bf16[2560,128]{1,0:T(8,128)(2,1)}, bf16[640,512]{1,0:T(8,128)(2,1)S(1)}) custom-call(bf16[512,512]{1,0:T(8,128)(2,1)S(1)} %bitcast.37, s32[640,3]{1,0:T(8,128)S(1)} %copy.18.info_ref), custom_call_target="tpu_custom_call" | custom-call | tf_op jit(solution)/shard_map/pallas_call | solution.py:28
  50.0 6.1 %all-to-all-start.1 = ((bf16[64,40,128]{2,1,0:T(8,128)(2,1)}), bf16[64,40,128]{2,1,0:T(8,128)(2,1)S(1)}, u32[]{:S(2)}, u32[]{:S(2)}) async-start(bf16[64,40,128]{2,1,0:T(8,128)(2,1)} %bitcast.13), calls=%async_computation.1 | async-start | bytes 1310720 | tf_op jit(solution)/shard_map/all_to_all | solution.py:266
  56.2 4.7 %collective-permute-start.3 = (bf16[224,512]{1,0:T(8,128)(2,1)S(1)}, bf16[224,512]{1,0:T(8,128)(2,1)S(1)}, u32[]{:S(2)}, u32[]{:S(2)}) collective-permute-start(bf16[224,512]{1,0:T(8,128)(2,1)S(1)} %slice.23), channel_id=1, source_target_pairs={{0,3},{1,0},{2,1},{3,2},{4,7},{5,4},{6,5},{7,6},{8,11},{9,8},{10,9... | collective-permute-start | bytes 688136 | tf_op jit(solution)/shard_map/ppermute | solution.py:287
  60.9 1.9 collective-permute-start.2
  62.8 0.6 pad_convert_fusion
  63.5 12.4 %collective-permute-done.3.refs_5_ = bf16[224,512]{1,0:T(8,128)(2,1)S(1)} collective-permute-done((bf16[224,512]{1,0:T(8,128)(2,1)S(1)}, bf16[224,512]{1,0:T(8,128)(2,1)S(1)}, u32[]{:S(2)}, u32[]{:S(2)}) %collective-permute-start.3) | collective-permute-done | bytes 229408 | tf_op jit(solution)/shard_map/ppermute | solution.py:287
  75.8 0.7 collective-permute-done.2.refs_4_
  76.5 0.0 all-gather.6.cloned.1.call-done
  76.6 0.6 copy-done.4
  77.2 0.3 copy-done.2
  77.5 5.1 %shard_map.131 = (bf16[160,512]{1,0:T(8,128)(2,1)}, bf16[160,512]{1,0:T(8,128)(2,1)}, bf16[160,512]{1,0:T(8,128)(2,1)}, bf16[160,512]{1,0:T(8,128)(2,1)}, bf16[8...) custom-call(s32[1]{0:T(128)} %bitcast.12.x_ref, bf16[4,640,128]{2,1,0:T(8,128)(2,1)} %bitcast.45, f32[1,256]{1,0:T(1,128)} %bitcast.56, ...), custom_call_target="tpu_custom_call" | custom-call | tf_op jit(solution)/shard_map/pallas_call | solution.py:28
  82.6 6.5 %all-to-all-start.2 = ((bf16[8,480,128]{2,1,0:T(8,128)(2,1)}), bf16[8,480,128]{2,1,0:T(8,128)(2,1)S(1)}, u32[]{:S(2)}, u32[]{:S(2)}) async-start(bf16[8,480,128]{2,1,0:T(8,128)(2,1)} %get-tuple-element.37), calls=%async_computation.2 | async-start | bytes 1966080 | tf_op jit(solution)/shard_map/all_to_all | solution.py:266
  89.1 0.0 all-gather.8.cloned.1.call-start
  89.1 4.6 %collective-permute-start.4 = (bf16[160,512]{1,0:T(8,128)(2,1)}, bf16[160,512]{1,0:T(8,128)(2,1)S(1)}, u32[]{:S(2)}, u32[]{:S(2)}) collective-permute-start(bf16[160,512]{1,0:T(8,128)(2,1)} %get-tuple-element.39), channel_id=1, source_target_pairs={{0,3},{1,0},{2,1},{3,2},{4,7},{5,4},{6,5},{7,6},{8,11},{9,8},{10,9... | collective-permute-start | bytes 491528 | tf_op jit(solution)/shard_map/ppermute | solution.py:287
  93.7 1.9 collective-permute-start.5
  95.6 3.5 %collective-permute-start.6 = (bf16[160,512]{1,0:T(8,128)(2,1)}, bf16[160,512]{1,0:T(8,128)(2,1)S(1)}, u32[]{:S(2)}, u32[]{:S(2)}) collective-permute-start(bf16[160,512]{1,0:T(8,128)(2,1)} %get-tuple-element.41), channel_id=1, source_target_pairs={{0,2},{1,3},{2,0},{3,1},{4,6},{5,7},{6,4},{7,5},{8,10},{9,11},{10,... | collective-permute-start | bytes 491528 | tf_op jit(solution)/shard_map/ppermute | solution.py:287
  99.2 6.9 %collective-permute-done.5.refs_1_ = bf16[160,512]{1,0:T(8,128)(2,1)S(1)} collective-permute-done((bf16[160,512]{1,0:T(8,128)(2,1)}, bf16[160,512]{1,0:T(8,128)(2,1)S(1)}, u32[]{:S(2)}, u32[]{:S(2)}) %collective-permute-start.5) | collective-permute-done | bytes 163872 | tf_op jit(solution)/shard_map/ppermute | solution.py:287
  106.1 10.7 %all-to-all-done.2.parts_ref = bf16[8,480,128]{2,1,0:T(8,128)(2,1)S(1)} async-done(((bf16[8,480,128]{2,1,0:T(8,128)(2,1)}), bf16[8,480,128]{2,1,0:T(8,128)(2,1)S(1)}, u32[]{:S(2)}, u32[]{:S(2)}) %all-to-all-start.2) | async-done | bytes 983072 | tf_op jit(solution)/shard_map/all_to_all | solution.py:266
  116.9 0.2 shard_map.132
  117.0 23.5 %all-gather.1 = bf16[3840,128]{1,0:T(8,128)(2,1)} all-gather(bf16[480,128]{1,0:T(8,128)(2,1)S(1)} %shard_map.132), channel_id=3, replica_groups=mesh['z'=8,'core'=2,'y'=8,'x'=4] {'y'}, dimensions={0}, use_global_device_ids=true | all-gather | bytes 1105920 | tf_op jit(solution)/shard_map/all_gather | solution.py:352
  140.5 0.0 all-gather.8.cloned.1.call-update
  140.5 7.2 %shard_map.133 = bf16[4,640,128]{2,1,0:T(8,128)(2,1)} custom-call(s32[1]{0:T(128)} %bitcast.12.x_ref, bf16[8,480,128]{2,1,0:T(8,128)(2,1)} %bitcast.42, f32[160,128]{1,0:T(8,128)} %get-tuple-element.43.prob_ref, bf16[4,448,1024]{2,1,0:T(8,128)(2,1)} %bitcast.40, bf16[224,1024]{1,0:T(8,128)(2,1)} %bitcast.49, bf16[224,1024]{1,0:T(8,128)(2,1)} %copy-done.1, ...), custom_call_target="tpu_custom_call" | custom-call | tf_op jit(solution)/shard_map/pallas_call | solution.py:28
  147.8 35.3 %all_to_all.25 = bf16[64,40,128]{2,1,0:T(8,128)(2,1)S(1)} all-to-all(bf16[64,40,128]{2,1,0:T(8,128)(2,1)} %bitcast.44), channel_id=1, replica_groups=mesh['z'=8,'core'=2,'y'=8,'x'=4] {'x','z','core'}, dimensions={0} | all-to-all | bytes 1310720 | tf_op jit(solution)/shard_map/all_to_all | solution.py:266
  183.1 1.4 shard_map.134
  184.5 4.8 %all-to-all-start.4 = ((bf16[16,32,512]{2,1,0:T(8,128)(2,1)}), bf16[16,32,512]{2,1,0:T(8,128)(2,1)S(1)}, u32[]{:S(2)}, u32[]{:S(2)}) async-start(bf16[16,32,512]{2,1,0:T(8,128)(2,1)} %bitcast.22), calls=%async_computation.4 | async-start | bytes 1048576 | tf_op jit(solution)/shard_map/all_to_all | solution.py:266
  189.3 11.2 %all-gather.8.cloned.1.call-done = bf16[32,480,128]{2,1,0:T(8,128)(2,1)} async-done(((bf16[8,480,128]{2,1,0:T(8,128)(2,1)}), bf16[32,480,128]{2,1,0:T(8,128)(2,1)}) %all-gather.8.cloned.1.call-update) | async-done | bytes 3932176 | tf_op jit(solution)/shard_map/all_gather | solution.py:353
  200.5 4.9 %shard_map.135 = (bf16[224,1024]{1,0:T(8,128)(2,1)}, bf16[224,1024]{1,0:T(8,128)(2,1)}, bf16[224,1024]{1,0:T(8,128)(2,1)}) custom-call(s32[1]{0:T(128)} %bitcast.12.x_ref, bf16[4,8,480,128]{3,2,1,0:T(8,128)(2,1)} %bitcast.43, bf16[160,512]{1,0:T(8,128)(2,1)} %get-tuple-element.44.refs_0_, bf16[160,512]{1,0:T(8,128)(2,1)} %copy-done.6, ...), custom_call_target="tpu_custom_call" | custom-call | tf_op jit(solution)/shard_map/pallas_call | solution.py:28
  205.5 1.2 all-to-all-done.4
  206.7 1.2 shard_map.136
  (30 shorter events, 0.1 us)
Async XLA Ops:
  7.2 23.0 %copy-start.9 = (s32[16]{0:T(128)S(1)}, s32[16]{0:T(128)}, u32[]{:S(2)}) copy-start(s32[16]{0:T(128)} %param.15) | copy-start | bytes 196
  7.2 23.0 %copy-start.8 = (s32[16,16]{1,0:T(8,128)S(1)}, s32[16,16]{1,0:T(8,128)}, u32[]{:S(2)}) copy-start(s32[16,16]{1,0:T(8,128)} %param.16) | copy-start | bytes 3076
  7.2 69.4 %all-gather.6.cloned.1.call-start = ((), (), s32[]{:S(2)}) async-start(), calls=%async_computation.5 | async-start | bytes 4587520 | tf_op jit(solution)/shard_map/all_gather | solution.py:299
  9.3 21.8 %collective-permute-start.1 = (bf16[224,1024]{1,0:T(8,128)(2,1)}, bf16[224,1024]{1,0:T(8,128)(2,1)S(1)}, u32[]{:S(2)}, u32[]{:S(2)}) collective-permute-start(bf16[224,1024]{1,0:T(8,128)(2,1)} %bitcast.46), channel_id=1, source_target_pairs={{0,3},{1,0},{2,1},{3,2},{4,7},{5,4},{6,5},{7,6},{8,11},{9,8},{10,9... | collective-permute-start | bytes 1376264 | tf_op jit(solution)/shard_map/ppermute | solution.py:287
  14.5 16.6 %collective-permute-start = (bf16[224,1024]{1,0:T(8,128)(2,1)}, bf16[224,1024]{1,0:T(8,128)(2,1)S(1)}, u32[]{:S(2)}, u32[]{:S(2)}) collective-permute-start(bf16[224,1024]{1,0:T(8,128)(2,1)} %bitcast.47), channel_id=1, source_target_pairs={{0,1},{1,2},{2,3},{3,0},{4,5},{5,6},{6,7},{7,4},{8,9},{9,10},{10,1... | collective-permute-start | bytes 1376264 | tf_op jit(solution)/shard_map/ppermute | solution.py:287
  18.9 28.6 %all-to-all-start = ((bf16[16,32,512]{2,1,0:T(8,128)(2,1)}), bf16[16,32,512]{2,1,0:T(8,128)(2,1)S(1)}, u32[]{:S(2)}, u32[]{:S(2)}) async-start(bf16[16,32,512]{2,1,0:T(8,128)(2,1)} %shard_map.128), calls=%async_computation | async-start | bytes 1048576 | tf_op jit(solution)/shard_map/all_to_all | solution.py:266
  31.2 45.4 %copy-start = (bf16[224,1024]{1,0:T(8,128)(2,1)}, bf16[224,1024]{1,0:T(8,128)(2,1)S(1)}, u32[]{:S(2)}) copy-start(bf16[224,1024]{1,0:T(8,128)(2,1)S(1)} %collective-permute-done.1.refs_3_) | copy-start | bytes 1376260
  31.2 45.4 %copy-start.1 = (bf16[224,1024]{1,0:T(8,128)(2,1)}, bf16[224,1024]{1,0:T(8,128)(2,1)S(1)}, u32[]{:S(2)}) copy-start(bf16[224,1024]{1,0:T(8,128)(2,1)S(1)} %collective-permute-done.refs_2_) | copy-start | bytes 1376260
  50.0 26.5 %all-to-all-start.1 = ((bf16[64,40,128]{2,1,0:T(8,128)(2,1)}), bf16[64,40,128]{2,1,0:T(8,128)(2,1)S(1)}, u32[]{:S(2)}, u32[]{:S(2)}) async-start(bf16[64,40,128]{2,1,0:T(8,128)(2,1)} %bitcast.13), calls=%async_computation.1 | async-start | bytes 1310720 | tf_op jit(solution)/shard_map/all_to_all | solution.py:266
  56.2 19.7 %collective-permute-start.3 = (bf16[224,512]{1,0:T(8,128)(2,1)S(1)}, bf16[224,512]{1,0:T(8,128)(2,1)S(1)}, u32[]{:S(2)}, u32[]{:S(2)}) collective-permute-start(bf16[224,512]{1,0:T(8,128)(2,1)S(1)} %slice.23), channel_id=1, source_target_pairs={{0,3},{1,0},{2,1},{3,2},{4,7},{5,4},{6,5},{7,6},{8,11},{9,8},{10,9... | collective-permute-start | bytes 688136 | tf_op jit(solution)/shard_map/ppermute | solution.py:287
  60.9 15.6 %collective-permute-start.2 = (bf16[224,512]{1,0:T(8,128)(2,1)S(1)}, bf16[224,512]{1,0:T(8,128)(2,1)S(1)}, u32[]{:S(2)}, u32[]{:S(2)}) collective-permute-start(bf16[224,512]{1,0:T(8,128)(2,1)S(1)} %slice.22), channel_id=1, source_target_pairs={{0,1},{1,2},{2,3},{3,0},{4,5},{5,6},{6,7},{7,4},{8,9},{9,10},{10,1... | collective-permute-start | bytes 688136 | tf_op jit(solution)/shard_map/ppermute | solution.py:287
  75.8 0.7 copy-start.3
  76.5 0.7 copy-start.4
  76.5 0.9 copy-start.2
  82.6 34.3 %all-to-all-start.2 = ((bf16[8,480,128]{2,1,0:T(8,128)(2,1)}), bf16[8,480,128]{2,1,0:T(8,128)(2,1)S(1)}, u32[]{:S(2)}, u32[]{:S(2)}) async-start(bf16[8,480,128]{2,1,0:T(8,128)(2,1)} %get-tuple-element.37), calls=%async_computation.2 | async-start | bytes 1966080 | tf_op jit(solution)/shard_map/all_to_all | solution.py:266
  89.1 111.5 %all-gather.8.cloned.1.call-start = ((), (), s32[]{:S(2)}) async-start(), calls=%async_computation.6 | async-start | bytes 4915200 | tf_op jit(solution)/shard_map/all_gather | solution.py:353
  89.1 10.1 %collective-permute-start.4 = (bf16[160,512]{1,0:T(8,128)(2,1)}, bf16[160,512]{1,0:T(8,128)(2,1)S(1)}, u32[]{:S(2)}, u32[]{:S(2)}) collective-permute-start(bf16[160,512]{1,0:T(8,128)(2,1)} %get-tuple-element.39), channel_id=1, source_target_pairs={{0,3},{1,0},{2,1},{3,2},{4,7},{5,4},{6,5},{7,6},{8,11},{9,8},{10,9... | collective-permute-start | bytes 491528 | tf_op jit(solution)/shard_map/ppermute | solution.py:287
  93.7 12.4 %collective-permute-start.5 = (bf16[160,512]{1,0:T(8,128)(2,1)}, bf16[160,512]{1,0:T(8,128)(2,1)S(1)}, u32[]{:S(2)}, u32[]{:S(2)}) collective-permute-start(bf16[160,512]{1,0:T(8,128)(2,1)} %get-tuple-element.40), channel_id=1, source_target_pairs={{0,1},{1,2},{2,3},{3,0},{4,5},{5,6},{6,7},{7,4},{8,9},{9,10},{10,1... | collective-permute-start | bytes 491528 | tf_op jit(solution)/shard_map/ppermute | solution.py:287
  95.6 10.5 %collective-permute-start.6 = (bf16[160,512]{1,0:T(8,128)(2,1)}, bf16[160,512]{1,0:T(8,128)(2,1)S(1)}, u32[]{:S(2)}, u32[]{:S(2)}) collective-permute-start(bf16[160,512]{1,0:T(8,128)(2,1)} %get-tuple-element.41), channel_id=1, source_target_pairs={{0,2},{1,3},{2,0},{3,1},{4,6},{5,7},{6,4},{7,5},{8,10},{9,11},{10,... | collective-permute-start | bytes 491528 | tf_op jit(solution)/shard_map/ppermute | solution.py:287
  99.2 48.6 %copy-start.5 = (bf16[160,512]{1,0:T(8,128)(2,1)}, bf16[160,512]{1,0:T(8,128)(2,1)S(1)}, u32[]{:S(2)}) copy-start(bf16[160,512]{1,0:T(8,128)(2,1)S(1)} %collective-permute-done.4.refs_3_) | copy-start | bytes 491524
  106.1 41.7 %copy-start.6 = (bf16[160,512]{1,0:T(8,128)(2,1)}, bf16[160,512]{1,0:T(8,128)(2,1)S(1)}, u32[]{:S(2)}) copy-start(bf16[160,512]{1,0:T(8,128)(2,1)S(1)} %collective-permute-done.5.refs_1_) | copy-start | bytes 491524
  106.1 41.7 %copy-start.7 = (bf16[160,512]{1,0:T(8,128)(2,1)}, bf16[160,512]{1,0:T(8,128)(2,1)S(1)}, u32[]{:S(2)}) copy-start(bf16[160,512]{1,0:T(8,128)(2,1)S(1)} %collective-permute-done.6.refs_2_) | copy-start | bytes 491524
  184.5 22.1 %all-to-all-start.4 = ((bf16[16,32,512]{2,1,0:T(8,128)(2,1)}), bf16[16,32,512]{2,1,0:T(8,128)(2,1)S(1)}, u32[]{:S(2)}, u32[]{:S(2)}) async-start(bf16[16,32,512]{2,1,0:T(8,128)(2,1)} %bitcast.22), calls=%async_computation.4 | async-start | bytes 1048576 | tf_op jit(solution)/shard_map/all_to_all | solution.py:266
Sparse Core Ops, SparseCore 0:
  10.1 65.0 all-gather.5
  140.6 59.8 all-gather.7

commit v12 on v10

--- a/solution.py
+++ b/solution.py
@@ -171,10 +171,15 @@
 
 
 def weight_kernel(x_ref, act_ref, *refs):
-    row_refs, out_refs, (buf_ref, sems) = refs[:4], refs[4:7], refs[7:]
+    sources, out_refs, (buf_ref, row_refs, sems, row_sems) = refs[:4], refs[4:7], refs[7:]
     width = out_refs[0].shape[0]
-    count = row_refs[0].shape[0]
+    count = row_refs.shape[1]
     parts = (1, 2, 0)
+    row_copies = [
+        pltpu.make_async_copy(sources[d], row_refs.at[d], row_sems.at[d]) for d in range(4)
+    ]
+    for copy in row_copies:
+        copy.start()
     copies = [
         [
             pltpu.make_async_copy(
@@ -189,8 +194,10 @@
     for group in copies:
         for copy in group:
             copy.start()
+    for copy in row_copies:
+        copy.wait()
     x, grad = (
-        jnp.concatenate([ref[:, lane : lane + width] for ref in row_refs], axis=0)
+        jnp.concatenate([row_refs[d, :, lane : lane + width] for d in range(4)], axis=0)
         for lane in (0, DY_LANE)
     )
     for i, part in enumerate(parts):
@@ -338,10 +345,12 @@
         (jax.ShapeDtypeStruct((width, hid), BF16),) * 3,
         (order, all_act, *(rows[STEPS.index(d)] for d in range(share_x))),
         VMEM_LARGE,
-        in_specs=[scalar_spec, panel_specs[0]] + [vmem_spec] * 4,
+        in_specs=[scalar_spec] + [panel_specs[0]] * 5,
         scratch_shapes=[
             pltpu.VMEM((3, share_x, share_y, count, hid // share_y), BF16),
+            pltpu.VMEM((share_x, count, LANES), BF16),
             pltpu.SemaphoreType.DMA((3, share_x)),
+            pltpu.SemaphoreType.DMA((share_x,)),
         ],
     )
     back = exchange(results.reshape(pieces), OWNERS).reshape(4 * total, 128)

time: 216 us -> 216 us (level)
  transfers between devices with their start and end apart: 13 -> 13, of which waited for: 7 -> 7; matrix products, arithmetic and copies ran while one was open for 1% -> 1% of each run, Pallas kernels for 9% -> 8%
where the time goes in v12:
time: 216 us; the launch traced here: 215 us
  waiting for transfers between devices  59.4 us (28%)
  blocking collectives  58.5 us (27%)
  starting transfers between devices  52.9 us (24%)
  Pallas kernels  24.5 us (11%)
  between operations  14.4 us (7%)
  other arithmetic  3.36 us (2%)
    all_to_all x1, blocking collectives, exchange(): return lax.all_to_all(array, axis, split_axis=0, concat_axis=0, tiled=True)  35.1 us
    all_to_all x4, starting transfers between devices, exchange(): return lax.all_to_all(array, axis, split_axis=0, concat_axis=0, tiled=True)  29 us
    all_to_all x4, waiting for transfers between devices, exchange(): return lax.all_to_all(array, axis, split_axis=0, concat_axis=0, tiled=True)  28.5 us
    pallas_call x8, Pallas kernels, call(): pl.pallas_call(kernel, out_shape=out_shape, compiler_params=pltpu.Compile...  24.5 us
    ppermute x7, starting transfers between devices, shift(): return lax.ppermute(array, 'x', shifts[d])  23.8 us
    all_gather x1, blocking collectives, body(): act = lax.all_gather(act, 'y', axis=0, tiled=False)  23.5 us
    ppermute x7, waiting for transfers between devices, shift(): return lax.ppermute(array, 'x', shifts[d])  19.6 us
    all_gather x1, waiting for transfers between devices, body(): all_act = lax.all_gather(act, 'x', axis=0, tiled=False)  11.3 us
  transfers between devices with their start and end apart: 13, of which 7 were waited for; matrix products, arithmetic and copies ran while one was open for 1% of the time, Pallas kernels for 8%

profile of v12, /device:TPU:1, one launch (start us, length us, event | category | flops | bytes accessed | tf_op | source)
XLA Modules:
  0.0 214.7 jit_solution(6097635428966710254)
XLA Ops:
  7.2 0.0 copy-start.3
  7.2 0.0 all-gather.6.cloned.1.call-start
  7.2 2.2 %pad_maximum_fusion = bf16[448,1024]{1,0:T(8,128)(2,1)} fusion(bf16[224,1024]{1,0:T(8,128)(2,1)} %bitcast.50, bf16[224,1024]{1,0:T(8,128)(2,1)} %bitcast.51), kind=kLoop, calls=%fused_computation | loop fusion | flops 1835008 | bytes 1835008 | tf_op jit(solution)/shard_map/concatenate | solution.py:278
  9.4 0.0 all-gather.6.cloned.1.call-update
  9.5 5.2 %collective-permute-start.1 = (bf16[224,1024]{1,0:T(8,128)(2,1)S(1)}, bf16[224,1024]{1,0:T(8,128)(2,1)S(1)}, u32[]{:S(2)}, u32[]{:S(2)}) collective-permute-start(bf16[224,1024]{1,0:T(8,128)(2,1)S(1)} %bitcast.48), channel_id=1, source_target_pairs={{0,3},{1,0},{2,1},{3,2},{4,7},{5,4},{6,5},{7,6},{8,11},{9,8},{10,9... | collective-permute-start | bytes 1376264 | tf_op jit(solution)/shard_map/ppermute | solution.py:276
  14.7 1.9 collective-permute-start
  16.6 2.4 %shard_map.128 = bf16[16,32,512]{2,1,0:T(8,128)(2,1)} custom-call(bf16[224,512]{1,0:T(8,128)(2,1)} %bitcast.52, bf16[224,512]{1,0:T(8,128)(2,1)} %bitcast.53, bf16[16,512]{1,0:T(8,128)(2,1)} %bitcast.54, s32[10,1,16]{2,1,0:T(1,128)} %bitcast.55), custom_call_target="tpu_custom_call" | custom-call | tf_op jit(solution)/shard_map/pallas_call | solution.py:28
  19.0 11.3 %all-to-all-start = ((bf16[16,32,512]{2,1,0:T(8,128)(2,1)}), bf16[16,32,512]{2,1,0:T(8,128)(2,1)S(1)}, u32[]{:S(2)}, u32[]{:S(2)}) async-start(bf16[16,32,512]{2,1,0:T(8,128)(2,1)} %shard_map.128), calls=%async_computation | async-start | bytes 1048576 | tf_op jit(solution)/shard_map/all_to_all | solution.py:255
  30.3 0.1 fusion.5
  30.3 0.1 multiply_reduce_fusion.1
  30.5 0.1 multiply_reduce_fusion
  30.6 0.1 select_reduce_fusion
  30.7 0.1 fusion
  30.8 0.1 reshape.243
  31.0 0.1 reshape.250
  31.1 0.1 reshape.247
  31.3 0.0 copy-start
  31.3 16.3 %all-to-all-done = bf16[16,32,512]{2,1,0:T(8,128)(2,1)S(1)} async-done(((bf16[16,32,512]{2,1,0:T(8,128)(2,1)}), bf16[16,32,512]{2,1,0:T(8,128)(2,1)S(1)}, u32[]{:S(2)}, u32[]{:S(2)}) %all-to-all-start) | async-done | bytes 524320 | tf_op jit(solution)/shard_map/all_to_all | solution.py:255
  47.6 0.2 copy.18.info_ref
  47.8 2.4 %shard_map.129 = (bf16[2560,128]{1,0:T(8,128)(2,1)}, bf16[640,512]{1,0:T(8,128)(2,1)S(1)}) custom-call(bf16[512,512]{1,0:T(8,128)(2,1)S(1)} %bitcast.37, s32[640,3]{1,0:T(8,128)S(1)} %copy.18.info_ref), custom_call_target="tpu_custom_call" | custom-call | tf_op jit(solution)/shard_map/pallas_call | solution.py:28
  50.1 6.1 %all-to-all-start.1 = ((bf16[64,40,128]{2,1,0:T(8,128)(2,1)}), bf16[64,40,128]{2,1,0:T(8,128)(2,1)S(1)}, u32[]{:S(2)}, u32[]{:S(2)}) async-start(bf16[64,40,128]{2,1,0:T(8,128)(2,1)} %bitcast.13), calls=%async_computation.1 | async-start | bytes 1310720 | tf_op jit(solution)/shard_map/all_to_all | solution.py:255
  56.3 4.7 %collective-permute-start.3 = (bf16[224,512]{1,0:T(8,128)(2,1)S(1)}, bf16[224,512]{1,0:T(8,128)(2,1)S(1)}, u32[]{:S(2)}, u32[]{:S(2)}) collective-permute-start(bf16[224,512]{1,0:T(8,128)(2,1)S(1)} %slice.23), channel_id=1, source_target_pairs={{0,3},{1,0},{2,1},{3,2},{4,7},{5,4},{6,5},{7,6},{8,11},{9,8},{10,9... | collective-permute-start | bytes 688136 | tf_op jit(solution)/shard_map/ppermute | solution.py:276
  61.0 1.9 collective-permute-start.2
  63.0 0.7 pad_convert_fusion
  63.6 12.2 %collective-permute-done.3.refs_5_ = bf16[224,512]{1,0:T(8,128)(2,1)S(1)} collective-permute-done((bf16[224,512]{1,0:T(8,128)(2,1)S(1)}, bf16[224,512]{1,0:T(8,128)(2,1)S(1)}, u32[]{:S(2)}, u32[]{:S(2)}) %collective-permute-start.3) | collective-permute-done | bytes 229408 | tf_op jit(solution)/shard_map/ppermute | solution.py:276
  75.8 0.7 collective-permute-done.2.refs_4_
  76.5 0.0 all-gather.6.cloned.1.call-done
  76.6 0.6 copy-done.5
  77.2 0.2 copy-done.2
  77.4 5.1 %shard_map.130 = (bf16[160,512]{1,0:T(8,128)(2,1)}, bf16[160,512]{1,0:T(8,128)(2,1)}, bf16[160,512]{1,0:T(8,128)(2,1)}, bf16[160,512]{1,0:T(8,128)(2,1)}, bf16[8...) custom-call(s32[1]{0:T(128)} %bitcast.12.x_ref, bf16[4,640,128]{2,1,0:T(8,128)(2,1)} %bitcast.45, f32[1,256]{1,0:T(1,128)} %bitcast.56, ...), custom_call_target="tpu_custom_call" | custom-call | tf_op jit(solution)/shard_map/pallas_call | solution.py:28
  82.6 6.8 %all-to-all-start.2 = ((bf16[8,480,128]{2,1,0:T(8,128)(2,1)}), bf16[8,480,128]{2,1,0:T(8,128)(2,1)S(1)}, u32[]{:S(2)}, u32[]{:S(2)}) async-start(bf16[8,480,128]{2,1,0:T(8,128)(2,1)} %get-tuple-element.37), calls=%async_computation.2 | async-start | bytes 1966080 | tf_op jit(solution)/shard_map/all_to_all | solution.py:255
  89.3 0.0 all-gather.8.cloned.1.call-start
  89.4 4.6 %collective-permute-start.4 = (bf16[160,512]{1,0:T(8,128)(2,1)S(1)}, bf16[160,512]{1,0:T(8,128)(2,1)S(1)}, u32[]{:S(2)}, u32[]{:S(2)}) collective-permute-start(bf16[160,512]{1,0:T(8,128)(2,1)S(1)} %copy-done.13), channel_id=1, source_target_pairs={{0,3},{1,0},{2,1},{3,2},{4,7},{5,4},{6,5},{7,6},{8,11},{9,8},{10,9... | collective-permute-start | bytes 491528 | tf_op jit(solution)/shard_map/ppermute | solution.py:276
  94.0 1.9 collective-permute-start.5
  95.9 3.5 %collective-permute-start.6 = (bf16[160,512]{1,0:T(8,128)(2,1)S(1)}, bf16[160,512]{1,0:T(8,128)(2,1)S(1)}, u32[]{:S(2)}, u32[]{:S(2)}) collective-permute-start(bf16[160,512]{1,0:T(8,128)(2,1)S(1)} %copy-done.11), channel_id=1, source_target_pairs={{0,2},{1,3},{2,0},{3,1},{4,6},{5,7},{6,4},{7,5},{8,10},{9,11},{10,... | collective-permute-start | bytes 491528 | tf_op jit(solution)/shard_map/ppermute | solution.py:276
  99.5 6.7 %collective-permute-done.5.refs_1_ = bf16[160,512]{1,0:T(8,128)(2,1)S(1)} collective-permute-done((bf16[160,512]{1,0:T(8,128)(2,1)S(1)}, bf16[160,512]{1,0:T(8,128)(2,1)S(1)}, u32[]{:S(2)}, u32[]{:S(2)}) %collective-permute-start.5) | collective-permute-done | bytes 163872 | tf_op jit(solution)/shard_map/ppermute | solution.py:276
  106.2 10.9 %all-to-all-done.2.parts_ref = bf16[8,480,128]{2,1,0:T(8,128)(2,1)S(1)} async-done(((bf16[8,480,128]{2,1,0:T(8,128)(2,1)}), bf16[8,480,128]{2,1,0:T(8,128)(2,1)S(1)}, u32[]{:S(2)}, u32[]{:S(2)}) %all-to-all-start.2) | async-done | bytes 983072 | tf_op jit(solution)/shard_map/all_to_all | solution.py:255
  117.1 0.2 shard_map.131
  117.3 23.5 %all-gather.1 = bf16[3840,128]{1,0:T(8,128)(2,1)} all-gather(bf16[480,128]{1,0:T(8,128)(2,1)S(1)} %shard_map.131), channel_id=3, replica_groups=mesh['z'=8,'core'=2,'y'=8,'x'=4] {'y'}, dimensions={0}, use_global_device_ids=true | all-gather | bytes 1105920 | tf_op jit(solution)/shard_map/all_gather | solution.py:332
  140.8 0.0 all-gather.8.cloned.1.call-update
  140.8 7.2 %shard_map.132 = bf16[4,640,128]{2,1,0:T(8,128)(2,1)} custom-call(s32[1]{0:T(128)} %bitcast.12.x_ref, bf16[8,480,128]{2,1,0:T(8,128)(2,1)} %bitcast.42, f32[160,128]{1,0:T(8,128)} %get-tuple-element.43.prob_ref, bf16[4,448,1024]{2,1,0:T(8,128)(2,1)} %bitcast.40, bf16[224,1024]{1,0:T(8,128)(2,1)} %bitcast.47, bf16[224,1024]{1,0:T(8,128)(2,1)} %copy-done.1, ...), custom_call_target="tpu_custom_call" | custom-call | tf_op jit(solution)/shard_map/pallas_call | solution.py:28
  148.0 35.1 %all_to_all.25 = bf16[64,40,128]{2,1,0:T(8,128)(2,1)S(1)} all-to-all(bf16[64,40,128]{2,1,0:T(8,128)(2,1)} %bitcast.44), channel_id=1, replica_groups=mesh['z'=8,'core'=2,'y'=8,'x'=4] {'x','z','core'}, dimensions={0} | all-to-all | bytes 1310720 | tf_op jit(solution)/shard_map/all_to_all | solution.py:255
  183.1 1.4 shard_map.133
  184.5 4.8 %all-to-all-start.4 = ((bf16[16,32,512]{2,1,0:T(8,128)(2,1)}), bf16[16,32,512]{2,1,0:T(8,128)(2,1)S(1)}, u32[]{:S(2)}, u32[]{:S(2)}) async-start(bf16[16,32,512]{2,1,0:T(8,128)(2,1)} %bitcast.22), calls=%async_computation.4 | async-start | bytes 1048576 | tf_op jit(solution)/shard_map/all_to_all | solution.py:255
  189.3 11.3 %all-gather.8.cloned.1.call-done = bf16[32,480,128]{2,1,0:T(8,128)(2,1)} async-done(((bf16[8,480,128]{2,1,0:T(8,128)(2,1)}), bf16[32,480,128]{2,1,0:T(8,128)(2,1)}) %all-gather.8.cloned.1.call-update) | async-done | bytes 3932176 | tf_op jit(solution)/shard_map/all_gather | solution.py:333
  200.6 4.7 %shard_map.134 = (bf16[224,1024]{1,0:T(8,128)(2,1)}, bf16[224,1024]{1,0:T(8,128)(2,1)}, bf16[224,1024]{1,0:T(8,128)(2,1)}) custom-call(s32[1]{0:T(128)} %bitcast.12.x_ref, bf16[4,8,480,128]{3,2,1,0:T(8,128)(2,1)} %bitcast.43, bf16[160,512]{1,0:T(8,128)(2,1)} %get-tuple-element.44.refs_0_, bf16[160,512]{1,0:T(8,128)(2,1)} %copy-done.7, ...), custom_call_target="tpu_custom_call" | custom-call | tf_op jit(solution)/shard_map/pallas_call | solution.py:28
  205.3 1.3 all-to-all-done.4
  206.7 1.2 shard_map.135
  (38 shorter events, 0.2 us)
Async XLA Ops:
  7.2 2.3 %copy-start.3 = (bf16[1,1024,224]{1,2,0:T(8,128)(2,1)S(1)}, bf16[1,1024,224]{1,2,0:T(8,128)(2,1)}, u32[]{:S(2)}) copy-start(bf16[1,1024,224]{1,2,0:T(8,128)(2,1)} %param.14) | copy-start | bytes 1376260
  7.2 69.4 %all-gather.6.cloned.1.call-start = ((), (), s32[]{:S(2)}) async-start(), calls=%async_computation.5 | async-start | bytes 4587520 | tf_op jit(solution)/shard_map/all_gather | solution.py:279
  9.4 20.9 %copy-start.10 = (s32[16]{0:T(128)S(1)}, s32[16]{0:T(128)}, u32[]{:S(2)}) copy-start(s32[16]{0:T(128)} %param.15) | copy-start | bytes 196
  9.4 20.9 %copy-start.9 = (s32[16,16]{1,0:T(8,128)S(1)}, s32[16,16]{1,0:T(8,128)}, u32[]{:S(2)}) copy-start(s32[16,16]{1,0:T(8,128)} %param.16) | copy-start | bytes 3076
  9.5 21.8 %collective-permute-start.1 = (bf16[224,1024]{1,0:T(8,128)(2,1)S(1)}, bf16[224,1024]{1,0:T(8,128)(2,1)S(1)}, u32[]{:S(2)}, u32[]{:S(2)}) collective-permute-start(bf16[224,1024]{1,0:T(8,128)(2,1)S(1)} %bitcast.48), channel_id=1, source_target_pairs={{0,3},{1,0},{2,1},{3,2},{4,7},{5,4},{6,5},{7,6},{8,11},{9,8},{10,9... | collective-permute-start | bytes 1376264 | tf_op jit(solution)/shard_map/ppermute | solution.py:276
  14.7 16.6 %collective-permute-start = (bf16[224,1024]{1,0:T(8,128)(2,1)S(1)}, bf16[224,1024]{1,0:T(8,128)(2,1)S(1)}, u32[]{:S(2)}, u32[]{:S(2)}) collective-permute-start(bf16[224,1024]{1,0:T(8,128)(2,1)S(1)} %bitcast.49), channel_id=1, source_target_pairs={{0,1},{1,2},{2,3},{3,0},{4,5},{5,6},{6,7},{7,4},{8,9},{9,10},{10,1... | collective-permute-start | bytes 1376264 | tf_op jit(solution)/shard_map/ppermute | solution.py:276
  19.0 28.6 %all-to-all-start = ((bf16[16,32,512]{2,1,0:T(8,128)(2,1)}), bf16[16,32,512]{2,1,0:T(8,128)(2,1)S(1)}, u32[]{:S(2)}, u32[]{:S(2)}) async-start(bf16[16,32,512]{2,1,0:T(8,128)(2,1)} %shard_map.128), calls=%async_computation | async-start | bytes 1048576 | tf_op jit(solution)/shard_map/all_to_all | solution.py:255
  31.3 45.3 %copy-start = (bf16[224,1024]{1,0:T(8,128)(2,1)}, bf16[224,1024]{1,0:T(8,128)(2,1)S(1)}, u32[]{:S(2)}) copy-start(bf16[224,1024]{1,0:T(8,128)(2,1)S(1)} %collective-permute-done.1.refs_3_) | copy-start | bytes 1376260
  31.3 45.2 %copy-start.1 = (bf16[224,1024]{1,0:T(8,128)(2,1)}, bf16[224,1024]{1,0:T(8,128)(2,1)S(1)}, u32[]{:S(2)}) copy-start(bf16[224,1024]{1,0:T(8,128)(2,1)S(1)} %collective-permute-done.refs_2_) | copy-start | bytes 1376260
  50.1 26.4 %all-to-all-start.1 = ((bf16[64,40,128]{2,1,0:T(8,128)(2,1)}), bf16[64,40,128]{2,1,0:T(8,128)(2,1)S(1)}, u32[]{:S(2)}, u32[]{:S(2)}) async-start(bf16[64,40,128]{2,1,0:T(8,128)(2,1)} %bitcast.13), calls=%async_computation.1 | async-start | bytes 1310720 | tf_op jit(solution)/shard_map/all_to_all | solution.py:255
  56.3 19.5 %collective-permute-start.3 = (bf16[224,512]{1,0:T(8,128)(2,1)S(1)}, bf16[224,512]{1,0:T(8,128)(2,1)S(1)}, u32[]{:S(2)}, u32[]{:S(2)}) collective-permute-start(bf16[224,512]{1,0:T(8,128)(2,1)S(1)} %slice.23), channel_id=1, source_target_pairs={{0,3},{1,0},{2,1},{3,2},{4,7},{5,4},{6,5},{7,6},{8,11},{9,8},{10,9... | collective-permute-start | bytes 688136 | tf_op jit(solution)/shard_map/ppermute | solution.py:276
  61.0 15.5 %collective-permute-start.2 = (bf16[224,512]{1,0:T(8,128)(2,1)S(1)}, bf16[224,512]{1,0:T(8,128)(2,1)S(1)}, u32[]{:S(2)}, u32[]{:S(2)}) collective-permute-start(bf16[224,512]{1,0:T(8,128)(2,1)S(1)} %slice.22), channel_id=1, source_target_pairs={{0,1},{1,2},{2,3},{3,0},{4,5},{5,6},{6,7},{7,4},{8,9},{9,10},{10,1... | collective-permute-start | bytes 688136 | tf_op jit(solution)/shard_map/ppermute | solution.py:276
  75.8 0.7 copy-start.4
  76.5 0.7 copy-start.5
  76.5 0.9 copy-start.2
  82.5 6.8 %copy-start.13 = (bf16[160,512]{1,0:T(8,128)(2,1)S(1)}, bf16[160,512]{1,0:T(8,128)(2,1)}, u32[]{:S(2)}) copy-start(bf16[160,512]{1,0:T(8,128)(2,1)} %get-tuple-element.39) | copy-start | bytes 491524
  82.6 11.4 %copy-start.12 = (bf16[160,512]{1,0:T(8,128)(2,1)S(1)}, bf16[160,512]{1,0:T(8,128)(2,1)}, u32[]{:S(2)}) copy-start(bf16[160,512]{1,0:T(8,128)(2,1)} %get-tuple-element.40) | copy-start | bytes 491524
  82.6 13.3 %copy-start.11 = (bf16[160,512]{1,0:T(8,128)(2,1)S(1)}, bf16[160,512]{1,0:T(8,128)(2,1)}, u32[]{:S(2)}) copy-start(bf16[160,512]{1,0:T(8,128)(2,1)} %get-tuple-element.41) | copy-start | bytes 491524
  82.6 34.5 %all-to-all-start.2 = ((bf16[8,480,128]{2,1,0:T(8,128)(2,1)}), bf16[8,480,128]{2,1,0:T(8,128)(2,1)S(1)}, u32[]{:S(2)}, u32[]{:S(2)}) async-start(bf16[8,480,128]{2,1,0:T(8,128)(2,1)} %get-tuple-element.37), calls=%async_computation.2 | async-start | bytes 1966080 | tf_op jit(solution)/shard_map/all_to_all | solution.py:255
  89.3 111.2 %all-gather.8.cloned.1.call-start = ((), (), s32[]{:S(2)}) async-start(), calls=%async_computation.6 | async-start | bytes 4915200 | tf_op jit(solution)/shard_map/all_gather | solution.py:333
  89.4 10.1 %collective-permute-start.4 = (bf16[160,512]{1,0:T(8,128)(2,1)S(1)}, bf16[160,512]{1,0:T(8,128)(2,1)S(1)}, u32[]{:S(2)}, u32[]{:S(2)}) collective-permute-start(bf16[160,512]{1,0:T(8,128)(2,1)S(1)} %copy-done.13), channel_id=1, source_target_pairs={{0,3},{1,0},{2,1},{3,2},{4,7},{5,4},{6,5},{7,6},{8,11},{9,8},{10,9... | collective-permute-start | bytes 491528 | tf_op jit(solution)/shard_map/ppermute | solution.py:276
  94.0 12.2 %collective-permute-start.5 = (bf16[160,512]{1,0:T(8,128)(2,1)S(1)}, bf16[160,512]{1,0:T(8,128)(2,1)S(1)}, u32[]{:S(2)}, u32[]{:S(2)}) collective-permute-start(bf16[160,512]{1,0:T(8,128)(2,1)S(1)} %copy-done.12), channel_id=1, source_target_pairs={{0,1},{1,2},{2,3},{3,0},{4,5},{5,6},{6,7},{7,4},{8,9},{9,10},{10,1... | collective-permute-start | bytes 491528 | tf_op jit(solution)/shard_map/ppermute | solution.py:276
  95.9 10.3 %collective-permute-start.6 = (bf16[160,512]{1,0:T(8,128)(2,1)S(1)}, bf16[160,512]{1,0:T(8,128)(2,1)S(1)}, u32[]{:S(2)}, u32[]{:S(2)}) collective-permute-start(bf16[160,512]{1,0:T(8,128)(2,1)S(1)} %copy-done.11), channel_id=1, source_target_pairs={{0,2},{1,3},{2,0},{3,1},{4,6},{5,7},{6,4},{7,5},{8,10},{9,11},{10,... | collective-permute-start | bytes 491528 | tf_op jit(solution)/shard_map/ppermute | solution.py:276
  99.5 48.5 %copy-start.6 = (bf16[160,512]{1,0:T(8,128)(2,1)}, bf16[160,512]{1,0:T(8,128)(2,1)S(1)}, u32[]{:S(2)}) copy-start(bf16[160,512]{1,0:T(8,128)(2,1)S(1)} %collective-permute-done.4.refs_3_) | copy-start | bytes 491524
  106.2 41.8 %copy-start.7 = (bf16[160,512]{1,0:T(8,128)(2,1)}, bf16[160,512]{1,0:T(8,128)(2,1)S(1)}, u32[]{:S(2)}) copy-start(bf16[160,512]{1,0:T(8,128)(2,1)S(1)} %collective-permute-done.5.refs_1_) | copy-start | bytes 491524
  106.2 41.8 %copy-start.8 = (bf16[160,512]{1,0:T(8,128)(2,1)}, bf16[160,512]{1,0:T(8,128)(2,1)S(1)}, u32[]{:S(2)}) copy-start(bf16[160,512]{1,0:T(8,128)(2,1)S(1)} %collective-permute-done.6.refs_2_) | copy-start | bytes 491524
  184.5 22.2 %all-to-all-start.4 = ((bf16[16,32,512]{2,1,0:T(8,128)(2,1)}), bf16[16,32,512]{2,1,0:T(8,128)(2,1)S(1)}, u32[]{:S(2)}, u32[]{:S(2)}) async-start(bf16[16,32,512]{2,1,0:T(8,128)(2,1)} %bitcast.22), calls=%async_computation.4 | async-start | bytes 1048576 | tf_op jit(solution)/shard_map/all_to_all | solution.py:255
Sparse Core Ops, SparseCore 0:
  10.1 64.8 all-gather.5
  140.9 59.6 all-gather.7
